TPU v7x, 32 devices: a whole 2x2x4 slice. The times are simulated.
32 devices in a mesh: dp: 8 (over z, y), cls: 4 (over x, core).
Axes of the slice: x: 2, y: 2, z: 4, core: 2. Of those that a mesh axis runs over, the one named last changes fastest.
Arguments:
- patches: bfloat16 [32768, 768], P(('dp', 'cls')), may hold values from -6 to 6
- image_ids: int32 [32, 1024], P(('dp', 'cls')), may hold values from 0 to 7, never falling along the last dimension, each value on 1 to 196 neighbouring positions
- keep: int32 [32, 1024], P(('dp', 'cls')), may hold values 0 or 1
- labels: int32 [256, 2], P('dp'), may hold values from 0 to 21842
- owner: int32 [52], replicated, may hold values from 0 to 55, as said below
- step: int32 [], replicated, may hold values from 2 to 20
- enc_weights: float32 [13, 768, 768], P(None, 'dp')
- stats_left: float32 [13, 768, 768], P(None, 'dp')
- stats_right: float32 [13, 768, 768], P(None, 'dp')
- root_left: float32 [13, 768, 768], P(None, 'dp')
- root_right: float32 [13, 768, 768], P(None, 'dp')
- head_weights: float32 [768, 21848], P('dp', 'cls'), may hold values from -0.21875 to 0.21875
- head_m: float32 [768, 21848], P('dp', 'cls'), may hold values from -0.0001 to 0.0001
- head_v: float32 [768, 21848], P('dp', 'cls'), may hold values from 6e-11 to 2.4e-10
- vectors: float32 [15, 768], P(None, 'dp')
- vec_m: float32 [15, 768], P(None, 'dp'), may hold values from -0.0005 to 0.0005
- vec_v: float32 [15, 768], P(None, 'dp'), may hold values from 1e-09 to 4e-09
Outputs:
- loss: float32 [], replicated
- grad_norm: float32 [], replicated
- new_enc_weights: float32 [13, 768, 768], P(None, 'dp')
- enc_grad: float32 [13, 768, 768], P(None, 'dp')
- new_stats_left: float32 [13, 768, 768], P(None, 'dp')
- new_stats_right: float32 [13, 768, 768], P(None, 'dp')
- new_vectors: float32 [15, 768], P(None, 'dp')
- new_vec_m: float32 [15, 768], P(None, 'dp')
- new_vec_v: float32 [15, 768], P(None, 'dp')
- new_head: float32 [768, 21848], P('dp', 'cls')
- new_head_m: float32 [768, 21848], P('dp', 'cls')
- new_head_v: float32 [768, 21848], P('dp', 'cls')
Inputs may be any that keep to these rules, and one draw needn't show every extreme that they name: `owner`: distinct slot numbers; the block with slot s is owned by index s // 7 of dp, so no index owns more than 7 blocks; one block has slot 0 and one has the last slot.
All inputs are finite; a program needn't handle non-finite values. No bound on the sum of `keep` on one device may be relied on, other than what follows from the above.
Results may differ from a plain program's by a relative error of at most 0.0008.
The roundings to bfloat16 on the way count: a program that leaves them out, or rounds other values in their place, can miss the bound.
Values may be sent and summed in bfloat16 or wider, within the bound.
A program may use at most 320 MiB of HBM per device.

v0:
```python
import jax
import jax.numpy as jnp
from jax import lax
from jax.sharding import PartitionSpec as P

HEADS = 12
HEAD = 64
LABELS_REAL = 21843
LEN = 1024
QBLOCK = 512
IMG_PACK = 8


FULL_PRECISION = lax.Precision.HIGHEST
NORM_EPS = 1e-06
CLIP_NORM = 1.0
ADAM_RATE = 0.02
SHAMPOO_RATE = 0.01
BETA_FIRST = 0.9
BETA_SECOND = 0.999
ADAM_EPS = 1e-08
WEIGHT_DECAY = 0.1
ROOT_EPS = 1e-06


def norm_rows(values, gain, shift):
    centred = values - jnp.mean(values, -1, keepdims=True)
    spread = jnp.mean(centred * centred, -1, keepdims=True)
    return centred * lax.rsqrt(spread + NORM_EPS) * gain + shift


def gelu_exact(values):
    return jax.nn.gelu(values, approximate=False)


def pool_rows(output, gain, shift, pack_ids, pack_keep):
    final = norm_rows(output, gain, shift)
    member = (
        (pack_ids[None, :] == jnp.arange(IMG_PACK)[:, None]) & (pack_keep[None, :] == 1)
    ).astype(jnp.float32)
    counted = jnp.maximum(jnp.sum(member, 1), 1.0)
    return jnp.dot(member, final, precision=FULL_PRECISION) / counted[:, None]


def masked_scores(qkv_rows, pack_ids, pack_keep, row_start):
    length = qkv_rows.shape[1]
    queries = lax.dynamic_slice_in_dim(qkv_rows[0], row_start, QBLOCK, 0).reshape(
        QBLOCK, HEADS, HEAD
    )
    keys_all = qkv_rows[1].reshape(length, HEADS, HEAD)
    scores = jnp.einsum(
        "qhd,khd->hqk", queries, keys_all, preferred_element_type=jnp.float32
    ) * HEAD ** (-0.5)
    query_ids = lax.dynamic_slice_in_dim(pack_ids, row_start, QBLOCK, 0)
    key_pos = jnp.arange(length)
    query_pos = row_start + jnp.arange(QBLOCK)
    allowed = (query_ids[:, None] == pack_ids[None, :]) & (
        (pack_keep[None, :] == 1) | (query_pos[:, None] == key_pos[None, :])
    )
    return (jnp.where(allowed[None], scores, -1e30), queries, keys_all)


def attention_forward(qkv_rows, pack_ids, pack_keep):
    length = qkv_rows.shape[1]
    values_all = qkv_rows[2].reshape(length, HEADS, HEAD)

    def block_out(row_start):
        scores, queries, keys_all = masked_scores(qkv_rows, pack_ids, pack_keep, row_start)
        row_top = jnp.max(scores, -1, keepdims=True)
        exp_scores = jnp.exp(scores - row_top)
        totals = jnp.sum(exp_scores, -1, keepdims=True)
        probs = (exp_scores / totals).astype(jnp.bfloat16)
        attended = jnp.einsum("hqk,khd->qhd", probs, values_all, preferred_element_type=jnp.float32)
        return (
            attended.reshape(QBLOCK, HEADS * HEAD).astype(jnp.bfloat16),
            (row_top + jnp.log(totals))[..., 0],
        )

    attended, log_totals = lax.map(block_out, jnp.arange(length // QBLOCK) * QBLOCK)
    return (attended.reshape(length, HEADS * HEAD), log_totals)


def attention_backward(qkv_rows, pack_ids, pack_keep, log_totals, grad_attended):
    length = qkv_rows.shape[1]
    values_all = qkv_rows[2].reshape(length, HEADS, HEAD)
    scale = HEAD ** (-0.5)

    def block_back(carried, inputs):
        row_start, block_lse = inputs
        scores, queries, keys_all = masked_scores(qkv_rows, pack_ids, pack_keep, row_start)
        probs = jnp.exp(scores - block_lse[:, :, None])
        grad_rows = lax.dynamic_slice_in_dim(grad_attended, row_start, QBLOCK, 0).reshape(
            QBLOCK, HEADS, HEAD
        )
        grad_probs = jnp.einsum(
            "qhd,khd->hqk", grad_rows, values_all, preferred_element_type=jnp.float32
        )
        grad_scores = (
            probs * (grad_probs - jnp.sum(probs * grad_probs, -1, keepdims=True))
        ).astype(jnp.bfloat16)
        grad_queries = (
            jnp.einsum("hqk,khd->qhd", grad_scores, keys_all, preferred_element_type=jnp.float32)
            * scale
        )
        grad_keys = (
            carried[0]
            + jnp.einsum("hqk,qhd->khd", grad_scores, queries, preferred_element_type=jnp.float32)
            * scale
        )
        grad_values = carried[1] + jnp.einsum(
            "hqk,qhd->khd",
            probs.astype(jnp.bfloat16),
            grad_rows,
            preferred_element_type=jnp.float32,
        )
        return ((grad_keys, grad_values), grad_queries)

    zeros_kv = jnp.zeros((length, HEADS, HEAD), jnp.float32)
    starts = jnp.arange(length // QBLOCK) * QBLOCK
    (grad_keys, grad_values), grad_queries = lax.scan(
        block_back, (zeros_kv, zeros_kv), (starts, log_totals)
    )
    return jnp.stack(
        [
            grad_queries.reshape(length, HEADS * HEAD),
            grad_keys.reshape(length, HEADS * HEAD),
            grad_values.reshape(length, HEADS * HEAD),
        ]
    )


def layer_forward(blocks, vec_all, patch, pack_ids, pack_keep):
    length, feature_dim = patch.shape
    up_count = (blocks.shape[0] - 5) // 2
    embedded = jnp.dot(patch, blocks[0], preferred_element_type=jnp.float32) + vec_all[0]
    normed_one = norm_rows(embedded, vec_all[1], vec_all[2]).astype(jnp.bfloat16)
    qkv_rows = jnp.einsum(
        "td,kde->kte", normed_one, blocks[1:4], preferred_element_type=jnp.float32
    )
    qkv_bias = jnp.stack([vec_all[3], jnp.zeros_like(vec_all[3]), vec_all[4]])
    qkv_rows = (qkv_rows + qkv_bias[:, None, :]).astype(jnp.bfloat16)
    attended, log_totals = attention_forward(qkv_rows, pack_ids, pack_keep)
    hidden = (
        embedded + jnp.dot(attended, blocks[4], preferred_element_type=jnp.float32) + vec_all[5]
    )
    normed_two = norm_rows(hidden, vec_all[6], vec_all[7]).astype(jnp.bfloat16)
    pre_act = jnp.einsum(
        "td,jde->tje", normed_two, blocks[5 : 5 + up_count], preferred_element_type=jnp.float32
    )
    pre_act = pre_act.reshape(length, up_count * feature_dim) + vec_all[8 : 8 + up_count].reshape(
        -1
    )
    units = gelu_exact(pre_act).astype(jnp.bfloat16)
    down_matrix = blocks[5 + up_count :].reshape(up_count * feature_dim, feature_dim)
    output = (
        hidden
        + jnp.dot(units, down_matrix, preferred_element_type=jnp.float32)
        + vec_all[8 + up_count]
    )
    return (
        output,
        (embedded, normed_one, qkv_rows, attended, log_totals, hidden, normed_two, pre_act, units),
    )


def layer_backward(
    blocks, vec_all, patch, saved, pack_ids, pack_keep, grad_output, grad_gain, grad_shift
):
    embedded, normed_one, qkv_rows, attended, log_totals, hidden, normed_two, pre_act, units = saved
    length, feature_dim = patch.shape
    up_count = (blocks.shape[0] - 5) // 2
    down_matrix = blocks[5 + up_count :].reshape(up_count * feature_dim, feature_dim)
    grad_branch = grad_output.astype(jnp.bfloat16)
    grad_down = jnp.einsum("tf,td->fd", units, grad_branch, preferred_element_type=jnp.float32)
    grad_units = jnp.einsum(
        "td,fd->tf", grad_branch, down_matrix, preferred_element_type=jnp.float32
    )
    gelu_back = jax.vjp(gelu_exact, pre_act)[1]
    grad_pre = gelu_back(grad_units)[0].astype(jnp.bfloat16)
    grad_pre_blocks = grad_pre.reshape(length, up_count, feature_dim)
    grad_up = jnp.einsum(
        "td,tje->jde", normed_two, grad_pre_blocks, preferred_element_type=jnp.float32
    )
    grad_normed_two = jnp.einsum(
        "tje,jde->td", grad_pre_blocks, blocks[5 : 5 + up_count], preferred_element_type=jnp.float32
    )
    norm_two_back = jax.vjp(norm_rows, hidden, vec_all[6], vec_all[7])[1]
    grad_hidden_norm, grad_gain_two, grad_shift_two = norm_two_back(grad_normed_two)
    grad_hidden = grad_output + grad_hidden_norm
    grad_attn_out = grad_hidden.astype(jnp.bfloat16)
    grad_out_proj = jnp.einsum(
        "te,td->ed", attended, grad_attn_out, preferred_element_type=jnp.float32
    )
    grad_attended = jnp.einsum(
        "td,ed->te", grad_attn_out, blocks[4], preferred_element_type=jnp.float32
    ).astype(jnp.bfloat16)
    grad_qkv = attention_backward(qkv_rows, pack_ids, pack_keep, log_totals, grad_attended).astype(
        jnp.bfloat16
    )
    grad_qkv_proj = jnp.einsum(
        "td,kte->kde", normed_one, grad_qkv, preferred_element_type=jnp.float32
    )
    grad_normed_one = jnp.einsum(
        "kte,kde->td", grad_qkv, blocks[1:4], preferred_element_type=jnp.float32
    )
    norm_one_back = jax.vjp(norm_rows, embedded, vec_all[1], vec_all[2])[1]
    grad_embed_norm, grad_gain_one, grad_shift_one = norm_one_back(grad_normed_one)
    grad_embedded = (grad_hidden + grad_embed_norm).astype(jnp.bfloat16)
    grad_patch = jnp.einsum("tp,td->pd", patch, grad_embedded, preferred_element_type=jnp.float32)
    grad_blocks = jnp.concatenate(
        [
            grad_patch[None],
            grad_qkv_proj,
            grad_out_proj[None],
            grad_up,
            grad_down.reshape(up_count, feature_dim, feature_dim),
        ],
        0,
    )
    bias_sums = jnp.stack(
        [
            jnp.sum(grad_embedded.astype(jnp.float32), 0),
            grad_gain_one,
            grad_shift_one,
            jnp.sum(grad_qkv[0].astype(jnp.float32), 0),
            jnp.sum(grad_qkv[2].astype(jnp.float32), 0),
            jnp.sum(grad_attn_out.astype(jnp.float32), 0),
            grad_gain_two,
            grad_shift_two,
        ]
    )
    up_sums = jnp.sum(grad_pre.astype(jnp.float32), 0).reshape(up_count, feature_dim)
    tail_sums = jnp.stack([jnp.sum(grad_branch.astype(jnp.float32), 0), grad_gain, grad_shift])
    return (grad_blocks, jnp.concatenate([bias_sums, up_sums, tail_sums], 0))


def adam_step(weight, grad, first, second, count):
    first = BETA_FIRST * first + (1.0 - BETA_FIRST) * grad
    second = BETA_SECOND * second + (1.0 - BETA_SECOND) * grad * grad
    fix_first = 1.0 - jnp.power(BETA_FIRST, count)
    fix_second = 1.0 - jnp.power(BETA_SECOND, count)
    update = first / fix_first / (jnp.sqrt(second / fix_second) + ADAM_EPS) + WEIGHT_DECAY * weight
    return (weight - ADAM_RATE * update, first, second)


def on_device(
    patches,
    image_ids,
    keep,
    labels,
    owner,
    step,
    enc_weights,
    stats_left,
    stats_right,
    root_left,
    root_right,
    head_weights,
    head_m,
    head_v,
    vectors,
    vec_m,
    vec_v,
):
    dp_count = lax.axis_size("dp")
    block_count, row_count, feature_dim = enc_weights.shape
    up_count = (block_count - 5) // 2
    blocks, vec_low = (
        lax.all_gather(enc_weights.astype(jnp.bfloat16), "dp", axis=1, tiled=True),
        lax.all_gather(vectors.astype(jnp.bfloat16), "dp", axis=1, tiled=True),
    )
    vec_all = vec_low.astype(jnp.float32)
    head_low = lax.all_gather(head_weights.astype(jnp.bfloat16), "dp", axis=0, tiled=True)
    pack_count = image_ids.shape[0]
    patch_packs = patches.reshape(pack_count, LEN, feature_dim)
    final_gain = vec_all[9 + up_count]
    final_shift = vec_all[10 + up_count]

    def forward_pack(inputs):
        patch, pack_ids, pack_keep = inputs
        output, saved = layer_forward(blocks, vec_all, patch, pack_ids, pack_keep)
        return (pool_rows(output, final_gain, final_shift, pack_ids, pack_keep), (output, saved))

    pooled, kept_state = lax.map(forward_pack, (patch_packs, image_ids, keep))
    group = lax.all_gather(
        pooled.reshape(-1, feature_dim).astype(jnp.bfloat16), "cls", axis=0, tiled=True
    )
    logits = jnp.dot(group, head_low, preferred_element_type=jnp.float32)
    class_dev = head_low.shape[1]
    class_ids = lax.axis_index("cls") * class_dev + jnp.arange(class_dev)
    valid = class_ids[None, :] < LABELS_REAL
    target = jnp.any(labels[:, :, None] == class_ids[None, None, :], 1).astype(jnp.float32)
    image_total = labels.shape[0] * dp_count
    loss_part = (
        jnp.sum(jnp.where(valid, jax.nn.softplus(logits) - target * logits, 0.0)) / image_total
    )
    loss = lax.psum(loss_part, ("dp", "cls"))
    grad_logits = (jnp.where(valid, jax.nn.sigmoid(logits) - target, 0.0) / image_total).astype(
        jnp.bfloat16
    )
    head_grad = lax.psum_scatter(
        jnp.einsum("gr,gc->rc", group, grad_logits, preferred_element_type=jnp.float32),
        "dp",
        scatter_dimension=0,
        tiled=True,
    )
    group_grad = jnp.einsum("gc,dc->gd", grad_logits, head_low, preferred_element_type=jnp.float32)
    grad_pooled = lax.psum_scatter(group_grad, "cls", scatter_dimension=0, tiled=True).reshape(
        pack_count, IMG_PACK, feature_dim
    )

    def backward_pack(totals, inputs):
        patch, pack_ids, pack_keep, state, grad_pack = inputs
        output, saved = state

        def pool_local(rows_in, gain, shift):
            return pool_rows(rows_in, gain, shift, pack_ids, pack_keep)

        pool_back = jax.vjp(pool_local, output, final_gain, final_shift)[1]
        grad_output, grad_gain, grad_shift = pool_back(grad_pack)
        grad_blocks, grad_vectors = layer_backward(
            blocks, vec_all, patch, saved, pack_ids, pack_keep, grad_output, grad_gain, grad_shift
        )
        return ((totals[0] + grad_blocks, totals[1] + grad_vectors), None)

    initial = (
        jnp.zeros((block_count, feature_dim, feature_dim), jnp.float32),
        jnp.zeros(vec_all.shape, jnp.float32),
    )
    (grad_blocks, grad_vectors), _ = lax.scan(
        backward_pack, initial, (patch_packs, image_ids, keep, kept_state, grad_pooled)
    )
    block_rows, vector_rows = (
        lax.psum_scatter(grad_blocks, "dp", scatter_dimension=1, tiled=True),
        lax.psum_scatter(grad_vectors, "dp", scatter_dimension=1, tiled=True),
    )
    block_rows, vector_rows = lax.psum((block_rows, vector_rows), "cls")
    layer_squares = jnp.sum(block_rows * block_rows) + jnp.sum(vector_rows * vector_rows)
    local_squares = jnp.where(lax.axis_index("cls") == 0, layer_squares, 0.0) + jnp.sum(
        head_grad * head_grad
    )
    all_squares = lax.psum(local_squares, ("dp", "cls"))
    grad_norm = jnp.sqrt(all_squares)
    factor = CLIP_NORM / jnp.maximum(grad_norm, CLIP_NORM)
    block_clip = block_rows * factor
    vector_clip = vector_rows * factor
    head_clip = head_grad * factor
    half_size = feature_dim // 2
    quad_count = 4 * block_count
    slots = (quad_count + dp_count - 1) // dp_count
    slot_total = dp_count * slots
    select = (owner[None, :] == jnp.arange(slot_total)[:, None]).astype(jnp.float32)
    row_half = lax.axis_index("dp") * row_count // half_size
    half_mask = (jnp.arange(2) == row_half).astype(jnp.float32)

    def to_slots(values):
        split = (
            values.reshape(block_count, 1, row_count, 2, half_size)
            * half_mask[None, :, None, None, None]
        )
        split = jnp.transpose(split, (0, 1, 3, 2, 4)).reshape(quad_count, row_count, half_size)
        placed = jnp.einsum("sq,qrd->srd", select, split, precision=FULL_PRECISION)
        return placed.reshape(dp_count, slots, row_count, half_size)

    def from_slots(values):
        flat = jnp.transpose(values, (1, 0, 2, 3)).reshape(slot_total, row_count, half_size)
        quads = jnp.einsum("sq,srd->qrd", select, flat, precision=FULL_PRECISION).reshape(
            block_count, 2, 2, row_count, half_size
        )
        mine = jnp.einsum("i,bijrd->bjrd", half_mask, quads, precision=FULL_PRECISION)
        return jnp.transpose(mine, (0, 2, 1, 3)).reshape(block_count, row_count, feature_dim)

    pieces = (
        lax.all_to_all(to_slots(block_clip), "dp", split_axis=0, concat_axis=2, tiled=True),
        lax.all_to_all(to_slots(stats_left), "dp", split_axis=0, concat_axis=2, tiled=True),
        lax.all_to_all(to_slots(stats_right), "dp", split_axis=0, concat_axis=2, tiled=True),
        lax.all_to_all(to_slots(root_left), "dp", split_axis=0, concat_axis=2, tiled=True),
        lax.all_to_all(to_slots(root_right), "dp", split_axis=0, concat_axis=2, tiled=True),
    )
    grad_full, left_full, right_full, left_root, right_root = tuple(
        (piece[0][:, :half_size] + piece[0][:, half_size:] for piece in pieces)
    )
    item_count = grad_full.shape[0]
    new_left = 0.5 * left_full + 0.5 * jnp.einsum(
        "kij,klj->kil", grad_full, grad_full, precision=FULL_PRECISION
    )
    new_right = 0.5 * right_full + 0.5 * jnp.einsum(
        "kji,kjl->kil", grad_full, grad_full, precision=FULL_PRECISION
    )
    direction = jnp.einsum("kij,kjl->kil", left_root, grad_full, precision=FULL_PRECISION)
    direction = jnp.einsum("kij,kjl->kil", direction, right_root, precision=FULL_PRECISION)
    direction = direction * lax.rsqrt(
        jnp.mean(direction * direction, (1, 2), keepdims=True) + ROOT_EPS
    )
    shape_back = (item_count, dp_count, row_count, half_size)

    def doubled(values):
        return jnp.concatenate([values, values], 1).reshape(shape_back)

    left_slots = lax.all_to_all(doubled(new_left), "dp", split_axis=1, concat_axis=1, tiled=True)
    right_slots = lax.all_to_all(doubled(new_right), "dp", split_axis=1, concat_axis=1, tiled=True)
    step_slots = lax.all_to_all(doubled(direction), "dp", split_axis=1, concat_axis=1, tiled=True)
    new_blocks = enc_weights - SHAMPOO_RATE * from_slots(step_slots)
    count = step.astype(jnp.float32)
    new_vec, new_vec_m, new_vec_v = adam_step(vectors, vector_clip, vec_m, vec_v, count)
    new_head, new_head_m, new_head_v = adam_step(head_weights, head_clip, head_m, head_v, count)
    return (
        loss,
        grad_norm,
        new_blocks,
        block_clip,
        from_slots(left_slots),
        from_slots(right_slots),
        new_vec,
        new_vec_m,
        new_vec_v,
        new_head,
        new_head_m,
        new_head_v,
    )


def solution(mesh):
    return jax.shard_map(
        on_device,
        mesh=mesh,
        in_specs=(
            P(("dp", "cls"), None),
            P(("dp", "cls"), None),
            P(("dp", "cls"), None),
            P("dp", None),
            P(),
            P(),
            P(None, "dp", None),
            P(None, "dp", None),
            P(None, "dp", None),
            P(None, "dp", None),
            P(None, "dp", None),
            P("dp", "cls"),
            P("dp", "cls"),
            P("dp", "cls"),
            P(None, "dp"),
            P(None, "dp"),
            P(None, "dp"),
        ),
        out_specs=(
            P(),
            P(),
            P(None, "dp", None),
            P(None, "dp", None),
            P(None, "dp", None),
            P(None, "dp", None),
            P(None, "dp"),
            P(None, "dp"),
            P(None, "dp"),
            P("dp", "cls"),
            P("dp", "cls"),
            P("dp", "cls"),
        ),
        check_vma=False,
    )
```

profile of v0, /device:TPU:0, one launch (start us, length us, event | category | flops | bytes accessed | tf_op | source)
XLA Modules:
  0.0 3493.3 jit_solution(561592891931950175)
XLA Ops:
  13.8 32.7 all-gather
  50.3 173.7 %all-gather.4.cloned.1.call-done = bf16[13,768,768]{2,1,0:T(8,128)(2,1)} async-done(((bf16[13,96,768]{2,1,0:T(8,128)(2,1)}), bf16[13,768,768]{2,1,0:T(8,128)(2,1)}) %all-gather.4.cloned.1.call-update) | async-done | bytes 15335440 | tf_op jit(solution)/shard_map/all_gather | solution.py:269
  236.8 86.7 %while.36 = (s32[]{:T(128)}, bf16[2,512,768]{2,1,0:T(8,128)(2,1)}, f32[2,12,512]{2,1,0:T(8,128)S(1)}, s32[2]{0:T(128)S(1)}, s32[1024]{0:T(1024)S(1)}, /*index=5*...) while((s32[]{:T(128)}, bf16[2,512,768]{2,1,0:T(8,128)(2,1)}, ...), condition=%wide.region_5.6_spmd, body=%wide.region_2.5_spmd.sunk | while | flops 1688595968 | bytes 194228944 | solution.py:79
  243.8 10.8 fusion.278
  254.6 12.4 fusion.279
  270.1 9.0 fusion.280
  286.8 10.8 fusion.278
  297.6 12.3 fusion.279
  313.1 9.0 fusion.280
  328.8 13.8 fusion.82
  342.6 39.7 %fusion.218 = (f32[1024]{0:T(1024)S(1)}, f32[1024,768]{0,1:T(8,128)S(1)}) fusion(f32[768]{0:T(1024)S(1)} %copy-done.99, f32[1024,768]{0,1:T(8,128)S(1)} %get-tuple-element.505, bf16[13,768,768]{2,1,0:T(8,128)(2,1)} %all-gather.4.cloned.1.call-done, f32[1024,4,768]{0,2,1:T(8,128)S(1)} %get-tuple-element.506, f32[4,768]{1,0:T(4,128)S(1)} %copy-done.67, ...), kind=kOutput, calls=%fused_computation.341 | convolution fusion | flops 5057543168 | bytes 25185280 | tf_op jit(solution)/shard_map/while/body/eval_jaxpr/dot_general | solution.py:157
  401.1 12.8 copy.318
  413.9 30.1 fusion.60
  444.1 8.6 copy.402
  470.2 16.5 convert_reduce_fusion
  486.7 8.6 copy.419
  495.3 10.4 fusion.220
  521.9 184.9 %while.37 = (s32[]{:T(128)}, f32[1024,12,64]{0,2,1:T(8,128)}, f32[1024,12,64]{0,2,1:T(8,128)}, bf16[2,512,12,64]{1,3,2,0:T(8,128)(2,1)}, bf16[3,1024,768]{1,2,0:...) while((s32[]{:T(128)}, f32[1024,12,64]{0,2,1:T(8,128)}, ...), condition=%wide.region_21.22_spmd.clone, body=%wide.region_19.21_spmd.clone.sunk | while | flops 4127321600 | bytes 239792960 | solution.py:120
  528.8 10.1 fusion.292
  542.4 18.1 multiply_reduce_fusion.15
  560.5 21.2 multiply_convert_fusion.6
  581.7 9.8 bitcast_dynamic-update-slice_fusion.9
  591.5 8.6 bitcast_add_fusion.5
  600.2 13.4 bitcast_add_fusion.6
  620.1 10.1 fusion.292
  633.7 18.1 multiply_reduce_fusion.15
  651.8 21.2 multiply_convert_fusion.6
  673.0 9.8 bitcast_dynamic-update-slice_fusion.9
  682.8 9.5 bitcast_add_fusion.5
  692.3 14.3 bitcast_add_fusion.6
  727.1 9.0 fusion.219
  762.1 7.9 bitcast_dynamic-update-slice_fusion.2
  777.6 34.9 copy.337
  814.6 9.3 fusion.206
  824.0 592.5 %reduce-scatter.9.cloned.1.call-done = f32[13,96,768]{2,0,1:T(8,128)} async-done(((f32[13,768,768]{2,0,1:T(8,128)}), f32[13,96,768]{2,0,1:T(8,128)}) %reduce-scatter.9.cloned.1.call-update) | async-done | bytes 3833872 | tf_op jit(solution)/shard_map/reduce_scatter | solution.py:334
  1428.8 52.2 %reduce-scatter.13.cloned.1.call-done = f32[96,15]{1,0:T(8,128)} async-done(((f32[768,15]{1,0:T(8,128)}), f32[96,15]{1,0:T(8,128)}) %reduce-scatter.13.cloned.1.call-update) | async-done | bytes 5776
  1488.3 282.6 %reduce-scatter.11.cloned.1.call-done = f32[96,5462]{1,0:T(8,128)} async-done(((f32[768,5462]{1,0:T(8,128)}), f32[96,5462]{1,0:T(8,128)}) %reduce-scatter.11.cloned.1.call-update) | async-done | bytes 2097424 | tf_op jit(solution)/shard_map/reduce_scatter | solution.py:301
  1773.7 92.7 %all-reduce.3.cloned.1.call-done = f32[13,96,768]{2,0,1:T(8,128)} async-done(((f32[13,96,768]{2,0,1:T(8,128)}), f32[13,96,768]{2,0,1:T(8,128)}) %all-reduce.3.cloned.1.call-update) | async-done | bytes 3833872 | tf_op jit(solution)/shard_map/psum | solution.py:337
  1872.7 39.5 %all-reduce = (f32[]{:T(128)}, f32[]{:T(128)}) all-reduce(f32[]{:T(128)S(6)} %div.167, f32[]{:T(128)S(6)} %add.391), channel_id=1, replica_groups=mesh['dp'=8,'cls'=4] {'dp','cls'}, use_global_device_ids=true, to_apply=%region_13.14 | all-reduce | flops 2 | bytes 16 | tf_op jit(solution)/shard_map/psum | solution.py:297
  1927.9 17.9 bitcast_multiply_fusion
  1945.8 9.4 fusion.45
  1965.7 10.4 fusion.35
  1980.8 164.2 %all-to-all-done.1 = f32[8,7,96,384]{3,2,1,0:T(8,128)} async-done(((f32[8,7,96,384]{3,2,1,0:T(8,128)}), f32[8,7,96,384]{3,2,1,0:T(8,128)}, u32[]{:S(2)}, u32[]{:S(2)}) %all-to-all-start.1) | async-done | bytes 8257568 | tf_op jit(solution)/shard_map/all_to_all | solution.py:374
  2150.0 10.4 fusion.39
  2165.1 164.5 %all-to-all-done.6 = f32[8,7,96,384]{3,2,1,0:T(8,128)} async-done(((f32[8,7,96,384]{3,2,1,0:T(8,128)}), f32[8,7,96,384]{3,2,1,0:T(8,128)}, u32[]{:S(2)}, u32[]{:S(2)}) %all-to-all-start.6) | async-done | bytes 8257568 | tf_op jit(solution)/shard_map/all_to_all | solution.py:376
  2334.9 10.4 fusion.47
  2350.0 164.0 %all-to-all-done.4 = f32[8,7,96,384]{3,2,1,0:T(8,128)} async-done(((f32[8,7,96,384]{3,2,1,0:T(8,128)}), f32[8,7,96,384]{3,2,1,0:T(8,128)}, u32[]{:S(2)}, u32[]{:S(2)}) %all-to-all-start.4) | async-done | bytes 8257568 | tf_op jit(solution)/shard_map/all_to_all | solution.py:375
  2519.0 10.4 fusion.43
  2534.1 164.3 %all-to-all-done = f32[8,7,96,384]{3,2,1,0:T(8,128)} async-done(((f32[8,7,96,384]{3,2,1,0:T(8,128)}), f32[8,7,96,384]{3,2,1,0:T(8,128)}, u32[]{:S(2)}, u32[]{:S(2)}) %all-to-all-start) | async-done | bytes 8257568 | tf_op jit(solution)/shard_map/all_to_all | solution.py:377
  2714.8 8.8 fusion.69
  2727.9 155.0 %all-to-all-done.2 = f32[8,7,96,384]{3,2,1,0:T(8,128)} async-done(((f32[8,7,96,384]{3,2,1,0:T(8,128)}), f32[8,7,96,384]{3,2,1,0:T(8,128)}, u32[]{:S(2)}, u32[]{:S(2)}) %all-to-all-start.2) | async-done | bytes 8257568 | tf_op jit(solution)/shard_map/all_to_all | solution.py:378
  2892.0 15.1 fusion.71
  2911.4 156.1 %all-to-all-done.7 = f32[7,8,96,384]{3,2,0,1:T(8,128)} async-done(((f32[7,8,96,384]{3,2,0,1:T(8,128)}), f32[7,8,96,384]{3,2,0,1:T(8,128)}, u32[]{:S(2)}, u32[]{:S(2)}) %all-to-all-start.7) | async-done | bytes 8257568 | tf_op jit(solution)/shard_map/all_to_all | solution.py:401
  3084.4 11.9 fusion.74
  3096.3 8.2 multiply_reduce_fusion.2
  3109.3 142.6 %all-to-all-done.5 = f32[7,8,96,384]{3,2,0,1:T(8,128)} async-done(((f32[7,8,96,384]{3,2,0,1:T(8,128)}), f32[7,8,96,384]{3,2,0,1:T(8,128)}, u32[]{:S(2)}, u32[]{:S(2)}) %all-to-all-start.5) | async-done | bytes 8257568 | tf_op jit(solution)/shard_map/all_to_all | solution.py:400
  3269.1 10.7 fusion.33
  3279.7 18.6 fusion.54
  3311.2 11.1 fusion.37
  3322.3 18.3 fusion.56
  3353.7 82.8 %all-to-all-done.3 = f32[7,8,96,384]{3,2,0,1:T(8,128)} async-done(((f32[7,8,96,384]{3,2,0,1:T(8,128)}), f32[7,8,96,384]{3,2,0,1:T(8,128)}, u32[]{:S(2)}, u32[]{:S(2)}) %all-to-all-start.3) | async-done | bytes 8257568 | tf_op jit(solution)/shard_map/all_to_all | solution.py:402
  3436.4 10.7 fusion.41
  3447.1 18.5 fusion.58
  3465.6 7.9 fusion.76
  (431 shorter events, 364.5 us)
Async XLA Ops:
  7.2 216.8 %copy-start = (bf16[1024,768]{1,0:T(8,128)(2,1)S(1)}, bf16[1024,768]{1,0:T(8,128)(2,1)}, u32[]{:S(2)}) copy-start(bf16[1024,768]{1,0:T(8,128)(2,1)} %param.21) | copy-start | bytes 4718596
  7.2 216.8 %all-gather.4.cloned.1.call-start = ((), (), s32[]{:S(2)}) async-start(), calls=%async_computation.12 | async-start | bytes 17252352 | tf_op jit(solution)/shard_map/all_gather | solution.py:269
  10.9 37.0 %copy-start.43 = (s32[1,1024]{1,0:T(1,128)S(1)}, s32[1,1024]{1,0:T(1,128)}, u32[]{:S(2)}) copy-start(s32[1,1024]{1,0:T(1,128)} %param.23) | copy-start | bytes 12292
  10.9 37.0 %copy-start.39 = (s32[1,1024]{1,0:T(1,128)S(1)}, s32[1,1024]{1,0:T(1,128)}, u32[]{:S(2)}) copy-start(s32[1,1024]{1,0:T(1,128)} %param.22) | copy-start | bytes 12292
  10.9 38.3 %copy-start.103 = (s32[32,2]{0,1:T(2,128)S(1)}, s32[32,2]{0,1:T(2,128)}, u32[]{:S(2)}) copy-start(s32[32,2]{0,1:T(2,128)} %param.24) | copy-start | bytes 772
  10.9 380.4 %all-gather.6.cloned.1.call-start = ((), (), s32[]{:S(2)}) async-start(), calls=%async_computation.13 | async-start | bytes 9510912 | tf_op jit(solution)/shard_map/all_gather | solution.py:273
  13.7 439.0 %reduce-scatter.7.cloned.1.call-start = ((), (), s32[]{:S(2)}) async-start(), calls=%async_computation.14 | async-start | bytes 122880 | tf_op jit(solution)/shard_map/reduce_scatter | solution.py:308
  47.2 180.1 %copy-start.47 = (f32[768]{0:T(1024)}, f32[768]{0:T(1024)S(1)}, u32[]{:S(2)}) copy-start(f32[768]{0:T(1024)S(1)} %get-tuple-element.426) | copy-start | bytes 9220
  47.2 180.1 %copy-start.62 = (f32[768]{0:T(1024)}, f32[768]{0:T(1024)S(1)}, u32[]{:S(2)}) copy-start(f32[768]{0:T(1024)S(1)} %get-tuple-element.425) | copy-start | bytes 9220
  47.2 180.1 %copy-start.97 = (f32[768]{0:T(1024)}, f32[768]{0:T(1024)S(1)}, u32[]{:S(2)}) copy-start(f32[768]{0:T(1024)S(1)} %get-tuple-element.424) | copy-start | bytes 9220
  47.2 179.5 %copy-start.66 = (f32[4,768]{1,0:T(4,128)}, f32[4,768]{1,0:T(4,128)S(1)}, u32[]{:S(2)}) copy-start(f32[4,768]{1,0:T(4,128)S(1)} %slice.173) | copy-start | bytes 36868
  47.9 178.8 %copy-start.84 = (pred[1024]{0:T(1024)(128)(4,1)}, pred[1024]{0:T(1024)(128)(4,1)S(1)}, u32[]{:S(2)}) copy-start(pred[1024]{0:T(1024)(128)(4,1)S(1)} %compare_reduce_fusion.1) | copy-start | bytes 3076
  236.8 86.7 %copy-start.48 = (f32[768]{0:T(1024)S(1)}, f32[768]{0:T(1024)}, u32[]{:S(2)}) copy-start(f32[768]{0:T(1024)} %copy-done.47) | copy-start | bytes 9220
  236.8 86.7 %copy-start.100 = (f32[768]{0:T(1024)S(1)}, f32[768]{0:T(1024)}, u32[]{:S(2)}) copy-start(f32[768]{0:T(1024)} %get-tuple-element.423) | copy-start | bytes 9220
  254.6 15.5 copy-start.1
  297.6 15.5 copy-start.1
  328.3 14.3 copy-start.15
  328.3 14.3 copy-start.57
  328.7 13.9 copy-start.70
  328.7 13.9 copy-start.75
  328.7 13.8 copy-start.99
  342.6 39.8 %copy-start.22 = (f32[1024,4,768]{0,2,1:T(8,128)}, f32[1024,4,768]{0,2,1:T(8,128)S(1)}, u32[]{:S(2)}) copy-start(f32[1024,4,768]{0,2,1:T(8,128)S(1)} %get-tuple-element.506) | copy-start | bytes 37748740
  342.6 41.5 %copy-start.40 = (s32[1,1024]{1,0:T(1,128)S(1)}, s32[1,1024]{1,0:T(1,128)}, u32[]{:S(2)}) copy-start(s32[1,1024]{1,0:T(1,128)} %param.22) | copy-start | bytes 12292
  342.6 41.5 %copy-start.56 = (f32[768]{0:T(1024)S(1)}, f32[768]{0:T(1024)}, u32[]{:S(2)}) copy-start(f32[768]{0:T(1024)} %get-tuple-element.418) | copy-start | bytes 9220
  342.6 41.4 %copy-start.85 = (pred[1024]{0:T(1024)(128)(4,1)S(1)}, pred[1024]{0:T(1024)(128)(4,1)}, u32[]{:S(2)}) copy-start(pred[1024]{0:T(1024)(128)(4,1)} %copy-done.84) | copy-start | bytes 3076
  342.6 41.4 %copy-start.86 = (f32[768]{0:T(1024)S(1)}, f32[768]{0:T(1024)}, u32[]{:S(2)}) copy-start(f32[768]{0:T(1024)} %get-tuple-element.419) | copy-start | bytes 9220
  342.6 41.4 %copy-start.102 = (f32[8]{0:T(128)S(1)}, f32[8]{0:T(128)}, u32[]{:S(2)}) copy-start(f32[8]{0:T(128)} %broadcast_maximum_fusion) | copy-start | bytes 100
  382.4 8.9 copy-start.29
  382.4 8.9 copy-start.52
  401.1 1015.5 %reduce-scatter.9.cloned.1.call-start = ((), (), s32[]{:S(2)}) async-start(), calls=%async_computation.15 | async-start | bytes 42467328 | tf_op jit(solution)/shard_map/reduce_scatter | solution.py:334
  401.1 12.8 copy-start.65
  466.2 48.6 %copy-start.60 = (f32[1024]{0:T(1024)}, f32[1024]{0:T(1024)S(1)}, u32[]{:S(2)}) copy-start(f32[1024]{0:T(1024)S(1)} %negate_multiply_fusion.4) | copy-start | bytes 12292
  528.4 10.6 copy-start.2
  528.8 10.1 copy-start.23
  591.5 8.6 copy-start.4
  619.7 10.5 copy-start.2
  620.1 10.1 copy-start.23
  682.8 9.5 copy-start.4
  748.9 13.2 slice-start.4
  751.7 7.5 copy-start.38
  751.7 10.3 slice-start.5
  759.2 10.8 slice-start.2
  762.1 8.0 slice-start.3
  762.1 8.0 copy-start.36
  812.5 668.5 %reduce-scatter.13.cloned.1.call-start = ((), (), s32[]{:S(2)}) async-start(), calls=%async_computation.18 | async-start | bytes 442368
  814.5 956.4 %reduce-scatter.11.cloned.1.call-start = ((), (), s32[]{:S(2)}) async-start(), calls=%async_computation.17 | async-start | bytes 19021824 | tf_op jit(solution)/shard_map/reduce_scatter | solution.py:301
  824.0 1042.4 %all-reduce.3.cloned.1.call-start = ((), (), s32[]{:S(2)}) async-start(), calls=%async_computation.16 | async-start | bytes 9437184 | tf_op jit(solution)/shard_map/psum | solution.py:337
  1416.6 7.5 copy-start.27
  1416.6 7.5 copy-start.28
  1487.7 430.1 %copy-start.54 = (f32[15,96]{1,0:T(8,128)}, f32[15,96]{1,0:T(8,128)S(1)}, u32[]{:S(2)}) copy-start(f32[15,96]{1,0:T(8,128)S(1)} %psum.30) | copy-start | bytes 17284
  1927.9 17.9 copy-start.64
  1960.0 185.0 %all-to-all-start.1 = ((f32[8,7,96,384]{3,2,1,0:T(8,128)}), f32[8,7,96,384]{3,2,1,0:T(8,128)}, u32[]{:S(2)}, u32[]{:S(2)}) async-start(f32[8,7,96,384]{3,2,1,0:T(8,128)} %copy.349), calls=%async_computation.4 | async-start | bytes 16515072 | tf_op jit(solution)/shard_map/all_to_all | solution.py:374
  2145.0 184.5 %all-to-all-start.6 = ((f32[8,7,96,384]{3,2,1,0:T(8,128)}), f32[8,7,96,384]{3,2,1,0:T(8,128)}, u32[]{:S(2)}, u32[]{:S(2)}) async-start(f32[8,7,96,384]{3,2,1,0:T(8,128)} %copy.365), calls=%async_computation.9 | async-start | bytes 16515072 | tf_op jit(solution)/shard_map/all_to_all | solution.py:376
  2329.6 184.5 %all-to-all-start.4 = ((f32[8,7,96,384]{3,2,1,0:T(8,128)}), f32[8,7,96,384]{3,2,1,0:T(8,128)}, u32[]{:S(2)}, u32[]{:S(2)}) async-start(f32[8,7,96,384]{3,2,1,0:T(8,128)} %copy.359), calls=%async_computation.7 | async-start | bytes 16515072 | tf_op jit(solution)/shard_map/all_to_all | solution.py:375
  2514.0 184.4 %all-to-all-start = ((f32[8,7,96,384]{3,2,1,0:T(8,128)}), f32[8,7,96,384]{3,2,1,0:T(8,128)}, u32[]{:S(2)}, u32[]{:S(2)}) async-start(f32[8,7,96,384]{3,2,1,0:T(8,128)} %copy.344), calls=%async_computation.3 | async-start | bytes 16515072 | tf_op jit(solution)/shard_map/all_to_all | solution.py:377
  2698.4 184.5 %all-to-all-start.2 = ((f32[8,7,96,384]{3,2,1,0:T(8,128)}), f32[8,7,96,384]{3,2,1,0:T(8,128)}, u32[]{:S(2)}, u32[]{:S(2)}) async-start(f32[8,7,96,384]{3,2,1,0:T(8,128)} %copy.353), calls=%async_computation.5 | async-start | bytes 16515072 | tf_op jit(solution)/shard_map/all_to_all | solution.py:378
  2882.9 184.6 %all-to-all-start.7 = ((f32[7,8,96,384]{3,2,0,1:T(8,128)}), f32[7,8,96,384]{3,2,0,1:T(8,128)}, u32[]{:S(2)}, u32[]{:S(2)}) async-start(f32[7,8,96,384]{3,2,0,1:T(8,128)} %copy.368), calls=%async_computation.10 | async-start | bytes 16515072 | tf_op jit(solution)/shard_map/all_to_all | solution.py:401
  3067.5 184.4 %all-to-all-start.5 = ((f32[7,8,96,384]{3,2,0,1:T(8,128)}), f32[7,8,96,384]{3,2,0,1:T(8,128)}, u32[]{:S(2)}, u32[]{:S(2)}) async-start(f32[7,8,96,384]{3,2,0,1:T(8,128)} %copy.361), calls=%async_computation.8 | async-start | bytes 16515072 | tf_op jit(solution)/shard_map/all_to_all | solution.py:400
  3072.5 11.6 slice-start
  3251.9 184.5 %all-to-all-start.3 = ((f32[7,8,96,384]{3,2,0,1:T(8,128)}), f32[7,8,96,384]{3,2,0,1:T(8,128)}, u32[]{:S(2)}, u32[]{:S(2)}) async-start(f32[7,8,96,384]{3,2,0,1:T(8,128)} %copy.355), calls=%async_computation.6 | async-start | bytes 16515072 | tf_op jit(solution)/shard_map/all_to_all | solution.py:402
  3257.1 7.6 copy-start.55
  3257.1 7.6 copy-start.83
  3257.1 7.6 copy-start.93
  3257.1 7.6 copy-start.94
  (69 other events, 274.3 us)
Sparse Core Ops, SparseCore 0:
  11.1 212.8 all-gather.3
  226.7 123.9 all-gather.5
  401.2 17.7 reduce-scatter.6
  812.7 603.8 reduce-scatter.8
  1420.5 60.4 reduce-scatter.12
  1485.3 285.5 reduce-scatter.10
  1773.3 93.0 all-reduce.2
where the time goes:
time: 3500 us; the launch traced here: 3490 us
  waiting for transfers between devices  2390 us (68%)
  matrix products  506 us (14%)
  local copies, waits for them, and re-layouts  254 us (7%)
  other arithmetic  191 us (5%)
  blocking collectives  83.2 us (2%)
  starting transfers between devices  42.2 us (1%)
    reduce_scatter x1, waiting for transfers between devices, on_device(): lax.psum_scatter(grad_blocks, 'dp', scatter_dimension=1, tiled=True)  592 us
    reduce_scatter x1, waiting for transfers between devices, on_device(): lax.psum_scatter(jnp.einsum('gr,gc->rc', group, grad_logits, preferred_el...  283 us
    all_gather x1, waiting for transfers between devices, on_device(): lax.all_gather(enc_weights.astype(jnp.bfloat16), 'dp', axis=1, tiled=True)  174 us
    all_to_all x1, waiting for transfers between devices, on_device(): lax.all_to_all(to_slots(stats_right), 'dp', split_axis=0, concat_axis=2,...  164 us
    all_to_all x1, waiting for transfers between devices, on_device(): lax.all_to_all(to_slots(root_left), 'dp', split_axis=0, concat_axis=2, ti...  164 us
    all_to_all x1, waiting for transfers between devices, on_device(): lax.all_to_all(to_slots(block_clip), 'dp', split_axis=0, concat_axis=2, t...  164 us
    all_to_all x1, waiting for transfers between devices, on_device(): lax.all_to_all(to_slots(stats_left), 'dp', split_axis=0, concat_axis=2, t...  164 us
    all_to_all x1, waiting for transfers between devices, on_device(): lax.all_to_all(doubled(new_right), 'dp', split_axis=1, concat_axis=1, til...  156 us
  transfers between devices with their start and end apart: 15, of which 13 were waited for; matrix products, arithmetic and copies ran while one was open for 13% of the time, Pallas kernels for 0%

commit v1 on v0

--- a/solution.py
+++ b/solution.py
@@ -207,15 +207,9 @@
     grad_embed_norm, grad_gain_one, grad_shift_one = norm_one_back(grad_normed_one)
     grad_embedded = (grad_hidden + grad_embed_norm).astype(jnp.bfloat16)
     grad_patch = jnp.einsum("tp,td->pd", patch, grad_embedded, preferred_element_type=jnp.float32)
-    grad_blocks = jnp.concatenate(
-        [
-            grad_patch[None],
-            grad_qkv_proj,
-            grad_out_proj[None],
-            grad_up,
-            grad_down.reshape(up_count, feature_dim, feature_dim),
-        ],
-        0,
+    grad_first = jnp.concatenate([grad_patch[None], grad_qkv_proj, grad_out_proj[None]], 0)
+    grad_mlp = jnp.concatenate(
+        [grad_up, grad_down.reshape(up_count, feature_dim, feature_dim)], 0
     )
     bias_sums = jnp.stack(
         [
@@ -231,7 +225,7 @@
     )
     up_sums = jnp.sum(grad_pre.astype(jnp.float32), 0).reshape(up_count, feature_dim)
     tail_sums = jnp.stack([jnp.sum(grad_branch.astype(jnp.float32), 0), grad_gain, grad_shift])
-    return (grad_blocks, jnp.concatenate([bias_sums, up_sums, tail_sums], 0))
+    return (grad_first, grad_mlp, jnp.concatenate([bias_sums, up_sums, tail_sums], 0))
 
 
 def adam_step(weight, grad, first, second, count):
@@ -241,6 +235,11 @@
     fix_second = 1.0 - jnp.power(BETA_SECOND, count)
     update = first / fix_first / (jnp.sqrt(second / fix_second) + ADAM_EPS) + WEIGHT_DECAY * weight
     return (weight - ADAM_RATE * update, first, second)
+
+
+def split_halves(values, half_size):
+    block_count, row_count, feature_dim = values.shape
+    return values.reshape(block_count, row_count, 2, half_size)
 
 
 def on_device(
@@ -263,154 +262,138 @@
     vec_v,
 ):
     dp_count = lax.axis_size("dp")
+    cls_count = lax.axis_size("cls")
+    dp_index = lax.axis_index("dp")
+    cls_index = lax.axis_index("cls")
     block_count, row_count, feature_dim = enc_weights.shape
     up_count = (block_count - 5) // 2
-    blocks, vec_low = (
-        lax.all_gather(enc_weights.astype(jnp.bfloat16), "dp", axis=1, tiled=True),
-        lax.all_gather(vectors.astype(jnp.bfloat16), "dp", axis=1, tiled=True),
-    )
+    half_size = feature_dim // 2
+    part_rows = row_count // cls_count
+    half_dp = dp_count // 2
+    half_group = half_dp * cls_count
+    half_groups = [
+        list(range(half_group)),
+        list(range(half_group, 2 * half_group)),
+    ]
+
+    def my_part(values):
+        return lax.dynamic_slice_in_dim(values, cls_index * part_rows, part_rows, 1)
+
+    blocks = lax.all_gather(
+        my_part(enc_weights.astype(jnp.bfloat16)), ("dp", "cls"), axis=1, tiled=True
+    )
+    vec_low = lax.all_gather(vectors.astype(jnp.bfloat16), "dp", axis=1, tiled=True)
     vec_all = vec_low.astype(jnp.float32)
     head_low = lax.all_gather(head_weights.astype(jnp.bfloat16), "dp", axis=0, tiled=True)
-    pack_count = image_ids.shape[0]
-    patch_packs = patches.reshape(pack_count, LEN, feature_dim)
+    right_half = lax.all_gather(
+        my_part(root_right), ("dp", "cls"), axis=1, tiled=True, axis_index_groups=half_groups
+    )
     final_gain = vec_all[9 + up_count]
     final_shift = vec_all[10 + up_count]
-
-    def forward_pack(inputs):
-        patch, pack_ids, pack_keep = inputs
-        output, saved = layer_forward(blocks, vec_all, patch, pack_ids, pack_keep)
-        return (pool_rows(output, final_gain, final_shift, pack_ids, pack_keep), (output, saved))
-
-    pooled, kept_state = lax.map(forward_pack, (patch_packs, image_ids, keep))
-    group = lax.all_gather(
-        pooled.reshape(-1, feature_dim).astype(jnp.bfloat16), "cls", axis=0, tiled=True
-    )
+    pack_ids, pack_keep = image_ids[0], keep[0]
+
+    output, saved = layer_forward(blocks, vec_all, patches, pack_ids, pack_keep)
+    pooled = pool_rows(output, final_gain, final_shift, pack_ids, pack_keep)
+    group = lax.all_gather(pooled.astype(jnp.bfloat16), "cls", axis=0, tiled=True)
+    pooled_all = lax.all_gather(group, "dp", axis=0, tiled=True)
     logits = jnp.dot(group, head_low, preferred_element_type=jnp.float32)
     class_dev = head_low.shape[1]
-    class_ids = lax.axis_index("cls") * class_dev + jnp.arange(class_dev)
+    class_ids = cls_index * class_dev + jnp.arange(class_dev)
     valid = class_ids[None, :] < LABELS_REAL
     target = jnp.any(labels[:, :, None] == class_ids[None, None, :], 1).astype(jnp.float32)
     image_total = labels.shape[0] * dp_count
     loss_part = (
         jnp.sum(jnp.where(valid, jax.nn.softplus(logits) - target * logits, 0.0)) / image_total
     )
-    loss = lax.psum(loss_part, ("dp", "cls"))
     grad_logits = (jnp.where(valid, jax.nn.sigmoid(logits) - target, 0.0) / image_total).astype(
         jnp.bfloat16
     )
-    head_grad = lax.psum_scatter(
-        jnp.einsum("gr,gc->rc", group, grad_logits, preferred_element_type=jnp.float32),
-        "dp",
-        scatter_dimension=0,
-        tiled=True,
-    )
     group_grad = jnp.einsum("gc,dc->gd", grad_logits, head_low, preferred_element_type=jnp.float32)
-    grad_pooled = lax.psum_scatter(group_grad, "cls", scatter_dimension=0, tiled=True).reshape(
-        pack_count, IMG_PACK, feature_dim
-    )
-
-    def backward_pack(totals, inputs):
-        patch, pack_ids, pack_keep, state, grad_pack = inputs
-        output, saved = state
-
-        def pool_local(rows_in, gain, shift):
-            return pool_rows(rows_in, gain, shift, pack_ids, pack_keep)
-
-        pool_back = jax.vjp(pool_local, output, final_gain, final_shift)[1]
-        grad_output, grad_gain, grad_shift = pool_back(grad_pack)
-        grad_blocks, grad_vectors = layer_backward(
-            blocks, vec_all, patch, saved, pack_ids, pack_keep, grad_output, grad_gain, grad_shift
-        )
-        return ((totals[0] + grad_blocks, totals[1] + grad_vectors), None)
-
-    initial = (
-        jnp.zeros((block_count, feature_dim, feature_dim), jnp.float32),
-        jnp.zeros(vec_all.shape, jnp.float32),
-    )
-    (grad_blocks, grad_vectors), _ = lax.scan(
-        backward_pack, initial, (patch_packs, image_ids, keep, kept_state, grad_pooled)
-    )
-    block_rows, vector_rows = (
-        lax.psum_scatter(grad_blocks, "dp", scatter_dimension=1, tiled=True),
-        lax.psum_scatter(grad_vectors, "dp", scatter_dimension=1, tiled=True),
-    )
-    block_rows, vector_rows = lax.psum((block_rows, vector_rows), "cls")
-    layer_squares = jnp.sum(block_rows * block_rows) + jnp.sum(vector_rows * vector_rows)
-    local_squares = jnp.where(lax.axis_index("cls") == 0, layer_squares, 0.0) + jnp.sum(
-        head_grad * head_grad
-    )
-    all_squares = lax.psum(local_squares, ("dp", "cls"))
-    grad_norm = jnp.sqrt(all_squares)
+    grad_pooled = lax.psum_scatter(group_grad, "cls", scatter_dimension=0, tiled=True)
+    grad_logits_all = lax.all_gather(grad_logits, "dp", axis=0, tiled=True)
+    pooled_mine = lax.dynamic_slice_in_dim(pooled_all, dp_index * row_count, row_count, 1)
+    head_grad = jnp.einsum(
+        "gr,gc->rc", pooled_mine, grad_logits_all, preferred_element_type=jnp.float32
+    )
+
+    def pool_local(rows_in, gain, shift):
+        return pool_rows(rows_in, gain, shift, pack_ids, pack_keep)
+
+    pool_back = jax.vjp(pool_local, output, final_gain, final_shift)[1]
+    grad_output, grad_gain, grad_shift = pool_back(grad_pooled)
+    grad_first, grad_mlp, grad_vectors = layer_backward(
+        blocks,
+        vec_all,
+        patches,
+        saved,
+        pack_ids,
+        pack_keep,
+        grad_output,
+        grad_gain,
+        grad_shift,
+    )
+
+    def reduced_half(values):
+        part = lax.psum_scatter(values, ("dp", "cls"), scatter_dimension=1, tiled=True)
+        return lax.all_gather(
+            part, ("dp", "cls"), axis=1, tiled=True, axis_index_groups=half_groups
+        )
+
+    grad_half = jnp.concatenate([reduced_half(grad_first), reduced_half(grad_mlp)], 0)
+    own_start = (dp_index % half_dp) * row_count
+    block_rows = lax.dynamic_slice_in_dim(grad_half, own_start, row_count, 1)
+    vector_sum = lax.psum(grad_vectors, ("dp", "cls"))
+    vector_rows = lax.dynamic_slice_in_dim(vector_sum, dp_index * row_count, row_count, 1)
+
+    precise = lax.Precision.HIGHEST
+    grad_quads = split_halves(grad_half, half_size)
+    rows_quads = split_halves(block_rows, half_size)
+    cols_quads = lax.dynamic_slice_in_dim(grad_quads, own_start, row_count, 3)
+    left_add = jnp.einsum("brjk,bljk->brjl", rows_quads, grad_quads, precision=precise)
+    right_add = jnp.einsum("bkja,bkjm->bajm", cols_quads, grad_quads, precision=precise)
+    direction = jnp.einsum(
+        "brjk,bkjm->brjm", split_halves(root_left, half_size), grad_quads, precision=precise
+    )
+    direction = jnp.einsum(
+        "brjk,bkjm->brjm", direction, split_halves(right_half, half_size), precision=precise
+    )
+    block_squares = jnp.sum(direction * direction, (1, 3))
+    in_top = (dp_index < half_dp).astype(jnp.float32)
+    once = (cls_index == 0).astype(jnp.float32)
+    layer_squares = once * jnp.sum(block_rows * block_rows)
+    vector_squares = once * jnp.sum(vector_rows * vector_rows)
+    packed = jnp.concatenate(
+        [
+            (once * in_top * block_squares).reshape(-1),
+            (once * (1.0 - in_top) * block_squares).reshape(-1),
+            jnp.stack([layer_squares + vector_squares + jnp.sum(head_grad * head_grad), loss_part]),
+        ]
+    )
+    packed = lax.psum(packed, ("dp", "cls"))
+    loss = packed[4 * block_count + 1]
+    grad_norm = jnp.sqrt(packed[4 * block_count])
     factor = CLIP_NORM / jnp.maximum(grad_norm, CLIP_NORM)
-    block_clip = block_rows * factor
-    vector_clip = vector_rows * factor
-    head_clip = head_grad * factor
-    half_size = feature_dim // 2
-    quad_count = 4 * block_count
-    slots = (quad_count + dp_count - 1) // dp_count
-    slot_total = dp_count * slots
-    select = (owner[None, :] == jnp.arange(slot_total)[:, None]).astype(jnp.float32)
-    row_half = lax.axis_index("dp") * row_count // half_size
-    half_mask = (jnp.arange(2) == row_half).astype(jnp.float32)
-
-    def to_slots(values):
-        split = (
-            values.reshape(block_count, 1, row_count, 2, half_size)
-            * half_mask[None, :, None, None, None]
-        )
-        split = jnp.transpose(split, (0, 1, 3, 2, 4)).reshape(quad_count, row_count, half_size)
-        placed = jnp.einsum("sq,qrd->srd", select, split, precision=FULL_PRECISION)
-        return placed.reshape(dp_count, slots, row_count, half_size)
-
-    def from_slots(values):
-        flat = jnp.transpose(values, (1, 0, 2, 3)).reshape(slot_total, row_count, half_size)
-        quads = jnp.einsum("sq,srd->qrd", select, flat, precision=FULL_PRECISION).reshape(
-            block_count, 2, 2, row_count, half_size
-        )
-        mine = jnp.einsum("i,bijrd->bjrd", half_mask, quads, precision=FULL_PRECISION)
-        return jnp.transpose(mine, (0, 2, 1, 3)).reshape(block_count, row_count, feature_dim)
-
-    pieces = (
-        lax.all_to_all(to_slots(block_clip), "dp", split_axis=0, concat_axis=2, tiled=True),
-        lax.all_to_all(to_slots(stats_left), "dp", split_axis=0, concat_axis=2, tiled=True),
-        lax.all_to_all(to_slots(stats_right), "dp", split_axis=0, concat_axis=2, tiled=True),
-        lax.all_to_all(to_slots(root_left), "dp", split_axis=0, concat_axis=2, tiled=True),
-        lax.all_to_all(to_slots(root_right), "dp", split_axis=0, concat_axis=2, tiled=True),
-    )
-    grad_full, left_full, right_full, left_root, right_root = tuple(
-        (piece[0][:, :half_size] + piece[0][:, half_size:] for piece in pieces)
-    )
-    item_count = grad_full.shape[0]
-    new_left = 0.5 * left_full + 0.5 * jnp.einsum(
-        "kij,klj->kil", grad_full, grad_full, precision=FULL_PRECISION
-    )
-    new_right = 0.5 * right_full + 0.5 * jnp.einsum(
-        "kji,kjl->kil", grad_full, grad_full, precision=FULL_PRECISION
-    )
-    direction = jnp.einsum("kij,kjl->kil", left_root, grad_full, precision=FULL_PRECISION)
-    direction = jnp.einsum("kij,kjl->kil", direction, right_root, precision=FULL_PRECISION)
-    direction = direction * lax.rsqrt(
-        jnp.mean(direction * direction, (1, 2), keepdims=True) + ROOT_EPS
-    )
-    shape_back = (item_count, dp_count, row_count, half_size)
-
-    def doubled(values):
-        return jnp.concatenate([values, values], 1).reshape(shape_back)
-
-    left_slots = lax.all_to_all(doubled(new_left), "dp", split_axis=1, concat_axis=1, tiled=True)
-    right_slots = lax.all_to_all(doubled(new_right), "dp", split_axis=1, concat_axis=1, tiled=True)
-    step_slots = lax.all_to_all(doubled(direction), "dp", split_axis=1, concat_axis=1, tiled=True)
-    new_blocks = enc_weights - SHAMPOO_RATE * from_slots(step_slots)
+    sums = packed[: 4 * block_count].reshape(2, block_count, 2)
+    mean_squares = jnp.where(dp_index < half_dp, sums[0], sums[1]) / (half_size * half_size)
+    mean_squares = mean_squares * factor * factor
+    scale = factor * lax.rsqrt(mean_squares + ROOT_EPS)
+    flat = (block_count, row_count, feature_dim)
+    new_blocks = enc_weights - SHAMPOO_RATE * (direction * scale[:, None, :, None]).reshape(flat)
+    square_factor = 0.5 * factor * factor
+    new_left = 0.5 * stats_left + square_factor * left_add.reshape(flat)
+    new_right = 0.5 * stats_right + square_factor * right_add.reshape(flat)
     count = step.astype(jnp.float32)
-    new_vec, new_vec_m, new_vec_v = adam_step(vectors, vector_clip, vec_m, vec_v, count)
-    new_head, new_head_m, new_head_v = adam_step(head_weights, head_clip, head_m, head_v, count)
+    new_vec, new_vec_m, new_vec_v = adam_step(vectors, vector_rows * factor, vec_m, vec_v, count)
+    new_head, new_head_m, new_head_v = adam_step(
+        head_weights, head_grad * factor, head_m, head_v, count
+    )
     return (
         loss,
         grad_norm,
         new_blocks,
-        block_clip,
-        from_slots(left_slots),
-        from_slots(right_slots),
+        block_rows * factor,
+        new_left,
+        new_right,
         new_vec,
         new_vec_m,
         new_vec_v,

time: 3500 us -> 1480 us (0.42)
  waiting for transfers between devices: 2390 us -> 507 us
  matrix products: 506 us -> 399 us
  blocking collectives: 83.2 us -> 149 us
  local copies, waits for them, and re-layouts: 254 us -> 199 us
  starting transfers between devices: 42.2 us -> 0.56 us
    all_to_all x8 -> x0, waiting for transfers between devices: 1190 us -> none  [the longest x1 164 us: on_device(): lax.all_to_all(to_slots(stats_right), 'dp', split_axis=0, concat_axis=2,...]
    reduce_scatter x2, waiting for transfers between devices: 875 us -> 432 us  [reduced_half(): lax.psum_scatter(values, ('dp', 'cls'), scatter_dimension=1, tiled=True)]
    dot_general x16 -> x5, matrix products: 192 us -> 79.3 us  [the longest x1 20.5 us: on_device(): jnp.einsum('brjk,bkjm->brjm', direction, split_halves(right_half, half_si...]
    all_gather x1 -> x5, waiting for transfers between devices: 174 us -> 74.4 us  [the longest x1 74.3 us: on_device(): lax.all_gather(my_part(enc_weights.astype(jnp.bfloat16)), ('dp', 'cls'),...]
    psum x1 -> x0, waiting for transfers between devices: 92.7 us -> none  [on_device(): block_rows, vector_rows = lax.psum((block_rows, vector_rows), 'cls')]
    unnamed x8 -> x9, waiting for transfers between devices: 52.3 us -> 0.66 us
    all_to_all x8 -> x0, starting transfers between devices: 41.5 us -> none  [the longest x1 5.72 us: on_device(): lax.all_to_all(to_slots(block_clip), 'dp', split_axis=0, concat_axis=2, t...]
    dot_general x7 -> x0, local copies, waits for them, and re-layouts: 37.2 us -> none  [the longest x5 23.4 us: to_slots(): placed = jnp.einsum('sq,qrd->srd', select, split, precision=FULL_PRECISION)]
  transfers between devices with their start and end apart: 15 -> 9, of which waited for: 13 -> 3; matrix products, arithmetic and copies ran while one was open for 13% -> 20% of each run, Pallas kernels for 0% -> 0%
where the time goes in v1:
time: 1480 us; the launch traced here: 1470 us
  waiting for transfers between devices  507 us (34%)
  matrix products  399 us (27%)
  local copies, waits for them, and re-layouts  199 us (13%)
  other arithmetic  188 us (13%)
  blocking collectives  149 us (10%)
  between operations  22.2 us (2%)
    reduce_scatter x2, waiting for transfers between devices, reduced_half(): lax.psum_scatter(values, ('dp', 'cls'), scatter_dimension=1, tiled=True)  432 us
    all_gather x1, waiting for transfers between devices, on_device(): lax.all_gather(my_part(enc_weights.astype(jnp.bfloat16)), ('dp', 'cls'),...  74.3 us
    dot_general x4, matrix products, masked_scores(): jnp.einsum('qhd,khd->hqk', queries, keys_all, preferred_element_type=jnp....  45 us
    convert_element_type x2, other arithmetic, block_back(): grad_scores = (probs * (grad_probs - jnp.sum(probs * grad_probs, -1, keep...  42.5 us
    psum x1, blocking collectives, on_device(): packed = lax.psum(packed, ('dp', 'cls'))  41.6 us
    dot_general x1, matrix products, layer_forward(): jnp.dot(units, down_matrix, preferred_element_type=jnp.float32)  41.1 us
    psum x1, blocking collectives, on_device(): vector_sum = lax.psum(grad_vectors, ('dp', 'cls'))  37.8 us
    dot_general x2, matrix products, block_back(): jnp.einsum('qhd,khd->hqk', grad_rows, values_all, preferred_element_type=...  36.3 us
  transfers between devices with their start and end apart: 9, of which 3 were waited for; matrix products, arithmetic and copies ran while one was open for 20% of the time, Pallas kernels for 0%

profile of v1, /device:TPU:0, one launch (start us, length us, event | category | flops | bytes accessed | tf_op | source)
XLA Modules:
  0.0 1473.6 jit_solution(9618977003069981576)
XLA Ops:
  13.7 32.3 %all-gather = bf16[8,96,15]{1,2,0:T(8,128)(2,1)S(1)} all-gather(bf16[1,96,15]{1,2,0:T(8,128)(2,1)S(1)} %convert_bitcast_fusion), channel_id=1, replica_groups=mesh['dp'=8,'cls'=4] {'dp'}, dimensions={0}, use_global_device_ids=true | all-gather | bytes 25920 | tf_op jit(solution)/shard_map/all_gather | solution.py:285
  49.2 74.3 %all-gather.10.cloned.1.call-done = bf16[13,768,768]{2,1,0:T(8,128)(2,1)} async-done(((bf16[13,24,768]{2,1,0:T(8,128)(2,1)}), bf16[13,768,768]{2,1,0:T(8,128)(2,1)}) %all-gather.10.cloned.1.call-update) | async-done | bytes 15335440 | tf_op jit(solution)/shard_map/all_gather | solution.py:282
  127.0 6.7 fusion.37
  136.3 86.1 %while.27 = (s32[]{:T(128)}, bf16[2,512,768]{2,1,0:T(8,128)(2,1)}, f32[2,12,512]{2,1,0:T(8,128)S(1)}, s32[2]{0:T(128)S(1)}, s32[1024]{0:T(1024)S(1)}, /*index=5*...) while((s32[]{:T(128)}, bf16[2,512,768]{2,1,0:T(8,128)(2,1)}, ...), condition=%wide.region_5.6_spmd, body=%wide.region_2.5_spmd.sunk | while | flops 1688595968 | bytes 194228432 | solution.py:79
  142.9 10.8 fusion.229
  153.8 12.3 fusion.230
  169.3 9.0 fusion.231
  186.0 10.8 fusion.229
  196.7 12.3 fusion.230
  212.2 9.0 fusion.231
  222.5 4.6 fusion.161
  227.6 15.8 %fusion.57 = (u8[1024,768]{0,1:T(8,128)(4,1)S(1)}, u8[1024,768]{0,1:T(8,128)(4,1)}, f32[1024,4,768]{0,2,1:T(8,128)}) fusion(f32[4,768]{1,0:T(4,128)S(1)} %copy-done.61, bf16[13,768,768]{2,1,0:T(8,128)(2,1)} %all-gather.10.cloned.1.call-done, f32[1024,768]{0,1:T(8,128)S(1)} %get-tuple-element.412, f32[768]{0:T(1024)S(1)} %copy-done.88, ...), kind=kOutput, calls=%fused_computation.139 | convolution fusion | flops 4878237696 | bytes 22046720 | tf_op jit(solution)/shard_map/td,jde->tje/dot_general | solution.py:147
  243.5 12.6 copy.256
  256.1 41.1 %fusion.162 = (f32[1024]{0:T(1024)S(1)}, f32[1024,768]{0,1:T(8,128)S(1)}) fusion(f32[768]{0:T(1024)S(1)} %copy-done.92, f32[1024,768]{0,1:T(8,128)} %copy-done.16, bf16[13,768,768]{2,1,0:T(8,128)(2,1)} %all-gather.10.cloned.1.call-done, f32[1024,4,768]{0,2,1:T(8,128)} %get-tuple-element.413, f32[4,768]{1,0:T(4,128)S(1)} %copy-done.61, ...), kind=kOutput, calls=%fused_computation.278 | convolution fusion | flops 5057543168 | bytes 25185280 | tf_op jit(solution)/shard_map/dot_general | solution.py:157
  300.9 5.2 all_gather.30
  306.2 5.8 multiply_convert_fusion.2
  312.0 6.6 fusion.167
  318.9 30.2 %fusion.33 = (bf16[3072,1024]{0,1:T(8,128)(2,1)}, f32[1024,3072]{1,0:T(8,128)}) fusion(f32[1024,3072]{1,0:T(8,128)} %copy.256, f32[3072]{0:T(1024)S(1)} %copy-done.59), kind=kLoop, calls=%fused_computation.82 | loop fusion | flops 207618048 | bytes 31469568 | tf_op jit(solution)/shard_map/tf,td->fd/dot_general | solution.py:174
  349.1 4.4 fusion.165
  357.1 4.5 multiply_reduce_fusion.3
  366.6 16.6 %convert_reduce_fusion = (f32[3072]{0:T(1024)}, bf16[1024,3072]{1,0:T(8,128)(2,1)}) fusion(f32[1024,3072]{1,0:T(8,128)} %get-tuple-element.392, bf16[1024,768]{0,1:T(8,128)(2,1)} %get-tuple-element.378, bf16[3072,768]{1,0:T(8,128)(2,1)S(1)} %bitcast.264, f32[1024,3072]{1,0:T(8,128)} %copy.256, f32[3072]{0:T(1024)S(1)} %copy-done.59), kind=kOutput, calls=%fused_computation.51 | convolution fusion | flops 4885312512 | bytes 37773312 | tf_op jit(solution)/shard_map/td,fd->tf/dot_general | solution.py:175
  383.2 8.6 copy.324
  391.8 10.4 fusion.164
  406.2 4.5 multiply_reduce_fusion.4
  421.2 191.6 %while.28 = (s32[]{:T(128)}, f32[1024,12,64]{0,2,1:T(8,128)}, f32[1024,12,64]{0,2,1:T(8,128)}, bf16[2,512,12,64]{1,3,2,0:T(8,128)(2,1)}, bf16[3,1024,768]{1,2,0:...) while((s32[]{:T(128)}, f32[1024,12,64]{0,2,1:T(8,128)}, ...), condition=%wide.region_19.20_spmd.clone, body=%wide.region_17.19_spmd.clone.sunk | while | flops 4127321600 | bytes 269152704 | solution.py:120
  429.1 11.7 fusion.243
  445.7 18.1 %multiply_reduce_fusion.15 = (f32[12,512]{1,0:T(8,128)S(1)}, f32[12,512,1024]{2,1,0:T(8,128)}) fusion(f32[12,512,1024]{2,1,0:T(8,128)} %fusion.243, f32[12,512]{1,0:T(8,128)S(1)} %dynamic-slice_bitcast_fusion.2, pred[512,1024]{1,0:T(8,128)(4,1)S(1)} %fusion.244, bf16[512,12,64]{0,2,1:T(8,128)(2,1)} %bitcast.242, ...), kind=kOutput, calls=%fused_computation.18.clone.1 | convolution fusion | flops 836757504 | bytes 53264384 | tf_op jit(solution)/shard_map/while/body/eval_jaxpr/qhd,khd->hqk/dot_general | solution.py:95
  463.8 21.3 %multiply_convert_fusion.4 = bf16[12,512,1024]{2,1,0:T(8,128)(2,1)} fusion(f32[12,512,1024]{2,1,0:T(8,128)} %get-tuple-element.572, f32[12,512,1024]{2,1,0:T(8,128)} %fusion.243, f32[12,512]{1,0:T(8,128)S(1)} %get-tuple-element.573, f32[12,512]{1,0:T(8,128)S(1)} %dynamic-slice_bitcast_fusion.2, pred[512,1024]{1,0:T(8,128)(4,1)S(1)} %fusion.244), kind=kLoop, calls=%fused_computation.17.clone.1 | loop fusion | flops 37748736 | bytes 63488000 | tf_op jit(solution)/shard_map/while/body/eval_jaxpr/convert_element_type | solution.py:100
  485.1 8.7 bitcast_add_fusion.6
  493.8 11.7 bitcast_add_fusion.7
  507.1 9.4 bitcast_dynamic-update-slice_fusion.5
  524.4 11.7 fusion.243
  540.9 18.1 %multiply_reduce_fusion.15 = (f32[12,512]{1,0:T(8,128)S(1)}, f32[12,512,1024]{2,1,0:T(8,128)}) fusion(f32[12,512,1024]{2,1,0:T(8,128)} %fusion.243, f32[12,512]{1,0:T(8,128)S(1)} %dynamic-slice_bitcast_fusion.2, pred[512,1024]{1,0:T(8,128)(4,1)S(1)} %fusion.244, bf16[512,12,64]{0,2,1:T(8,128)(2,1)} %bitcast.242, ...), kind=kOutput, calls=%fused_computation.18.clone.1 | convolution fusion | flops 836757504 | bytes 53264384 | tf_op jit(solution)/shard_map/while/body/eval_jaxpr/qhd,khd->hqk/dot_general | solution.py:95
  559.1 21.3 %multiply_convert_fusion.4 = bf16[12,512,1024]{2,1,0:T(8,128)(2,1)} fusion(f32[12,512,1024]{2,1,0:T(8,128)} %get-tuple-element.572, f32[12,512,1024]{2,1,0:T(8,128)} %fusion.243, f32[12,512]{1,0:T(8,128)S(1)} %get-tuple-element.573, f32[12,512]{1,0:T(8,128)S(1)} %dynamic-slice_bitcast_fusion.2, pred[512,1024]{1,0:T(8,128)(4,1)S(1)} %fusion.244), kind=kLoop, calls=%fused_computation.17.clone.1 | loop fusion | flops 37748736 | bytes 63488000 | tf_op jit(solution)/shard_map/while/body/eval_jaxpr/convert_element_type | solution.py:100
  580.4 9.6 bitcast_add_fusion.6
  589.9 11.7 bitcast_add_fusion.7
  603.3 9.4 bitcast_dynamic-update-slice_fusion.5
  620.8 4.2 copy.261
  629.5 10.7 convolution_bitcast_fusion.1
  640.2 8.2 fusion.163
  663.5 4.6 pad_maximum_fusion.2
  668.1 16.4 %copy.270 = f32[5,768,768]{2,0,1:T(8,128)} copy(f32[5,768,768]{1,2,0:T(8,128)} %pad_maximum_fusion.2) | data formatting | bytes 23592960 | tf_op jit(solution)/shard_map/concatenate | solution.py:210
  684.6 8.8 copy.315
  693.4 8.2 fusion.75
  701.7 8.0 convolution_bitcast_fusion
  709.7 7.9 pad_maximum_fusion.1
  717.6 20.1 %copy.277 = f32[8,768,768]{2,0,1:T(8,128)} copy(f32[8,768,768]{1,2,0:T(8,128)} %pad_maximum_fusion.1) | data formatting | bytes 37748736 | tf_op jit(solution)/shard_map/concatenate | solution.py:211
  740.7 222.5 %reduce-scatter.6.cloned.1.call-done = f32[5,24,768]{2,0,1:T(8,128)} async-done(((f32[5,768,768]{2,0,1:T(8,128)}), f32[5,24,768]{2,0,1:T(8,128)}) %reduce-scatter.6.cloned.1.call-update) | async-done | bytes 368656 | tf_op jit(solution)/shard_map/reduce_scatter | solution.py:337
  965.2 209.8 %reduce-scatter.8.cloned.1.call-done = f32[8,24,768]{2,0,1:T(8,128)} async-done(((f32[8,768,768]{2,0,1:T(8,128)}), f32[8,24,768]{2,0,1:T(8,128)}) %reduce-scatter.8.cloned.1.call-update) | async-done | bytes 589840 | tf_op jit(solution)/shard_map/reduce_scatter | solution.py:337
  1175.8 16.7 %copy.246 = f32[13,384,768]{1,2,0:T(8,128)} copy(f32[13,384,768]{2,1,0:T(8,128)} %all-gather.8.cloned.1.call-done) | data formatting | bytes 30670848 | tf_op jit(solution)/shard_map/all_gather | solution.py:288
  1193.2 32.5 %all_gather.34 = bf16[256,768]{1,0:T(8,128)(2,1)S(1)} all-gather(bf16[32,768]{1,0:T(8,128)(2,1)} %copy-done.43), channel_id=1, replica_groups=mesh['dp'=8,'cls'=4] {'dp'}, dimensions={0}, use_global_device_ids=true | all-gather | bytes 442368 | tf_op jit(solution)/shard_map/all_gather | solution.py:298
  1233.4 37.8 %psum.14 = f32[15,768]{1,0:T(8,128)S(1)} all-reduce(f32[15,768]{1,0:T(8,128)S(1)} %concatenate.18), channel_id=1, replica_groups=mesh['dp'=8,'cls'=4] {'dp','cls'}, use_global_device_ids=true, to_apply=%region_38.39 | all-reduce | flops 11520 | bytes 92160 | tf_op jit(solution)/shard_map/psum | solution.py:345
  1272.6 4.4 multiply_reduce_fusion.12
  1277.1 7.6 copy.278
  1284.7 9.8 copy.279
  1294.5 12.6 pad_maximum_fusion
  1309.4 4.6 multiply_reduce_fusion.1
  1314.6 19.3 %fusion.42 = f32[13,2,384,96]{2,3,1,0:T(8,128)S(1)} fusion(f32[13,384,2,384]{1,3,2,0:T(8,128)} %bitcast.237, f32[13,12,2,8,384]{4,3,2,1,0:T(8,128)} %bitcast.265), kind=kOutput, calls=%fused_computation.95 | convolution fusion | flops 4416602112 | bytes 23003136 | tf_op jit(solution)/shard_map/brjk,bkjm->brjm/dot_general | solution.py:354
  1334.0 20.5 %multiply_reduce_fusion.2 = (f32[13,2]{1,0:T(8,128)S(1)}, f32[13,2,384,96]{2,3,1,0:T(8,128)}) fusion(f32[13,384,2,384]{1,3,2,0:T(8,128)} %bitcast.244, f32[13,2,384,96]{2,3,1,0:T(8,128)S(1)} %fusion.42), kind=kOutput, calls=%fused_computation.107 | convolution fusion | flops 4418519040 | bytes 23003240 | tf_op jit(solution)/shard_map/brjk,bkjm->brjm/dot_general | solution.py:357
  1355.4 41.6 %psum.15 = f32[54]{0:T(128)S(1)} all-reduce(f32[54]{0:T(128)S(1)} %pad_maximum_fusion.9), channel_id=1, replica_groups=mesh['dp'=8,'cls'=4] {'dp','cls'}, use_global_device_ids=true, to_apply=%region_42.43 | all-reduce | flops 54 | bytes 432 | tf_op jit(solution)/shard_map/psum | solution.py:372
  1407.3 6.0 copy.293
  1413.2 19.6 %multiply_bitcast_fusion = f32[13,2,12,8,384]{4,3,2,1,0:T(8,128)S(1)} fusion(f32[13,384,2,384]{1,3,2,0:T(8,128)} %bitcast.238, s32[]{:T(128)S(6)} %select_n.58, f32[]{:T(128)S(6)} %mul.563), kind=kOutput, calls=%fused_computation.100 | convolution fusion | flops 4417560576 | bytes 23003144 | tf_op jit(solution)/shard_map/bkja,bkjm->bajm/dot_general | solution.py:353
  1435.1 15.5 %multiply_bitcast_fusion.1 = f32[13,2,12,8,384]{4,3,2,1,0:T(8,128)S(1)} fusion(f32[13,384,2,384]{1,3,2,0:T(8,128)} %bitcast.239, f32[13,96,2,384]{1,3,2,0:T(8,128)S(1)} %bitcast.251, f32[]{:T(128)S(6)} %mul.563), kind=kOutput, calls=%fused_computation.104 | convolution fusion | flops 4417560576 | bytes 23003140 | tf_op jit(solution)/shard_map/brjk,bljk->brjl/dot_general | solution.py:352
  1457.4 7.4 multiply_add_fusion
  (391 shorter events, 146.7 us)
Async XLA Ops:
  8.0 115.6 %copy-start = (bf16[1024,768]{1,0:T(8,128)(2,1)S(1)}, bf16[1024,768]{1,0:T(8,128)(2,1)}, u32[]{:S(2)}) copy-start(bf16[1024,768]{1,0:T(8,128)(2,1)} %param.21) | copy-start | bytes 4718596
  8.0 38.8 %copy-start.39 = (s32[1,1024]{1,0:T(1,128)S(1)}, s32[1,1024]{1,0:T(1,128)}, u32[]{:S(2)}) copy-start(s32[1,1024]{1,0:T(1,128)} %param.23) | copy-start | bytes 12292
  8.0 38.8 %copy-start.37 = (s32[1,1024]{1,0:T(1,128)S(1)}, s32[1,1024]{1,0:T(1,128)}, u32[]{:S(2)}) copy-start(s32[1,1024]{1,0:T(1,128)} %param.22) | copy-start | bytes 12292
  8.1 40.1 %copy-start.95 = (s32[32,2]{0,1:T(2,128)S(1)}, s32[32,2]{0,1:T(2,128)}, u32[]{:S(2)}) copy-start(s32[32,2]{0,1:T(2,128)} %param.24) | copy-start | bytes 772
  8.1 115.5 %all-gather.10.cloned.1.call-start = ((), (), s32[]{:S(2)}) async-start(), calls=%async_computation.4 | async-start | bytes 15814656 | tf_op jit(solution)/shard_map/all_gather | solution.py:282
  10.3 295.9 %all-gather.12.cloned.1.call-start = ((), (), s32[]{:S(2)}) async-start(), calls=%async_computation.5 | async-start | bytes 9510912 | tf_op jit(solution)/shard_map/all_gather | solution.py:287
  13.0 336.1 %reduce-scatter.4.cloned.1.call-start = ((), (), s32[]{:S(2)}) async-start(), calls=%async_computation.6 | async-start | bytes 122880 | tf_op jit(solution)/shard_map/reduce_scatter | solution.py:312
  46.8 80.2 %copy-start.45 = (f32[768]{0:T(1024)}, f32[768]{0:T(1024)S(1)}, u32[]{:S(2)}) copy-start(f32[768]{0:T(1024)S(1)} %get-tuple-element.328) | copy-start | bytes 9220
  46.8 80.2 %copy-start.57 = (f32[768]{0:T(1024)}, f32[768]{0:T(1024)S(1)}, u32[]{:S(2)}) copy-start(f32[768]{0:T(1024)S(1)} %get-tuple-element.327) | copy-start | bytes 9220
  46.8 80.2 %copy-start.90 = (f32[768]{0:T(1024)}, f32[768]{0:T(1024)S(1)}, u32[]{:S(2)}) copy-start(f32[768]{0:T(1024)S(1)} %get-tuple-element.326) | copy-start | bytes 9220
  46.8 79.6 %copy-start.60 = (f32[4,768]{1,0:T(4,128)}, f32[4,768]{1,0:T(4,128)S(1)}, u32[]{:S(2)}) copy-start(f32[4,768]{1,0:T(4,128)S(1)} %slice.146) | copy-start | bytes 36868
  46.9 79.5 %copy-start.78 = (pred[1024]{0:T(1024)(128)(4,1)}, pred[1024]{0:T(1024)(128)(4,1)S(1)}, u32[]{:S(2)}) copy-start(pred[1024]{0:T(1024)(128)(4,1)S(1)} %compare_reduce_fusion.3) | copy-start | bytes 3076
  136.3 86.2 %copy-start.46 = (f32[768]{0:T(1024)S(1)}, f32[768]{0:T(1024)}, u32[]{:S(2)}) copy-start(f32[768]{0:T(1024)} %copy-done.45) | copy-start | bytes 9220
  136.3 86.2 %copy-start.93 = (f32[768]{0:T(1024)S(1)}, f32[768]{0:T(1024)}, u32[]{:S(2)}) copy-start(f32[768]{0:T(1024)} %get-tuple-element.325) | copy-start | bytes 9220
  153.8 15.5 %copy-start.1 = (f32[12,512,1024]{2,1,0:T(8,128)S(1)}, f32[12,512,1024]{2,1,0:T(8,128)}, u32[]{:S(2)}) copy-start(f32[12,512,1024]{2,1,0:T(8,128)} %get-tuple-element.556) | copy-start | bytes 75497472 | tf_op jit(solution)/shard_map/while
  196.7 15.5 %copy-start.1 = (f32[12,512,1024]{2,1,0:T(8,128)S(1)}, f32[12,512,1024]{2,1,0:T(8,128)}, u32[]{:S(2)}) copy-start(f32[12,512,1024]{2,1,0:T(8,128)} %get-tuple-element.556) | copy-start | bytes 75497472 | tf_op jit(solution)/shard_map/while
  227.1 16.3 %copy-start.16 = (f32[1024,768]{0,1:T(8,128)}, f32[1024,768]{0,1:T(8,128)S(1)}, u32[]{:S(2)}) copy-start(f32[1024,768]{0,1:T(8,128)S(1)} %get-tuple-element.412) | copy-start | bytes 9437188
  227.2 16.3 %copy-start.52 = (f32[1024]{0:T(1024)}, f32[1024]{0:T(1024)S(1)}, u32[]{:S(2)}) copy-start(f32[1024]{0:T(1024)S(1)} %broadcast_multiply_fusion.4) | copy-start | bytes 12292
  227.6 15.9 %copy-start.64 = (f32[1024]{0:T(1024)}, f32[1024]{0:T(1024)S(1)}, u32[]{:S(2)}) copy-start(f32[1024]{0:T(1024)S(1)} %multiply_reduce_fusion.10) | copy-start | bytes 12292
  227.6 15.9 %copy-start.69 = (f32[1024]{0:T(1024)}, f32[1024]{0:T(1024)S(1)}, u32[]{:S(2)}) copy-start(f32[1024]{0:T(1024)S(1)} %fusion.106) | copy-start | bytes 12292
  243.5 12.6 copy-start.92
  256.1 42.8 %copy-start.38 = (s32[1,1024]{1,0:T(1,128)S(1)}, s32[1,1024]{1,0:T(1,128)}, u32[]{:S(2)}) copy-start(s32[1,1024]{1,0:T(1,128)} %param.22) | copy-start | bytes 12292
  256.1 42.8 %copy-start.51 = (f32[768]{0:T(1024)S(1)}, f32[768]{0:T(1024)}, u32[]{:S(2)}) copy-start(f32[768]{0:T(1024)} %get-tuple-element.320) | copy-start | bytes 9220
  256.1 42.8 %copy-start.79 = (pred[1024]{0:T(1024)(128)(4,1)S(1)}, pred[1024]{0:T(1024)(128)(4,1)}, u32[]{:S(2)}) copy-start(pred[1024]{0:T(1024)(128)(4,1)} %copy-done.78) | copy-start | bytes 3076
  256.1 42.8 %copy-start.80 = (f32[768]{0:T(1024)S(1)}, f32[768]{0:T(1024)}, u32[]{:S(2)}) copy-start(f32[768]{0:T(1024)} %get-tuple-element.321) | copy-start | bytes 9220
  256.1 42.8 %copy-start.94 = (f32[8]{0:T(128)S(1)}, f32[8]{0:T(128)}, u32[]{:S(2)}) copy-start(f32[8]{0:T(128)} %broadcast_maximum_fusion) | copy-start | bytes 100
  297.3 8.9 copy-start.44
  297.3 8.9 copy-start.87
  318.6 644.5 %reduce-scatter.6.cloned.1.call-start = ((), (), s32[]{:S(2)}) async-start(), calls=%async_computation.7 | async-start | bytes 19464192 | tf_op jit(solution)/shard_map/reduce_scatter | solution.py:337
  362.6 49.1 %copy-start.55 = (f32[1024]{0:T(1024)}, f32[1024]{0:T(1024)S(1)}, u32[]{:S(2)}) copy-start(f32[1024]{0:T(1024)S(1)} %negate_multiply_fusion.4) | copy-start | bytes 12292
  429.1 13.2 copy-start.24
  442.2 21.6 %copy-start.4 = (pred[512,1024]{1,0:T(8,128)(4,1)}, pred[512,1024]{1,0:T(8,128)(4,1)S(1)}, u32[]{:S(2)}) copy-start(pred[512,1024]{1,0:T(8,128)(4,1)S(1)} %fusion.244) | copy-start | bytes 1572868 | tf_op jit(solution)/shard_map/while
  485.1 8.7 copy-start.5
  485.1 8.7 copy-start.7
  485.1 8.7 copy-start.28
  493.8 13.3 copy-start.2
  524.4 13.2 copy-start.24
  537.5 21.6 %copy-start.4 = (pred[512,1024]{1,0:T(8,128)(4,1)}, pred[512,1024]{1,0:T(8,128)(4,1)S(1)}, u32[]{:S(2)}) copy-start(pred[512,1024]{1,0:T(8,128)(4,1)S(1)} %fusion.244) | copy-start | bytes 1572868 | tf_op jit(solution)/shard_map/while
  580.3 9.6 copy-start.5
  580.4 9.6 copy-start.7
  580.4 9.6 copy-start.28
  589.9 13.3 copy-start.2
  629.4 10.7 copy-start.33
  629.4 10.7 copy-start.34
  629.5 10.7 copy-start.35
  684.5 490.4 %reduce-scatter.8.cloned.1.call-start = ((), (), s32[]{:S(2)}) async-start(), calls=%async_computation.9 | async-start | bytes 19464192 | tf_op jit(solution)/shard_map/reduce_scatter | solution.py:337
  693.4 8.2 copy-start.68
  693.4 8.3 copy-start.71
  693.4 8.3 copy-start.89
  737.8 438.1 %all-gather.8.cloned.1.call-start = ((), (), s32[]{:S(2)}) async-start(), calls=%async_computation.3 | async-start | bytes 16293888 | tf_op jit(solution)/shard_map/all_gather | solution.py:288
  740.0 532.6 %all-gather.18.cloned.1.call-start = ((), (), s32[]{:S(2)}) async-start(), calls=%async_computation.11 | async-start | bytes 3170304 | tf_op jit(solution)/shard_map/all_gather | solution.py:313
  740.6 536.4 %all-gather.14.cloned.1.call-start = ((), (), s32[]{:S(2)}) async-start(), calls=%async_computation.8 | async-start | bytes 6266880 | tf_op jit(solution)/shard_map/all_gather | solution.py:338
  965.1 319.6 %all-gather.16.cloned.1.call-start = ((), (), s32[]{:S(2)}) async-start(), calls=%async_computation.10 | async-start | bytes 10027008 | tf_op jit(solution)/shard_map/all_gather | solution.py:338
  1175.8 54.7 %copy-start.83 = (f32[768]{0:T(1024)S(1)}, f32[768]{0:T(1024)}, u32[]{:S(2)}) copy-start(f32[768]{0:T(1024)} %get-tuple-element.379) | copy-start | bytes 9220
  1175.8 56.8 %copy-start.82 = (f32[768]{0:T(1024)S(1)}, f32[768]{0:T(1024)}, u32[]{:S(2)}) copy-start(f32[768]{0:T(1024)} %get-tuple-element.377) | copy-start | bytes 9220
  1175.8 56.8 %copy-start.84 = (f32[768]{0:T(1024)S(1)}, f32[768]{0:T(1024)}, u32[]{:S(2)}) copy-start(f32[768]{0:T(1024)} %get-tuple-element.316) | copy-start | bytes 9220
  1175.8 56.8 %copy-start.81 = (f32[768]{0:T(1024)S(1)}, f32[768]{0:T(1024)}, u32[]{:S(2)}) copy-start(f32[768]{0:T(1024)} %get-tuple-element.422) | copy-start | bytes 9220
  1271.3 13.4 copy-start.50
  1284.7 22.4 %slice-start = ((s8[5898240]{0:T(1024)(128)(4,1)}), s8[1703936]{0:T(1024)(128)(4,1)S(1)}, s32[]{:S(2)}) async-start(s8[5898240]{0:T(1024)(128)(4,1)} %bitcast.245), calls=%async_computation.12 | async-start | bytes 3407872
  1294.5 13.7 copy-start.6
  1294.5 14.9 %slice-start.1 = ((s8[5898240]{0:T(1024)(128)(4,1)}), s8[4194304]{0:T(1024)(128)(4,1)S(1)}, s32[]{:S(2)}) async-start(s8[5898240]{0:T(1024)(128)(4,1)} %bitcast.245), calls=%async_computation.13 | async-start | bytes 8388608
  1407.3 27.8 %slice-start.4 = ((s8[5111808]{0:T(1024)(128)(4,1)}), s8[917504]{0:T(1024)(128)(4,1)S(1)}, s32[]{:S(2)}) async-start(s8[5111808]{0:T(1024)(128)(4,1)} %bitcast.249), calls=%async_computation.16 | async-start | bytes 1835008
  1413.2 21.8 %slice-start.5 = ((s8[5111808]{0:T(1024)(128)(4,1)}), s8[4194304]{0:T(1024)(128)(4,1)S(1)}, s32[]{:S(2)}) async-start(s8[5111808]{0:T(1024)(128)(4,1)} %bitcast.249), calls=%async_computation.17 | async-start | bytes 8388608
  1435.1 18.0 %copy-start.32 = (f32[96,5462]{1,0:T(8,128)S(1)}, f32[96,5462]{1,0:T(8,128)}, u32[]{:S(2)}) copy-start(f32[96,5462]{1,0:T(8,128)} %param.32) | copy-start | bytes 6292228
  (61 other events, 246.5 us)
Sparse Core Ops, SparseCore 0:
  12.4 111.1 all-gather.9
  126.3 124.0 all-gather.11
  318.7 17.8 reduce-scatter.3
  684.6 278.4 reduce-scatter.5
  969.4 205.5 reduce-scatter.7
Sparse Core Ops, SparseCore 1:
  740.4 129.0 all-gather.7
  871.5 71.0 all-gather.17
  965.2 37.2 all-gather.13
  1175.1 58.9 all-gather.15

commit v2 on v1

--- a/solution.py
+++ b/solution.py
@@ -1,13 +1,18 @@
 import jax
 import jax.numpy as jnp
 from jax import lax
+from jax.experimental import pallas as pl
+from jax.experimental.pallas import tpu as pltpu
 from jax.sharding import PartitionSpec as P
 
 HEADS = 12
 HEAD = 64
 LABELS_REAL = 21843
-LEN = 1024
-QBLOCK = 512
+IMAGE_MAX = 196
+QTILE = 256
+PAIR = 2 * HEAD
+ROWS = 256
+HIDDEN_TILE = 384
 IMG_PACK = 8
 
 
@@ -29,10 +34,6 @@
     return centred * lax.rsqrt(spread + NORM_EPS) * gain + shift
 
 
-def gelu_exact(values):
-    return jax.nn.gelu(values, approximate=False)
-
-
 def pool_rows(output, gain, shift, pack_ids, pack_keep):
     final = norm_rows(output, gain, shift)
     member = (
@@ -42,95 +43,273 @@
     return jnp.dot(member, final, precision=FULL_PRECISION) / counted[:, None]
 
 
-def masked_scores(qkv_rows, pack_ids, pack_keep, row_start):
-    length = qkv_rows.shape[1]
-    queries = lax.dynamic_slice_in_dim(qkv_rows[0], row_start, QBLOCK, 0).reshape(
-        QBLOCK, HEADS, HEAD
-    )
-    keys_all = qkv_rows[1].reshape(length, HEADS, HEAD)
-    scores = jnp.einsum(
-        "qhd,khd->hqk", queries, keys_all, preferred_element_type=jnp.float32
-    ) * HEAD ** (-0.5)
-    query_ids = lax.dynamic_slice_in_dim(pack_ids, row_start, QBLOCK, 0)
-    key_pos = jnp.arange(length)
-    query_pos = row_start + jnp.arange(QBLOCK)
-    allowed = (query_ids[:, None] == pack_ids[None, :]) & (
-        (pack_keep[None, :] == 1) | (query_pos[:, None] == key_pos[None, :])
-    )
-    return (jnp.where(allowed[None], scores, -1e30), queries, keys_all)
-
-
-def attention_forward(qkv_rows, pack_ids, pack_keep):
-    length = qkv_rows.shape[1]
-    values_all = qkv_rows[2].reshape(length, HEADS, HEAD)
-
-    def block_out(row_start):
-        scores, queries, keys_all = masked_scores(qkv_rows, pack_ids, pack_keep, row_start)
-        row_top = jnp.max(scores, -1, keepdims=True)
-        exp_scores = jnp.exp(scores - row_top)
-        totals = jnp.sum(exp_scores, -1, keepdims=True)
-        probs = (exp_scores / totals).astype(jnp.bfloat16)
-        attended = jnp.einsum("hqk,khd->qhd", probs, values_all, preferred_element_type=jnp.float32)
-        return (
-            attended.reshape(QBLOCK, HEADS * HEAD).astype(jnp.bfloat16),
-            (row_top + jnp.log(totals))[..., 0],
-        )
-
-    attended, log_totals = lax.map(block_out, jnp.arange(length // QBLOCK) * QBLOCK)
-    return (attended.reshape(length, HEADS * HEAD), log_totals)
-
-
-def attention_backward(qkv_rows, pack_ids, pack_keep, log_totals, grad_attended):
-    length = qkv_rows.shape[1]
-    values_all = qkv_rows[2].reshape(length, HEADS, HEAD)
-    scale = HEAD ** (-0.5)
-
-    def block_back(carried, inputs):
-        row_start, block_lse = inputs
-        scores, queries, keys_all = masked_scores(qkv_rows, pack_ids, pack_keep, row_start)
-        probs = jnp.exp(scores - block_lse[:, :, None])
-        grad_rows = lax.dynamic_slice_in_dim(grad_attended, row_start, QBLOCK, 0).reshape(
-            QBLOCK, HEADS, HEAD
-        )
-        grad_probs = jnp.einsum(
-            "qhd,khd->hqk", grad_rows, values_all, preferred_element_type=jnp.float32
-        )
-        grad_scores = (
-            probs * (grad_probs - jnp.sum(probs * grad_probs, -1, keepdims=True))
-        ).astype(jnp.bfloat16)
-        grad_queries = (
-            jnp.einsum("hqk,khd->qhd", grad_scores, keys_all, preferred_element_type=jnp.float32)
-            * scale
-        )
-        grad_keys = (
-            carried[0]
-            + jnp.einsum("hqk,qhd->khd", grad_scores, queries, preferred_element_type=jnp.float32)
-            * scale
-        )
-        grad_values = carried[1] + jnp.einsum(
-            "hqk,qhd->khd",
-            probs.astype(jnp.bfloat16),
-            grad_rows,
+def key_window(tile, length):
+    reach = -(-(IMAGE_MAX - 1) // 128) * 128
+    low = max(0, tile * QTILE - reach)
+    high = min(length, (tile + 1) * QTILE + reach)
+    return low, high
+
+
+def attention_forward_kernel(qids_ref, kcodes_ref, q_ref, k_ref, v_ref, out_ref, bias_ref):
+    length = q_ref.shape[0]
+    lane = lax.broadcasted_iota(jnp.int32, (QTILE, PAIR), 1)
+
+    @pl.when(pl.program_id(0) == 0)
+    def _():
+        for tile in range(length // QTILE):
+            low, high = key_window(tile, length)
+            shape = (QTILE, high - low)
+            rows = lax.broadcasted_iota(jnp.int32, shape, 0) + tile * QTILE
+            cols = lax.broadcasted_iota(jnp.int32, shape, 1) + low
+            same = qids_ref[tile * QTILE : (tile + 1) * QTILE, :] == kcodes_ref[:, low:high]
+            bias_ref[tile, :, : high - low] = jnp.where(same | (rows == cols), 0.0, -1e30)
+
+    for tile in range(length // QTILE):
+        low, high = key_window(tile, length)
+        rows = pl.ds(tile * QTILE, QTILE)
+        queries = q_ref[rows, :] * jnp.bfloat16(HEAD ** (-0.5))
+        keys = k_ref[low:high, :]
+        values = v_ref[low:high, :]
+        halves = []
+        for head in range(2):
+            mine = (lane >= head * HEAD) & (lane < (head + 1) * HEAD)
+            picked = jnp.where(mine, queries, jnp.zeros_like(queries))
+            scores = lax.dot_general(
+                picked, keys, (((1,), (1,)), ((), ())), preferred_element_type=jnp.float32
+            )
+            scores = scores + bias_ref[tile, :, : high - low]
+            top = jnp.max(scores, -1, keepdims=True)
+            weights = jnp.exp(scores - top)
+            probs = weights * (1.0 / jnp.sum(weights, -1, keepdims=True))
+            halves.append(
+                jnp.dot(probs.astype(jnp.bfloat16), values, preferred_element_type=jnp.float32)
+            )
+        out_ref[rows, :] = jnp.where(lane < HEAD, halves[0], halves[1]).astype(jnp.bfloat16)
+
+
+def attention_backward_kernel(
+    qids_ref, kcodes_ref, q_ref, k_ref, v_ref, do_ref, out_ref, bias_ref, dk_ref, dv_ref
+):
+    length = q_ref.shape[0]
+    lane = lax.broadcasted_iota(jnp.int32, (QTILE, PAIR), 1)
+    scale = jnp.bfloat16(HEAD ** (-0.5))
+
+    @pl.when(pl.program_id(0) == 0)
+    def _():
+        for tile in range(length // QTILE):
+            low, high = key_window(tile, length)
+            shape = (high - low, QTILE)
+            rows = lax.broadcasted_iota(jnp.int32, shape, 0) + low
+            cols = lax.broadcasted_iota(jnp.int32, shape, 1) + tile * QTILE
+            same = kcodes_ref[low:high, :] == qids_ref[:, tile * QTILE : (tile + 1) * QTILE]
+            bias_ref[tile, : high - low, :] = jnp.where(same | (rows == cols), 0.0, -1e30)
+
+    dk_ref[...] = jnp.zeros_like(dk_ref)
+    dv_ref[...] = jnp.zeros_like(dv_ref)
+    for tile in range(length // QTILE):
+        low, high = key_window(tile, length)
+        rows = pl.ds(tile * QTILE, QTILE)
+        window = pl.ds(low, high - low)
+        queries = q_ref[rows, :] * scale
+        keys = k_ref[window, :]
+        values = v_ref[window, :]
+        grads = do_ref[rows, :]
+        halves = []
+        for head in range(2):
+            mine = (lane >= head * HEAD) & (lane < (head + 1) * HEAD)
+            picked = jnp.where(mine, queries, jnp.zeros_like(queries))
+            picked_grads = jnp.where(mine, grads, jnp.zeros_like(grads))
+            scores = lax.dot_general(
+                keys, picked, (((1,), (1,)), ((), ())), preferred_element_type=jnp.float32
+            )
+            scores = scores + bias_ref[tile, : high - low, :]
+            top = jnp.max(scores, 0, keepdims=True)
+            weights = jnp.exp(scores - top)
+            probs = weights * (1.0 / jnp.sum(weights, 0, keepdims=True))
+            grad_probs = lax.dot_general(
+                values, picked_grads, (((1,), (1,)), ((), ())), preferred_element_type=jnp.float32
+            )
+            inner = jnp.sum(probs * grad_probs, 0, keepdims=True)
+            grad_scores = (probs * (grad_probs - inner)).astype(jnp.bfloat16)
+            dv_ref[window, :] += jnp.dot(
+                probs.astype(jnp.bfloat16), picked_grads, preferred_element_type=jnp.float32
+            )
+            dk_ref[window, :] += jnp.dot(
+                grad_scores, picked, preferred_element_type=jnp.float32
+            )
+            halves.append(
+                lax.dot_general(
+                    grad_scores,
+                    keys,
+                    (((0,), (0,)), ((), ())),
+                    preferred_element_type=jnp.float32,
+                )
+            )
+        grad_queries = jnp.where(lane < HEAD, halves[0], halves[1]) * HEAD ** (-0.5)
+        out_ref[0, rows, :] = grad_queries.astype(jnp.bfloat16)
+    out_ref[1] = dk_ref[...].astype(jnp.bfloat16)
+    out_ref[2] = dv_ref[...].astype(jnp.bfloat16)
+
+
+def pair_spec(length, part=None):
+    if part is None:
+        return pl.BlockSpec((length, PAIR), lambda pair: (0, pair))
+    return pl.BlockSpec((None, length, PAIR), lambda pair: (part, 0, pair))
+
+
+def whole_spec(shape):
+    return pl.BlockSpec(shape, lambda pair: (0,) * len(shape))
+
+
+def attention_forward(qkv_rows, pack_ids, key_codes):
+    _, length, width = qkv_rows.shape
+    tiles = length // QTILE
+    window = max(high - low for low, high in (key_window(t, length) for t in range(tiles)))
+    return pl.pallas_call(
+        attention_forward_kernel,
+        grid=(width // PAIR,),
+        out_shape=jax.ShapeDtypeStruct((length, width), jnp.bfloat16),
+        in_specs=[whole_spec((length, 1)), whole_spec((1, length))]
+        + [pair_spec(length, part) for part in range(3)],
+        out_specs=pair_spec(length),
+        scratch_shapes=[pltpu.VMEM((tiles, QTILE, window), jnp.float32)],
+        compiler_params=pltpu.CompilerParams(vmem_limit_bytes=40 << 20),
+        name="attention_forward",
+    )(pack_ids[:, None], key_codes[None, :], qkv_rows, qkv_rows, qkv_rows)
+
+
+def attention_backward(qkv_rows, pack_ids, key_codes, grad_attended):
+    _, length, width = qkv_rows.shape
+    tiles = length // QTILE
+    window = max(high - low for low, high in (key_window(t, length) for t in range(tiles)))
+    return pl.pallas_call(
+        attention_backward_kernel,
+        grid=(width // PAIR,),
+        out_shape=jax.ShapeDtypeStruct((3, length, width), jnp.bfloat16),
+        in_specs=[whole_spec((1, length)), whole_spec((length, 1))]
+        + [pair_spec(length, part) for part in range(3)]
+        + [pair_spec(length)],
+        out_specs=pl.BlockSpec((3, length, PAIR), lambda pair: (0, 0, pair)),
+        scratch_shapes=[
+            pltpu.VMEM((tiles, window, QTILE), jnp.float32),
+            pltpu.VMEM((length, PAIR), jnp.float32),
+            pltpu.VMEM((length, PAIR), jnp.float32),
+        ],
+        compiler_params=pltpu.CompilerParams(vmem_limit_bytes=40 << 20),
+        name="attention_backward",
+    )(pack_ids[None, :], key_codes[:, None], qkv_rows, qkv_rows, qkv_rows, grad_attended)
+
+
+def mlp_forward_kernel(x_ref, up_ref, bias_ref, down_ref, units_ref, slope_ref, out_ref):
+    first = pl.program_id(0) == 0
+
+    @pl.when(first)
+    def _():
+        out_ref[...] = jnp.zeros_like(out_ref)
+
+    for start in range(0, x_ref.shape[0], ROWS):
+        rows = pl.ds(start, ROWS)
+        pre = jnp.dot(x_ref[rows, :], up_ref[...], preferred_element_type=jnp.float32)
+        pre = pre + bias_ref[...]
+        half = 0.5 + 0.5 * lax.erf(pre * 0.7071067811865476)
+        bell = jnp.exp(-0.5 * pre * pre) * 0.3989422804014327
+        units = (pre * half).astype(jnp.bfloat16)
+        units_ref[rows, :] = units
+        slope_ref[rows, :] = half + pre * bell
+        out_ref[rows, :] += jnp.dot(units, down_ref[...], preferred_element_type=jnp.float32)
+
+
+def mlp_backward_kernel(
+    x_ref, dm_ref, up_ref, down_ref, units_ref, slope_ref,
+    grad_up_ref, grad_down_ref, bias_ref, dx_ref, dpre_ref
+):
+    @pl.when(pl.program_id(0) == 0)
+    def _():
+        dx_ref[...] = jnp.zeros_like(dx_ref)
+
+    total = jnp.zeros((1, HIDDEN_TILE), jnp.float32)
+    for start in range(0, x_ref.shape[0], ROWS):
+        rows = pl.ds(start, ROWS)
+        units_back = lax.dot_general(
+            dm_ref[rows, :], down_ref[...], (((1,), (1,)), ((), ())),
             preferred_element_type=jnp.float32,
         )
-        return ((grad_keys, grad_values), grad_queries)
-
-    zeros_kv = jnp.zeros((length, HEADS, HEAD), jnp.float32)
-    starts = jnp.arange(length // QBLOCK) * QBLOCK
-    (grad_keys, grad_values), grad_queries = lax.scan(
-        block_back, (zeros_kv, zeros_kv), (starts, log_totals)
-    )
-    return jnp.stack(
-        [
-            grad_queries.reshape(length, HEADS * HEAD),
-            grad_keys.reshape(length, HEADS * HEAD),
-            grad_values.reshape(length, HEADS * HEAD),
-        ]
-    )
-
-
-def layer_forward(blocks, vec_all, patch, pack_ids, pack_keep):
-    length, feature_dim = patch.shape
+        grad_pre = (units_back * slope_ref[rows, :]).astype(jnp.bfloat16)
+        dpre_ref[rows, :] = grad_pre
+        total = total + jnp.sum(grad_pre.astype(jnp.float32), 0, keepdims=True)
+        dx_ref[rows, :] += lax.dot_general(
+            grad_pre, up_ref[...], (((1,), (1,)), ((), ())), preferred_element_type=jnp.float32
+        )
+    bias_ref[...] = total
+    over_rows = (((0,), (0,)), ((), ()))
+    grad_down_ref[...] = lax.dot_general(
+        units_ref[...], dm_ref[...], over_rows, preferred_element_type=jnp.float32
+    )
+    grad_up_ref[...] = lax.dot_general(
+        x_ref[...], dpre_ref[...], over_rows, preferred_element_type=jnp.float32
+    )
+
+
+def mlp_specs(length, width, up_count):
+    split = width // HIDDEN_TILE
+    resident = pl.BlockSpec((length, width), lambda t: (0, 0))
+    up = pl.BlockSpec((None, width, HIDDEN_TILE), lambda t: (5 + t // split, 0, t % split))
+    down = pl.BlockSpec(
+        (None, HIDDEN_TILE, width), lambda t: (5 + up_count + t // split, t % split, 0)
+    )
+    hidden = pl.BlockSpec((length, HIDDEN_TILE), lambda t: (0, t))
+    bias = pl.BlockSpec((1, HIDDEN_TILE), lambda t: (0, t))
+    return split, resident, up, down, hidden, bias
+
+
+def mlp_forward(rows, blocks, up_bias):
+    length, width = rows.shape
+    up_count = (blocks.shape[0] - 5) // 2
+    split, resident, up, down, hidden, bias = mlp_specs(length, width, up_count)
+    hidden_size = up_count * width
+    return pl.pallas_call(
+        mlp_forward_kernel,
+        grid=(up_count * split,),
+        out_shape=(
+            jax.ShapeDtypeStruct((length, hidden_size), jnp.bfloat16),
+            jax.ShapeDtypeStruct((length, hidden_size), jnp.float32),
+            jax.ShapeDtypeStruct((length, width), jnp.float32),
+        ),
+        in_specs=[resident, up, bias, down],
+        out_specs=(hidden, hidden, resident),
+        compiler_params=pltpu.CompilerParams(vmem_limit_bytes=48 << 20),
+        name="mlp_forward",
+    )(rows, blocks, up_bias.reshape(1, hidden_size), blocks)
+
+
+def mlp_backward(rows, grad_branch, blocks, units, slopes):
+    length, width = rows.shape
+    up_count = (blocks.shape[0] - 5) // 2
+    split, resident, up, down, hidden, bias = mlp_specs(length, width, up_count)
+    hidden_size = up_count * width
+    return pl.pallas_call(
+        mlp_backward_kernel,
+        grid=(up_count * split,),
+        out_shape=(
+            jax.ShapeDtypeStruct((up_count, width, width), jnp.float32),
+            jax.ShapeDtypeStruct((up_count, width, width), jnp.float32),
+            jax.ShapeDtypeStruct((1, hidden_size), jnp.float32),
+            jax.ShapeDtypeStruct((length, width), jnp.float32),
+        ),
+        in_specs=[resident, resident, up, down, hidden, hidden],
+        out_specs=(
+            pl.BlockSpec((None, width, HIDDEN_TILE), lambda t: (t // split, 0, t % split)),
+            pl.BlockSpec((None, HIDDEN_TILE, width), lambda t: (t // split, t % split, 0)),
+            bias,
+            resident,
+        ),
+        scratch_shapes=[pltpu.VMEM((length, HIDDEN_TILE), jnp.bfloat16)],
+        compiler_params=pltpu.CompilerParams(vmem_limit_bytes=48 << 20),
+        name="mlp_backward",
+    )(rows, grad_branch, blocks, blocks, units, slopes)
+
+
+def layer_forward(blocks, vec_all, patch, pack_ids, key_codes):
     up_count = (blocks.shape[0] - 5) // 2
     embedded = jnp.dot(patch, blocks[0], preferred_element_type=jnp.float32) + vec_all[0]
     normed_one = norm_rows(embedded, vec_all[1], vec_all[2]).astype(jnp.bfloat16)
@@ -139,50 +318,28 @@
     )
     qkv_bias = jnp.stack([vec_all[3], jnp.zeros_like(vec_all[3]), vec_all[4]])
     qkv_rows = (qkv_rows + qkv_bias[:, None, :]).astype(jnp.bfloat16)
-    attended, log_totals = attention_forward(qkv_rows, pack_ids, pack_keep)
+    attended = attention_forward(qkv_rows, pack_ids, key_codes)
     hidden = (
         embedded + jnp.dot(attended, blocks[4], preferred_element_type=jnp.float32) + vec_all[5]
     )
     normed_two = norm_rows(hidden, vec_all[6], vec_all[7]).astype(jnp.bfloat16)
-    pre_act = jnp.einsum(
-        "td,jde->tje", normed_two, blocks[5 : 5 + up_count], preferred_element_type=jnp.float32
-    )
-    pre_act = pre_act.reshape(length, up_count * feature_dim) + vec_all[8 : 8 + up_count].reshape(
-        -1
-    )
-    units = gelu_exact(pre_act).astype(jnp.bfloat16)
-    down_matrix = blocks[5 + up_count :].reshape(up_count * feature_dim, feature_dim)
-    output = (
-        hidden
-        + jnp.dot(units, down_matrix, preferred_element_type=jnp.float32)
-        + vec_all[8 + up_count]
-    )
+    units, slopes, branch = mlp_forward(normed_two, blocks, vec_all[8 : 8 + up_count])
+    output = hidden + branch + vec_all[8 + up_count]
     return (
         output,
-        (embedded, normed_one, qkv_rows, attended, log_totals, hidden, normed_two, pre_act, units),
+        (embedded, normed_one, qkv_rows, attended, hidden, normed_two, slopes, units),
     )
 
 
 def layer_backward(
-    blocks, vec_all, patch, saved, pack_ids, pack_keep, grad_output, grad_gain, grad_shift
+    blocks, vec_all, patch, saved, pack_ids, key_codes, grad_output, grad_gain, grad_shift
 ):
-    embedded, normed_one, qkv_rows, attended, log_totals, hidden, normed_two, pre_act, units = saved
-    length, feature_dim = patch.shape
+    embedded, normed_one, qkv_rows, attended, hidden, normed_two, slopes, units = saved
+    feature_dim = patch.shape[1]
     up_count = (blocks.shape[0] - 5) // 2
-    down_matrix = blocks[5 + up_count :].reshape(up_count * feature_dim, feature_dim)
     grad_branch = grad_output.astype(jnp.bfloat16)
-    grad_down = jnp.einsum("tf,td->fd", units, grad_branch, preferred_element_type=jnp.float32)
-    grad_units = jnp.einsum(
-        "td,fd->tf", grad_branch, down_matrix, preferred_element_type=jnp.float32
-    )
-    gelu_back = jax.vjp(gelu_exact, pre_act)[1]
-    grad_pre = gelu_back(grad_units)[0].astype(jnp.bfloat16)
-    grad_pre_blocks = grad_pre.reshape(length, up_count, feature_dim)
-    grad_up = jnp.einsum(
-        "td,tje->jde", normed_two, grad_pre_blocks, preferred_element_type=jnp.float32
-    )
-    grad_normed_two = jnp.einsum(
-        "tje,jde->td", grad_pre_blocks, blocks[5 : 5 + up_count], preferred_element_type=jnp.float32
+    grad_up, grad_down, up_sums, grad_normed_two = mlp_backward(
+        normed_two, grad_branch, blocks, units, slopes
     )
     norm_two_back = jax.vjp(norm_rows, hidden, vec_all[6], vec_all[7])[1]
     grad_hidden_norm, grad_gain_two, grad_shift_two = norm_two_back(grad_normed_two)
@@ -194,9 +351,7 @@
     grad_attended = jnp.einsum(
         "td,ed->te", grad_attn_out, blocks[4], preferred_element_type=jnp.float32
     ).astype(jnp.bfloat16)
-    grad_qkv = attention_backward(qkv_rows, pack_ids, pack_keep, log_totals, grad_attended).astype(
-        jnp.bfloat16
-    )
+    grad_qkv = attention_backward(qkv_rows, pack_ids, key_codes, grad_attended)
     grad_qkv_proj = jnp.einsum(
         "td,kte->kde", normed_one, grad_qkv, preferred_element_type=jnp.float32
     )
@@ -208,9 +363,7 @@
     grad_embedded = (grad_hidden + grad_embed_norm).astype(jnp.bfloat16)
     grad_patch = jnp.einsum("tp,td->pd", patch, grad_embedded, preferred_element_type=jnp.float32)
     grad_first = jnp.concatenate([grad_patch[None], grad_qkv_proj, grad_out_proj[None]], 0)
-    grad_mlp = jnp.concatenate(
-        [grad_up, grad_down.reshape(up_count, feature_dim, feature_dim)], 0
-    )
+    grad_mlp = jnp.concatenate([grad_up, grad_down], 0)
     bias_sums = jnp.stack(
         [
             jnp.sum(grad_embedded.astype(jnp.float32), 0),
@@ -223,7 +376,7 @@
             grad_shift_two,
         ]
     )
-    up_sums = jnp.sum(grad_pre.astype(jnp.float32), 0).reshape(up_count, feature_dim)
+    up_sums = up_sums.reshape(up_count, feature_dim)
     tail_sums = jnp.stack([jnp.sum(grad_branch.astype(jnp.float32), 0), grad_gain, grad_shift])
     return (grad_first, grad_mlp, jnp.concatenate([bias_sums, up_sums, tail_sums], 0))
 
@@ -291,8 +444,9 @@
     final_gain = vec_all[9 + up_count]
     final_shift = vec_all[10 + up_count]
     pack_ids, pack_keep = image_ids[0], keep[0]
-
-    output, saved = layer_forward(blocks, vec_all, patches, pack_ids, pack_keep)
+    key_codes = jnp.where(pack_keep == 1, pack_ids, -1)
+
+    output, saved = layer_forward(blocks, vec_all, patches, pack_ids, key_codes)
     pooled = pool_rows(output, final_gain, final_shift, pack_ids, pack_keep)
     group = lax.all_gather(pooled.astype(jnp.bfloat16), "cls", axis=0, tiled=True)
     pooled_all = lax.all_gather(group, "dp", axis=0, tiled=True)
@@ -327,7 +481,7 @@
         patches,
         saved,
         pack_ids,
-        pack_keep,
+        key_codes,
         grad_output,
         grad_gain,
         grad_shift,

time: 1480 us -> 1110 us (0.75)
  matrix products: 399 us -> 128 us
  other arithmetic: 188 us -> 66.3 us
  Pallas kernels: 0 us -> 120 us
  local copies, waits for them, and re-layouts: 199 us -> 80.2 us
  waiting for transfers between devices: 507 us -> 543 us
    dot_general x20 -> x0, matrix products: 260 us -> none  [the longest x4 45 us: masked_scores(): jnp.einsum('qhd,khd->hqk', queries, keys_all, preferred_element_type=jnp....]
    pallas_call x0 -> x4, Pallas kernels: none -> 120 us  [the longest x1 40.5 us: attention_backward(): pl.pallas_call(attention_backward_kernel, grid=(width // PAIR,), out_shap...]
    all_gather x1, waiting for transfers between devices: 0.01 us -> 56.8 us  [on_device(): lax.all_gather(head_weights.astype(jnp.bfloat16), 'dp', axis=0, tiled=True)]
    convert_element_type x2 -> x1, other arithmetic: 42.5 us -> 0.56 us  [layer_forward(): normed_two = norm_rows(hidden, vec_all[6], vec_all[7]).astype(jnp.bfloat16)]
    reduce_scatter x2, waiting for transfers between devices: 432 us -> 395 us  [reduced_half(): lax.psum_scatter(values, ('dp', 'cls'), scatter_dimension=1, tiled=True)]
    dot_general x1 -> x0, other arithmetic: 30.2 us -> none  [layer_backward(): jnp.einsum('tf,td->fd', units, grad_branch, preferred_element_type=jnp.fl...]
    concatenate x2 -> x1, local copies, waits for them, and re-layouts: 36.5 us -> 7.95 us  [on_device(): jnp.concatenate([reduced_half(grad_first), reduced_half(grad_mlp)], 0)]
    reduce_sum x3 -> x0, other arithmetic: 24.9 us -> none  [the longest x2 24.6 us: block_out(): totals = jnp.sum(exp_scores, -1, keepdims=True)]
  transfers between devices with their start and end apart: 9 -> 9, of which waited for: 3 -> 5; matrix products, arithmetic and copies ran while one was open for 20% -> 7% of each run, Pallas kernels for 0% -> 4%
where the time goes in v2:
time: 1110 us
  waiting for transfers between devices  543 us (49%)
  blocking collectives  150 us (14%)
  matrix products  128 us (12%)
  Pallas kernels  120 us (11%)
  local copies, waits for them, and re-layouts  80.2 us (7%)
  other arithmetic  66.3 us (6%)
  between operations  22 us (2%)
    reduce_scatter x2, waiting for transfers between devices, reduced_half(): lax.psum_scatter(values, ('dp', 'cls'), scatter_dimension=1, tiled=True)  395 us
    all_gather x1, waiting for transfers between devices, on_device(): lax.all_gather(my_part(enc_weights.astype(jnp.bfloat16)), ('dp', 'cls'),...  74.7 us
    all_gather x1, waiting for transfers between devices, on_device(): lax.all_gather(head_weights.astype(jnp.bfloat16), 'dp', axis=0, tiled=True)  56.8 us
    psum x1, blocking collectives, on_device(): packed = lax.psum(packed, ('dp', 'cls'))  41.7 us
    pallas_call x1, Pallas kernels, attention_backward(): pl.pallas_call(attention_backward_kernel, grid=(width // PAIR,), out_shap...  40.5 us
    psum x1, blocking collectives, on_device(): vector_sum = lax.psum(grad_vectors, ('dp', 'cls'))  37.4 us
    pallas_call x1, Pallas kernels, mlp_backward(): pl.pallas_call(mlp_backward_kernel, grid=(up_count * split,), out_shape=(...  33 us
    all_gather x1, blocking collectives, on_device(): pooled_all = lax.all_gather(group, 'dp', axis=0, tiled=True)  32.5 us
  transfers between devices with their start and end apart: 9, of which 5 were waited for; matrix products, arithmetic and copies ran while one was open for 7% of the time, Pallas kernels for 4%

profile of v2, /device:TPU:0, one launch (start us, length us, event | category | flops | bytes accessed | tf_op | source)
XLA Modules:
  0.0 1109.0 jit_solution(4341922414114539053)
XLA Ops:
  8.1 2.1 dynamic-slice_convert_fusion
  10.3 2.7 convert_element_type.84
  13.1 32.5 %all-gather = bf16[8,96,15]{1,2,0:T(8,128)(2,1)S(1)} all-gather(bf16[1,96,15]{1,2,0:T(8,128)(2,1)S(1)} %convert_bitcast_fusion), channel_id=1, replica_groups=mesh['dp'=8,'cls'=4] {'dp'}, dimensions={0}, use_global_device_ids=true | all-gather | bytes 25920 | tf_op jit(solution)/shard_map/all_gather | solution.py:438
  46.0 0.9 copy.112
  47.7 1.0 compare_reduce_fusion
  48.8 74.7 %all-gather.10.cloned.1.call-done.up_ref.down_ref = bf16[13,768,768]{2,1,0:T(8,128)(2,1)} async-done(((bf16[13,24,768]{2,1,0:T(8,128)(2,1)}), bf16[13,768,768]{2,1,0:T(8,128)(2,1)}) %all-gather.10.cloned.1.call-update) | async-done | bytes 15335440 | tf_op jit(solution)/shard_map/all_gather | solution.py:435
  123.5 2.7 add_reduce_fusion
  126.9 7.0 fusion.10.q_ref.k_ref.v_ref
  133.9 25.6 %attention_forward.1 = bf16[1024,768]{1,0:T(8,128)(2,1)S(1)} custom-call(s32[1024,1]{1,0:T(8,128)S(1)} %copy.110.qids_ref, s32[1,1024]{1,0:T(1,128)S(1)} %broadcast_select_fusion.1.kcodes_ref, bf16[3,1024,768]{2,1,0:T(8,128)(2,1)S(1)} %fusion.10.q_ref.k_ref.v_ref, bf16[3,1024,768]{2,1,0:T(8,128)(2,1)S(1)} %fusion.10.q_ref.k_ref.v_ref, ...), custom_call_target="tpu_custom_call" | custom-call | tf_op jit(solution)/shard_map/attention_forward/pallas_call | solution.py:168
  159.5 3.4 fusion.86
  164.0 21.1 %mlp_forward.1 = (bf16[1024,3072]{1,0:T(8,128)(2,1)}, f32[1024,3072]{1,0:T(8,128)}, f32[1024,768]{1,0:T(8,128)S(1)}) custom-call(bf16[1024,768]{1,0:T(8,128)(2,1)S(1)} %add_convert_fusion.2.x_ref, bf16[13,768,768]{2,1,0:T(8,128)(2,1)} %all-gather.10.cloned.1.call-done.up_ref.down_ref, f32[1,3072]{1,0:T(1,128)S(1)} %bitcast.135, ...), custom_call_target="tpu_custom_call" | custom-call | tf_op jit(solution)/shard_map/mlp_forward/pallas_call | solution.py:270
  186.1 1.7 fusion.48
  187.8 5.7 all_gather.30
  193.4 56.8 %all-gather.12.cloned.1.call-done = bf16[768,5462]{1,0:T(8,128)(2,1)} async-done(((bf16[96,5462]{1,0:T(8,128)(2,1)}), bf16[768,5462]{1,0:T(8,128)(2,1)}) %all-gather.12.cloned.1.call-update) | async-done | bytes 8389648 | tf_op jit(solution)/shard_map/all_gather | solution.py:440
  250.2 5.7 multiply_convert_fusion
  255.9 6.6 fusion.87
  262.6 2.0 broadcast_select_fusion.kcodes_ref
  264.5 15.8 %reduce-scatter.4.cloned.1.call-done = f32[8,768]{1,0:T(8,128)} async-done(((f32[32,768]{1,0:T(8,128)}), f32[8,768]{1,0:T(8,128)}) %reduce-scatter.4.cloned.1.call-update) | async-done | bytes 24592 | tf_op jit(solution)/shard_map/reduce_scatter | solution.py:466
  280.4 4.1 multiply_reduce_fusion.2
  284.5 1.5 fusion.83
  286.3 33.0 %mlp_backward.1 = (f32[4,768,768]{2,1,0:T(8,128)}, f32[4,768,768]{2,1,0:T(8,128)}, f32[1,3072]{1,0:T(1,128)S(1)}, f32[1024,768]{1,0:T(8,128)}) custom-call(bf16[1024,768]{1,0:T(8,128)(2,1)S(1)} %add_convert_fusion.2.x_ref, bf16[1024,768]{1,0:T(8,128)(2,1)S(1)} %get-tuple-element.53.dm_ref, ...), custom_call_target="tpu_custom_call" | custom-call | tf_op jit(solution)/shard_map/mlp_backward/pallas_call | solution.py:290
  319.4 3.0 multiply_reduce_fusion.3
  322.4 1.4 fusion.82
  324.3 0.9 copy-done.7
  325.2 2.9 convolution_bitcast_fusion.1
  328.1 2.7 convolution_convert_fusion.do_ref
  330.9 40.5 %attention_backward.1 = bf16[3,1024,768]{2,1,0:T(8,128)(2,1)S(1)} custom-call(s32[1,1024]{1,0:T(1,128)S(1)} %copy-done.8, s32[1024,1]{1,0:T(8,128)S(1)} %copy-done.5, bf16[3,1024,768]{2,1,0:T(8,128)(2,1)S(1)} %bitcast.130, bf16[3,1024,768]{2,1,0:T(8,128)(2,1)S(1)} %bitcast.130, bf16[3,1024,768]{2,1,0:T(8,128)(2,1)S(1)} %bitcast.130, ...), custom_call_target="tpu_custom_call" | custom-call | tf_op jit(solution)/shard_map/attention_backward/pallas_call | solution.py:185
  371.5 4.6 convolution_bitcast_fusion
  376.1 6.4 fusion.17
  382.5 1.6 fusion.81
  384.7 1.5 convolution_bitcast_fusion.2
  386.3 4.7 pad_maximum_fusion.1
  391.1 14.9 %pad_maximum_fusion = f32[8,768,768]{2,1,0:T(8,128)} fusion(f32[4,768,768]{2,1,0:T(8,128)} %get-tuple-element.24, f32[4,768,768]{2,1,0:T(8,128)} %get-tuple-element.23), kind=kLoop, calls=%fused_computation | loop fusion | flops 4718592 | bytes 37748736 | tf_op jit(solution)/shard_map/concatenate | solution.py:366
  406.1 2.3 constant_dynamic-slice_fusion.2
  409.0 181.6 %reduce-scatter.6.cloned.1.call-done = f32[5,24,768]{2,1,0:T(8,128)} async-done(((f32[5,768,768]{2,1,0:T(8,128)}), f32[5,24,768]{2,1,0:T(8,128)}) %reduce-scatter.6.cloned.1.call-update) | async-done | bytes 368656 | tf_op jit(solution)/shard_map/reduce_scatter | solution.py:491
  590.7 213.0 %reduce-scatter.8.cloned.1.call-done = f32[8,24,768]{2,1,0:T(8,128)} async-done(((f32[8,768,768]{2,1,0:T(8,128)}), f32[8,24,768]{2,1,0:T(8,128)}) %reduce-scatter.8.cloned.1.call-update) | async-done | bytes 589840 | tf_op jit(solution)/shard_map/reduce_scatter | solution.py:491
  804.5 16.7 %copy.105 = f32[13,384,768]{1,2,0:T(8,128)} copy(f32[13,384,768]{2,1,0:T(8,128)} %all-gather.8.cloned.1.call-done) | data formatting | bytes 30670848 | tf_op jit(solution)/shard_map/all_gather | solution.py:441
  821.9 32.5 %all_gather.34 = bf16[256,768]{1,0:T(8,128)(2,1)S(1)} all-gather(bf16[32,768]{1,0:T(8,128)(2,1)S(1)} %copy-done.26), channel_id=1, replica_groups=mesh['dp'=8,'cls'=4] {'dp'}, dimensions={0}, use_global_device_ids=true | all-gather | bytes 442368 | tf_op jit(solution)/shard_map/all_gather | solution.py:452
  854.4 2.4 convert_reduce_fusion.2
  857.4 0.7 reduce.27
  858.2 37.4 %psum.14 = f32[15,768]{1,0:T(8,128)S(1)} all-reduce(f32[15,768]{1,0:T(8,128)S(1)} %concatenate.18), channel_id=1, replica_groups=mesh['dp'=8,'cls'=4] {'dp','cls'}, use_global_device_ids=true, to_apply=%region_30.31 | all-reduce | flops 11520 | bytes 92160 | tf_op jit(solution)/shard_map/psum | solution.py:499
  895.6 0.7 multiply_reduce_fusion.11
  897.0 4.4 multiply_reduce_fusion.10
  901.4 5.7 constant_dynamic-update-slice_fusion.1
  907.1 8.0 constant_dynamic-update-slice_fusion
  915.1 19.1 %reshape.235 = f32[13,384,2,384]{3,2,1,0:T(2,128)} reshape(f32[13,384,768]{2,1,0:T(8,128)} %constant_dynamic-update-slice_fusion) | data formatting | bytes 30670848 | tf_op jit(solution)/shard_map/reshape | solution.py:395
  934.2 5.5 multiply_reduce_fusion
  940.3 15.0 %fusion.4 = f32[13,2,384,96]{2,3,1,0:T(8,128)S(1)} fusion(f32[13,48,2,8,384]{4,3,2,1,0:T(8,128)} %bitcast.136, f32[13,12,2,8,384]{4,3,2,1,0:T(8,128)} %bitcast.146), kind=kOutput, calls=%fused_computation.5 | convolution fusion | flops 4416602112 | bytes 23003136 | tf_op jit(solution)/shard_map/brjk,bkjm->brjm/dot_general | solution.py:508
  955.4 20.7 %multiply_reduce_fusion.1 = (f32[13,2]{1,0:T(8,128)S(1)}, f32[13,2,384,96]{2,3,1,0:T(8,128)}) fusion(f32[13,384,2,384]{1,3,2,0:T(8,128)} %bitcast.141, f32[13,2,384,96]{2,3,1,0:T(8,128)S(1)} %fusion.4), kind=kOutput, calls=%fused_computation.29 | convolution fusion | flops 4418519040 | bytes 23003240 | tf_op jit(solution)/shard_map/brjk,bkjm->brjm/dot_general | solution.py:511
  977.0 41.7 %psum.15 = f32[54]{0:T(128)S(1)} all-reduce(f32[54]{0:T(128)S(1)} %pad_maximum_fusion.3), channel_id=1, replica_groups=mesh['dp'=8,'cls'=4] {'dp','cls'}, use_global_device_ids=true, to_apply=%region_34.35 | all-reduce | flops 54 | bytes 432 | tf_op jit(solution)/shard_map/psum | solution.py:526
  1020.2 2.6 multiply_bitcast_fusion.2
  1023.2 1.7 copy-done.21
  1024.9 2.5 sub.71
  1027.5 0.8 copy-done.13
  1028.3 2.3 broadcast_multiply_fusion
  1030.6 11.6 %constant_dynamic-slice_fusion = f32[13,384,2,96]{3,2,1,0:T(2,128)} fusion(f32[13,384,2,384]{3,2,1,0:T(2,128)} %reshape.235, s32[]{:T(128)S(6)} %select_n.58), kind=kLoop, calls=%fused_computation.147 | loop fusion | bytes 7667716 | tf_op jit(solution)/shard_map/dynamic_slice | solution.py:505
  1042.2 20.2 %multiply_bitcast_fusion = f32[13,2,12,8,384]{4,3,2,1,0:T(8,128)} fusion(f32[]{:T(128)S(6)} %mul.478, f32[13,384,2,96]{3,2,1,0:T(2,128)} %constant_dynamic-slice_fusion, f32[13,48,2,8,384]{4,3,2,1,0:T(8,128)} %bitcast.137), kind=kOutput, calls=%fused_computation.23 | convolution fusion | flops 4417560576 | bytes 23003140 | tf_op jit(solution)/shard_map/bkja,bkjm->bajm/dot_general | solution.py:507
  1062.4 4.4 copy.141
  1066.9 18.0 %multiply_bitcast_fusion.1 = f32[13,2,12,8,384]{4,3,2,1,0:T(8,128)} fusion(f32[13,12,2,8,384]{4,3,2,1,0:T(8,128)S(1)} %bitcast.142, f32[13,48,2,8,384]{4,3,2,1,0:T(8,128)S(1)} %bitcast.140, f32[]{:T(128)S(6)} %mul.478), kind=kOutput, calls=%fused_computation.25 | convolution fusion | flops 4417560576 | bytes 23003140 | tf_op jit(solution)/shard_map/brjk,bljk->brjl/dot_general | solution.py:506
  1084.9 2.6 copy.140
  1087.5 0.7 multiply_subtract_fusion.1
  1088.3 0.6 copy-done.23
  1088.9 3.8 multiply_subtract_fusion
  1092.7 7.5 multiply_add_fusion
  (165 shorter events, 8.8 us)
Async XLA Ops:
  8.0 115.5 %copy-start = (bf16[1024,768]{1,0:T(8,128)(2,1)S(1)}, bf16[1024,768]{1,0:T(8,128)(2,1)}, u32[]{:S(2)}) copy-start(bf16[1024,768]{1,0:T(8,128)(2,1)} %param.17) | copy-start | bytes 4718596
  8.0 5.1 copy-start.27
  8.0 37.6 %copy-start.8 = (s32[1,1024]{1,0:T(1,128)S(1)}, s32[1,1024]{1,0:T(1,128)}, u32[]{:S(2)}) copy-start(s32[1,1024]{1,0:T(1,128)} %qids_ref.1) | copy-start | bytes 12292
  8.1 115.5 %all-gather.10.cloned.1.call-start = ((), (), s32[]{:S(2)}) async-start(), calls=%async_computation.4 | async-start | bytes 15814656 | tf_op jit(solution)/shard_map/all_gather | solution.py:435
  8.1 37.8 %copy-start.31 = (s32[1,1024]{1,0:T(1,128)S(1)}, s32[1,1024]{1,0:T(1,128)}, u32[]{:S(2)}) copy-start(s32[1,1024]{1,0:T(1,128)} %param.19) | copy-start | bytes 12292
  8.1 39.6 %copy-start.37 = (s32[32,2]{0,1:T(2,128)S(1)}, s32[32,2]{0,1:T(2,128)}, u32[]{:S(2)}) copy-start(s32[32,2]{0,1:T(2,128)} %param.20) | copy-start | bytes 772
  10.3 239.9 %all-gather.12.cloned.1.call-start = ((), (), s32[]{:S(2)}) async-start(), calls=%async_computation.5 | async-start | bytes 9510912 | tf_op jit(solution)/shard_map/all_gather | solution.py:440
  13.0 267.3 %reduce-scatter.4.cloned.1.call-start = ((), (), s32[]{:S(2)}) async-start(), calls=%async_computation.6 | async-start | bytes 122880 | tf_op jit(solution)/shard_map/reduce_scatter | solution.py:466
  45.9 88.0 %copy-start.4 = (s32[1024,1]{1,0:T(8,128)}, s32[1024,1]{1,0:T(8,128)S(1)}, u32[]{:S(2)}) copy-start(s32[1024,1]{1,0:T(8,128)S(1)} %copy.110.qids_ref) | copy-start | bytes 12292
  48.6 137.4 %copy-start.36 = (f32[8]{0:T(128)}, f32[8]{0:T(128)S(1)}, u32[]{:S(2)}) copy-start(f32[8]{0:T(128)S(1)} %broadcast_maximum_fusion) | copy-start | bytes 100
  48.7 78.2 %copy-start.34 = (f32[768]{0:T(1024)}, f32[768]{0:T(1024)S(1)}, u32[]{:S(2)}) copy-start(f32[768]{0:T(1024)S(1)} %get-tuple-element.43) | copy-start | bytes 9220
  126.3 33.3 %copy-start.16 = (f32[768,1024]{0,1:T(8,128)}, f32[768,1024]{0,1:T(8,128)S(1)}, u32[]{:S(2)}) copy-start(f32[768,1024]{0,1:T(8,128)S(1)} %get-tuple-element.79) | copy-start | bytes 9437188
  126.9 7.0 copy-start.29
  133.9 25.6 %copy-start.2 = (bf16[3,1024,768]{2,1,0:T(8,128)(2,1)}, bf16[3,1024,768]{2,1,0:T(8,128)(2,1)S(1)}, u32[]{:S(2)}) copy-start(bf16[3,1024,768]{2,1,0:T(8,128)(2,1)S(1)} %fusion.10.q_ref.k_ref.v_ref) | copy-start | bytes 14155780
  159.5 3.4 copy-start.6
  163.0 22.2 %copy-start.9 = (f32[1024,768]{1,0:T(8,128)}, f32[1024,768]{1,0:T(8,128)S(1)}, u32[]{:S(2)}) copy-start(f32[1024,768]{1,0:T(8,128)S(1)} %get-tuple-element.81) | copy-start | bytes 9437188
  185.5 2.2 copy-start.11
  255.9 6.6 copy-start.25
  262.5 328.1 %reduce-scatter.6.cloned.1.call-start = ((), (), s32[]{:S(2)}) async-start(), calls=%async_computation.7 | async-start | bytes 12165120 | tf_op jit(solution)/shard_map/reduce_scatter | solution.py:491
  280.4 4.1 copy-start.12
  286.3 33.1 %copy-start.10 = (f32[1024,768]{1,0:T(8,128)S(1)}, f32[1024,768]{1,0:T(8,128)}, u32[]{:S(2)}) copy-start(f32[1024,768]{1,0:T(8,128)} %copy-done.9) | copy-start | bytes 9437188
  319.4 3.0 copy-start.18
  323.8 1.4 copy-start.7
  323.8 7.0 slice-start
  325.2 5.6 slice-start.1
  328.1 2.8 copy-start.5
  330.9 40.5 %copy-start.17 = (f32[768,1024]{0,1:T(8,128)S(1)}, f32[768,1024]{0,1:T(8,128)}, u32[]{:S(2)}) copy-start(f32[768,1024]{0,1:T(8,128)} %copy-done.16) | copy-start | bytes 9437188
  330.9 40.5 %copy-start.30 = (f32[1024]{0:T(1024)S(1)}, f32[1024]{0:T(1024)}, u32[]{:S(2)}) copy-start(f32[1024]{0:T(1024)} %copy-done.29) | copy-start | bytes 12292
  330.9 40.5 %copy-start.35 = (f32[768]{0:T(1024)S(1)}, f32[768]{0:T(1024)}, u32[]{:S(2)}) copy-start(f32[768]{0:T(1024)} %copy-done.34) | copy-start | bytes 9220
  371.5 4.6 copy-start.3
  384.6 1.7 copy-start.22
  391.0 412.7 %reduce-scatter.8.cloned.1.call-start = ((), (), s32[]{:S(2)}) async-start(), calls=%async_computation.9 | async-start | bytes 19464192 | tf_op jit(solution)/shard_map/reduce_scatter | solution.py:491
  406.0 398.5 %all-gather.8.cloned.1.call-start = ((), (), s32[]{:S(2)}) async-start(), calls=%async_computation.3 | async-start | bytes 16293888 | tf_op jit(solution)/shard_map/all_gather | solution.py:441
  408.4 488.6 %all-gather.18.cloned.1.call-start = ((), (), s32[]{:S(2)}) async-start(), calls=%async_computation.11 | async-start | bytes 3170304 | tf_op jit(solution)/shard_map/all_gather | solution.py:467
  409.0 492.4 %all-gather.14.cloned.1.call-start = ((), (), s32[]{:S(2)}) async-start(), calls=%async_computation.8 | async-start | bytes 6266880 | tf_op jit(solution)/shard_map/all_gather | solution.py:492
  590.6 316.5 %all-gather.16.cloned.1.call-start = ((), (), s32[]{:S(2)}) async-start(), calls=%async_computation.10 | async-start | bytes 10027008 | tf_op jit(solution)/shard_map/all_gather | solution.py:492
  804.5 17.4 %copy-start.26 = (bf16[32,768]{1,0:T(8,128)(2,1)S(1)}, bf16[32,768]{1,0:T(8,128)(2,1)}, u32[]{:S(2)}) copy-start(bf16[32,768]{1,0:T(8,128)(2,1)} %all_gather.30) | copy-start | bytes 147460
  1022.8 2.1 copy-start.21
  1024.9 3.4 copy-start.13
  1030.6 36.3 %slice-start.2 = ((s8[15335424]{0:T(1024)(128)(4,1)}), s8[2752512]{0:T(1024)(128)(4,1)S(1)}, s32[]{:S(2)}) async-start(s8[15335424]{0:T(1024)(128)(4,1)} %bitcast.138), calls=%async_computation.14 | async-start | bytes 5505024
  1042.2 24.7 %slice-start.3 = ((s8[15335424]{0:T(1024)(128)(4,1)}), s8[4194304]{0:T(1024)(128)(4,1)S(1)}, s32[]{:S(2)}) async-start(s8[15335424]{0:T(1024)(128)(4,1)} %bitcast.138), calls=%async_computation.15 | async-start | bytes 8388608
  1042.2 24.7 %slice-start.4 = ((s8[15335424]{0:T(1024)(128)(4,1)}), s8[4194304]{0:T(1024)(128)(4,1)S(1)}, s32[]{:S(2)}) async-start(s8[15335424]{0:T(1024)(128)(4,1)} %bitcast.138), calls=%async_computation.16 | async-start | bytes 8388608
  1042.2 24.7 %slice-start.5 = ((s8[15335424]{0:T(1024)(128)(4,1)}), s8[4194304]{0:T(1024)(128)(4,1)S(1)}, s32[]{:S(2)}) async-start(s8[15335424]{0:T(1024)(128)(4,1)} %bitcast.138), calls=%async_computation.17 | async-start | bytes 8388608
  1062.4 4.4 copy-start.14
  1066.9 21.3 %copy-start.24 = (f32[96,5462]{1,0:T(8,128)S(1)}, f32[96,5462]{1,0:T(8,128)}, u32[]{:S(2)}) copy-start(f32[96,5462]{1,0:T(8,128)} %param.28) | copy-start | bytes 6292228
  1084.9 2.6 copy-start.28
  1084.9 2.6 copy-start.32
  1084.9 2.6 copy-start.33
  1084.9 3.3 copy-start.19
  1084.9 3.4 copy-start.20
  1084.9 4.1 copy-start.23
  1088.9 3.8 copy-start.15
  1092.7 7.5 copy-start.1
Sparse Core Ops, SparseCore 0:
  12.4 111.0 all-gather.9
  126.3 123.8 all-gather.11
  262.6 17.6 reduce-scatter.3
  391.1 199.4 reduce-scatter.5
  598.0 205.6 reduce-scatter.7
Sparse Core Ops, SparseCore 1:
  408.6 113.8 all-gather.7
  525.1 73.1 all-gather.17
  599.8 38.0 all-gather.13
  803.8 58.7 all-gather.15

commit v3 on v2

--- a/solution.py
+++ b/solution.py
@@ -1,3 +1,5 @@
+import functools
+
 import jax
 import jax.numpy as jnp
 from jax import lax
@@ -13,6 +15,10 @@
 PAIR = 2 * HEAD
 ROWS = 256
 HIDDEN_TILE = 384
+MESH = pl.DeviceIdType.MESH
+CODE_TOP = 32766.0
+CODE_FLOOR = 1e-33
+PIECE = 48
 IMG_PACK = 8
 
 
@@ -362,8 +368,7 @@
     grad_embed_norm, grad_gain_one, grad_shift_one = norm_one_back(grad_normed_one)
     grad_embedded = (grad_hidden + grad_embed_norm).astype(jnp.bfloat16)
     grad_patch = jnp.einsum("tp,td->pd", patch, grad_embedded, preferred_element_type=jnp.float32)
-    grad_first = jnp.concatenate([grad_patch[None], grad_qkv_proj, grad_out_proj[None]], 0)
-    grad_mlp = jnp.concatenate([grad_up, grad_down], 0)
+    grad_arrays = (grad_patch[None], grad_qkv_proj, grad_out_proj[None], grad_up, grad_down)
     bias_sums = jnp.stack(
         [
             jnp.sum(grad_embedded.astype(jnp.float32), 0),
@@ -378,7 +383,551 @@
     )
     up_sums = up_sums.reshape(up_count, feature_dim)
     tail_sums = jnp.stack([jnp.sum(grad_branch.astype(jnp.float32), 0), grad_gain, grad_shift])
-    return (grad_first, grad_mlp, jnp.concatenate([bias_sums, up_sums, tail_sums], 0))
+    return (grad_arrays, jnp.concatenate([bias_sums, up_sums, tail_sums], 0))
+
+
+def torus_place():
+    dp, cls = lax.axis_index("dp"), lax.axis_index("cls")
+    return dp // 2, dp % 2, cls // 2, cls % 2
+
+
+def torus_device(z, y, x, core):
+    return (z * 2 + y, x * 2 + core)
+
+
+def encode(pieces, code_refs, scale_ref):
+    top = None
+    for piece in pieces:
+        peak = jnp.max(jnp.abs(piece()), 0, keepdims=True)
+        top = peak if top is None else jnp.maximum(top, peak)
+    top = jnp.maximum(top, CODE_FLOOR)
+    inverse = CODE_TOP / top
+    for piece, code_ref in zip(pieces, code_refs):
+        code_ref[...] = jnp.round(piece() * inverse).astype(jnp.int32).astype(jnp.int16)
+    scale_ref[...] = top * (1.0 / CODE_TOP)
+
+
+def decode(code, scale):
+    return code.astype(jnp.int32).astype(jnp.float32) * scale
+
+
+def reduce_kernel(counts, *refs):
+    sources, refs = refs[: len(counts)], refs[len(counts) :]
+    (vec_ref, codes_hbm, scales_hbm, vec_out_ref,
+     acc, spare, kept, sent0, got0, sent1, got1, sent2, got2, sent3, got3, sent4, got4,
+     ss0, gs0, ss1, gs1, ss2, gs2, ss3, gs3, ss4, gs4, codes, scales, vec_got,
+     load_sem, out_sem, send_sem, recv_sem, send_scale_sem, recv_scale_sem,
+     vec_send_sem, vec_recv_sem) = refs
+    total = sum(counts)
+    half, width = codes.shape[1], codes.shape[2]
+    cols = width // 2
+    z, y, x, core = torus_place()
+    upper = z // 2
+    inner = (z % 2) != upper
+    mate_core = torus_device(z, y, x, 1 - core)
+    mate_x = torus_device(z, y, 1 - x, core)
+    mate_y = torus_device(z, 1 - y, x, core)
+    mate_z = torus_device(z + 1 - 2 * (z % 2), y, x, core)
+    mate_mid = torus_device(3 - z, y, x, core)
+    mate_far = torus_device((z + 2) % 4, y, x, core)
+
+    barrier = pltpu.get_barrier_semaphore()
+    mates = (mate_core, mate_x, mate_y, mate_z, mate_mid, mate_far)
+    for mate in mates:
+        pl.semaphore_signal(barrier, inc=1, device_id=mate, device_id_type=MESH)
+    pl.semaphore_wait(barrier, len(mates))
+
+    own_cols = pl.ds(pl.multiple_of(core * cols, 128), cols)
+    other_cols = pl.ds(pl.multiple_of((1 - core) * cols, 128), cols)
+
+    def rows_at(start, size):
+        return pl.ds(pl.multiple_of(start, PIECE), size)
+
+    def loads(m, body):
+        start = 0
+        for source, count in zip(sources, counts):
+            def one(source=source, start=start):
+                pair = (
+                    pltpu.make_async_copy(
+                        source.at[m - start, :, own_cols], acc.at[m % 5], load_sem.at[m % 2, 0]
+                    ),
+                    pltpu.make_async_copy(
+                        source.at[m - start, :, other_cols], spare.at[m % 2], load_sem.at[m % 2, 1]
+                    ),
+                )
+                for copy in pair:
+                    body(copy)
+
+            pl.when((m >= start) & (m < start + count))(one)
+            start += count
+
+    def message(stage, m, source, scale_source, target, scale_target, mate):
+        return (
+            pltpu.make_async_remote_copy(
+                src_ref=source, dst_ref=target,
+                send_sem=send_sem.at[stage, m % 2], recv_sem=recv_sem.at[stage, m],
+                device_id=mate, device_id_type=MESH,
+            ),
+            pltpu.make_async_remote_copy(
+                src_ref=scale_source, dst_ref=scale_target,
+                send_sem=send_scale_sem.at[stage, m % 2], recv_sem=recv_scale_sem.at[stage, m],
+                device_id=mate, device_id_type=MESH,
+            ),
+        )
+
+    def first(m):
+        return message(0, m, sent0.at[m % 2], ss0.at[m % 2], got0.at[m], gs0.at[m], mate_core)
+
+    def second(m, b):
+        return message(
+            1 + b, m, sent1.at[m % 2, b], ss1.at[m % 2, b], got1.at[m, b], gs1.at[m, b],
+            mate_y if b else mate_x,
+        )
+
+    def third(m, b):
+        return message(
+            3 + b, m, sent2.at[m % 2, b], ss2.at[m % 2, b], got2.at[m, b], gs2.at[m, b],
+            mate_x if b else mate_y,
+        )
+
+    def fourth(m):
+        return message(5, m, sent3.at[m % 2], ss3.at[m % 2], got3.at[m], gs3.at[m], mate_z)
+
+    def fifth(m):
+        return message(6, m, sent4.at[m % 2], ss4.at[m % 2], got4.at[m], gs4.at[m], mate_mid)
+
+    piece_a = 2 * x + y
+    piece_b = 4 + 2 * y + x
+
+    def spread(stage, m, piece, count, mate, columns=own_cols):
+        rows = pl.ds(pl.multiple_of(piece * PIECE, PIECE), count * PIECE)
+        block = codes.at[m, rows, columns]
+        scale = scales.at[m, pl.ds(piece, count), :, columns]
+        return message(stage, m, block, scale, block, scale, mate)
+
+    def start(copies):
+        for copy in copies:
+            copy.start()
+
+    def wait_send(copies):
+        for copy in copies:
+            copy.wait_send()
+
+    def wait_recv(copies):
+        for copy in copies:
+            copy.wait_recv()
+
+    def vec_copy(step, mate):
+        return pltpu.make_async_remote_copy(
+            src_ref=vec_got.at[step, 0], dst_ref=vec_got.at[step, 1],
+            send_sem=vec_send_sem.at[step], recv_sem=vec_recv_sem.at[step],
+            device_id=mate, device_id_type=MESH,
+        )
+
+    vec_mates = (mate_core, mate_x, mate_y, mate_z, mate_far)
+
+    loads(jnp.int32(0), lambda copy: copy.start())
+    vec_got[0, 0] = vec_ref[...]
+    vec_copy(0, vec_mates[0]).start()
+
+    def step(t, carry):
+        for n in range(1, 6):
+            @pl.when(t == n)
+            def _(n=n):
+                vec_copy(n - 1, vec_mates[n - 1]).wait()
+                value = vec_got[n - 1, 0] + vec_got[n - 1, 1]
+                if n < 5:
+                    vec_got[n, 0] = value
+                    vec_copy(n, vec_mates[n]).start()
+                else:
+                    vec_out_ref[...] = value
+
+        @pl.when(t < total)
+        def _():
+            m = t
+            loads(m, lambda copy: copy.wait())
+
+            @pl.when(m + 1 < total)
+            def _():
+                loads(m + 1, lambda copy: copy.start())
+
+            span = 2 * PIECE
+            encode(
+                [lambda r=r: spare[m % 2, r : r + span, :] for r in range(0, 2 * half, span)],
+                [sent0.at[m % 2, r : r + span, :] for r in range(0, 2 * half, span)],
+                ss0.at[m % 2],
+            )
+            start(first(m))
+
+        @pl.when((t >= 1) & (t < total + 1))
+        def _():
+            m = t - 1
+            copies = first(m)
+            wait_send(copies)
+            wait_recv(copies)
+            slot = m % 5
+            span = 2 * PIECE
+            for r in range(0, 2 * half, span):
+                acc[slot, r : r + span, :] += decode(got0[m, r : r + span, :], gs0[m])
+            for b in range(2):
+                other = (1 - y) if b else (1 - x)
+                begins = [h * half + b * 4 * PIECE + other * span for h in range(2)]
+                encode(
+                    [lambda s=s: acc[slot, rows_at(s, span), :] for s in begins],
+                    [sent1.at[m % 2, b, h] for h in range(2)],
+                    ss1.at[m % 2, b],
+                )
+                start(second(m, b))
+
+        @pl.when((t >= 2) & (t < total + 2))
+        def _():
+            m = t - 2
+            slot = m % 5
+            span = 2 * PIECE
+            for b in range(2):
+                copies = second(m, b)
+                wait_send(copies)
+                wait_recv(copies)
+                mine = y if b else x
+                other = (1 - x) if b else (1 - y)
+                begins = [h * half + b * 4 * PIECE + mine * span for h in range(2)]
+                for h, s in enumerate(begins):
+                    acc[slot, rows_at(s, span), :] += decode(got1[m, b, h], gs1[m, b])
+                encode(
+                    [lambda s=s: acc[slot, rows_at(s + other * PIECE, PIECE), :] for s in begins],
+                    [sent2.at[m % 2, b, h] for h in range(2)],
+                    ss2.at[m % 2, b],
+                )
+                start(third(m, b))
+
+        @pl.when((t >= 3) & (t < total + 3))
+        def _():
+            m = t - 3
+            slot = m % 5
+            for b in range(2):
+                copies = third(m, b)
+                wait_send(copies)
+                wait_recv(copies)
+                place = piece_b if b else piece_a
+                for h in range(2):
+                    kept[m % 3, h, b] = acc[
+                        slot, rows_at(h * half + place * PIECE, PIECE), :
+                    ] + decode(got2[m, b, h], gs2[m, b])
+
+            @pl.when(jnp.logical_not(inner))
+            def _():
+                pairs = [(h, b) for h in range(2) for b in range(2)]
+                encode(
+                    [lambda h=h, b=b: kept[m % 3, h, b] for h, b in pairs],
+                    [sent3.at[m % 2, h, b] for h, b in pairs],
+                    ss3.at[m % 2],
+                )
+                start(fourth(m))
+
+        @pl.when((t >= 4) & (t < total + 4))
+        def _():
+            m = t - 4
+            copies = fourth(m)
+
+            @pl.when(jnp.logical_not(inner))
+            def _():
+                wait_send(copies)
+
+            @pl.when(inner)
+            def _():
+                wait_recv(copies)
+                for h in range(2):
+                    for b in range(2):
+                        kept[m % 3, h, b] += decode(got3[m, h, b], gs3[m])
+                encode(
+                    [lambda b=b: kept[m % 3, 1 - upper, b] for b in range(2)],
+                    [sent4.at[m % 2, b] for b in range(2)],
+                    ss4.at[m % 2],
+                )
+                start(fifth(m))
+
+        @pl.when((t >= 5) & (t < total + 5))
+        def _():
+            m = t - 5
+
+            @pl.when(inner)
+            def _():
+                copies = fifth(m)
+                wait_send(copies)
+                wait_recv(copies)
+                for b in range(2):
+                    place = piece_b if b else piece_a
+                    value = kept[m % 3, upper, b] + decode(got4[m, b], gs4[m])
+                    encode(
+                        [lambda value=value: value],
+                        [codes.at[m, rows_at(place * PIECE, PIECE), own_cols]],
+                        scales.at[m, place, :, own_cols],
+                    )
+                    start(spread(7 + b, m, place, 1, mate_z))
+
+        @pl.when((t >= 6) & (t < total + 6))
+        def _():
+            m = t - 6
+            for b in range(2):
+                place = piece_b if b else piece_a
+                copies = spread(7 + b, m, place, 1, mate_z)
+
+                @pl.when(inner)
+                def _(copies=copies):
+                    wait_send(copies)
+
+                @pl.when(jnp.logical_not(inner))
+                def _(copies=copies):
+                    wait_recv(copies)
+
+                start(spread(9 + b, m, place, 1, mate_x if b else mate_y))
+
+        @pl.when((t >= 7) & (t < total + 7))
+        def _():
+            m = t - 7
+            for b in range(2):
+                place = piece_b if b else piece_a
+                theirs = (4 + 2 * y + 1 - x) if b else (2 * x + 1 - y)
+                wait_send(spread(9 + b, m, place, 1, mate_x if b else mate_y))
+                wait_recv(spread(9 + b, m, theirs, 1, mate_x if b else mate_y))
+                begin = (4 + 2 * y) if b else 2 * x
+                start(spread(11 + b, m, begin, 2, mate_y if b else mate_x))
+
+        @pl.when((t >= 8) & (t < total + 8))
+        def _():
+            m = t - 8
+            for b in range(2):
+                begin = (4 + 2 * y) if b else 2 * x
+                theirs = (4 + 2 * (1 - y)) if b else 2 * (1 - x)
+                wait_send(spread(11 + b, m, begin, 2, mate_y if b else mate_x))
+                wait_recv(spread(11 + b, m, theirs, 2, mate_y if b else mate_x))
+            start(spread(13, m, 0, 8, mate_core))
+
+        def outs(m):
+            return (
+                pltpu.make_async_copy(codes.at[m], codes_hbm.at[m], out_sem.at[m % 2, 0]),
+                pltpu.make_async_copy(scales.at[m], scales_hbm.at[m], out_sem.at[m % 2, 1]),
+            )
+
+        @pl.when((t >= 9) & (t < total + 9))
+        def _():
+            m = t - 9
+            wait_send(spread(13, m, 0, 8, mate_core))
+            wait_recv(spread(13, m, 0, 8, mate_core, other_cols))
+            start(outs(m))
+
+        @pl.when((t >= 10) & (t < total + 10))
+        def _():
+            for copy in outs(t - 10):
+                copy.wait()
+
+        return carry
+
+    lax.fori_loop(0, total + 10, step, 0)
+
+
+def reduce_gradients(arrays, vec_sums):
+    counts = tuple(array.shape[0] for array in arrays)
+    total = sum(counts)
+    width = arrays[0].shape[1]
+    half, cols = width // 2, width // 2
+    f32, i16 = jnp.float32, jnp.int16
+
+    def pair(*shape):
+        return [pltpu.VMEM((2,) + shape, i16), pltpu.VMEM((total,) + shape, i16)]
+
+    def scale_pair(*shape):
+        return [
+            pltpu.VMEM((2,) + shape + (1, cols), f32),
+            pltpu.VMEM((total,) + shape + (1, cols), f32),
+        ]
+
+    hbm = pl.BlockSpec(memory_space=pl.ANY)
+    vmem = pl.BlockSpec(memory_space=pltpu.VMEM)
+    return pl.pallas_call(
+        functools.partial(reduce_kernel, counts),
+        out_shape=(
+            jax.ShapeDtypeStruct((total, half, width), i16),
+            jax.ShapeDtypeStruct((total, half // PIECE, 1, width), f32),
+            jax.ShapeDtypeStruct(vec_sums.shape, f32),
+        ),
+        in_specs=[hbm] * len(arrays) + [vmem],
+        out_specs=(hbm, hbm, vmem),
+        scratch_shapes=[
+            pltpu.VMEM((5, width, cols), f32),
+            pltpu.VMEM((2, width, cols), f32),
+            pltpu.VMEM((3, 2, 2, PIECE, cols), f32),
+        ]
+        + pair(width, cols)
+        + pair(2, 2, 2 * PIECE, cols)
+        + pair(2, 2, PIECE, cols)
+        + pair(2, 2, PIECE, cols)
+        + pair(2, PIECE, cols)
+        + scale_pair()
+        + scale_pair(2)
+        + scale_pair(2)
+        + scale_pair()
+        + scale_pair()
+        + [
+            pltpu.VMEM((total, half, width), i16),
+            pltpu.VMEM((total, half // PIECE, 1, width), f32),
+            pltpu.VMEM((5, 2) + vec_sums.shape, f32),
+            pltpu.SemaphoreType.DMA((2, 2)),
+            pltpu.SemaphoreType.DMA((2, 2)),
+            pltpu.SemaphoreType.DMA((14, 2)),
+            pltpu.SemaphoreType.DMA((14, total)),
+            pltpu.SemaphoreType.DMA((14, 2)),
+            pltpu.SemaphoreType.DMA((14, total)),
+            pltpu.SemaphoreType.DMA((5,)),
+            pltpu.SemaphoreType.DMA((5,)),
+        ],
+        compiler_params=pltpu.CompilerParams(
+            collective_id=1, has_side_effects=True, vmem_limit_bytes=60 << 20
+        ),
+        name="reduce_gradients",
+    )(*arrays, vec_sums)
+
+
+def split_float(values):
+    high = values.astype(jnp.bfloat16)
+    return high, (values - high.astype(jnp.float32)).astype(jnp.bfloat16)
+
+
+def stacked_dot(lefts, right, contract_last):
+    rows = lefts[0].shape[0]
+    left = jnp.concatenate(lefts, 0) if len(lefts) > 1 else lefts[0]
+    dims = (((1,), (1 if contract_last else 0,)), ((), ()))
+    out = lax.dot_general(left, right, dims, preferred_element_type=jnp.float32)
+    return [out[n * rows : (n + 1) * rows] for n in range(len(lefts))]
+
+
+def precondition_kernel(
+    own_count, codes_ref, scales_ref, left_ref, right_ref,
+    left_out, right_out, step_out, own_out, squares_ref, high_ref, low_ref
+):
+    half, width = codes_ref.shape
+    rows = left_ref.shape[0]
+    own = lax.rem(lax.axis_index("dp"), own_count) * rows
+    own_rows = pl.ds(pl.multiple_of(own, PIECE), rows)
+    for piece in range(half // PIECE):
+        part = slice(piece * PIECE, (piece + 1) * PIECE)
+        value = codes_ref[part, :].astype(jnp.int32).astype(jnp.float32) * scales_ref[piece]
+        high_ref[part, :], low_ref[part, :] = split_float(value)
+    own_value = high_ref[own_rows, :].astype(jnp.float32) + low_ref[own_rows, :].astype(jnp.float32)
+    own_out[...] = own_value
+    squares_ref[0:1, :] = jnp.sum(own_value * own_value, 0, keepdims=True)
+    picks = (
+        lax.broadcasted_iota(jnp.int32, (rows, half), 1)
+        == lax.broadcasted_iota(jnp.int32, (rows, half), 0) + own
+    ).astype(jnp.float32).astype(jnp.bfloat16)
+    for quad in range(2):
+        cols = slice(quad * half, (quad + 1) * half)
+        high, low = high_ref[:, cols], low_ref[:, cols]
+        mine_high, mine_low = high_ref[own_rows, cols], low_ref[own_rows, cols]
+        hh, lh, turned_high = stacked_dot([mine_high, mine_low, picks], high, True)
+        hl, turned_low = stacked_dot([mine_high, picks], low, True)
+        left_out[:, cols] = hh + (lh + hl)
+        turned_high = turned_high.astype(jnp.bfloat16)
+        turned_low = turned_low.astype(jnp.bfloat16)
+        root_high, root_low = split_float(left_ref[:, cols])
+        thh, tlh, rhh, rlh = stacked_dot([turned_high, turned_low, root_high, root_low], high, False)
+        thl, rhl = stacked_dot([turned_high, root_high], low, False)
+        right_out[:, cols] = thh + (tlh + thl)
+        half_step = rhh + (rlh + rhl)
+        step_high, step_low = split_float(half_step)
+        right_high, right_low = split_float(right_ref[:, cols])
+        shh, slh = stacked_dot([step_high, step_low], right_high, False)
+        (shl,) = stacked_dot([step_high], right_low, False)
+        direction = shh + (slh + shl)
+        step_out[:, cols] = direction
+        squares_ref[1:2, cols] = jnp.sum(direction * direction, 0, keepdims=True)
+
+
+def precondition(codes, scales, root_left, right_half, own_count):
+    count, half, width = codes.shape
+    rows = root_left.shape[1]
+
+    def spec(*shape):
+        return pl.BlockSpec((None,) + shape, lambda b: (b,) + (0,) * len(shape))
+
+    mine = jax.ShapeDtypeStruct((count, rows, width), jnp.float32)
+    return pl.pallas_call(
+        functools.partial(precondition_kernel, own_count),
+        grid=(count,),
+        out_shape=(mine, mine, mine, mine, jax.ShapeDtypeStruct((count, 2, width), jnp.float32)),
+        in_specs=[
+            spec(half, width),
+            spec(half // PIECE, 1, width),
+            spec(rows, width),
+            spec(half, width),
+        ],
+        out_specs=(spec(rows, width),) * 4 + (spec(2, width),),
+        scratch_shapes=[
+            pltpu.VMEM((half, width), jnp.bfloat16),
+            pltpu.VMEM((half, width), jnp.bfloat16),
+        ],
+        compiler_params=pltpu.CompilerParams(vmem_limit_bytes=32 << 20),
+        name="precondition",
+    )(codes, scales, root_left, right_half)
+
+
+def sum_kernel(dp_count, cls_count, in_ref, out_ref, slots, send_sem, recv_sem):
+    dp, cls = lax.axis_index("dp"), lax.axis_index("cls")
+    total = dp_count * cls_count
+    me = dp * cls_count + cls
+    barrier = pltpu.get_barrier_semaphore()
+
+    def mate(n):
+        other = lax.rem(me + n, total)
+        return (other // cls_count, lax.rem(other, cls_count))
+
+    for n in range(1, total):
+        pl.semaphore_signal(barrier, inc=1, device_id=mate(n), device_id_type=MESH)
+    pl.semaphore_wait(barrier, total - 1)
+
+    def copy(n):
+        return pltpu.make_async_remote_copy(
+            src_ref=in_ref, dst_ref=slots.at[me],
+            send_sem=send_sem.at[n], recv_sem=recv_sem.at[me],
+            device_id=mate(n), device_id_type=MESH,
+        )
+
+    def arrival(n):
+        source = lax.rem(me + n, total)
+        return pltpu.make_async_remote_copy(
+            src_ref=in_ref, dst_ref=slots.at[source],
+            send_sem=send_sem.at[n], recv_sem=recv_sem.at[source],
+            device_id=mate(n), device_id_type=MESH,
+        )
+
+    for n in range(1, total):
+        copy(n).start()
+    slots[me] = in_ref[...]
+    for n in range(1, total):
+        copy(n).wait_send()
+        arrival(n).wait_recv()
+    value = slots[0]
+    for n in range(1, total):
+        value = value + slots[n]
+    out_ref[...] = value
+
+
+def sum_everywhere(values, dp_count, cls_count):
+    total = dp_count * cls_count
+    vmem = pl.BlockSpec(memory_space=pltpu.VMEM)
+    return pl.pallas_call(
+        functools.partial(sum_kernel, dp_count, cls_count),
+        out_shape=jax.ShapeDtypeStruct(values.shape, jnp.float32),
+        in_specs=[vmem],
+        out_specs=vmem,
+        scratch_shapes=[
+            pltpu.VMEM((total,) + values.shape, jnp.float32),
+            pltpu.SemaphoreType.DMA((total,)),
+            pltpu.SemaphoreType.DMA((total,)),
+        ],
+        compiler_params=pltpu.CompilerParams(collective_id=2, has_side_effects=True),
+        name="sum_everywhere",
+    )(values)
 
 
 def adam_step(weight, grad, first, second, count):
@@ -393,6 +942,31 @@
 def split_halves(values, half_size):
     block_count, row_count, feature_dim = values.shape
     return values.reshape(block_count, row_count, 2, half_size)
+
+
+def reduced_half(values, half_groups):
+    part = lax.psum_scatter(values, ("dp", "cls"), scatter_dimension=1, tiled=True)
+    return lax.all_gather(part, ("dp", "cls"), axis=1, tiled=True, axis_index_groups=half_groups)
+
+
+def preconditioned_rows(grad_half, root_left, right_half, own_start):
+    count, row_count, width = root_left.shape
+    half_size = width // 2
+    block_rows = lax.dynamic_slice_in_dim(grad_half, own_start, row_count, 1)
+    grad_quads = split_halves(grad_half, half_size)
+    rows_quads = split_halves(block_rows, half_size)
+    cols_quads = lax.dynamic_slice_in_dim(grad_quads, own_start, row_count, 3)
+    precise = FULL_PRECISION
+    left_add = jnp.einsum("brjk,bljk->brjl", rows_quads, grad_quads, precision=precise)
+    right_add = jnp.einsum("bkja,bkjm->bajm", cols_quads, grad_quads, precision=precise)
+    direction = jnp.einsum(
+        "brjk,bkjm->brjm", split_halves(root_left, half_size), grad_quads, precision=precise
+    )
+    direction = jnp.einsum(
+        "brjk,bkjm->brjm", direction, split_halves(right_half, half_size), precision=precise
+    )
+    flat = (count, row_count, width)
+    return left_add.reshape(flat), right_add.reshape(flat), direction.reshape(flat), block_rows
 
 
 def on_device(
@@ -475,7 +1049,7 @@
 
     pool_back = jax.vjp(pool_local, output, final_gain, final_shift)[1]
     grad_output, grad_gain, grad_shift = pool_back(grad_pooled)
-    grad_first, grad_mlp, grad_vectors = layer_backward(
+    grad_arrays, grad_vectors = layer_backward(
         blocks,
         vec_all,
         patches,
@@ -487,43 +1061,42 @@
         grad_shift,
     )
 
-    def reduced_half(values):
-        part = lax.psum_scatter(values, ("dp", "cls"), scatter_dimension=1, tiled=True)
-        return lax.all_gather(
-            part, ("dp", "cls"), axis=1, tiled=True, axis_index_groups=half_groups
+    on_torus = dp_count == 8 and cls_count == 4
+    if on_torus:
+        padded = jnp.pad(grad_vectors, ((0, -grad_vectors.shape[0] % 8), (0, 0)))
+        codes, scales, vector_sum = reduce_gradients(grad_arrays, padded)
+        vector_sum = vector_sum[: grad_vectors.shape[0]]
+        left_add, right_add, direction, block_rows, squares = precondition(
+            codes, scales, root_left, right_half, half_dp
         )
-
-    grad_half = jnp.concatenate([reduced_half(grad_first), reduced_half(grad_mlp)], 0)
-    own_start = (dp_index % half_dp) * row_count
-    block_rows = lax.dynamic_slice_in_dim(grad_half, own_start, row_count, 1)
-    vector_sum = lax.psum(grad_vectors, ("dp", "cls"))
+        layer_squares = jnp.sum(squares[:, 0])
+        block_squares = jnp.sum(squares[:, 1].reshape(block_count, 2, half_size), -1)
+    else:
+        grad_half = reduced_half(jnp.concatenate(grad_arrays, 0), half_groups)
+        vector_sum = lax.psum(grad_vectors, ("dp", "cls"))
+        left_add, right_add, direction, block_rows = preconditioned_rows(
+            grad_half, root_left, right_half, (dp_index % half_dp) * row_count
+        )
+        layer_squares = jnp.sum(block_rows * block_rows)
+        block_squares = jnp.sum(split_halves(direction * direction, half_size), (1, 3))
     vector_rows = lax.dynamic_slice_in_dim(vector_sum, dp_index * row_count, row_count, 1)
-
-    precise = lax.Precision.HIGHEST
-    grad_quads = split_halves(grad_half, half_size)
-    rows_quads = split_halves(block_rows, half_size)
-    cols_quads = lax.dynamic_slice_in_dim(grad_quads, own_start, row_count, 3)
-    left_add = jnp.einsum("brjk,bljk->brjl", rows_quads, grad_quads, precision=precise)
-    right_add = jnp.einsum("bkja,bkjm->bajm", cols_quads, grad_quads, precision=precise)
-    direction = jnp.einsum(
-        "brjk,bkjm->brjm", split_halves(root_left, half_size), grad_quads, precision=precise
-    )
-    direction = jnp.einsum(
-        "brjk,bkjm->brjm", direction, split_halves(right_half, half_size), precision=precise
-    )
-    block_squares = jnp.sum(direction * direction, (1, 3))
     in_top = (dp_index < half_dp).astype(jnp.float32)
     once = (cls_index == 0).astype(jnp.float32)
-    layer_squares = once * jnp.sum(block_rows * block_rows)
-    vector_squares = once * jnp.sum(vector_rows * vector_rows)
+    own_squares = once * (layer_squares + jnp.sum(vector_rows * vector_rows))
     packed = jnp.concatenate(
         [
             (once * in_top * block_squares).reshape(-1),
             (once * (1.0 - in_top) * block_squares).reshape(-1),
-            jnp.stack([layer_squares + vector_squares + jnp.sum(head_grad * head_grad), loss_part]),
+            jnp.stack([own_squares + jnp.sum(head_grad * head_grad), loss_part]),
         ]
     )
-    packed = lax.psum(packed, ("dp", "cls"))
+    if on_torus:
+        spare = -packed.shape[0] % 1024
+        packed = sum_everywhere(
+            jnp.pad(packed, (0, spare)).reshape(8, 128), dp_count, cls_count
+        ).reshape(-1)
+    else:
+        packed = lax.psum(packed, ("dp", "cls"))
     loss = packed[4 * block_count + 1]
     grad_norm = jnp.sqrt(packed[4 * block_count])
     factor = CLIP_NORM / jnp.maximum(grad_norm, CLIP_NORM)
@@ -531,11 +1104,11 @@
     mean_squares = jnp.where(dp_index < half_dp, sums[0], sums[1]) / (half_size * half_size)
     mean_squares = mean_squares * factor * factor
     scale = factor * lax.rsqrt(mean_squares + ROOT_EPS)
-    flat = (block_count, row_count, feature_dim)
-    new_blocks = enc_weights - SHAMPOO_RATE * (direction * scale[:, None, :, None]).reshape(flat)
+    wide_scale = jnp.repeat(SHAMPOO_RATE * scale, half_size, axis=1)
+    new_blocks = enc_weights - direction * wide_scale[:, None, :]
     square_factor = 0.5 * factor * factor
-    new_left = 0.5 * stats_left + square_factor * left_add.reshape(flat)
-    new_right = 0.5 * stats_right + square_factor * right_add.reshape(flat)
+    new_left = 0.5 * stats_left + square_factor * left_add
+    new_right = 0.5 * stats_right + square_factor * right_add
     count = step.astype(jnp.float32)
     new_vec, new_vec_m, new_vec_v = adam_step(vectors, vector_rows * factor, vec_m, vec_v, count)
     new_head, new_head_m, new_head_v = adam_step(

time: 1110 us -> 646 us (0.58)
  waiting for transfers between devices: 543 us -> 131 us
  Pallas kernels: 120 us -> 276 us
  blocking collectives: 150 us -> 70.6 us
  matrix products: 128 us -> 62.4 us
  local copies, waits for them, and re-layouts: 80.2 us -> 34.6 us
  other arithmetic: 66.3 us -> 45.1 us
    reduce_scatter x2 -> x0, waiting for transfers between devices: 395 us -> none  [reduced_half(): lax.psum_scatter(values, ('dp', 'cls'), scatter_dimension=1, tiled=True)]
    pallas_call x0 -> x3, Pallas kernels: none -> 154 us  [the longest x1 115 us: reduce_gradients(): pl.pallas_call(functools.partial(reduce_kernel, counts), out_shape=(jax.S...]
    psum x2 -> x0, blocking collectives: 79.1 us -> none  [the longest x1 41.7 us: on_device(): packed = lax.psum(packed, ('dp', 'cls'))]
    dot_general x4 -> x0, matrix products: 73.9 us -> none  [the longest x1 20.7 us: on_device(): jnp.einsum('brjk,bkjm->brjm', direction, split_halves(right_half, half_si...]
    concatenate x3 -> x0, other arithmetic: 19.7 us -> none  [the longest x1 14.9 us: layer_backward(): grad_mlp = jnp.concatenate([grad_up, grad_down], 0)]
    reshape x1 -> x0, local copies, waits for them, and re-layouts: 19.1 us -> none  [split_halves(): return values.reshape(block_count, row_count, 2, half_size)]
    all_gather x1 -> x0, local copies, waits for them, and re-layouts: 16.7 us -> none  [on_device(): lax.all_gather(my_part(root_right), ('dp', 'cls'), axis=1, tiled=True, ax...]
    reduce_scatter x1, waiting for transfers between devices: 15.8 us -> 0.02 us  [on_device(): lax.psum_scatter(group_grad, 'cls', scatter_dimension=0, tiled=True)]
  transfers between devices with their start and end apart: 9 -> 5, of which waited for: 5 -> 2; matrix products, arithmetic and copies ran while one was open for 7% -> 13% of each run, Pallas kernels for 4% -> 42%
where the time goes in v3:
time: 646 us; the launch traced here: 642 us
  Pallas kernels  276 us (43%)
  waiting for transfers between devices  131 us (20%)
  blocking collectives  70.6 us (11%)
  matrix products  62.4 us (10%)
  other arithmetic  45.1 us (7%)
  local copies, waits for them, and re-layouts  34.6 us (5%)
  between operations  22.3 us (3%)
    pallas_call x1, Pallas kernels, reduce_gradients(): pl.pallas_call(functools.partial(reduce_kernel, counts), out_shape=(jax.S...  115 us
    all_gather x1, waiting for transfers between devices, on_device(): lax.all_gather(my_part(enc_weights.astype(jnp.bfloat16)), ('dp', 'cls'),...  76.1 us
    all_gather x1, waiting for transfers between devices, on_device(): lax.all_gather(head_weights.astype(jnp.bfloat16), 'dp', axis=0, tiled=True)  54.4 us
    pallas_call x1, Pallas kernels, attention_backward(): pl.pallas_call(attention_backward_kernel, grid=(width // PAIR,), out_shap...  40.1 us
    pallas_call x1, Pallas kernels, mlp_backward(): pl.pallas_call(mlp_backward_kernel, grid=(up_count * split,), out_shape=(...  33.6 us
    all_gather x1, blocking collectives, on_device(): pooled_all = lax.all_gather(group, 'dp', axis=0, tiled=True)  32.5 us
    all_gather x1, blocking collectives, on_device(): lax.all_gather(vectors.astype(jnp.bfloat16), 'dp', axis=1, tiled=True)  32.5 us
    pallas_call x1, Pallas kernels, precondition(): pl.pallas_call(functools.partial(precondition_kernel, own_count), grid=(c...  30.1 us
  transfers between devices with their start and end apart: 5, of which 2 were waited for; matrix products, arithmetic and copies ran while one was open for 13% of the time, Pallas kernels for 42%

profile of v3, /device:TPU:0, one launch (start us, length us, event | category | flops | bytes accessed | tf_op | source)
XLA Modules:
  0.0 641.5 jit_solution(18055255794552076395)
XLA Ops:
  8.1 2.1 dynamic-slice_convert_fusion
  10.3 2.7 convert_element_type.88
  13.1 32.5 %all-gather = bf16[8,96,15]{1,2,0:T(8,128)(2,1)S(1)} all-gather(bf16[1,96,15]{1,2,0:T(8,128)(2,1)S(1)} %convert_bitcast_fusion), channel_id=1, replica_groups=mesh['dp'=8,'cls'=4] {'dp'}, dimensions={0}, use_global_device_ids=true | all-gather | bytes 25920 | tf_op jit(solution)/shard_map/all_gather | solution.py:1012
  46.2 1.0 compare_reduce_fusion
  47.4 76.1 %all-gather.6.cloned.1.call-done.up_ref.down_ref = bf16[13,768,768]{2,1,0:T(8,128)(2,1)} async-done(((bf16[13,24,768]{2,1,0:T(8,128)(2,1)}), bf16[13,768,768]{2,1,0:T(8,128)(2,1)}) %all-gather.6.cloned.1.call-update) | async-done | bytes 15335440 | tf_op jit(solution)/shard_map/all_gather | solution.py:1009
  123.5 2.7 add_reduce_fusion
  126.3 0.6 multiply_reduce_fusion.7
  127.0 6.9 %fusion.q_ref.k_ref.v_ref = bf16[3,1024,768]{2,1,0:T(8,128)(2,1)S(1)} fusion(f32[3,768]{1,0:T(4,128)S(1)} %pad_maximum_fusion, bf16[13,768,768]{2,1,0:T(8,128)(2,1)} %all-gather.6.cloned.1.call-done.up_ref.down_ref, f32[768,1024]{0,1:T(8,128)S(1)} %get-tuple-element.95, f32[768]{0:T(1024)S(1)} %get-tuple-element.61, f32[768]{0:T(1024)S(1)} %get-tuple-element.62, ...), kind=kOutput, calls=%fused_computation.4 | convolution fusion | flops 3633315840 | bytes 11429888 | tf_op jit(solution)/shard_map/td,kde->kte/dot_general | solution.py:322
  134.0 25.6 %attention_forward.1 = bf16[1024,768]{1,0:T(8,128)(2,1)S(1)} custom-call(s32[1024,1]{1,0:T(8,128)S(1)} %copy.75.qids_ref, s32[1,1024]{1,0:T(1,128)S(1)} %broadcast_select_fusion.1.kcodes_ref, bf16[3,1024,768]{2,1,0:T(8,128)(2,1)S(1)} %fusion.q_ref.k_ref.v_ref, bf16[3,1024,768]{2,1,0:T(8,128)(2,1)S(1)} %fusion.q_ref.k_ref.v_ref, ...), custom_call_target="tpu_custom_call" | custom-call | tf_op jit(solution)/shard_map/attention_forward/pallas_call | solution.py:174
  159.6 3.4 fusion.67
  164.4 22.0 %mlp_forward.1 = (bf16[1024,3072]{1,0:T(8,128)(2,1)}, f32[1024,3072]{1,0:T(8,128)}, f32[1024,768]{1,0:T(8,128)S(1)}) custom-call(bf16[1024,768]{1,0:T(8,128)(2,1)S(1)} %add_convert_fusion.2.x_ref, bf16[13,768,768]{2,1,0:T(8,128)(2,1)} %all-gather.6.cloned.1.call-done.up_ref.down_ref, f32[1,3072]{1,0:T(1,128)S(1)} %bitcast.103, ...), custom_call_target="tpu_custom_call" | custom-call | tf_op jit(solution)/shard_map/mlp_forward/pallas_call | solution.py:276
  187.5 1.0 copy-done.57
  188.5 1.7 fusion.24
  190.2 5.7 all_gather.23
  195.8 54.4 %all-gather.8.cloned.1.call-done = bf16[768,5462]{1,0:T(8,128)(2,1)} async-done(((bf16[96,5462]{1,0:T(8,128)(2,1)}), bf16[768,5462]{1,0:T(8,128)(2,1)}) %all-gather.8.cloned.1.call-update) | async-done | bytes 8389648 | tf_op jit(solution)/shard_map/all_gather | solution.py:1014
  250.3 5.7 multiply_convert_fusion
  256.0 6.6 %fusion.68 = f32[32,768]{1,0:T(8,128)} fusion(bf16[32,5462]{1,0:T(8,128)(2,1)S(1)} %get-tuple-element.84, bf16[768,5462]{1,0:T(8,128)(2,1)} %all-gather.8.cloned.1.call-done), kind=kOutput, calls=%fused_computation.150 | convolution fusion | flops 268468224 | bytes 8837504 | tf_op jit(solution)/shard_map/gc,dc->gd/dot_general | solution.py:1039
  262.6 2.2 constant_dynamic-slice_fusion
  265.9 1.9 broadcast_select_fusion.kcodes_ref
  267.8 32.5 %all_gather.26 = bf16[256,768]{1,0:T(8,128)(2,1)S(1)} all-gather(bf16[32,768]{1,0:T(8,128)(2,1)} %all_gather.23), channel_id=1, replica_groups=mesh['dp'=8,'cls'=4] {'dp'}, dimensions={0}, use_global_device_ids=true | all-gather | bytes 442368 | tf_op jit(solution)/shard_map/all_gather | solution.py:1026
  301.1 5.1 multiply_reduce_fusion
  306.2 1.5 fusion.64
  307.7 0.9 convert_reduce_fusion
  308.7 33.6 %mlp_backward.1 = (f32[4,768,768]{2,1,0:T(8,128)}, f32[4,768,768]{2,1,0:T(8,128)}, f32[1,3072]{1,0:T(1,128)S(1)}, f32[1024,768]{1,0:T(8,128)}) custom-call(bf16[1024,768]{1,0:T(8,128)(2,1)S(1)} %add_convert_fusion.2.x_ref, bf16[1024,768]{1,0:T(8,128)(2,1)S(1)} %get-tuple-element.71.dm_ref, ...), custom_call_target="tpu_custom_call" | custom-call | tf_op jit(solution)/shard_map/mlp_backward/pallas_call | solution.py:296
  342.4 3.8 multiply_reduce_fusion.1
  346.2 1.4 fusion.63
  348.3 3.6 convolution_convert_fusion.do_ref
  352.0 40.1 %attention_backward.1 = bf16[3,1024,768]{2,1,0:T(8,128)(2,1)S(1)} custom-call(s32[1,1024]{1,0:T(1,128)S(1)} %copy-done.15, s32[1024,1]{1,0:T(8,128)S(1)} %copy-done.11, bf16[3,1024,768]{2,1,0:T(8,128)(2,1)S(1)} %bitcast.96, bf16[3,1024,768]{2,1,0:T(8,128)(2,1)S(1)} %bitcast.96, bf16[3,1024,768]{2,1,0:T(8,128)(2,1)S(1)} %bitcast.96, ...), custom_call_target="tpu_custom_call" | custom-call | tf_op jit(solution)/shard_map/attention_backward/pallas_call | solution.py:191
  392.2 8.2 %fusion.1 = (f32[768]{0:T(1024)S(1)}, f32[1024]{0:T(1024)S(1)}, f32[768]{0:T(1024)S(1)}, f32[1024,768,1]{1,0,2:T(8,128)S(1)}) fusion(f32[768,1024]{0,1:T(8,128)S(1)} %copy-done.22, f32[1024]{0:T(1024)S(1)} %copy-done.69, f32[1024]{0:T(1024)S(1)} %copy-done.51, f32[768]{0:T(1024)S(1)} %copy-done.48, f32[768]{0:T(1024)S(1)} %copy-done.63, ...), kind=kOutput, calls=%fused_computation.12 | convolution fusion | flops 3630953984 | bytes 14573568 | tf_op jit(solution)/shard_map/kte,kde->td/dot_general | solution.py:364
  400.5 1.8 fusion.62
  402.9 0.6 stack.31
  403.4 0.6 reshape.199
  405.1 0.6 stack.32
  405.6 0.6 stack.33
  406.2 0.6 stack.34
  408.5 1.3 reduce.29
  409.8 0.7 reshape.203
  410.5 1.3 stack.35
  411.8 1.3 reshape.204
  413.6 2.7 concatenate.6
  416.3 1.4 pad.8.refs_5_
  417.8 2.9 convolution_bitcast_fusion.2.refs_0_
  420.7 4.9 convolution_bitcast_fusion.1.refs_2_
  425.7 6.2 convolution_bitcast_fusion.refs_1_
  431.9 114.8 %reduce_gradients.1 = (s16[13,384,768]{2,1,0:T(8,128)(2,1)}, f32[13,8,1,768]{3,2,1,0:T(1,128)}, f32[16,768]{1,0:T(8,128)}) custom-call(f32[1,768,768]{2,1,0:T(8,128)} %convolution_bitcast_fusion.2.refs_0_, f32[3,768,768]{2,1,0:T(8,128)} %convolution_bitcast_fusion.refs_1_, f32[1,768,768]{2,1,0:T(8,128)} %convolution_bitcast_fusion.1.refs_2_, ...), custom_call_target="tpu_custom_call" | custom-call | tf_op jit(solution)/shard_map/reduce_gradients/pallas_call | solution.py:747
  546.7 2.1 copy-done.10
  548.8 1.0 copy-done.14
  549.8 30.1 %precondition.1 = (f32[13,96,768]{2,1,0:T(8,128)S(1)}, f32[13,96,768]{2,1,0:T(8,128)S(1)}, f32[13,96,768]{2,1,0:T(8,128)S(1)}, f32[13,96,768]{2,1,0:T(8,128)S(1)}, f32[13,2,768]{2,1,0:T(2,128)S(1)}) custom-call(s16[13,384,768]{2,1,0:T(8,128)(2,1)} %get-tuple-element.34.codes_ref, f32[13,8,1,768]{3,2,1,0:T(1,128)S(1)} %copy-done.14, ...), custom_call_target="tpu_custom_call" | custom-call | tf_op jit(solution)/shard_map/precondition/pallas_call | solution.py:854
  579.9 1.9 copy-done.4
  581.8 1.9 copy-done.6
  583.7 1.9 copy-done.8
  585.5 1.9 copy-done.9
  587.4 1.4 multiply_reduce_fusion.9
  588.8 0.7 slice_reduce_fusion.1
  591.2 4.4 multiply_reduce_fusion.8
  596.3 0.7 fusion.49.in_ref
  597.0 9.4 %sum_everywhere.1 = f32[8,128]{1,0:T(8,128)} custom-call(f32[8,128]{1,0:T(8,128)} %fusion.49.in_ref), custom_call_target="tpu_custom_call" | custom-call | tf_op jit(solution)/shard_map/sum_everywhere/pallas_call | solution.py:918
  606.3 0.9 slice.109
  607.2 1.3 fusion.66
  609.6 8.7 %multiply_subtract_fusion = (f32[13,96,768]{2,1,0:T(8,128)}, f32[13,96,768]{2,1,0:T(8,128)}) fusion(f32[13,96,768]{2,1,0:T(8,128)} %param.22, f32[13,96,768]{2,1,0:T(8,128)} %copy-done.8, f32[13,768]{1,0:T(8,128)S(1)} %bitcast.104, f32[13,96,768]{2,1,0:T(8,128)} %copy-done.9, f32[]{:T(128)S(6)} %div.138), kind=kLoop, calls=%fused_computation.7 | loop fusion | flops 2875392 | bytes 19209220 | tf_op jit(solution)/shard_map/sub | solution.py:1108
  618.3 1.4 multiply_subtract_fusion.2
  619.7 3.8 multiply_subtract_fusion.1
  623.6 1.7 copy-done.7
  625.2 7.6 %multiply_add_fusion = (f32[13,96,768]{2,1,0:T(8,128)}, f32[13,96,768]{2,1,0:T(8,128)}) fusion(f32[13,96,768]{2,1,0:T(8,128)S(1)} %copy-done.7, f32[13,96,768]{2,1,0:T(8,128)} %param.24, f32[]{:T(128)S(6)} %mul.434, f32[13,96,768]{2,1,0:T(8,128)S(1)} %copy-done.5, f32[13,96,768]{2,1,0:T(8,128)} %param.23), kind=kLoop, calls=%fused_computation.5 | loop fusion | flops 5750784 | bytes 23003140 | tf_op jit(solution)/shard_map/add | solution.py:1111
  (220 shorter events, 8.8 us)
Async XLA Ops:
  8.0 115.5 %copy-start = (bf16[1024,768]{1,0:T(8,128)(2,1)S(1)}, bf16[1024,768]{1,0:T(8,128)(2,1)}, u32[]{:S(2)}) copy-start(bf16[1024,768]{1,0:T(8,128)(2,1)} %param.17) | copy-start | bytes 4718596
  8.0 5.1 copy-start.59
  8.0 37.6 %copy-start.15 = (s32[1,1024]{1,0:T(1,128)S(1)}, s32[1,1024]{1,0:T(1,128)}, u32[]{:S(2)}) copy-start(s32[1,1024]{1,0:T(1,128)} %qids_ref.1) | copy-start | bytes 12292
  8.0 115.5 %all-gather.6.cloned.1.call-start = ((), (), s32[]{:S(2)}) async-start(), calls=%async_computation.1 | async-start | bytes 15814656 | tf_op jit(solution)/shard_map/all_gather | solution.py:1009
  8.1 37.9 %copy-start.71 = (s32[1,1024]{1,0:T(1,128)S(1)}, s32[1,1024]{1,0:T(1,128)}, u32[]{:S(2)}) copy-start(s32[1,1024]{1,0:T(1,128)} %param.19) | copy-start | bytes 12292
  8.1 38.1 %copy-start.77 = (s32[32,2]{0,1:T(2,128)S(1)}, s32[32,2]{0,1:T(2,128)}, u32[]{:S(2)}) copy-start(s32[32,2]{0,1:T(2,128)} %param.20) | copy-start | bytes 772
  10.3 240.0 %all-gather.8.cloned.1.call-start = ((), (), s32[]{:S(2)}) async-start(), calls=%async_computation.2 | async-start | bytes 9510912 | tf_op jit(solution)/shard_map/all_gather | solution.py:1014
  13.0 288.0 %reduce-scatter.2.cloned.1.call-start = ((), (), s32[]{:S(2)}) async-start(), calls=%async_computation.3 | async-start | bytes 122880 | tf_op jit(solution)/shard_map/reduce_scatter | solution.py:1040
  45.9 88.0 %copy-start.3 = (s32[1024,1]{1,0:T(8,128)}, s32[1024,1]{1,0:T(8,128)S(1)}, u32[]{:S(2)}) copy-start(s32[1024,1]{1,0:T(8,128)S(1)} %copy.75.qids_ref) | copy-start | bytes 12292
  46.1 142.4 %copy-start.61 = (pred[1024]{0:T(1024)(128)(4,1)}, pred[1024]{0:T(1024)(128)(4,1)S(1)}, u32[]{:S(2)}) copy-start(pred[1024]{0:T(1024)(128)(4,1)S(1)} %get-tuple-element.93) | copy-start | bytes 3076
  47.2 141.3 %copy-start.76 = (f32[8]{0:T(128)}, f32[8]{0:T(128)S(1)}, u32[]{:S(2)}) copy-start(f32[8]{0:T(128)S(1)} %broadcast_maximum_fusion) | copy-start | bytes 100
  47.3 79.7 %copy-start.62 = (f32[768]{0:T(1024)}, f32[768]{0:T(1024)S(1)}, u32[]{:S(2)}) copy-start(f32[768]{0:T(1024)S(1)} %get-tuple-element.62) | copy-start | bytes 9220
  47.3 79.7 %copy-start.74 = (f32[768]{0:T(1024)}, f32[768]{0:T(1024)S(1)}, u32[]{:S(2)}) copy-start(f32[768]{0:T(1024)S(1)} %get-tuple-element.61) | copy-start | bytes 9220
  47.3 112.3 %copy-start.47 = (f32[768]{0:T(1024)}, f32[768]{0:T(1024)S(1)}, u32[]{:S(2)}) copy-start(f32[768]{0:T(1024)S(1)} %get-tuple-element.63) | copy-start | bytes 9220
  47.3 116.3 %copy-start.35 = (f32[768]{0:T(1024)}, f32[768]{0:T(1024)S(1)}, u32[]{:S(2)}) copy-start(f32[768]{0:T(1024)S(1)} %get-tuple-element.59) | copy-start | bytes 9220
  47.3 141.1 %copy-start.38 = (f32[768]{0:T(1024)}, f32[768]{0:T(1024)S(1)}, u32[]{:S(2)}) copy-start(f32[768]{0:T(1024)S(1)} %get-tuple-element.55) | copy-start | bytes 9220
  126.3 33.3 %copy-start.21 = (f32[768,1024]{0,1:T(8,128)}, f32[768,1024]{0,1:T(8,128)S(1)}, u32[]{:S(2)}) copy-start(f32[768,1024]{0,1:T(8,128)S(1)} %get-tuple-element.95) | copy-start | bytes 9437188
  126.3 7.6 %copy-start.50 = (f32[1024]{0:T(1024)}, f32[1024]{0:T(1024)S(1)}, u32[]{:S(2)}) copy-start(f32[1024]{0:T(1024)S(1)} %broadcast_multiply_fusion.5) | copy-start | bytes 12292
  126.9 7.0 %copy-start.53 = (f32[1024]{0:T(1024)}, f32[1024]{0:T(1024)S(1)}, u32[]{:S(2)}) copy-start(f32[1024]{0:T(1024)S(1)} %multiply_reduce_fusion.7) | copy-start | bytes 12292
  126.9 7.0 %copy-start.68 = (f32[1024]{0:T(1024)}, f32[1024]{0:T(1024)S(1)}, u32[]{:S(2)}) copy-start(f32[1024]{0:T(1024)S(1)} %fusion.50) | copy-start | bytes 12292
  133.9 25.6 %copy-start.1 = (bf16[3,1024,768]{2,1,0:T(8,128)(2,1)}, bf16[3,1024,768]{2,1,0:T(8,128)(2,1)S(1)}, u32[]{:S(2)}) copy-start(bf16[3,1024,768]{2,1,0:T(8,128)(2,1)S(1)} %fusion.q_ref.k_ref.v_ref) | copy-start | bytes 14155780
  163.0 23.4 %copy-start.16 = (f32[1024,768]{1,0:T(8,128)}, f32[1024,768]{1,0:T(8,128)S(1)}, u32[]{:S(2)}) copy-start(f32[1024,768]{1,0:T(8,128)S(1)} %get-tuple-element.97) | copy-start | bytes 9437188
  163.6 22.8 %copy-start.55 = (f32[1024]{0:T(1024)}, f32[1024]{0:T(1024)S(1)}, u32[]{:S(2)}) copy-start(f32[1024]{0:T(1024)S(1)} %multiply_reduce_fusion.6) | copy-start | bytes 12292
  163.6 22.8 %copy-start.40 = (f32[1024]{0:T(1024)}, f32[1024]{0:T(1024)S(1)}, u32[]{:S(2)}) copy-start(f32[1024]{0:T(1024)S(1)} %fusion.51) | copy-start | bytes 12292
  187.5 68.5 %copy-start.43 = (f32[1024]{0:T(1024)}, f32[1024]{0:T(1024)S(1)}, u32[]{:S(2)}) copy-start(f32[1024]{0:T(1024)S(1)} %fusion.52) | copy-start | bytes 12292
  256.0 6.6 %copy-start.29 = (bf16[32,5462]{1,0:T(8,128)(2,1)}, bf16[32,5462]{1,0:T(8,128)(2,1)S(1)}, u32[]{:S(2)}) copy-start(bf16[32,5462]{1,0:T(8,128)(2,1)S(1)} %get-tuple-element.84) | copy-start | bytes 1048708
  262.6 284.2 %all-gather.10.cloned.1.call-start = ((), (), s32[]{:S(2)}) async-start(), calls=%async_computation.4 | async-start | bytes 16293888 | tf_op jit(solution)/shard_map/all_gather | solution.py:1015
  264.8 326.4 %all-gather.12.cloned.1.call-start = ((), (), s32[]{:S(2)}) async-start(), calls=%async_computation.5 | async-start | bytes 3170304 | tf_op jit(solution)/shard_map/all_gather | solution.py:1041
  301.0 5.2 copy-start.34
  301.0 5.2 copy-start.39
  301.0 5.2 copy-start.44
  301.0 5.1 copy-start.58
  301.0 5.2 copy-start.19
  308.7 33.7 %copy-start.17 = (f32[1024,768]{1,0:T(8,128)S(1)}, f32[1024,768]{1,0:T(8,128)}, u32[]{:S(2)}) copy-start(f32[1024,768]{1,0:T(8,128)} %copy-done.16) | copy-start | bytes 9437188
  308.7 33.7 %copy-start.31 = (f32[1024]{0:T(1024)S(1)}, f32[1024]{0:T(1024)}, u32[]{:S(2)}) copy-start(f32[1024]{0:T(1024)} %copy-done.30) | copy-start | bytes 12292
  308.7 33.7 %copy-start.36 = (f32[768]{0:T(1024)S(1)}, f32[768]{0:T(1024)}, u32[]{:S(2)}) copy-start(f32[768]{0:T(1024)} %copy-done.35) | copy-start | bytes 9220
  308.7 33.7 %copy-start.41 = (f32[1024]{0:T(1024)S(1)}, f32[1024]{0:T(1024)}, u32[]{:S(2)}) copy-start(f32[1024]{0:T(1024)} %copy-done.40) | copy-start | bytes 12292
  346.2 5.7 slice-start
  348.3 54.1 %copy-start.20 = (f32[1024,768]{1,0:T(8,128)}, f32[1024,768]{1,0:T(8,128)S(1)}, u32[]{:S(2)}) copy-start(f32[1024,768]{1,0:T(8,128)S(1)} %get-tuple-element.73) | copy-start | bytes 9437188
  352.0 40.2 %copy-start.22 = (f32[768,1024]{0,1:T(8,128)S(1)}, f32[768,1024]{0,1:T(8,128)}, u32[]{:S(2)}) copy-start(f32[768,1024]{0,1:T(8,128)} %copy-done.21) | copy-start | bytes 9437188
  352.0 40.2 %copy-start.48 = (f32[768]{0:T(1024)S(1)}, f32[768]{0:T(1024)}, u32[]{:S(2)}) copy-start(f32[768]{0:T(1024)} %copy-done.47) | copy-start | bytes 9220
  352.0 40.2 %copy-start.51 = (f32[1024]{0:T(1024)S(1)}, f32[1024]{0:T(1024)}, u32[]{:S(2)}) copy-start(f32[1024]{0:T(1024)} %copy-done.50) | copy-start | bytes 12292
  352.0 40.2 %copy-start.63 = (f32[768]{0:T(1024)S(1)}, f32[768]{0:T(1024)}, u32[]{:S(2)}) copy-start(f32[768]{0:T(1024)} %copy-done.62) | copy-start | bytes 9220
  352.0 40.2 %copy-start.69 = (f32[1024]{0:T(1024)S(1)}, f32[1024]{0:T(1024)}, u32[]{:S(2)}) copy-start(f32[1024]{0:T(1024)} %copy-done.68) | copy-start | bytes 12292
  392.2 12.3 %copy-start.2 = (bf16[3,1024,768]{2,1,0:T(8,128)(2,1)}, bf16[3,1024,768]{2,1,0:T(8,128)(2,1)S(1)}, u32[]{:S(2)}) copy-start(bf16[3,1024,768]{2,1,0:T(8,128)(2,1)S(1)} %attention_backward.1) | copy-start | bytes 14155780
  392.2 8.3 %copy-start.54 = (f32[1024]{0:T(1024)S(1)}, f32[1024]{0:T(1024)}, u32[]{:S(2)}) copy-start(f32[1024]{0:T(1024)} %copy-done.53) | copy-start | bytes 12292
  402.8 4.6 copy-start.66
  402.9 10.2 %copy-start.65 = (f32[768]{0:T(1024)S(1)}, f32[768]{0:T(1024)}, u32[]{:S(2)}) copy-start(f32[768]{0:T(1024)} %get-tuple-element.50) | copy-start | bytes 9220
  417.8 7.8 %slice-start.2 = ((s8[4718592]{0:T(1024)(128)(4,1)}), s8[4194304]{0:T(1024)(128)(4,1)S(1)}, s32[]{:S(2)}) async-start(s8[4718592]{0:T(1024)(128)(4,1)} %bitcast.97), calls=%async_computation.8 | async-start | bytes 8388608
  420.6 4.9 slice-start.3
  420.6 4.9 copy-start.23
  420.6 4.9 copy-start.49
  420.7 5.0 copy-start.52
  420.7 5.0 copy-start.64
  420.7 5.0 copy-start.70
  420.7 5.0 copy-start.75
  609.5 8.8 %copy-start.60 = (f32[15,96]{1,0:T(8,128)S(1)}, f32[15,96]{1,0:T(8,128)}, u32[]{:S(2)}) copy-start(f32[15,96]{1,0:T(8,128)} %param.30) | copy-start | bytes 17284
  609.5 8.8 %copy-start.72 = (f32[15,96]{1,0:T(8,128)S(1)}, f32[15,96]{1,0:T(8,128)}, u32[]{:S(2)}) copy-start(f32[15,96]{1,0:T(8,128)} %param.32) | copy-start | bytes 17284
  609.5 8.8 %copy-start.73 = (f32[15,96]{1,0:T(8,128)S(1)}, f32[15,96]{1,0:T(8,128)}, u32[]{:S(2)}) copy-start(f32[15,96]{1,0:T(8,128)} %param.31) | copy-start | bytes 17284
  609.5 10.2 %copy-start.25 = (f32[96,5462]{1,0:T(8,128)S(1)}, f32[96,5462]{1,0:T(8,128)}, u32[]{:S(2)}) copy-start(f32[96,5462]{1,0:T(8,128)} %param.27) | copy-start | bytes 6292228
  609.5 10.2 %copy-start.26 = (f32[96,5462]{1,0:T(8,128)S(1)}, f32[96,5462]{1,0:T(8,128)}, u32[]{:S(2)}) copy-start(f32[96,5462]{1,0:T(8,128)} %get-tuple-element.101) | copy-start | bytes 6292228
  609.5 10.2 %copy-start.27 = (f32[96,5462]{1,0:T(8,128)S(1)}, f32[96,5462]{1,0:T(8,128)}, u32[]{:S(2)}) copy-start(f32[96,5462]{1,0:T(8,128)} %param.29) | copy-start | bytes 6292228
  609.5 10.2 %copy-start.28 = (f32[96,5462]{1,0:T(8,128)S(1)}, f32[96,5462]{1,0:T(8,128)}, u32[]{:S(2)}) copy-start(f32[96,5462]{1,0:T(8,128)} %param.28) | copy-start | bytes 6292228
  619.7 5.5 copy-start.7
  (23 other events, 63.1 us)
Sparse Core Ops, SparseCore 0:
  12.4 111.0 all-gather.5
  126.3 123.9 all-gather.7
  262.7 21.4 reduce-scatter.1
Sparse Core Ops, SparseCore 1:
  265.2 83.8 all-gather.9
  351.1 60.0 all-gather.11

commit v4 on v3

--- a/solution.py
+++ b/solution.py
@@ -19,6 +19,8 @@
 CODE_TOP = 32766.0
 CODE_FLOOR = 1e-33
 PIECE = 48
+SPAN = 48
+SHARES = 8
 IMG_PACK = 8
 
 
@@ -930,6 +932,214 @@
     )(values)
 
 
+def gather_kernel(own_ref, vec_ref, out_ref, vec_out_ref, send_sem, recv_sem, copy_sem, vec_send, vec_recv):
+    count, rows, width = own_ref.shape
+    cols = width // 2
+    z, y, x, core = torus_place()
+    me = z * 2 + y
+    mate_core = torus_device(z, y, x, 1 - core)
+    mate_x = torus_device(z, y, 1 - x, core)
+    mate_y = torus_device(z, 1 - y, x, core)
+    mate_up = torus_device(jnp.minimum(z + 1, 3), y, x, core)
+    mate_down = torus_device(jnp.maximum(z - 1, 0), y, x, core)
+    has_up = z < 3
+    has_down = z > 0
+
+    def column_mate(n):
+        other = lax.rem(me + n, SHARES)
+        return torus_device(other // 2, lax.rem(other, 2), x, core)
+
+    barrier = pltpu.get_barrier_semaphore()
+    for mate in [mate_core, mate_x] + [column_mate(n) for n in range(1, SHARES)]:
+        pl.semaphore_signal(barrier, inc=1, device_id=mate, device_id_type=MESH)
+    pl.semaphore_wait(barrier, SHARES + 1)
+
+    own_cols = pl.ds(pl.multiple_of(core * cols, 128), cols)
+    other_cols = pl.ds(pl.multiple_of((1 - core) * cols, 128), cols)
+
+    def vec_copy(n, slot):
+        return pltpu.make_async_remote_copy(
+            src_ref=vec_ref, dst_ref=vec_out_ref.at[slot],
+            send_sem=vec_send.at[n], recv_sem=vec_recv.at[slot],
+            device_id=column_mate(n), device_id_type=MESH,
+        )
+
+    for n in range(1, SHARES):
+        vec_copy(n, me).start()
+    vec_out_ref[me] = vec_ref[...]
+
+    def share(m, zz, yy, start, size, columns=own_cols):
+        begin = (zz * 2 + yy) * rows + start
+        return out_ref.at[m, pl.ds(pl.multiple_of(begin, 16), size), columns]
+
+    def copy(stage, m, source, target, mate):
+        return pltpu.make_async_remote_copy(
+            src_ref=source, dst_ref=target,
+            send_sem=send_sem.at[stage, m % 2], recv_sem=recv_sem.at[stage, m],
+            device_id=mate, device_id_type=MESH,
+        )
+
+    span_start = x * (rows - SPAN)
+    lack = rows - SPAN
+    lack_mine = x * SPAN
+    lack_theirs = (1 - x) * SPAN
+
+    def local(m):
+        return pltpu.make_async_copy(
+            own_ref.at[m, :, own_cols], share(m, z, y, 0, rows), copy_sem.at[m % 2]
+        )
+
+    def chain(m, turn, upward):
+        origin = z - (turn - 1) if upward else z + (turn - 1)
+        stage = (turn - 1) * 2 + (0 if upward else 1)
+        target = share(m, origin, y, span_start, SPAN)
+        if turn == 1:
+            source = own_ref.at[m, pl.ds(pl.multiple_of(span_start, 16), SPAN), own_cols]
+        else:
+            source = target
+        return copy(stage, m, source, target, mate_up if upward else mate_down)
+
+    def chain_sends(turn, upward):
+        if upward:
+            return has_up & (z - (turn - 1) >= 0)
+        return has_down & (z + (turn - 1) <= 3)
+
+    def chain_comes(turn, upward):
+        return (z - turn >= 0) if upward else (z + turn <= 3)
+
+    def arriving(m, turn, upward):
+        origin = z - turn if upward else z + turn
+        stage = (turn - 1) * 2 + (0 if upward else 1)
+        target = share(m, origin, y, span_start, SPAN)
+        return copy(stage, m, target, target, mate_up)
+
+    def patch_out(m, n):
+        zz = lax.rem(z + n, 4)
+        block = share(m, zz, y, lack_mine, lack)
+        return copy(5 + n, m, block, block, mate_x)
+
+    def patch_in(m, n):
+        zz = lax.rem(z + n, 4)
+        block = share(m, zz, y, lack_theirs, lack)
+        return copy(5 + n, m, block, block, mate_x)
+
+    def cross(m, n, yy, stage, plane, mate):
+        block = share(m, plane * 2 + n, yy, 0, rows)
+        return copy(stage + n, m, block, block, mate)
+
+    def swap(m, columns):
+        block = out_ref.at[m, :, columns]
+        return copy(13, m, block, block, mate_core)
+
+    def step(t, carry):
+        @pl.when(t < count)
+        def _():
+            local(t).start()
+            for upward in (True, False):
+                @pl.when(chain_sends(1, upward))
+                def _(upward=upward):
+                    chain(t, 1, upward).start()
+
+        for turn in (2, 3):
+            @pl.when((t >= turn - 1) & (t < count + turn - 1))
+            def _(turn=turn):
+                m = t - (turn - 1)
+                if turn == 2:
+                    local(m).wait()
+                for upward in (True, False):
+                    @pl.when(chain_sends(turn - 1, upward))
+                    def _(upward=upward):
+                        chain(m, turn - 1, upward).wait_send()
+
+                    @pl.when(chain_comes(turn - 1, upward))
+                    def _(upward=upward):
+                        arriving(m, turn - 1, upward).wait_recv()
+
+                    @pl.when(chain_sends(turn, upward))
+                    def _(upward=upward):
+                        chain(m, turn, upward).start()
+
+        @pl.when((t >= 3) & (t < count + 3))
+        def _():
+            m = t - 3
+            for upward in (True, False):
+                @pl.when(chain_sends(3, upward))
+                def _(upward=upward):
+                    chain(m, 3, upward).wait_send()
+
+                @pl.when(chain_comes(3, upward))
+                def _(upward=upward):
+                    arriving(m, 3, upward).wait_recv()
+            if lack:
+                for n in range(1, 4):
+                    patch_out(m, n).start()
+
+        @pl.when((t >= 4) & (t < count + 4))
+        def _():
+            m = t - 4
+            if lack:
+                for n in range(1, 4):
+                    patch_out(m, n).wait_send()
+                    patch_in(m, n).wait_recv()
+            for n in range(2):
+                cross(m, n, y, 9, x, mate_y).start()
+
+        @pl.when((t >= 5) & (t < count + 5))
+        def _():
+            m = t - 5
+            for n in range(2):
+                cross(m, n, y, 9, x, mate_y).wait_send()
+                cross(m, n, 1 - y, 9, x, mate_y).wait_recv()
+                cross(m, n, 1 - y, 11, x, mate_x).start()
+
+        @pl.when((t >= 6) & (t < count + 6))
+        def _():
+            m = t - 6
+            for n in range(2):
+                cross(m, n, 1 - y, 11, x, mate_x).wait_send()
+                cross(m, n, 1 - y, 11, 1 - x, mate_x).wait_recv()
+            swap(m, own_cols).start()
+
+        @pl.when((t >= 7) & (t < count + 7))
+        def _():
+            m = t - 7
+            swap(m, own_cols).wait_send()
+            swap(m, other_cols).wait_recv()
+
+        return carry
+
+    lax.fori_loop(0, count + 7, step, 0)
+    for n in range(1, SHARES):
+        vec_copy(n, me).wait_send()
+        vec_copy(n, lax.rem(me + n, SHARES)).wait_recv()
+
+
+def gather_weights(own, vec):
+    count, rows, width = own.shape
+    hbm = pl.BlockSpec(memory_space=pl.ANY)
+    vmem = pl.BlockSpec(memory_space=pltpu.VMEM)
+    return pl.pallas_call(
+        gather_kernel,
+        out_shape=(
+            jax.ShapeDtypeStruct((count, SHARES * rows, width), own.dtype),
+            jax.ShapeDtypeStruct((SHARES,) + vec.shape, vec.dtype),
+        ),
+        in_specs=[vmem, vmem],
+        out_specs=(hbm, vmem),
+        scratch_shapes=[
+            pltpu.SemaphoreType.DMA((14, 2)),
+            pltpu.SemaphoreType.DMA((14, count)),
+            pltpu.SemaphoreType.DMA((2,)),
+            pltpu.SemaphoreType.DMA((SHARES,)),
+            pltpu.SemaphoreType.DMA((SHARES,)),
+        ],
+        compiler_params=pltpu.CompilerParams(
+            collective_id=3, has_side_effects=True, vmem_limit_bytes=32 << 20
+        ),
+        name="gather_weights",
+    )(own, vec)
+
+
 def adam_step(weight, grad, first, second, count):
     first = BETA_FIRST * first + (1.0 - BETA_FIRST) * grad
     second = BETA_SECOND * second + (1.0 - BETA_SECOND) * grad * grad
@@ -1006,11 +1216,18 @@
     def my_part(values):
         return lax.dynamic_slice_in_dim(values, cls_index * part_rows, part_rows, 1)
 
-    blocks = lax.all_gather(
-        my_part(enc_weights.astype(jnp.bfloat16)), ("dp", "cls"), axis=1, tiled=True
-    )
-    vec_low = lax.all_gather(vectors.astype(jnp.bfloat16), "dp", axis=1, tiled=True)
-    vec_all = vec_low.astype(jnp.float32)
+    on_torus = dp_count == 8 and cls_count == 4
+    if on_torus:
+        vec_block = jnp.pad(vectors, ((0, -vectors.shape[0] % 8), (0, -row_count % 128)))
+        blocks, vec_blocks = gather_weights(enc_weights.astype(jnp.bfloat16), vec_block)
+        vec_low = jnp.transpose(vec_blocks[:, : vectors.shape[0], :row_count], (1, 0, 2))
+        vec_all = lax.reduce_precision(vec_low.reshape(vectors.shape[0], feature_dim), 8, 7)
+    else:
+        blocks = lax.all_gather(
+            my_part(enc_weights.astype(jnp.bfloat16)), ("dp", "cls"), axis=1, tiled=True
+        )
+        vec_low = lax.all_gather(vectors.astype(jnp.bfloat16), "dp", axis=1, tiled=True)
+        vec_all = vec_low.astype(jnp.float32)
     head_low = lax.all_gather(head_weights.astype(jnp.bfloat16), "dp", axis=0, tiled=True)
     right_half = lax.all_gather(
         my_part(root_right), ("dp", "cls"), axis=1, tiled=True, axis_index_groups=half_groups
@@ -1023,7 +1240,6 @@
     output, saved = layer_forward(blocks, vec_all, patches, pack_ids, key_codes)
     pooled = pool_rows(output, final_gain, final_shift, pack_ids, pack_keep)
     group = lax.all_gather(pooled.astype(jnp.bfloat16), "cls", axis=0, tiled=True)
-    pooled_all = lax.all_gather(group, "dp", axis=0, tiled=True)
     logits = jnp.dot(group, head_low, preferred_element_type=jnp.float32)
     class_dev = head_low.shape[1]
     class_ids = cls_index * class_dev + jnp.arange(class_dev)
@@ -1038,7 +1254,10 @@
     )
     group_grad = jnp.einsum("gc,dc->gd", grad_logits, head_low, preferred_element_type=jnp.float32)
     grad_pooled = lax.psum_scatter(group_grad, "cls", scatter_dimension=0, tiled=True)
-    grad_logits_all = lax.all_gather(grad_logits, "dp", axis=0, tiled=True)
+    head_rows = lax.all_gather(
+        jnp.concatenate([group, grad_logits], 1), "dp", axis=0, tiled=True
+    )
+    pooled_all, grad_logits_all = head_rows[:, :feature_dim], head_rows[:, feature_dim:]
     pooled_mine = lax.dynamic_slice_in_dim(pooled_all, dp_index * row_count, row_count, 1)
     head_grad = jnp.einsum(
         "gr,gc->rc", pooled_mine, grad_logits_all, preferred_element_type=jnp.float32
@@ -1061,7 +1280,6 @@
         grad_shift,
     )
 
-    on_torus = dp_count == 8 and cls_count == 4
     if on_torus:
         padded = jnp.pad(grad_vectors, ((0, -grad_vectors.shape[0] % 8), (0, 0)))
         codes, scales, vector_sum = reduce_gradients(grad_arrays, padded)

time: 646 us -> 596 us (0.923)
  Pallas kernels: 276 us -> 414 us
  waiting for transfers between devices: 131 us -> 13.6 us
  blocking collectives: 70.6 us -> 5.84 us
  local copies, waits for them, and re-layouts: 34.6 us -> 27.5 us
    pallas_call x0 -> x1, Pallas kernels: none -> 118 us  [gather_weights(): pl.pallas_call(gather_kernel, out_shape=(jax.ShapeDtypeStruct((count, SHA...]
    all_gather x2 -> x1, waiting for transfers between devices: 76.1 us -> 0.01 us  [on_device(): lax.all_gather(jnp.concatenate([group, grad_logits], 1), 'dp', axis=0, ti...]
    all_gather x2 -> x0, blocking collectives: 64.9 us -> none  [the longest x1 32.5 us: on_device(): pooled_all = lax.all_gather(group, 'dp', axis=0, tiled=True)]
    all_gather x1, waiting for transfers between devices: 54.4 us -> 0.01 us  [on_device(): lax.all_gather(head_weights.astype(jnp.bfloat16), 'dp', axis=0, tiled=True)]
    pallas_call x1, Pallas kernels: 115 us -> 137 us  [reduce_gradients(): pl.pallas_call(functools.partial(reduce_kernel, counts), out_shape=(jax.S...]
    reduce_scatter x1, waiting for transfers between devices: 0.02 us -> 13.6 us  [on_device(): lax.psum_scatter(group_grad, 'cls', scatter_dimension=0, tiled=True)]
    unnamed x168 -> x146, local copies, waits for them, and re-layouts: 13.9 us -> 18.9 us
  transfers between devices with their start and end apart: 5 -> 4, of which waited for: 2 -> 1; matrix products, arithmetic and copies ran while one was open for 13% -> 13% of each run, Pallas kernels for 42% -> 64%
where the time goes in v4:
time: 596 us; the launch traced here: 587 us
  Pallas kernels  414 us (69%)
  matrix products  58.5 us (10%)
  other arithmetic  47.3 us (8%)
  local copies, waits for them, and re-layouts  27.5 us (5%)
  between operations  20.6 us (3%)
  waiting for transfers between devices  13.6 us (2%)
    pallas_call x1, Pallas kernels, reduce_gradients(): pl.pallas_call(functools.partial(reduce_kernel, counts), out_shape=(jax.S...  137 us
    pallas_call x1, Pallas kernels, gather_weights(): pl.pallas_call(gather_kernel, out_shape=(jax.ShapeDtypeStruct((count, SHA...  118 us
    pallas_call x1, Pallas kernels, attention_backward(): pl.pallas_call(attention_backward_kernel, grid=(width // PAIR,), out_shap...  40.1 us
    pallas_call x1, Pallas kernels, mlp_backward(): pl.pallas_call(mlp_backward_kernel, grid=(up_count * split,), out_shape=(...  33 us
    pallas_call x1, Pallas kernels, precondition(): pl.pallas_call(functools.partial(precondition_kernel, own_count), grid=(c...  29.8 us
    pallas_call x1, Pallas kernels, attention_forward(): pl.pallas_call(attention_forward_kernel, grid=(width // PAIR,), out_shape...  25.6 us
    pallas_call x1, Pallas kernels, mlp_forward(): pl.pallas_call(mlp_forward_kernel, grid=(up_count * split,), out_shape=(j...  21.1 us
    unnamed x146, local copies, waits for them, and re-layouts  18.9 us
  transfers between devices with their start and end apart: 4, of which 1 were waited for; matrix products, arithmetic and copies ran while one was open for 13% of the time, Pallas kernels for 64%

profile of v4, /device:TPU:0, one launch (start us, length us, event | category | flops | bytes accessed | tf_op | source)
XLA Modules:
  0.0 587.2 jit_solution(17266647897367033840)
XLA Ops:
  7.2 2.8 convert_element_type.82
  10.1 2.3 convert_element_type.75.own_ref
  12.5 117.8 %gather_weights.1 = (bf16[13,768,768]{2,1,0:T(8,128)(2,1)S(1)}, f32[8,16,128]{2,1,0:T(8,128)S(1)}) custom-call(bf16[13,96,768]{2,1,0:T(8,128)(2,1)S(1)} %convert_element_type.75.own_ref, f32[16,128]{1,0:T(8,128)S(1)} %pad.12.vec_ref), custom_call_target="tpu_custom_call" | custom-call | tf_op jit(solution)/shard_map/gather_weights/pallas_call | solution.py:1121
  130.3 5.4 copy-done.1
  137.1 2.8 add_reduce_fusion
  139.9 0.6 multiply_reduce_fusion.7
  140.5 1.0 copy-done.45
  141.6 6.5 %fusion.q_ref.k_ref.v_ref = bf16[3,1024,768]{2,1,0:T(8,128)(2,1)S(1)} fusion(f32[3,768]{1,0:T(4,128)S(1)} %pad_maximum_fusion.1, bf16[13,768,768]{2,1,0:T(8,128)(2,1)} %copy-done.1, f32[768,1024]{0,1:T(8,128)S(1)} %get-tuple-element.99, f32[768]{0:T(1024)S(1)} %add.205, f32[768]{0:T(1024)S(1)} %mul.371, f32[1024]{0:T(1024)S(1)} %fusion.57, ...), kind=kOutput, calls=%fused_computation.4 | convolution fusion | flops 3633315840 | bytes 11429888 | tf_op jit(solution)/shard_map/td,kde->kte/dot_general | solution.py:324
  148.2 25.6 %attention_forward.1 = bf16[1024,768]{1,0:T(8,128)(2,1)S(1)} custom-call(s32[1024,1]{1,0:T(8,128)S(1)} %copy.52.qids_ref, s32[1,1024]{1,0:T(1,128)S(1)} %broadcast_select_fusion.1.kcodes_ref, bf16[3,1024,768]{2,1,0:T(8,128)(2,1)S(1)} %fusion.q_ref.k_ref.v_ref, bf16[3,1024,768]{2,1,0:T(8,128)(2,1)S(1)} %fusion.q_ref.k_ref.v_ref, ...), custom_call_target="tpu_custom_call" | custom-call | tf_op jit(solution)/shard_map/attention_forward/pallas_call | solution.py:176
  173.8 3.4 fusion.74
  177.2 0.5 multiply_reduce_fusion.6
  177.8 0.5 add_convert_fusion.2.x_ref
  178.3 21.1 %mlp_forward.1 = (bf16[1024,3072]{1,0:T(8,128)(2,1)}, f32[1024,3072]{1,0:T(8,128)}, f32[1024,768]{1,0:T(8,128)S(1)}) custom-call(bf16[1024,768]{1,0:T(8,128)(2,1)S(1)} %add_convert_fusion.2.x_ref, bf16[13,768,768]{2,1,0:T(8,128)(2,1)} %copy-done.1, f32[1,3072]{1,0:T(1,128)S(1)} %reshape.222.bias_ref, bf16[13,768,768]{2,1,0:T(8,128)(2,1)} %copy-done.1), custom_call_target="tpu_custom_call" | custom-call | tf_op jit(solution)/shard_map/mlp_forward/pallas_call | solution.py:278
  199.4 0.6 fusion.60
  200.6 0.5 multiply_reduce_fusion.5
  201.1 1.0 copy-done.49
  202.2 1.7 fusion.30
  203.9 5.8 all_gather.12
  209.7 0.6 broadcast_compare_fusion
  210.3 1.0 compare_reduce_fusion
  211.3 6.0 %multiply_convert_fusion = (bf16[32,5462]{1,0:T(8,128)(2,1)S(1)}, f32[]{:T(128)}) fusion(pred[32,5462]{1,0:T(8,128)(4,1)} %compare_reduce_fusion, pred[5462]{0:T(1024)(128)(4,1)} %broadcast_compare_fusion, bf16[32,768]{1,0:T(8,128)(2,1)S(1)} %all_gather.12, bf16[768,5462]{1,0:T(8,128)(2,1)} %all-gather.4.cloned.1.call-done), kind=kOutput, calls=%fused_computation.75 | convolution fusion | flops 271614336 | bytes 8968602 | tf_op jit(solution)/shard_map/dot_general | solution.py:1243
  217.3 3.0 fusion.75
  220.4 0.8 pad_maximum_fusion
  221.3 2.2 constant_dynamic-slice_fusion
  224.6 1.9 broadcast_select_fusion.kcodes_ref
  227.1 13.6 %reduce-scatter.2.cloned.1.call-done = f32[8,768]{1,0:T(8,128)} async-done(((f32[32,768]{1,0:T(8,128)}), f32[8,768]{1,0:T(8,128)}) %reduce-scatter.2.cloned.1.call-update) | async-done | bytes 24592 | tf_op jit(solution)/shard_map/reduce_scatter | solution.py:1256
  240.7 4.6 multiply_reduce_fusion
  245.4 1.5 fusion.71
  247.2 33.0 %mlp_backward.1 = (f32[4,768,768]{2,1,0:T(8,128)}, f32[4,768,768]{2,1,0:T(8,128)}, f32[1,3072]{1,0:T(1,128)S(1)}, f32[1024,768]{1,0:T(8,128)}) custom-call(bf16[1024,768]{1,0:T(8,128)(2,1)S(1)} %add_convert_fusion.2.x_ref, bf16[1024,768]{1,0:T(8,128)(2,1)S(1)} %get-tuple-element.77.dm_ref, bf16[13,768,768]{2,1,0:T(8,128)(2,1)} %copy-done.1, ...), custom_call_target="tpu_custom_call" | custom-call | tf_op jit(solution)/shard_map/mlp_backward/pallas_call | solution.py:298
  280.3 3.0 multiply_reduce_fusion.1
  283.3 1.4 fusion.70
  284.7 0.5 convert_reduce_fusion.1
  285.2 3.6 convolution_convert_fusion.do_ref
  289.0 40.1 %attention_backward.1 = bf16[3,1024,768]{2,1,0:T(8,128)(2,1)S(1)} custom-call(s32[1,1024]{1,0:T(1,128)S(1)} %copy-done.16, s32[1024,1]{1,0:T(8,128)S(1)} %copy-done.12, bf16[3,1024,768]{2,1,0:T(8,128)(2,1)S(1)} %bitcast.87, bf16[3,1024,768]{2,1,0:T(8,128)(2,1)S(1)} %bitcast.87, bf16[3,1024,768]{2,1,0:T(8,128)(2,1)S(1)} %bitcast.87, ...), custom_call_target="tpu_custom_call" | custom-call | tf_op jit(solution)/shard_map/attention_backward/pallas_call | solution.py:193
  329.2 8.3 %fusion.1 = (f32[768]{0:T(1024)S(1)}, f32[1024]{0:T(1024)S(1)}, f32[768]{0:T(1024)S(1)}, f32[1024,768,1]{1,0,2:T(8,128)S(1)}) fusion(f32[768,1024]{0,1:T(8,128)S(1)} %copy-done.23, f32[1024]{0:T(1024)S(1)} %copy-done.58, f32[1024]{0:T(1024)S(1)} %copy-done.44, f32[768]{0:T(1024)S(1)} %copy-done.42, f32[768]{0:T(1024)S(1)} %copy-done.56, ...), kind=kOutput, calls=%fused_computation.12 | convolution fusion | flops 3630953984 | bytes 14573568 | tf_op jit(solution)/shard_map/kte,kde->td/dot_general | solution.py:366
  337.4 1.8 fusion.69
  339.2 0.4 convert_reduce_fusion.4
  339.7 0.5 convert_reduce_fusion.2
  340.3 0.5 broadcast.299
  340.8 0.7 reduce.55
  341.6 0.6 pad.13.refs_5_
  342.2 2.8 convolution_bitcast_fusion.2.refs_0_
  345.1 5.0 convolution_bitcast_fusion.1.refs_2_
  350.1 6.4 %convolution_bitcast_fusion.refs_1_ = f32[3,768,768]{2,1,0:T(8,128)} fusion(bf16[3,1024,768]{2,1,0:T(8,128)(2,1)S(1)} %bitcast.89, f32[768,1024]{0,1:T(8,128)S(1)} %copy-done.24, f32[768]{0:T(1024)S(1)} %copy-done.64, f32[768]{0:T(1024)S(1)} %copy-done.56, f32[1024]{0:T(1024)S(1)} %copy-done.58, f32[1024]{0:T(1024)S(1)} %copy-done.44, f32[768]{0:T(1024)S(1)} %copy-done.42), kind=kOutput, calls=%fused_computation.43 | convolution fusion | flops 3628597248 | bytes 14959616 | tf_op jit(solution)/shard_map/td,kte->kde/dot_general | solution.py:363
  356.5 136.9 %reduce_gradients.1 = (s16[13,384,768]{2,1,0:T(8,128)(2,1)}, f32[13,8,1,768]{3,2,1,0:T(1,128)}, f32[16,768]{1,0:T(8,128)}) custom-call(f32[1,768,768]{2,1,0:T(8,128)} %convolution_bitcast_fusion.2.refs_0_, f32[3,768,768]{2,1,0:T(8,128)} %convolution_bitcast_fusion.refs_1_, f32[1,768,768]{2,1,0:T(8,128)} %convolution_bitcast_fusion.1.refs_2_, ...), custom_call_target="tpu_custom_call" | custom-call | tf_op jit(solution)/shard_map/reduce_gradients/pallas_call | solution.py:749
  493.4 1.4 multiply_reduce_fusion.9
  494.9 1.0 slice.156
  495.9 4.4 multiply_reduce_fusion.8
  500.3 2.1 copy-done.11
  502.4 29.8 %precondition.1 = (f32[13,96,768]{2,1,0:T(8,128)S(1)}, f32[13,96,768]{2,1,0:T(8,128)S(1)}, f32[13,96,768]{2,1,0:T(8,128)S(1)}, f32[13,96,768]{2,1,0:T(8,128)S(1)}, f32[13,2,768]{2,1,0:T(2,128)S(1)}) custom-call(s16[13,384,768]{2,1,0:T(8,128)(2,1)} %get-tuple-element.38.codes_ref, f32[13,8,1,768]{3,2,1,0:T(1,128)S(1)} %copy-done.15, ...), custom_call_target="tpu_custom_call" | custom-call | tf_op jit(solution)/shard_map/precondition/pallas_call | solution.py:856
  532.2 1.9 copy-done.5
  534.1 1.8 copy-done.7
  535.9 1.9 copy-done.9
  537.8 1.9 copy-done.10
  539.7 0.7 slice_reduce_fusion.1
  542.7 0.7 fusion.56.in_ref
  543.4 9.4 %sum_everywhere.1 = f32[8,128]{1,0:T(8,128)} custom-call(f32[8,128]{1,0:T(8,128)} %fusion.56.in_ref), custom_call_target="tpu_custom_call" | custom-call | tf_op jit(solution)/shard_map/sum_everywhere/pallas_call | solution.py:920
  552.7 0.9 slice.139
  553.6 1.3 fusion.73
  555.9 8.7 %multiply_subtract_fusion = (f32[13,96,768]{2,1,0:T(8,128)}, f32[13,96,768]{2,1,0:T(8,128)}) fusion(f32[13,96,768]{2,1,0:T(8,128)} %param.22, f32[13,96,768]{2,1,0:T(8,128)} %copy-done.9, f32[13,768]{1,0:T(8,128)S(1)} %bitcast.94, f32[13,96,768]{2,1,0:T(8,128)} %copy-done.10, f32[]{:T(128)S(6)} %div.138), kind=kLoop, calls=%fused_computation.7 | loop fusion | flops 2875392 | bytes 19209220 | tf_op jit(solution)/shard_map/sub | solution.py:1326
  564.7 1.4 multiply_subtract_fusion.2
  566.1 3.9 multiply_subtract_fusion.1
  570.0 1.6 copy-done.8
  571.6 7.5 %multiply_add_fusion = (f32[13,96,768]{2,1,0:T(8,128)}, f32[13,96,768]{2,1,0:T(8,128)}) fusion(f32[13,96,768]{2,1,0:T(8,128)S(1)} %copy-done.8, f32[13,96,768]{2,1,0:T(8,128)} %param.24, f32[]{:T(128)S(6)} %mul.433, f32[13,96,768]{2,1,0:T(8,128)S(1)} %copy-done.6, f32[13,96,768]{2,1,0:T(8,128)} %param.23), kind=kLoop, calls=%fused_computation.5 | loop fusion | flops 5750784 | bytes 23003140 | tf_op jit(solution)/shard_map/add | solution.py:1329
  (209 shorter events, 3.8 us)
Async XLA Ops:
  7.2 129.9 %copy-start = (bf16[1024,768]{1,0:T(8,128)(2,1)S(1)}, bf16[1024,768]{1,0:T(8,128)(2,1)}, u32[]{:S(2)}) copy-start(bf16[1024,768]{1,0:T(8,128)(2,1)} %param.17) | copy-start | bytes 4718596
  7.2 204.1 %all-gather.4.cloned.1.call-start = ((), (), s32[]{:S(2)}) async-start(), calls=%async_computation.1 | async-start | bytes 9510912 | tf_op jit(solution)/shard_map/all_gather | solution.py:1231
  10.1 230.6 %reduce-scatter.2.cloned.1.call-start = ((), (), s32[]{:S(2)}) async-start(), calls=%async_computation.2 | async-start | bytes 122880 | tf_op jit(solution)/shard_map/reduce_scatter | solution.py:1256
  10.1 125.9 %copy-start.16 = (s32[1,1024]{1,0:T(1,128)S(1)}, s32[1,1024]{1,0:T(1,128)}, u32[]{:S(2)}) copy-start(s32[1,1024]{1,0:T(1,128)} %qids_ref.1) | copy-start | bytes 12292
  130.3 5.4 copy-start.1
  136.2 11.9 %copy-start.4 = (s32[1024,1]{1,0:T(8,128)}, s32[1024,1]{1,0:T(8,128)S(1)}, u32[]{:S(2)}) copy-start(s32[1024,1]{1,0:T(8,128)S(1)} %copy.52.qids_ref) | copy-start | bytes 12292
  136.5 37.3 %copy-start.41 = (f32[768]{0:T(1024)}, f32[768]{0:T(1024)S(1)}, u32[]{:S(2)}) copy-start(f32[768]{0:T(1024)S(1)} %add.200) | copy-start | bytes 9220
  136.5 5.0 copy-start.63
  136.6 5.0 copy-start.55
  136.8 41.0 %copy-start.33 = (f32[768]{0:T(1024)}, f32[768]{0:T(1024)S(1)}, u32[]{:S(2)}) copy-start(f32[768]{0:T(1024)S(1)} %mul.377) | copy-start | bytes 9220
  137.0 65.1 %copy-start.37 = (f32[768]{0:T(1024)}, f32[768]{0:T(1024)S(1)}, u32[]{:S(2)}) copy-start(f32[768]{0:T(1024)S(1)} %mul.383) | copy-start | bytes 9220
  139.8 33.9 %copy-start.22 = (f32[768,1024]{0,1:T(8,128)}, f32[768,1024]{0,1:T(8,128)S(1)}, u32[]{:S(2)}) copy-start(f32[768,1024]{0,1:T(8,128)S(1)} %get-tuple-element.99) | copy-start | bytes 9437188
  139.9 8.3 %copy-start.43 = (f32[1024]{0:T(1024)}, f32[1024]{0:T(1024)S(1)}, u32[]{:S(2)}) copy-start(f32[1024]{0:T(1024)S(1)} %broadcast_multiply_fusion.5) | copy-start | bytes 12292
  141.5 6.7 %copy-start.57 = (f32[1024]{0:T(1024)}, f32[1024]{0:T(1024)S(1)}, u32[]{:S(2)}) copy-start(f32[1024]{0:T(1024)S(1)} %fusion.57) | copy-start | bytes 12292
  148.2 25.6 %copy-start.2 = (bf16[3,1024,768]{2,1,0:T(8,128)(2,1)}, bf16[3,1024,768]{2,1,0:T(8,128)(2,1)S(1)}, u32[]{:S(2)}) copy-start(bf16[3,1024,768]{2,1,0:T(8,128)(2,1)S(1)} %fusion.q_ref.k_ref.v_ref) | copy-start | bytes 14155780
  173.8 3.4 copy-start.13
  177.2 22.9 %copy-start.17 = (f32[1024,768]{1,0:T(8,128)}, f32[1024,768]{1,0:T(8,128)S(1)}, u32[]{:S(2)}) copy-start(f32[1024,768]{1,0:T(8,128)S(1)} %get-tuple-element.101) | copy-start | bytes 9437188
  177.7 21.7 %copy-start.47 = (f32[1024]{0:T(1024)}, f32[1024]{0:T(1024)S(1)}, u32[]{:S(2)}) copy-start(f32[1024]{0:T(1024)S(1)} %multiply_reduce_fusion.6) | copy-start | bytes 12292
  177.8 21.6 %copy-start.35 = (f32[1024]{0:T(1024)}, f32[1024]{0:T(1024)S(1)}, u32[]{:S(2)}) copy-start(f32[1024]{0:T(1024)S(1)} %fusion.58) | copy-start | bytes 12292
  200.6 3.3 copy-start.19
  200.6 3.2 copy-start.31
  200.6 9.7 %copy-start.67 = (s32[32,2]{0,1:T(2,128)S(1)}, s32[32,2]{0,1:T(2,128)}, u32[]{:S(2)}) copy-start(s32[32,2]{0,1:T(2,128)} %param.20) | copy-start | bytes 772
  202.2 7.5 %copy-start.39 = (f32[1024]{0:T(1024)}, f32[1024]{0:T(1024)S(1)}, u32[]{:S(2)}) copy-start(f32[1024]{0:T(1024)S(1)} %fusion.59) | copy-start | bytes 12292
  211.3 6.0 %copy-start.26 = (bf16[768,5462]{1,0:T(8,128)(2,1)S(1)}, bf16[768,5462]{1,0:T(8,128)(2,1)}, u32[]{:S(2)}) copy-start(bf16[768,5462]{1,0:T(8,128)(2,1)} %all-gather.4.cloned.1.call-done) | copy-start | bytes 25168900
  220.3 274.5 %all-gather.8.cloned.1.call-start = ((), (), s32[]{:S(2)}) async-start(), calls=%async_computation.4 | async-start | bytes 3612672 | tf_op jit(solution)/shard_map/all_gather | solution.py:1257
  221.2 19.5 %copy-start.32 = (f32[1024]{0:T(1024)S(1)}, f32[1024]{0:T(1024)}, u32[]{:S(2)}) copy-start(f32[1024]{0:T(1024)} %copy-done.31) | copy-start | bytes 12292
  221.2 19.5 %copy-start.38 = (f32[768]{0:T(1024)S(1)}, f32[768]{0:T(1024)}, u32[]{:S(2)}) copy-start(f32[768]{0:T(1024)} %copy-done.37) | copy-start | bytes 9220
  221.2 19.5 %copy-start.40 = (f32[1024]{0:T(1024)S(1)}, f32[1024]{0:T(1024)}, u32[]{:S(2)}) copy-start(f32[1024]{0:T(1024)} %copy-done.39) | copy-start | bytes 12292
  221.2 19.5 %copy-start.54 = (pred[1024]{0:T(1024)(128)(4,1)S(1)}, pred[1024]{0:T(1024)(128)(4,1)}, u32[]{:S(2)}) copy-start(pred[1024]{0:T(1024)(128)(4,1)} %copy-done.53) | copy-start | bytes 3076
  221.2 19.5 %copy-start.66 = (f32[8]{0:T(128)S(1)}, f32[8]{0:T(128)}, u32[]{:S(2)}) copy-start(f32[8]{0:T(128)} %copy-done.65) | copy-start | bytes 100
  221.2 279.1 %all-gather.6.cloned.1.call-start = ((), (), s32[]{:S(2)}) async-start(), calls=%async_computation.3 | async-start | bytes 16293888 | tf_op jit(solution)/shard_map/all_gather | solution.py:1232
  227.1 18.2 %copy-start.50 = (f32[1024]{0:T(1024)S(1)}, f32[1024]{0:T(1024)}, u32[]{:S(2)}) copy-start(f32[1024]{0:T(1024)} %copy-done.49) | copy-start | bytes 12292
  240.7 4.6 copy-start.20
  247.2 33.1 %copy-start.18 = (f32[1024,768]{1,0:T(8,128)S(1)}, f32[1024,768]{1,0:T(8,128)}, u32[]{:S(2)}) copy-start(f32[1024,768]{1,0:T(8,128)} %copy-done.17) | copy-start | bytes 9437188
  247.2 33.0 %copy-start.34 = (f32[768]{0:T(1024)S(1)}, f32[768]{0:T(1024)}, u32[]{:S(2)}) copy-start(f32[768]{0:T(1024)} %copy-done.33) | copy-start | bytes 9220
  247.2 33.0 %copy-start.36 = (f32[1024]{0:T(1024)S(1)}, f32[1024]{0:T(1024)}, u32[]{:S(2)}) copy-start(f32[1024]{0:T(1024)} %copy-done.35) | copy-start | bytes 12292
  280.3 3.0 copy-start.48
  280.3 3.0 copy-start.25
  283.3 5.6 slice-start
  284.7 4.2 slice-start.1
  285.2 54.0 %copy-start.21 = (f32[1024,768]{1,0:T(8,128)}, f32[1024,768]{1,0:T(8,128)S(1)}, u32[]{:S(2)}) copy-start(f32[1024,768]{1,0:T(8,128)S(1)} %get-tuple-element.79) | copy-start | bytes 9437188
  285.2 3.7 copy-start.12
  288.9 40.2 %copy-start.23 = (f32[768,1024]{0,1:T(8,128)S(1)}, f32[768,1024]{0,1:T(8,128)}, u32[]{:S(2)}) copy-start(f32[768,1024]{0,1:T(8,128)} %copy-done.22) | copy-start | bytes 9437188
  288.9 40.2 %copy-start.42 = (f32[768]{0:T(1024)S(1)}, f32[768]{0:T(1024)}, u32[]{:S(2)}) copy-start(f32[768]{0:T(1024)} %copy-done.41) | copy-start | bytes 9220
  288.9 40.2 %copy-start.44 = (f32[1024]{0:T(1024)S(1)}, f32[1024]{0:T(1024)}, u32[]{:S(2)}) copy-start(f32[1024]{0:T(1024)} %copy-done.43) | copy-start | bytes 12292
  289.0 40.2 %copy-start.56 = (f32[768]{0:T(1024)S(1)}, f32[768]{0:T(1024)}, u32[]{:S(2)}) copy-start(f32[768]{0:T(1024)} %copy-done.55) | copy-start | bytes 9220
  289.0 40.2 %copy-start.58 = (f32[1024]{0:T(1024)S(1)}, f32[1024]{0:T(1024)}, u32[]{:S(2)}) copy-start(f32[1024]{0:T(1024)} %copy-done.57) | copy-start | bytes 12292
  329.1 10.6 %copy-start.3 = (bf16[3,1024,768]{2,1,0:T(8,128)(2,1)}, bf16[3,1024,768]{2,1,0:T(8,128)(2,1)S(1)}, u32[]{:S(2)}) copy-start(bf16[3,1024,768]{2,1,0:T(8,128)(2,1)S(1)} %attention_backward.1) | copy-start | bytes 14155780
  329.1 8.3 %copy-start.46 = (f32[1024]{0:T(1024)S(1)}, f32[1024]{0:T(1024)}, u32[]{:S(2)}) copy-start(f32[1024]{0:T(1024)} %copy-done.45) | copy-start | bytes 12292
  342.2 2.9 copy-start.14
  342.2 7.8 %slice-start.2 = ((s8[4718592]{0:T(1024)(128)(4,1)}), s8[4194304]{0:T(1024)(128)(4,1)S(1)}, s32[]{:S(2)}) async-start(s8[4718592]{0:T(1024)(128)(4,1)} %bitcast.88), calls=%async_computation.7 | async-start | bytes 8388608
  345.1 5.0 slice-start.3
  345.1 5.0 copy-start.24
  345.1 5.0 copy-start.64
  493.4 6.9 %copy-start.15 = (f32[13,8,1,768]{3,2,1,0:T(1,128)S(1)}, f32[13,8,1,768]{3,2,1,0:T(1,128)}, u32[]{:S(2)}) copy-start(f32[13,8,1,768]{3,2,1,0:T(1,128)} %get-tuple-element.39.scales_ref) | copy-start | bytes 958468
  555.8 8.8 %copy-start.52 = (f32[15,96]{1,0:T(8,128)S(1)}, f32[15,96]{1,0:T(8,128)}, u32[]{:S(2)}) copy-start(f32[15,96]{1,0:T(8,128)} %param.30) | copy-start | bytes 17284
  555.8 8.8 %copy-start.61 = (f32[15,96]{1,0:T(8,128)S(1)}, f32[15,96]{1,0:T(8,128)}, u32[]{:S(2)}) copy-start(f32[15,96]{1,0:T(8,128)} %param.32) | copy-start | bytes 17284
  555.9 8.8 %copy-start.62 = (f32[15,96]{1,0:T(8,128)S(1)}, f32[15,96]{1,0:T(8,128)}, u32[]{:S(2)}) copy-start(f32[15,96]{1,0:T(8,128)} %param.31) | copy-start | bytes 17284
  555.9 10.2 %copy-start.27 = (f32[96,5462]{1,0:T(8,128)S(1)}, f32[96,5462]{1,0:T(8,128)}, u32[]{:S(2)}) copy-start(f32[96,5462]{1,0:T(8,128)} %param.27) | copy-start | bytes 6292228
  555.9 10.2 %copy-start.28 = (f32[96,5462]{1,0:T(8,128)S(1)}, f32[96,5462]{1,0:T(8,128)}, u32[]{:S(2)}) copy-start(f32[96,5462]{1,0:T(8,128)} %get-tuple-element.105) | copy-start | bytes 6292228
  555.9 10.2 %copy-start.29 = (f32[96,5462]{1,0:T(8,128)S(1)}, f32[96,5462]{1,0:T(8,128)}, u32[]{:S(2)}) copy-start(f32[96,5462]{1,0:T(8,128)} %param.29) | copy-start | bytes 6292228
  555.9 10.2 %copy-start.30 = (f32[96,5462]{1,0:T(8,128)S(1)}, f32[96,5462]{1,0:T(8,128)}, u32[]{:S(2)}) copy-start(f32[96,5462]{1,0:T(8,128)} %param.28) | copy-start | bytes 6292228
  566.1 3.9 copy-start.6
  566.1 5.5 copy-start.8
  (12 other events, 22.1 us)
Sparse Core Ops, SparseCore 0:
  10.8 162.2 all-gather.3
  220.4 20.1 reduce-scatter.1
  242.9 61.0 all-gather.7
  306.0 101.8 all-gather.5

commit v5 on v4

--- a/solution.py
+++ b/solution.py
@@ -415,7 +415,10 @@
 
 def reduce_kernel(counts, *refs):
     sources, refs = refs[: len(counts)], refs[len(counts) :]
-    (vec_ref, codes_hbm, scales_hbm, vec_out_ref,
+    (vec_ref, tail_ref, left_hbm, right_hbm,
+     own_hbm, left_out_hbm, right_out_hbm, step_hbm, sums_ref, tail_out_ref, vec_out_ref,
+     left_buf, right_buf, outs_buf, squares, high_buf, low_buf, sum_slots, tail_slots,
+     in_sem, sum_send, sum_recv, tail_send, tail_recv,
      acc, spare, kept, sent0, got0, sent1, got1, sent2, got2, sent3, got3, sent4, got4,
      ss0, gs0, ss1, gs1, ss2, gs2, ss3, gs3, ss4, gs4, codes, scales, vec_got,
      load_sem, out_sem, send_sem, recv_sem, send_scale_sem, recv_scale_sem,
@@ -434,10 +437,22 @@
     mate_far = torus_device((z + 2) % 4, y, x, core)
 
     barrier = pltpu.get_barrier_semaphore()
-    mates = (mate_core, mate_x, mate_y, mate_z, mate_mid, mate_far)
-    for mate in mates:
-        pl.semaphore_signal(barrier, inc=1, device_id=mate, device_id_type=MESH)
-    pl.semaphore_wait(barrier, len(mates))
+    dp, cls = lax.axis_index("dp"), lax.axis_index("cls")
+    everyone = tail_slots.shape[0]
+    quarter = sum_slots.shape[0]
+    me = dp * 4 + cls
+
+    def any_mate(n):
+        other = lax.rem(me + n, everyone)
+        return (other // 4, lax.rem(other, 4))
+
+    def half_mate(n):
+        return (upper * quarter + lax.rem(dp + n, quarter), cls)
+
+    for n in range(1, everyone):
+        pl.semaphore_signal(barrier, inc=1, device_id=any_mate(n), device_id_type=MESH)
+    pl.semaphore_wait(barrier, everyone - 1)
+    own = lax.rem(dp, quarter) * left_buf.shape[1]
 
     own_cols = pl.ds(pl.multiple_of(core * cols, 128), cols)
     other_cols = pl.ds(pl.multiple_of((1 - core) * cols, 128), cols)
@@ -705,34 +720,103 @@
                 wait_recv(spread(11 + b, m, theirs, 2, mate_y if b else mate_x))
             start(spread(13, m, 0, 8, mate_core))
 
+        def ins(m):
+            return (
+                pltpu.make_async_copy(left_hbm.at[m], left_buf.at[m % 2], in_sem.at[m % 2, 0]),
+                pltpu.make_async_copy(right_hbm.at[m], right_buf.at[m % 2], in_sem.at[m % 2, 1]),
+            )
+
         def outs(m):
-            return (
-                pltpu.make_async_copy(codes.at[m], codes_hbm.at[m], out_sem.at[m % 2, 0]),
-                pltpu.make_async_copy(scales.at[m], scales_hbm.at[m], out_sem.at[m % 2, 1]),
-            )
+            targets = (own_hbm, left_out_hbm, right_out_hbm, step_hbm)
+            return [
+                pltpu.make_async_copy(
+                    outs_buf.at[m % 2, n], target.at[m], out_sem.at[m % 2, n]
+                )
+                for n, target in enumerate(targets)
+            ]
+
+        @pl.when((t >= 8) & (t < total + 8))
+        def _():
+            start(ins(t - 8))
+
+        @pl.when((t >= 11) & (t < total + 11))
+        def _():
+            for copy in outs(t - 11):
+                copy.wait()
 
         @pl.when((t >= 9) & (t < total + 9))
         def _():
             m = t - 9
             wait_send(spread(13, m, 0, 8, mate_core))
             wait_recv(spread(13, m, 0, 8, mate_core, other_cols))
+            for copy in ins(m):
+                copy.wait()
+            precondition_block(
+                own, codes.at[m], scales.at[m], left_buf.at[m % 2], right_buf.at[m % 2],
+                outs_buf.at[m % 2], squares.at[m], high_buf, low_buf,
+            )
             start(outs(m))
 
-        @pl.when((t >= 10) & (t < total + 10))
-        def _():
-            for copy in outs(t - 10):
-                copy.wait()
-
         return carry
 
-    lax.fori_loop(0, total + 10, step, 0)
-
-
-def reduce_gradients(arrays, vec_sums):
+    lax.fori_loop(0, total + 11, step, 0)
+
+    def folded(row):
+        return sum(row[:, n * 128 : (n + 1) * 128] for n in range(row.shape[1] // 128))
+
+    sums_ref[...] = jnp.zeros_like(sums_ref)
+    layer = jnp.zeros((1, 128), jnp.float32)
+    for m in range(total):
+        layer = layer + folded(squares[m, 0:1, :])
+        for quad in range(2):
+            part = squares[m, 1:2, quad * cols : (quad + 1) * cols]
+            sums_ref[2 * m + quad : 2 * m + quad + 1, :] = folded(part)
+    sum_slots[lax.rem(dp, quarter)] = sums_ref[...]
+    once = (cls == 0).astype(jnp.float32)
+    first_row = lax.broadcasted_iota(jnp.int32, tail_ref.shape, 0) == 0
+    tail_slots[me] = tail_ref[...] + jnp.where(first_row, once * layer, 0.0)
+
+    def sum_copy(n, slot):
+        return pltpu.make_async_remote_copy(
+            src_ref=sum_slots.at[slot], dst_ref=sum_slots.at[slot],
+            send_sem=sum_send.at[n], recv_sem=sum_recv.at[slot],
+            device_id=half_mate(n), device_id_type=MESH,
+        )
+
+    def tail_copy(n, slot):
+        return pltpu.make_async_remote_copy(
+            src_ref=tail_slots.at[slot], dst_ref=tail_slots.at[slot],
+            send_sem=tail_send.at[n], recv_sem=tail_recv.at[slot],
+            device_id=any_mate(n), device_id_type=MESH,
+        )
+
+    for n in range(1, quarter):
+        sum_copy(n, lax.rem(dp, quarter)).start()
+    for n in range(1, everyone):
+        tail_copy(n, me).start()
+    for n in range(1, quarter):
+        sum_copy(n, lax.rem(dp, quarter)).wait_send()
+        sum_copy(n, lax.rem(dp + n, quarter)).wait_recv()
+    for n in range(1, everyone):
+        tail_copy(n, me).wait_send()
+        tail_copy(n, lax.rem(me + n, everyone)).wait_recv()
+    value = sum_slots[0]
+    for n in range(1, quarter):
+        value = value + sum_slots[n]
+    sums_ref[...] = value
+    value = tail_slots[0]
+    for n in range(1, everyone):
+        value = value + tail_slots[n]
+    tail_out_ref[...] = value
+
+
+def reduce_gradients(arrays, vec_sums, tail, root_left, right_half, dp_count, cls_count):
     counts = tuple(array.shape[0] for array in arrays)
     total = sum(counts)
     width = arrays[0].shape[1]
+    rows = root_left.shape[1]
     half, cols = width // 2, width // 2
+    sum_rows = 2 * total + -2 * total % 8
     f32, i16 = jnp.float32, jnp.int16
 
     def pair(*shape):
@@ -748,14 +832,28 @@
     vmem = pl.BlockSpec(memory_space=pltpu.VMEM)
     return pl.pallas_call(
         functools.partial(reduce_kernel, counts),
-        out_shape=(
-            jax.ShapeDtypeStruct((total, half, width), i16),
-            jax.ShapeDtypeStruct((total, half // PIECE, 1, width), f32),
+        out_shape=(jax.ShapeDtypeStruct((total, rows, width), f32),) * 4
+        + (
+            jax.ShapeDtypeStruct((sum_rows, 128), f32),
+            jax.ShapeDtypeStruct(tail.shape, f32),
             jax.ShapeDtypeStruct(vec_sums.shape, f32),
         ),
-        in_specs=[hbm] * len(arrays) + [vmem],
-        out_specs=(hbm, hbm, vmem),
+        in_specs=[hbm] * len(arrays) + [vmem, vmem, hbm, hbm],
+        out_specs=(hbm,) * 4 + (vmem,) * 3,
         scratch_shapes=[
+            pltpu.VMEM((2, rows, width), f32),
+            pltpu.VMEM((2, half, width), f32),
+            pltpu.VMEM((2, 4, rows, width), f32),
+            pltpu.VMEM((total, 2, width), f32),
+            pltpu.VMEM((half, width), jnp.bfloat16),
+            pltpu.VMEM((half, width), jnp.bfloat16),
+            pltpu.VMEM((dp_count // 2, sum_rows, 128), f32),
+            pltpu.VMEM((dp_count * cls_count,) + tail.shape, f32),
+            pltpu.SemaphoreType.DMA((2, 2)),
+            pltpu.SemaphoreType.DMA((dp_count // 2,)),
+            pltpu.SemaphoreType.DMA((dp_count // 2,)),
+            pltpu.SemaphoreType.DMA((dp_count * cls_count,)),
+            pltpu.SemaphoreType.DMA((dp_count * cls_count,)),
             pltpu.VMEM((5, width, cols), f32),
             pltpu.VMEM((2, width, cols), f32),
             pltpu.VMEM((3, 2, 2, PIECE, cols), f32),
@@ -775,7 +873,7 @@
             pltpu.VMEM((total, half // PIECE, 1, width), f32),
             pltpu.VMEM((5, 2) + vec_sums.shape, f32),
             pltpu.SemaphoreType.DMA((2, 2)),
-            pltpu.SemaphoreType.DMA((2, 2)),
+            pltpu.SemaphoreType.DMA((2, 4)),
             pltpu.SemaphoreType.DMA((14, 2)),
             pltpu.SemaphoreType.DMA((14, total)),
             pltpu.SemaphoreType.DMA((14, 2)),
@@ -787,7 +885,7 @@
             collective_id=1, has_side_effects=True, vmem_limit_bytes=60 << 20
         ),
         name="reduce_gradients",
-    )(*arrays, vec_sums)
+    )(*arrays, vec_sums, tail, root_left, right_half)
 
 
 def split_float(values):
@@ -803,20 +901,19 @@
     return [out[n * rows : (n + 1) * rows] for n in range(len(lefts))]
 
 
-def precondition_kernel(
-    own_count, codes_ref, scales_ref, left_ref, right_ref,
-    left_out, right_out, step_out, own_out, squares_ref, high_ref, low_ref
+def precondition_block(
+    own, codes_ref, scales_ref, left_ref, right_ref, outs_ref, squares_ref, high_ref, low_ref
 ):
     half, width = codes_ref.shape
     rows = left_ref.shape[0]
-    own = lax.rem(lax.axis_index("dp"), own_count) * rows
     own_rows = pl.ds(pl.multiple_of(own, PIECE), rows)
     for piece in range(half // PIECE):
         part = slice(piece * PIECE, (piece + 1) * PIECE)
-        value = codes_ref[part, :].astype(jnp.int32).astype(jnp.float32) * scales_ref[piece]
-        high_ref[part, :], low_ref[part, :] = split_float(value)
+        high_ref[part, :], low_ref[part, :] = split_float(
+            decode(codes_ref[part, :], scales_ref[piece])
+        )
     own_value = high_ref[own_rows, :].astype(jnp.float32) + low_ref[own_rows, :].astype(jnp.float32)
-    own_out[...] = own_value
+    outs_ref[0] = own_value
     squares_ref[0:1, :] = jnp.sum(own_value * own_value, 0, keepdims=True)
     picks = (
         lax.broadcasted_iota(jnp.int32, (rows, half), 1)
@@ -828,107 +925,71 @@
         mine_high, mine_low = high_ref[own_rows, cols], low_ref[own_rows, cols]
         hh, lh, turned_high = stacked_dot([mine_high, mine_low, picks], high, True)
         hl, turned_low = stacked_dot([mine_high, picks], low, True)
-        left_out[:, cols] = hh + (lh + hl)
+        outs_ref[1, :, cols] = hh + (lh + hl)
         turned_high = turned_high.astype(jnp.bfloat16)
         turned_low = turned_low.astype(jnp.bfloat16)
         root_high, root_low = split_float(left_ref[:, cols])
         thh, tlh, rhh, rlh = stacked_dot([turned_high, turned_low, root_high, root_low], high, False)
         thl, rhl = stacked_dot([turned_high, root_high], low, False)
-        right_out[:, cols] = thh + (tlh + thl)
+        outs_ref[2, :, cols] = thh + (tlh + thl)
         half_step = rhh + (rlh + rhl)
         step_high, step_low = split_float(half_step)
         right_high, right_low = split_float(right_ref[:, cols])
         shh, slh = stacked_dot([step_high, step_low], right_high, False)
         (shl,) = stacked_dot([step_high], right_low, False)
         direction = shh + (slh + shl)
-        step_out[:, cols] = direction
+        outs_ref[3, :, cols] = direction
         squares_ref[1:2, cols] = jnp.sum(direction * direction, 0, keepdims=True)
 
 
-def precondition(codes, scales, root_left, right_half, own_count):
-    count, half, width = codes.shape
-    rows = root_left.shape[1]
-
-    def spec(*shape):
-        return pl.BlockSpec((None,) + shape, lambda b: (b,) + (0,) * len(shape))
-
-    mine = jax.ShapeDtypeStruct((count, rows, width), jnp.float32)
-    return pl.pallas_call(
-        functools.partial(precondition_kernel, own_count),
-        grid=(count,),
-        out_shape=(mine, mine, mine, mine, jax.ShapeDtypeStruct((count, 2, width), jnp.float32)),
-        in_specs=[
-            spec(half, width),
-            spec(half // PIECE, 1, width),
-            spec(rows, width),
-            spec(half, width),
-        ],
-        out_specs=(spec(rows, width),) * 4 + (spec(2, width),),
-        scratch_shapes=[
-            pltpu.VMEM((half, width), jnp.bfloat16),
-            pltpu.VMEM((half, width), jnp.bfloat16),
-        ],
-        compiler_params=pltpu.CompilerParams(vmem_limit_bytes=32 << 20),
-        name="precondition",
-    )(codes, scales, root_left, right_half)
-
-
-def sum_kernel(dp_count, cls_count, in_ref, out_ref, slots, send_sem, recv_sem):
+def class_sum_kernel(in_ref, out_ref, slots, send_sem, recv_sem):
     dp, cls = lax.axis_index("dp"), lax.axis_index("cls")
-    total = dp_count * cls_count
-    me = dp * cls_count + cls
+    total, rows = slots.shape[0], slots.shape[1]
     barrier = pltpu.get_barrier_semaphore()
-
-    def mate(n):
-        other = lax.rem(me + n, total)
-        return (other // cls_count, lax.rem(other, cls_count))
-
     for n in range(1, total):
-        pl.semaphore_signal(barrier, inc=1, device_id=mate(n), device_id_type=MESH)
+        pl.semaphore_signal(
+            barrier, inc=1, device_id=(dp, lax.rem(cls + n, total)), device_id_type=MESH
+        )
     pl.semaphore_wait(barrier, total - 1)
 
-    def copy(n):
+    def part(index):
+        return in_ref.at[pl.ds(pl.multiple_of(index * rows, 8), rows)]
+
+    def copy(n, slot):
+        mate = lax.rem(cls + n, total)
         return pltpu.make_async_remote_copy(
-            src_ref=in_ref, dst_ref=slots.at[me],
-            send_sem=send_sem.at[n], recv_sem=recv_sem.at[me],
-            device_id=mate(n), device_id_type=MESH,
-        )
-
-    def arrival(n):
-        source = lax.rem(me + n, total)
-        return pltpu.make_async_remote_copy(
-            src_ref=in_ref, dst_ref=slots.at[source],
-            send_sem=send_sem.at[n], recv_sem=recv_sem.at[source],
-            device_id=mate(n), device_id_type=MESH,
+            src_ref=part(mate), dst_ref=slots.at[slot],
+            send_sem=send_sem.at[n], recv_sem=recv_sem.at[slot],
+            device_id=(dp, mate), device_id_type=MESH,
         )
 
     for n in range(1, total):
-        copy(n).start()
-    slots[me] = in_ref[...]
+        copy(n, cls).start()
+    slots[cls] = part(cls)[...]
     for n in range(1, total):
-        copy(n).wait_send()
-        arrival(n).wait_recv()
+        copy(n, cls).wait_send()
+        copy(n, lax.rem(cls + n, total)).wait_recv()
     value = slots[0]
     for n in range(1, total):
         value = value + slots[n]
     out_ref[...] = value
 
 
-def sum_everywhere(values, dp_count, cls_count):
-    total = dp_count * cls_count
+def class_sum(values, cls_count):
+    rows = values.shape[0] // cls_count
     vmem = pl.BlockSpec(memory_space=pltpu.VMEM)
     return pl.pallas_call(
-        functools.partial(sum_kernel, dp_count, cls_count),
-        out_shape=jax.ShapeDtypeStruct(values.shape, jnp.float32),
+        class_sum_kernel,
+        out_shape=jax.ShapeDtypeStruct((rows, values.shape[1]), jnp.float32),
         in_specs=[vmem],
         out_specs=vmem,
         scratch_shapes=[
-            pltpu.VMEM((total,) + values.shape, jnp.float32),
-            pltpu.SemaphoreType.DMA((total,)),
-            pltpu.SemaphoreType.DMA((total,)),
+            pltpu.VMEM((cls_count, rows, values.shape[1]), jnp.float32),
+            pltpu.SemaphoreType.DMA((cls_count,)),
+            pltpu.SemaphoreType.DMA((cls_count,)),
         ],
         compiler_params=pltpu.CompilerParams(collective_id=2, has_side_effects=True),
-        name="sum_everywhere",
+        name="class_sum",
     )(values)
 
 
@@ -1229,15 +1290,16 @@
         vec_low = lax.all_gather(vectors.astype(jnp.bfloat16), "dp", axis=1, tiled=True)
         vec_all = vec_low.astype(jnp.float32)
     head_low = lax.all_gather(head_weights.astype(jnp.bfloat16), "dp", axis=0, tiled=True)
-    right_half = lax.all_gather(
-        my_part(root_right), ("dp", "cls"), axis=1, tiled=True, axis_index_groups=half_groups
-    )
     final_gain = vec_all[9 + up_count]
     final_shift = vec_all[10 + up_count]
     pack_ids, pack_keep = image_ids[0], keep[0]
     key_codes = jnp.where(pack_keep == 1, pack_ids, -1)
 
     output, saved = layer_forward(blocks, vec_all, patches, pack_ids, key_codes)
+    right_part, output = lax.optimization_barrier((my_part(root_right), output))
+    right_half = lax.all_gather(
+        right_part, ("dp", "cls"), axis=1, tiled=True, axis_index_groups=half_groups
+    )
     pooled = pool_rows(output, final_gain, final_shift, pack_ids, pack_keep)
     group = lax.all_gather(pooled.astype(jnp.bfloat16), "cls", axis=0, tiled=True)
     logits = jnp.dot(group, head_low, preferred_element_type=jnp.float32)
@@ -1253,7 +1315,10 @@
         jnp.bfloat16
     )
     group_grad = jnp.einsum("gc,dc->gd", grad_logits, head_low, preferred_element_type=jnp.float32)
-    grad_pooled = lax.psum_scatter(group_grad, "cls", scatter_dimension=0, tiled=True)
+    if on_torus:
+        grad_pooled = class_sum(group_grad, cls_count)
+    else:
+        grad_pooled = lax.psum_scatter(group_grad, "cls", scatter_dimension=0, tiled=True)
     head_rows = lax.all_gather(
         jnp.concatenate([group, grad_logits], 1), "dp", axis=0, tiled=True
     )
@@ -1280,46 +1345,43 @@
         grad_shift,
     )
 
+    head_squares = jnp.sum(head_grad * head_grad)
     if on_torus:
         padded = jnp.pad(grad_vectors, ((0, -grad_vectors.shape[0] % 8), (0, 0)))
-        codes, scales, vector_sum = reduce_gradients(grad_arrays, padded)
+        tail = jnp.pad(jnp.stack([head_squares, loss_part])[:, None], ((0, 6), (0, 127)))
+        block_rows, left_add, right_add, direction, sums, tail, vector_sum = reduce_gradients(
+            grad_arrays, padded, tail, root_left, right_half, dp_count, cls_count
+        )
         vector_sum = vector_sum[: grad_vectors.shape[0]]
-        left_add, right_add, direction, block_rows, squares = precondition(
-            codes, scales, root_left, right_half, half_dp
-        )
-        layer_squares = jnp.sum(squares[:, 0])
-        block_squares = jnp.sum(squares[:, 1].reshape(block_count, 2, half_size), -1)
+        loss = tail[1, 0]
+        all_squares = jnp.sum(tail[0])
+        block_squares = jnp.sum(sums[: 2 * block_count], -1).reshape(block_count, 2)
     else:
         grad_half = reduced_half(jnp.concatenate(grad_arrays, 0), half_groups)
         vector_sum = lax.psum(grad_vectors, ("dp", "cls"))
         left_add, right_add, direction, block_rows = preconditioned_rows(
             grad_half, root_left, right_half, (dp_index % half_dp) * row_count
         )
-        layer_squares = jnp.sum(block_rows * block_rows)
-        block_squares = jnp.sum(split_halves(direction * direction, half_size), (1, 3))
+        squares = jnp.sum(split_halves(direction * direction, half_size), (1, 3))
+        in_top = (dp_index < half_dp).astype(jnp.float32)
+        once = (cls_index == 0).astype(jnp.float32)
+        all_squares = head_squares + once * jnp.sum(block_rows * block_rows)
+        packed = jnp.concatenate(
+            [
+                (once * in_top * squares).reshape(-1),
+                (once * (1.0 - in_top) * squares).reshape(-1),
+                jnp.stack([all_squares, loss_part]),
+            ]
+        )
+        packed = lax.psum(packed, ("dp", "cls"))
+        loss = packed[4 * block_count + 1]
+        all_squares = packed[4 * block_count]
+        sums = packed[: 4 * block_count].reshape(2, block_count, 2)
+        block_squares = jnp.where(dp_index < half_dp, sums[0], sums[1])
     vector_rows = lax.dynamic_slice_in_dim(vector_sum, dp_index * row_count, row_count, 1)
-    in_top = (dp_index < half_dp).astype(jnp.float32)
-    once = (cls_index == 0).astype(jnp.float32)
-    own_squares = once * (layer_squares + jnp.sum(vector_rows * vector_rows))
-    packed = jnp.concatenate(
-        [
-            (once * in_top * block_squares).reshape(-1),
-            (once * (1.0 - in_top) * block_squares).reshape(-1),
-            jnp.stack([own_squares + jnp.sum(head_grad * head_grad), loss_part]),
-        ]
-    )
-    if on_torus:
-        spare = -packed.shape[0] % 1024
-        packed = sum_everywhere(
-            jnp.pad(packed, (0, spare)).reshape(8, 128), dp_count, cls_count
-        ).reshape(-1)
-    else:
-        packed = lax.psum(packed, ("dp", "cls"))
-    loss = packed[4 * block_count + 1]
-    grad_norm = jnp.sqrt(packed[4 * block_count])
+    grad_norm = jnp.sqrt(all_squares + jnp.sum(vector_sum * vector_sum))
     factor = CLIP_NORM / jnp.maximum(grad_norm, CLIP_NORM)
-    sums = packed[: 4 * block_count].reshape(2, block_count, 2)
-    mean_squares = jnp.where(dp_index < half_dp, sums[0], sums[1]) / (half_size * half_size)
+    mean_squares = block_squares / (half_size * half_size)
     mean_squares = mean_squares * factor * factor
     scale = factor * lax.rsqrt(mean_squares + ROOT_EPS)
     wide_scale = jnp.repeat(SHAMPOO_RATE * scale, half_size, axis=1)

time: 596 us -> 551 us (0.924)
  Pallas kernels: 414 us -> 372 us
  other arithmetic: 47.3 us -> 57 us
  waiting for transfers between devices: 13.6 us -> 4.43 us
  local copies, waits for them, and re-layouts: 27.5 us -> 21.1 us
    pallas_call x2 -> x1, Pallas kernels: 39.1 us -> 5.4 us  [class_sum(): pl.pallas_call(class_sum_kernel, out_shape=jax.ShapeDtypeStruct((rows, va...]
    reduce_scatter x1 -> x0, waiting for transfers between devices: 13.6 us -> none  [on_device(): lax.psum_scatter(group_grad, 'cls', scatter_dimension=0, tiled=True)]
    pallas_call x1, Pallas kernels: 137 us -> 128 us  [reduce_gradients(): pl.pallas_call(functools.partial(reduce_kernel, counts), out_shape=(jax.S...]
    unnamed x146 -> x132, local copies, waits for them, and re-layouts: 18.9 us -> 11.7 us
  transfers between devices with their start and end apart: 4 -> 3, of which waited for: 1 -> 1; matrix products, arithmetic and copies ran while one was open for 13% -> 17% of each run, Pallas kernels for 64% -> 45%
where the time goes in v5:
time: 551 us; the launch traced here: 542 us
  Pallas kernels  372 us (68%)
  matrix products  62 us (11%)
  other arithmetic  57 us (10%)
  local copies, waits for them, and re-layouts  21.1 us (4%)
  between operations  19.2 us (3%)
  blocking collectives  5.8 us (1%)
    pallas_call x1, Pallas kernels, reduce_gradients(): pl.pallas_call(functools.partial(reduce_kernel, counts), out_shape=(jax.S...  128 us
    pallas_call x1, Pallas kernels, gather_weights(): pl.pallas_call(gather_kernel, out_shape=(jax.ShapeDtypeStruct((count, SHA...  118 us
    pallas_call x1, Pallas kernels, attention_backward(): pl.pallas_call(attention_backward_kernel, grid=(width // PAIR,), out_shap...  40.1 us
    pallas_call x1, Pallas kernels, mlp_backward(): pl.pallas_call(mlp_backward_kernel, grid=(up_count * split,), out_shape=(...  33.5 us
    pallas_call x1, Pallas kernels, attention_forward(): pl.pallas_call(attention_forward_kernel, grid=(width // PAIR,), out_shape...  25.6 us
    pallas_call x1, Pallas kernels, mlp_forward(): pl.pallas_call(mlp_forward_kernel, grid=(up_count * split,), out_shape=(j...  21.6 us
    unnamed x132, local copies, waits for them, and re-layouts  11.7 us
  transfers between devices with their start and end apart: 3, of which 1 were waited for; matrix products, arithmetic and copies ran while one was open for 17% of the time, Pallas kernels for 45%

profile of v5, /device:TPU:0, one launch (start us, length us, event | category | flops | bytes accessed | tf_op | source)
XLA Modules:
  0.0 542.1 jit_solution(6090556374328144373)
XLA Ops:
  7.2 2.8 convert_element_type.75
  10.1 2.3 convert_element_type.68.own_ref
  12.5 117.8 %gather_weights.1 = (bf16[13,768,768]{2,1,0:T(8,128)(2,1)S(1)}, f32[8,16,128]{2,1,0:T(8,128)S(1)}) custom-call(bf16[13,96,768]{2,1,0:T(8,128)(2,1)S(1)} %convert_element_type.68.own_ref, f32[16,128]{1,0:T(8,128)S(1)} %pad.12.vec_ref), custom_call_target="tpu_custom_call" | custom-call | tf_op jit(solution)/shard_map/gather_weights/pallas_call | solution.py:1182
  130.3 5.4 copy-done.1
  136.9 2.8 add_reduce_fusion
  139.7 0.6 multiply_reduce_fusion.7
  140.4 1.0 copy-done.39
  141.4 6.6 %fusion.q_ref.k_ref.v_ref = bf16[3,1024,768]{2,1,0:T(8,128)(2,1)S(1)} fusion(f32[3,768]{1,0:T(4,128)S(1)} %pad_maximum_fusion.1, bf16[13,768,768]{2,1,0:T(8,128)(2,1)} %copy-done.1, f32[768,1024]{0,1:T(8,128)S(1)} %get-tuple-element.95, f32[768]{0:T(1024)S(1)} %add.202, f32[768]{0:T(1024)S(1)} %mul.345, f32[1024]{0:T(1024)S(1)} %fusion.50, ...), kind=kOutput, calls=%fused_computation.4 | convolution fusion | flops 3633315840 | bytes 11429888 | tf_op jit(solution)/shard_map/td,kde->kte/dot_general | solution.py:324
  148.1 25.6 %attention_forward.1 = bf16[1024,768]{1,0:T(8,128)(2,1)S(1)} custom-call(s32[1024,1]{1,0:T(8,128)S(1)} %copy.54.qids_ref, s32[1,1024]{1,0:T(1,128)S(1)} %broadcast_select_fusion.1.kcodes_ref, bf16[3,1024,768]{2,1,0:T(8,128)(2,1)S(1)} %fusion.q_ref.k_ref.v_ref, bf16[3,1024,768]{2,1,0:T(8,128)(2,1)S(1)} %fusion.q_ref.k_ref.v_ref, ...), custom_call_target="tpu_custom_call" | custom-call | tf_op jit(solution)/shard_map/attention_forward/pallas_call | solution.py:176
  173.7 3.4 fusion.66
  177.2 0.5 multiply_reduce_fusion.6
  177.7 1.1 copy-done.12
  178.8 0.5 add_convert_fusion.2.x_ref
  179.4 21.6 %mlp_forward.1 = (bf16[1024,3072]{1,0:T(8,128)(2,1)}, f32[1024,3072]{1,0:T(8,128)}, f32[1024,768]{1,0:T(8,128)S(1)}) custom-call(bf16[1024,768]{1,0:T(8,128)(2,1)S(1)} %add_convert_fusion.2.x_ref, bf16[13,768,768]{2,1,0:T(8,128)(2,1)} %copy-done.1, f32[1,3072]{1,0:T(1,128)S(1)} %reshape.204.bias_ref, bf16[13,768,768]{2,1,0:T(8,128)(2,1)} %copy-done.1), custom_call_target="tpu_custom_call" | custom-call | tf_op jit(solution)/shard_map/mlp_forward/pallas_call | solution.py:278
  201.0 1.7 copy-done.5
  202.7 2.2 constant_dynamic-slice_fusion
  204.9 4.9 add_add_fusion.4
  209.8 2.1 reduce_sum.260
  212.0 0.6 fusion.53
  212.8 2.5 multiply_reduce_fusion.5
  215.4 0.6 copy-done.43
  216.0 1.7 fusion.30
  217.7 5.8 %all_gather.12 = bf16[32,768]{1,0:T(8,128)(2,1)S(1)} all-gather(bf16[8,768]{1,0:T(8,128)(2,1)S(1)} %fusion.30), channel_id=1, replica_groups=mesh['dp'=8,'cls'=4] {'cls'}, dimensions={0}, use_global_device_ids=true | all-gather | bytes 61440 | tf_op jit(solution)/shard_map/all_gather | solution.py:1304
  223.5 0.6 broadcast_compare_fusion
  224.1 1.0 compare_reduce_fusion
  225.0 5.8 %fusion.37 = (f32[]{:T(128)}, bf16[32,5462]{1,0:T(8,128)(2,1)S(1)}) fusion(pred[32,5462]{1,0:T(8,128)(4,1)} %compare_reduce_fusion, pred[5462]{0:T(1024)(128)(4,1)} %broadcast_compare_fusion, bf16[32,768]{1,0:T(8,128)(2,1)S(1)} %all_gather.12, bf16[768,5462]{1,0:T(8,128)(2,1)} %all-gather.4.cloned.1.call-done), kind=kOutput, calls=%fused_computation.74 | convolution fusion | flops 271614336 | bytes 8968602 | tf_op jit(solution)/shard_map/dot_general | solution.py:1305
  230.9 0.8 pad_maximum_fusion
  231.7 0.7 all-gather.8.cloned.1.call-update
  232.4 1.6 copy.57
  234.7 2.0 broadcast_select_fusion.kcodes_ref
  236.7 6.6 %fusion.67.in_ref = f32[32,768]{1,0:T(8,128)} fusion(bf16[32,5462]{1,0:T(8,128)(2,1)S(1)} %get-tuple-element.89, bf16[768,5462]{1,0:T(8,128)(2,1)} %all-gather.4.cloned.1.call-done), kind=kOutput, calls=%fused_computation.143 | convolution fusion | flops 268468224 | bytes 8837504 | tf_op jit(solution)/shard_map/gc,dc->gd/dot_general | solution.py:1317
  243.2 5.4 class_sum.1
  248.7 4.7 multiply_reduce_fusion
  253.4 1.5 fusion.64
  255.3 33.5 %mlp_backward.1 = (f32[4,768,768]{2,1,0:T(8,128)}, f32[4,768,768]{2,1,0:T(8,128)}, f32[1,3072]{1,0:T(1,128)S(1)}, f32[1024,768]{1,0:T(8,128)}) custom-call(bf16[1024,768]{1,0:T(8,128)(2,1)S(1)} %add_convert_fusion.2.x_ref, bf16[1024,768]{1,0:T(8,128)(2,1)S(1)} %get-tuple-element.77.dm_ref, bf16[13,768,768]{2,1,0:T(8,128)(2,1)} %copy-done.1, ...), custom_call_target="tpu_custom_call" | custom-call | tf_op jit(solution)/shard_map/mlp_backward/pallas_call | solution.py:298
  288.8 3.1 multiply_reduce_fusion.1
  292.0 1.4 fusion.63
  293.5 0.5 convert_reduce_fusion.1
  294.1 3.6 convolution_convert_fusion.do_ref
  297.8 40.1 %attention_backward.1 = bf16[3,1024,768]{2,1,0:T(8,128)(2,1)S(1)} custom-call(s32[1,1024]{1,0:T(1,128)S(1)} %copy-done.9, s32[1024,1]{1,0:T(8,128)S(1)} %copy-done.6, bf16[3,1024,768]{2,1,0:T(8,128)(2,1)S(1)} %bitcast.84, bf16[3,1024,768]{2,1,0:T(8,128)(2,1)S(1)} %bitcast.84, bf16[3,1024,768]{2,1,0:T(8,128)(2,1)S(1)} %bitcast.84, ...), custom_call_target="tpu_custom_call" | custom-call | tf_op jit(solution)/shard_map/attention_backward/pallas_call | solution.py:193
  338.0 8.3 %fusion.1 = (f32[768]{0:T(1024)S(1)}, f32[1024]{0:T(1024)S(1)}, f32[768]{0:T(1024)S(1)}, f32[1024,768,1]{1,0,2:T(8,128)S(1)}) fusion(f32[768,1024]{0,1:T(8,128)S(1)} %copy-done.16, f32[1024]{0:T(1024)S(1)} %copy-done.52, f32[1024]{0:T(1024)S(1)} %copy-done.38, f32[768]{0:T(1024)S(1)} %copy-done.36, f32[768]{0:T(1024)S(1)} %copy-done.50, ...), kind=kOutput, calls=%fused_computation.12 | convolution fusion | flops 3630953984 | bytes 14573568 | tf_op jit(solution)/shard_map/kte,kde->td/dot_general | solution.py:366
  346.3 1.8 fusion.62
  348.6 0.5 convert_reduce_fusion.2
  349.2 0.5 broadcast.290
  349.7 0.7 reduce.53
  350.5 0.6 pad.13.refs_5_
  351.8 2.9 convolution_bitcast_fusion.2.refs_0_
  354.7 5.0 convolution_bitcast_fusion.1.refs_2_
  359.7 6.2 %convolution_bitcast_fusion.refs_1_ = f32[3,768,768]{2,1,0:T(8,128)} fusion(bf16[3,1024,768]{2,1,0:T(8,128)(2,1)S(1)} %bitcast.86, f32[768,1024]{0,1:T(8,128)S(1)} %copy-done.17, f32[768]{0:T(1024)S(1)} %copy-done.57, f32[768]{0:T(1024)S(1)} %copy-done.50, f32[1024]{0:T(1024)S(1)} %copy-done.52, f32[1024]{0:T(1024)S(1)} %copy-done.38, f32[768]{0:T(1024)S(1)} %copy-done.36), kind=kOutput, calls=%fused_computation.43 | convolution fusion | flops 3628597248 | bytes 14959616 | tf_op jit(solution)/shard_map/td,kte->kde/dot_general | solution.py:363
  366.0 1.0 slice.132
  367.0 4.5 multiply_reduce_fusion.8
  371.5 0.7 maximum_bitcast_fusion
  372.3 0.6 pad.14.refs_6_
  372.9 3.7 all-gather.8.cloned.1.call-done.refs_8_
  376.7 128.4 %reduce_gradients.1 = (f32[13,96,768]{2,1,0:T(8,128)}, f32[13,96,768]{2,1,0:T(8,128)}, f32[13,96,768]{2,1,0:T(8,128)}, f32[13,96,768]{2,1,0:T(8,128)}, f32[32,12...) custom-call(f32[1,768,768]{2,1,0:T(8,128)} %convolution_bitcast_fusion.2.refs_0_, ...), custom_call_target="tpu_custom_call" | custom-call | tf_op jit(solution)/shard_map/reduce_gradients/pallas_call | solution.py:833
  505.0 1.2 slice.114
  506.2 1.3 slice_reduce_fusion.12
  507.5 1.4 fusion.65
  510.3 0.8 slice_reduce_fusion
  511.5 8.7 %multiply_subtract_fusion = (f32[13,96,768]{2,1,0:T(8,128)}, f32[13,96,768]{2,1,0:T(8,128)}) fusion(f32[13,96,768]{2,1,0:T(8,128)} %param.22, f32[13,96,768]{2,1,0:T(8,128)} %get-tuple-element.43, f32[13,768]{1,0:T(8,128)S(1)} %bitcast.91, f32[13,96,768]{2,1,0:T(8,128)} %get-tuple-element.45, f32[]{:T(128)S(6)} %div.138), kind=kLoop, calls=%fused_computation.7 | loop fusion | flops 2875392 | bytes 19209220 | tf_op jit(solution)/shard_map/sub | solution.py:1388
  520.2 0.7 multiply_subtract_fusion.2
  520.9 3.8 multiply_subtract_fusion.1
  524.7 1.6 copy-done.22
  526.4 7.6 %multiply_add_fusion = (f32[13,96,768]{2,1,0:T(8,128)}, f32[13,96,768]{2,1,0:T(8,128)}) fusion(f32[13,96,768]{2,1,0:T(8,128)} %get-tuple-element.47, f32[13,96,768]{2,1,0:T(8,128)S(1)} %copy-done.21, f32[]{:T(128)S(6)} %mul.400, f32[13,96,768]{2,1,0:T(8,128)} %get-tuple-element.46, f32[13,96,768]{2,1,0:T(8,128)S(1)} %copy-done.22), kind=kLoop, calls=%fused_computation.5 | loop fusion | flops 5750784 | bytes 23003140 | tf_op jit(solution)/shard_map/add | solution.py:1391
  (190 shorter events, 3.3 us)
Async XLA Ops:
  7.2 129.8 %copy-start = (bf16[1024,768]{1,0:T(8,128)(2,1)S(1)}, bf16[1024,768]{1,0:T(8,128)(2,1)}, u32[]{:S(2)}) copy-start(bf16[1024,768]{1,0:T(8,128)(2,1)} %param.17) | copy-start | bytes 4718596
  7.2 217.9 %all-gather.4.cloned.1.call-start = ((), (), s32[]{:S(2)}) async-start(), calls=%async_computation | async-start | bytes 9510912 | tf_op jit(solution)/shard_map/all_gather | solution.py:1292
  10.0 2.4 copy-start.45
  10.1 355.9 %all-gather.6.cloned.1.call-start = ((), (), s32[]{:S(2)}) async-start(), calls=%async_computation.1 | async-start | bytes 3612672 | tf_op jit(solution)/shard_map/all_gather | solution.py:1322
  10.1 125.8 %copy-start.9 = (s32[1,1024]{1,0:T(1,128)S(1)}, s32[1,1024]{1,0:T(1,128)}, u32[]{:S(2)}) copy-start(s32[1,1024]{1,0:T(1,128)} %qids_ref.1) | copy-start | bytes 12292
  130.3 5.4 copy-start.1
  136.1 11.9 %copy-start.4 = (s32[1024,1]{1,0:T(8,128)}, s32[1024,1]{1,0:T(8,128)S(1)}, u32[]{:S(2)}) copy-start(s32[1024,1]{1,0:T(8,128)S(1)} %copy.54.qids_ref) | copy-start | bytes 12292
  136.4 37.3 %copy-start.35 = (f32[768]{0:T(1024)}, f32[768]{0:T(1024)S(1)}, u32[]{:S(2)}) copy-start(f32[768]{0:T(1024)S(1)} %add.197) | copy-start | bytes 9220
  136.5 5.0 copy-start.56
  136.5 4.9 copy-start.49
  136.7 41.0 %copy-start.27 = (f32[768]{0:T(1024)}, f32[768]{0:T(1024)S(1)}, u32[]{:S(2)}) copy-start(f32[768]{0:T(1024)S(1)} %mul.351) | copy-start | bytes 9220
  139.7 34.0 %copy-start.15 = (f32[768,1024]{0,1:T(8,128)}, f32[768,1024]{0,1:T(8,128)S(1)}, u32[]{:S(2)}) copy-start(f32[768,1024]{0,1:T(8,128)S(1)} %get-tuple-element.95) | copy-start | bytes 9437188
  139.7 8.3 %copy-start.37 = (f32[1024]{0:T(1024)}, f32[1024]{0:T(1024)S(1)}, u32[]{:S(2)}) copy-start(f32[1024]{0:T(1024)S(1)} %broadcast_multiply_fusion.3) | copy-start | bytes 12292
  141.3 6.7 %copy-start.51 = (f32[1024]{0:T(1024)}, f32[1024]{0:T(1024)S(1)}, u32[]{:S(2)}) copy-start(f32[1024]{0:T(1024)S(1)} %fusion.50) | copy-start | bytes 12292
  148.0 25.6 %copy-start.2 = (bf16[3,1024,768]{2,1,0:T(8,128)(2,1)}, bf16[3,1024,768]{2,1,0:T(8,128)(2,1)S(1)}, u32[]{:S(2)}) copy-start(bf16[3,1024,768]{2,1,0:T(8,128)(2,1)S(1)} %fusion.q_ref.k_ref.v_ref) | copy-start | bytes 14155780
  173.7 3.5 copy-start.7
  177.2 1.7 copy-start.12
  177.7 23.3 %copy-start.41 = (f32[1024]{0:T(1024)}, f32[1024]{0:T(1024)S(1)}, u32[]{:S(2)}) copy-start(f32[1024]{0:T(1024)S(1)} %multiply_reduce_fusion.6) | copy-start | bytes 12292
  178.8 22.2 %copy-start.29 = (f32[1024]{0:T(1024)}, f32[1024]{0:T(1024)S(1)}, u32[]{:S(2)}) copy-start(f32[1024]{0:T(1024)S(1)} %fusion.51) | copy-start | bytes 12292
  211.9 5.7 %copy-start.31 = (f32[768]{0:T(1024)}, f32[768]{0:T(1024)S(1)}, u32[]{:S(2)}) copy-start(f32[768]{0:T(1024)S(1)} %mul.357) | copy-start | bytes 9220
  212.0 3.9 copy-start.10
  212.6 5.0 copy-start.47
  212.8 4.9 copy-start.58
  212.8 4.9 copy-start.25
  212.8 11.3 %copy-start.60 = (s32[32,2]{0,1:T(2,128)S(1)}, s32[32,2]{0,1:T(2,128)}, u32[]{:S(2)}) copy-start(s32[32,2]{0,1:T(2,128)} %param.20) | copy-start | bytes 772
  216.0 7.5 %copy-start.33 = (f32[1024]{0:T(1024)}, f32[1024]{0:T(1024)S(1)}, u32[]{:S(2)}) copy-start(f32[1024]{0:T(1024)S(1)} %fusion.52) | copy-start | bytes 12292
  231.7 145.0 %all-gather.8.cloned.1.call-start = ((), (), s32[]{:S(2)}) async-start(), calls=%async_computation.2 | async-start | bytes 16293888 | tf_op jit(solution)/shard_map/all_gather | solution.py:1300
  236.7 12.0 %copy-start.26 = (f32[1024]{0:T(1024)S(1)}, f32[1024]{0:T(1024)}, u32[]{:S(2)}) copy-start(f32[1024]{0:T(1024)} %copy-done.25) | copy-start | bytes 12292
  236.7 12.0 %copy-start.32 = (f32[768]{0:T(1024)S(1)}, f32[768]{0:T(1024)}, u32[]{:S(2)}) copy-start(f32[768]{0:T(1024)} %copy-done.31) | copy-start | bytes 9220
  236.7 12.0 %copy-start.34 = (f32[1024]{0:T(1024)S(1)}, f32[1024]{0:T(1024)}, u32[]{:S(2)}) copy-start(f32[1024]{0:T(1024)} %copy-done.33) | copy-start | bytes 12292
  236.7 12.0 %copy-start.48 = (pred[1024]{0:T(1024)(128)(4,1)S(1)}, pred[1024]{0:T(1024)(128)(4,1)}, u32[]{:S(2)}) copy-start(pred[1024]{0:T(1024)(128)(4,1)} %copy-done.47) | copy-start | bytes 3076
  236.7 12.0 %copy-start.59 = (f32[8]{0:T(128)S(1)}, f32[8]{0:T(128)}, u32[]{:S(2)}) copy-start(f32[8]{0:T(128)} %copy-done.58) | copy-start | bytes 100
  248.7 4.7 copy-start.44
  248.7 4.7 copy-start.11
  255.3 33.5 %copy-start.13 = (f32[1024,768]{1,0:T(8,128)S(1)}, f32[1024,768]{1,0:T(8,128)}, u32[]{:S(2)}) copy-start(f32[1024,768]{1,0:T(8,128)} %copy-done.12) | copy-start | bytes 9437188
  255.3 33.5 %copy-start.28 = (f32[768]{0:T(1024)S(1)}, f32[768]{0:T(1024)}, u32[]{:S(2)}) copy-start(f32[768]{0:T(1024)} %copy-done.27) | copy-start | bytes 9220
  255.3 33.5 %copy-start.30 = (f32[1024]{0:T(1024)S(1)}, f32[1024]{0:T(1024)}, u32[]{:S(2)}) copy-start(f32[1024]{0:T(1024)} %copy-done.29) | copy-start | bytes 12292
  288.8 3.2 copy-start.42
  288.8 3.2 copy-start.18
  292.0 5.7 %slice-start = ((s8[4718592]{0:T(1024)(128)(4,1)}), s8[4194304]{0:T(1024)(128)(4,1)S(1)}, s32[]{:S(2)}) async-start(s8[4718592]{0:T(1024)(128)(4,1)} %bitcast.83), calls=%async_computation.3 | async-start | bytes 8388608
  293.5 4.2 slice-start.1
  294.1 54.1 %copy-start.14 = (f32[1024,768]{1,0:T(8,128)}, f32[1024,768]{1,0:T(8,128)S(1)}, u32[]{:S(2)}) copy-start(f32[1024,768]{1,0:T(8,128)S(1)} %get-tuple-element.79) | copy-start | bytes 9437188
  294.1 3.7 copy-start.6
  297.8 40.2 %copy-start.16 = (f32[768,1024]{0,1:T(8,128)S(1)}, f32[768,1024]{0,1:T(8,128)}, u32[]{:S(2)}) copy-start(f32[768,1024]{0,1:T(8,128)} %copy-done.15) | copy-start | bytes 9437188
  297.8 40.2 %copy-start.36 = (f32[768]{0:T(1024)S(1)}, f32[768]{0:T(1024)}, u32[]{:S(2)}) copy-start(f32[768]{0:T(1024)} %copy-done.35) | copy-start | bytes 9220
  297.8 40.2 %copy-start.38 = (f32[1024]{0:T(1024)S(1)}, f32[1024]{0:T(1024)}, u32[]{:S(2)}) copy-start(f32[1024]{0:T(1024)} %copy-done.37) | copy-start | bytes 12292
  297.8 40.2 %copy-start.50 = (f32[768]{0:T(1024)S(1)}, f32[768]{0:T(1024)}, u32[]{:S(2)}) copy-start(f32[768]{0:T(1024)} %copy-done.49) | copy-start | bytes 9220
  297.8 40.2 %copy-start.52 = (f32[1024]{0:T(1024)S(1)}, f32[1024]{0:T(1024)}, u32[]{:S(2)}) copy-start(f32[1024]{0:T(1024)} %copy-done.51) | copy-start | bytes 12292
  338.0 10.6 %copy-start.3 = (bf16[3,1024,768]{2,1,0:T(8,128)(2,1)}, bf16[3,1024,768]{2,1,0:T(8,128)(2,1)S(1)}, u32[]{:S(2)}) copy-start(bf16[3,1024,768]{2,1,0:T(8,128)(2,1)S(1)} %attention_backward.1) | copy-start | bytes 14155780
  338.0 8.3 %copy-start.40 = (f32[1024]{0:T(1024)S(1)}, f32[1024]{0:T(1024)}, u32[]{:S(2)}) copy-start(f32[1024]{0:T(1024)} %copy-done.39) | copy-start | bytes 12292
  351.8 2.9 copy-start.8
  351.8 7.9 %slice-start.2 = ((s8[4718592]{0:T(1024)(128)(4,1)}), s8[4194304]{0:T(1024)(128)(4,1)S(1)}, s32[]{:S(2)}) async-start(s8[4718592]{0:T(1024)(128)(4,1)} %bitcast.85), calls=%async_computation.5 | async-start | bytes 8388608
  354.7 5.0 slice-start.3
  354.7 5.0 copy-start.17
  354.7 5.0 copy-start.57
  511.4 8.8 %copy-start.46 = (f32[15,96]{1,0:T(8,128)S(1)}, f32[15,96]{1,0:T(8,128)}, u32[]{:S(2)}) copy-start(f32[15,96]{1,0:T(8,128)} %param.30) | copy-start | bytes 17284
  511.4 8.8 %copy-start.54 = (f32[15,96]{1,0:T(8,128)S(1)}, f32[15,96]{1,0:T(8,128)}, u32[]{:S(2)}) copy-start(f32[15,96]{1,0:T(8,128)} %param.32) | copy-start | bytes 17284
  511.4 8.8 %copy-start.55 = (f32[15,96]{1,0:T(8,128)S(1)}, f32[15,96]{1,0:T(8,128)}, u32[]{:S(2)}) copy-start(f32[15,96]{1,0:T(8,128)} %param.31) | copy-start | bytes 17284
  511.4 9.5 %copy-start.19 = (f32[96,5462]{1,0:T(8,128)S(1)}, f32[96,5462]{1,0:T(8,128)}, u32[]{:S(2)}) copy-start(f32[96,5462]{1,0:T(8,128)} %param.27) | copy-start | bytes 6292228
  511.4 9.5 %copy-start.20 = (f32[96,5462]{1,0:T(8,128)S(1)}, f32[96,5462]{1,0:T(8,128)}, u32[]{:S(2)}) copy-start(f32[96,5462]{1,0:T(8,128)} %get-tuple-element.101) | copy-start | bytes 6292228
  511.4 9.5 %copy-start.23 = (f32[96,5462]{1,0:T(8,128)S(1)}, f32[96,5462]{1,0:T(8,128)}, u32[]{:S(2)}) copy-start(f32[96,5462]{1,0:T(8,128)} %param.29) | copy-start | bytes 6292228
  511.5 9.4 %copy-start.24 = (f32[96,5462]{1,0:T(8,128)S(1)}, f32[96,5462]{1,0:T(8,128)}, u32[]{:S(2)}) copy-start(f32[96,5462]{1,0:T(8,128)} %param.28) | copy-start | bytes 6292228
  520.9 3.8 copy-start.21
  520.9 5.5 %copy-start.22 = (f32[13,96,768]{2,1,0:T(8,128)S(1)}, f32[13,96,768]{2,1,0:T(8,128)}, u32[]{:S(2)}) copy-start(f32[13,96,768]{2,1,0:T(8,128)} %param.23) | copy-start | bytes 11501572
  (4 other events, 4.9 us)
Sparse Core Ops, SparseCore 0:
  10.8 162.2 all-gather.3
  231.8 61.7 all-gather.5
  295.7 80.8 all-gather.7

commit v6 on v5

--- a/solution.py
+++ b/solution.py
@@ -21,6 +21,7 @@
 PIECE = 48
 SPAN = 48
 SHARES = 8
+GATHER_DEPTH = 7
 IMG_PACK = 8
 
 
@@ -58,9 +59,8 @@
     return low, high
 
 
-def attention_forward_kernel(qids_ref, kcodes_ref, q_ref, k_ref, v_ref, out_ref, bias_ref):
-    length = q_ref.shape[0]
-    lane = lax.broadcasted_iota(jnp.int32, (QTILE, PAIR), 1)
+def attention_bias(qids_ref, kcodes_ref, bias_ref):
+    length = qids_ref.shape[0]
 
     @pl.when(pl.program_id(0) == 0)
     def _():
@@ -72,27 +72,35 @@
             same = qids_ref[tile * QTILE : (tile + 1) * QTILE, :] == kcodes_ref[:, low:high]
             bias_ref[tile, :, : high - low] = jnp.where(same | (rows == cols), 0.0, -1e30)
 
-    for tile in range(length // QTILE):
-        low, high = key_window(tile, length)
-        rows = pl.ds(tile * QTILE, QTILE)
-        queries = q_ref[rows, :] * jnp.bfloat16(HEAD ** (-0.5))
-        keys = k_ref[low:high, :]
-        values = v_ref[low:high, :]
-        halves = []
-        for head in range(2):
-            mine = (lane >= head * HEAD) & (lane < (head + 1) * HEAD)
-            picked = jnp.where(mine, queries, jnp.zeros_like(queries))
-            scores = lax.dot_general(
-                picked, keys, (((1,), (1,)), ((), ())), preferred_element_type=jnp.float32
-            )
-            scores = scores + bias_ref[tile, :, : high - low]
-            top = jnp.max(scores, -1, keepdims=True)
-            weights = jnp.exp(scores - top)
-            probs = weights * (1.0 / jnp.sum(weights, -1, keepdims=True))
-            halves.append(
-                jnp.dot(probs.astype(jnp.bfloat16), values, preferred_element_type=jnp.float32)
-            )
-        out_ref[rows, :] = jnp.where(lane < HEAD, halves[0], halves[1]).astype(jnp.bfloat16)
+
+def attention_tile(tile, q_ref, k_ref, v_ref, out_ref, bias_ref):
+    lane = lax.broadcasted_iota(jnp.int32, (QTILE, PAIR), 1)
+    low, high = key_window(tile, q_ref.shape[0])
+    rows = pl.ds(tile * QTILE, QTILE)
+    queries = q_ref[rows, :] * jnp.bfloat16(HEAD ** (-0.5))
+    keys = k_ref[low:high, :]
+    values = v_ref[low:high, :]
+    halves = []
+    for head in range(2):
+        mine = (lane >= head * HEAD) & (lane < (head + 1) * HEAD)
+        picked = jnp.where(mine, queries, jnp.zeros_like(queries))
+        scores = lax.dot_general(
+            picked, keys, (((1,), (1,)), ((), ())), preferred_element_type=jnp.float32
+        )
+        scores = scores + bias_ref[tile, :, : high - low]
+        top = jnp.max(scores, -1, keepdims=True)
+        weights = jnp.exp(scores - top)
+        probs = weights * (1.0 / jnp.sum(weights, -1, keepdims=True))
+        halves.append(
+            jnp.dot(probs.astype(jnp.bfloat16), values, preferred_element_type=jnp.float32)
+        )
+    out_ref[rows, :] = jnp.where(lane < HEAD, halves[0], halves[1]).astype(jnp.bfloat16)
+
+
+def attention_forward_kernel(qids_ref, kcodes_ref, q_ref, k_ref, v_ref, out_ref, bias_ref):
+    attention_bias(qids_ref, kcodes_ref, bias_ref)
+    for tile in range(q_ref.shape[0] // QTILE):
+        attention_tile(tile, q_ref, k_ref, v_ref, out_ref, bias_ref)
 
 
 def attention_backward_kernel(
@@ -169,10 +177,14 @@
     return pl.BlockSpec(shape, lambda pair: (0,) * len(shape))
 
 
+def bias_shape(length):
+    tiles = length // QTILE
+    window = max(high - low for low, high in (key_window(t, length) for t in range(tiles)))
+    return tiles, QTILE, window
+
+
 def attention_forward(qkv_rows, pack_ids, key_codes):
     _, length, width = qkv_rows.shape
-    tiles = length // QTILE
-    window = max(high - low for low, high in (key_window(t, length) for t in range(tiles)))
     return pl.pallas_call(
         attention_forward_kernel,
         grid=(width // PAIR,),
@@ -180,7 +192,7 @@
         in_specs=[whole_spec((length, 1)), whole_spec((1, length))]
         + [pair_spec(length, part) for part in range(3)],
         out_specs=pair_spec(length),
-        scratch_shapes=[pltpu.VMEM((tiles, QTILE, window), jnp.float32)],
+        scratch_shapes=[pltpu.VMEM(bias_shape(length), jnp.float32)],
         compiler_params=pltpu.CompilerParams(vmem_limit_bytes=40 << 20),
         name="attention_forward",
     )(pack_ids[:, None], key_codes[None, :], qkv_rows, qkv_rows, qkv_rows)
@@ -261,9 +273,9 @@
 def mlp_specs(length, width, up_count):
     split = width // HIDDEN_TILE
     resident = pl.BlockSpec((length, width), lambda t: (0, 0))
-    up = pl.BlockSpec((None, width, HIDDEN_TILE), lambda t: (5 + t // split, 0, t % split))
+    up = pl.BlockSpec((None, width, HIDDEN_TILE), lambda t: (t // split, 0, t % split))
     down = pl.BlockSpec(
-        (None, HIDDEN_TILE, width), lambda t: (5 + up_count + t // split, t % split, 0)
+        (None, HIDDEN_TILE, width), lambda t: (up_count + t // split, t % split, 0)
     )
     hidden = pl.BlockSpec((length, HIDDEN_TILE), lambda t: (0, t))
     bias = pl.BlockSpec((1, HIDDEN_TILE), lambda t: (0, t))
@@ -272,7 +284,7 @@
 
 def mlp_forward(rows, blocks, up_bias):
     length, width = rows.shape
-    up_count = (blocks.shape[0] - 5) // 2
+    up_count = blocks.shape[0] // 2
     split, resident, up, down, hidden, bias = mlp_specs(length, width, up_count)
     hidden_size = up_count * width
     return pl.pallas_call(
@@ -292,7 +304,7 @@
 
 def mlp_backward(rows, grad_branch, blocks, units, slopes):
     length, width = rows.shape
-    up_count = (blocks.shape[0] - 5) // 2
+    up_count = blocks.shape[0] // 2
     split, resident, up, down, hidden, bias = mlp_specs(length, width, up_count)
     hidden_size = up_count * width
     return pl.pallas_call(
@@ -317,8 +329,7 @@
     )(rows, grad_branch, blocks, blocks, units, slopes)
 
 
-def layer_forward(blocks, vec_all, patch, pack_ids, key_codes):
-    up_count = (blocks.shape[0] - 5) // 2
+def layer_forward(blocks, vec_all, patch, attend):
     embedded = jnp.dot(patch, blocks[0], preferred_element_type=jnp.float32) + vec_all[0]
     normed_one = norm_rows(embedded, vec_all[1], vec_all[2]).astype(jnp.bfloat16)
     qkv_rows = jnp.einsum(
@@ -326,28 +337,39 @@
     )
     qkv_bias = jnp.stack([vec_all[3], jnp.zeros_like(vec_all[3]), vec_all[4]])
     qkv_rows = (qkv_rows + qkv_bias[:, None, :]).astype(jnp.bfloat16)
-    attended = attention_forward(qkv_rows, pack_ids, key_codes)
+    attended, mlp_blocks = attend(qkv_rows)
+    up_count = mlp_blocks.shape[0] // 2
     hidden = (
         embedded + jnp.dot(attended, blocks[4], preferred_element_type=jnp.float32) + vec_all[5]
     )
     normed_two = norm_rows(hidden, vec_all[6], vec_all[7]).astype(jnp.bfloat16)
-    units, slopes, branch = mlp_forward(normed_two, blocks, vec_all[8 : 8 + up_count])
+    units, slopes, branch = mlp_forward(normed_two, mlp_blocks, vec_all[8 : 8 + up_count])
     output = hidden + branch + vec_all[8 + up_count]
     return (
         output,
+        mlp_blocks,
         (embedded, normed_one, qkv_rows, attended, hidden, normed_two, slopes, units),
     )
 
 
 def layer_backward(
-    blocks, vec_all, patch, saved, pack_ids, key_codes, grad_output, grad_gain, grad_shift
+    blocks,
+    mlp_blocks,
+    vec_all,
+    patch,
+    saved,
+    pack_ids,
+    key_codes,
+    grad_output,
+    grad_gain,
+    grad_shift,
 ):
     embedded, normed_one, qkv_rows, attended, hidden, normed_two, slopes, units = saved
     feature_dim = patch.shape[1]
-    up_count = (blocks.shape[0] - 5) // 2
+    up_count = mlp_blocks.shape[0] // 2
     grad_branch = grad_output.astype(jnp.bfloat16)
     grad_up, grad_down, up_sums, grad_normed_two = mlp_backward(
-        normed_two, grad_branch, blocks, units, slopes
+        normed_two, grad_branch, mlp_blocks, units, slopes
     )
     norm_two_back = jax.vjp(norm_rows, hidden, vec_all[6], vec_all[7])[1]
     grad_hidden_norm, grad_gain_two, grad_shift_two = norm_two_back(grad_normed_two)
@@ -993,11 +1015,10 @@
     )(values)
 
 
-def gather_kernel(own_ref, vec_ref, out_ref, vec_out_ref, send_sem, recv_sem, copy_sem, vec_send, vec_recv):
+def gather_steps(own_ref, out_ref, send_sem, recv_sem, copy_sem):
     count, rows, width = own_ref.shape
     cols = width // 2
     z, y, x, core = torus_place()
-    me = z * 2 + y
     mate_core = torus_device(z, y, x, 1 - core)
     mate_x = torus_device(z, y, 1 - x, core)
     mate_y = torus_device(z, 1 - y, x, core)
@@ -1005,29 +1026,8 @@
     mate_down = torus_device(jnp.maximum(z - 1, 0), y, x, core)
     has_up = z < 3
     has_down = z > 0
-
-    def column_mate(n):
-        other = lax.rem(me + n, SHARES)
-        return torus_device(other // 2, lax.rem(other, 2), x, core)
-
-    barrier = pltpu.get_barrier_semaphore()
-    for mate in [mate_core, mate_x] + [column_mate(n) for n in range(1, SHARES)]:
-        pl.semaphore_signal(barrier, inc=1, device_id=mate, device_id_type=MESH)
-    pl.semaphore_wait(barrier, SHARES + 1)
-
     own_cols = pl.ds(pl.multiple_of(core * cols, 128), cols)
     other_cols = pl.ds(pl.multiple_of((1 - core) * cols, 128), cols)
-
-    def vec_copy(n, slot):
-        return pltpu.make_async_remote_copy(
-            src_ref=vec_ref, dst_ref=vec_out_ref.at[slot],
-            send_sem=vec_send.at[n], recv_sem=vec_recv.at[slot],
-            device_id=column_mate(n), device_id_type=MESH,
-        )
-
-    for n in range(1, SHARES):
-        vec_copy(n, me).start()
-    vec_out_ref[me] = vec_ref[...]
 
     def share(m, zz, yy, start, size, columns=own_cols):
         begin = (zz * 2 + yy) * rows + start
@@ -1092,7 +1092,7 @@
         block = out_ref.at[m, :, columns]
         return copy(13, m, block, block, mate_core)
 
-    def step(t, carry):
+    def step(t):
         @pl.when(t < count)
         def _():
             local(t).start()
@@ -1167,12 +1167,107 @@
             swap(m, own_cols).wait_send()
             swap(m, other_cols).wait_recv()
 
+    return step, count + GATHER_DEPTH
+
+
+def column_mate(n):
+    z, y, x, core = torus_place()
+    other = lax.rem(z * 2 + y + n, SHARES)
+    return torus_device(other // 2, lax.rem(other, 2), x, core)
+
+
+def gather_barrier():
+    z, y, x, core = torus_place()
+    barrier = pltpu.get_barrier_semaphore()
+    mates = [torus_device(z, y, x, 1 - core), torus_device(z, y, 1 - x, core)]
+    for mate in mates + [column_mate(n) for n in range(1, SHARES)]:
+        pl.semaphore_signal(barrier, inc=1, device_id=mate, device_id_type=MESH)
+    pl.semaphore_wait(barrier, SHARES + 1)
+
+
+def gather_kernel(
+    own_ref, vec_ref, out_ref, vec_out_ref, send_sem, recv_sem, copy_sem, vec_send, vec_recv
+):
+    z, y, _, _ = torus_place()
+    me = z * 2 + y
+    gather_barrier()
+
+    def vec_copy(n, slot):
+        return pltpu.make_async_remote_copy(
+            src_ref=vec_ref, dst_ref=vec_out_ref.at[slot],
+            send_sem=vec_send.at[n], recv_sem=vec_recv.at[slot],
+            device_id=column_mate(n), device_id_type=MESH,
+        )
+
+    for n in range(1, SHARES):
+        vec_copy(n, me).start()
+    vec_out_ref[me] = vec_ref[...]
+    gather_step, turns = gather_steps(own_ref, out_ref, send_sem, recv_sem, copy_sem)
+
+    def step(t, carry):
+        gather_step(t)
         return carry
 
-    lax.fori_loop(0, count + 7, step, 0)
+    lax.fori_loop(0, turns, step, 0)
     for n in range(1, SHARES):
         vec_copy(n, me).wait_send()
         vec_copy(n, lax.rem(me + n, SHARES)).wait_recv()
+
+
+def gather_semaphores(count):
+    return [
+        pltpu.SemaphoreType.DMA((14, 2)),
+        pltpu.SemaphoreType.DMA((14, count)),
+        pltpu.SemaphoreType.DMA((2,)),
+    ]
+
+
+def attention_gather_kernel(
+    qids_ref, kcodes_ref, q_ref, k_ref, v_ref, own_ref, out_ref, blocks_ref,
+    bias_ref, send_sem, recv_sem, copy_sem
+):
+    pair, tiles = pl.program_id(0), q_ref.shape[0] // QTILE
+    slots = pl.num_programs(0) * tiles
+
+    @pl.when(pair == 0)
+    def _():
+        gather_barrier()
+
+    gather_step, turns = gather_steps(own_ref, blocks_ref, send_sem, recv_sem, copy_sem)
+    attention_bias(qids_ref, kcodes_ref, bias_ref)
+    for tile in range(tiles):
+        slot = pair * tiles + tile
+        begin, end = slot * turns // slots, (slot + 1) * turns // slots
+
+        @pl.when(begin < end)
+        def _(begin=begin):
+            gather_step(begin)
+
+        attention_tile(tile, q_ref, k_ref, v_ref, out_ref, bias_ref)
+
+
+def attention_forward_gathering(qkv_rows, pack_ids, key_codes, own):
+    _, length, width = qkv_rows.shape
+    count, rows, _ = own.shape
+    tiles = length // QTILE
+    assert count + GATHER_DEPTH <= tiles * (width // PAIR)
+    return pl.pallas_call(
+        attention_gather_kernel,
+        grid=(width // PAIR,),
+        out_shape=(
+            jax.ShapeDtypeStruct((length, width), jnp.bfloat16),
+            jax.ShapeDtypeStruct((count, SHARES * rows, width), own.dtype),
+        ),
+        in_specs=[whole_spec((length, 1)), whole_spec((1, length))]
+        + [pair_spec(length, part) for part in range(3)]
+        + [whole_spec(own.shape)],
+        out_specs=(pair_spec(length), pl.BlockSpec(memory_space=pl.ANY)),
+        scratch_shapes=[pltpu.VMEM(bias_shape(length), jnp.float32)] + gather_semaphores(count),
+        compiler_params=pltpu.CompilerParams(
+            collective_id=4, has_side_effects=True, vmem_limit_bytes=40 << 20
+        ),
+        name="attention_forward",
+    )(pack_ids[:, None], key_codes[None, :], qkv_rows, qkv_rows, qkv_rows, own)
 
 
 def gather_weights(own, vec):
@@ -1187,13 +1282,8 @@
         ),
         in_specs=[vmem, vmem],
         out_specs=(hbm, vmem),
-        scratch_shapes=[
-            pltpu.SemaphoreType.DMA((14, 2)),
-            pltpu.SemaphoreType.DMA((14, count)),
-            pltpu.SemaphoreType.DMA((2,)),
-            pltpu.SemaphoreType.DMA((SHARES,)),
-            pltpu.SemaphoreType.DMA((SHARES,)),
-        ],
+        scratch_shapes=gather_semaphores(count)
+        + [pltpu.SemaphoreType.DMA((SHARES,)), pltpu.SemaphoreType.DMA((SHARES,))],
         compiler_params=pltpu.CompilerParams(
             collective_id=3, has_side_effects=True, vmem_limit_bytes=32 << 20
         ),
@@ -1280,13 +1370,17 @@
     on_torus = dp_count == 8 and cls_count == 4
     if on_torus:
         vec_block = jnp.pad(vectors, ((0, -vectors.shape[0] % 8), (0, -row_count % 128)))
-        blocks, vec_blocks = gather_weights(enc_weights.astype(jnp.bfloat16), vec_block)
+        own_low = enc_weights.astype(jnp.bfloat16)
+        blocks, vec_blocks = gather_weights(own_low[:5], vec_block)
+        right_part, vec_blocks = lax.optimization_barrier((my_part(root_right), vec_blocks))
         vec_low = jnp.transpose(vec_blocks[:, : vectors.shape[0], :row_count], (1, 0, 2))
         vec_all = lax.reduce_precision(vec_low.reshape(vectors.shape[0], feature_dim), 8, 7)
     else:
-        blocks = lax.all_gather(
+        right_part = my_part(root_right)
+        all_blocks = lax.all_gather(
             my_part(enc_weights.astype(jnp.bfloat16)), ("dp", "cls"), axis=1, tiled=True
         )
+        blocks = all_blocks[:5]
         vec_low = lax.all_gather(vectors.astype(jnp.bfloat16), "dp", axis=1, tiled=True)
         vec_all = vec_low.astype(jnp.float32)
     head_low = lax.all_gather(head_weights.astype(jnp.bfloat16), "dp", axis=0, tiled=True)
@@ -1295,8 +1389,12 @@
     pack_ids, pack_keep = image_ids[0], keep[0]
     key_codes = jnp.where(pack_keep == 1, pack_ids, -1)
 
-    output, saved = layer_forward(blocks, vec_all, patches, pack_ids, key_codes)
-    right_part, output = lax.optimization_barrier((my_part(root_right), output))
+    def attend(qkv_rows):
+        if on_torus:
+            return attention_forward_gathering(qkv_rows, pack_ids, key_codes, own_low[5:])
+        return attention_forward(qkv_rows, pack_ids, key_codes), all_blocks[5:]
+
+    output, mlp_blocks, saved = layer_forward(blocks, vec_all, patches, attend)
     right_half = lax.all_gather(
         right_part, ("dp", "cls"), axis=1, tiled=True, axis_index_groups=half_groups
     )
@@ -1335,6 +1433,7 @@
     grad_output, grad_gain, grad_shift = pool_back(grad_pooled)
     grad_arrays, grad_vectors = layer_backward(
         blocks,
+        mlp_blocks,
         vec_all,
         patches,
         saved,

time: 551 us -> 539 us (0.978)
  matrix products: 62 us -> 52 us
  other arithmetic: 57 us -> 49.1 us
    pallas_call x1, Pallas kernels: 25.6 us -> 88.7 us  [attention_forward_gathering(): pl.pallas_call(attention_gather_kernel, grid=(width // PAIR,), out_shape=...]
    pallas_call x1, Pallas kernels: 118 us -> 58.2 us  [gather_weights(): pl.pallas_call(gather_kernel, out_shape=(jax.ShapeDtypeStruct((count, SHA...]
    unnamed x132 -> x146, local copies, waits for them, and re-layouts: 11.7 us -> 11.5 us
  transfers between devices with their start and end apart: 3 -> 3, of which waited for: 1 -> 1; matrix products, arithmetic and copies ran while one was open for 17% -> 14% of each run, Pallas kernels for 45% -> 47%
where the time goes in v6:
time: 539 us; the launch traced here: 531 us
  Pallas kernels  376 us (70%)
  matrix products  52 us (10%)
  other arithmetic  49.1 us (9%)
  local copies, waits for them, and re-layouts  21.1 us (4%)
  between operations  19.3 us (4%)
  waiting for transfers between devices  8.15 us (2%)
    pallas_call x1, Pallas kernels, reduce_gradients(): pl.pallas_call(functools.partial(reduce_kernel, counts), out_shape=(jax.S...  128 us
    pallas_call x1, Pallas kernels, attention_forward_gathering(): pl.pallas_call(attention_gather_kernel, grid=(width // PAIR,), out_shape=...  88.7 us
    pallas_call x1, Pallas kernels, gather_weights(): pl.pallas_call(gather_kernel, out_shape=(jax.ShapeDtypeStruct((count, SHA...  58.2 us
    pallas_call x1, Pallas kernels, attention_backward(): pl.pallas_call(attention_backward_kernel, grid=(width // PAIR,), out_shap...  40.1 us
    pallas_call x1, Pallas kernels, mlp_backward(): pl.pallas_call(mlp_backward_kernel, grid=(up_count * split,), out_shape=(...  33.4 us
    pallas_call x1, Pallas kernels, mlp_forward(): pl.pallas_call(mlp_forward_kernel, grid=(up_count * split,), out_shape=(j...  21.4 us
    unnamed x146, local copies, waits for them, and re-layouts  11.5 us
  transfers between devices with their start and end apart: 3, of which 1 were waited for; matrix products, arithmetic and copies ran while one was open for 14% of the time, Pallas kernels for 47%

profile of v6, /device:TPU:0, one launch (start us, length us, event | category | flops | bytes accessed | tf_op | source)
XLA Modules:
  0.0 530.7 jit_solution(13400879860594565250)
XLA Ops:
  7.2 2.8 convert_element_type.75
  10.1 2.3 convert_element_type.68
  12.6 0.5 copy-done.48
  13.1 58.2 %gather_weights.1 = (bf16[5,768,768]{2,1,0:T(8,128)(2,1)S(1)}, f32[8,16,128]{2,1,0:T(8,128)S(1)}) custom-call(bf16[5,96,768]{2,1,0:T(8,128)(2,1)S(1)} %slice.126.own_ref, f32[16,128]{1,0:T(8,128)S(1)} %pad.12.vec_ref), custom_call_target="tpu_custom_call" | custom-call | tf_op jit(solution)/shard_map/gather_weights/pallas_call | solution.py:1277
  71.3 0.6 copy-done.6
  72.0 2.8 copy-done.7
  74.8 2.2 constant_dynamic-slice_fusion
  77.0 0.8 reduce-precision_bitcast_fusion
  79.2 2.9 add_reduce_fusion
  82.2 0.6 multiply_reduce_fusion.7
  83.0 4.6 fusion.q_ref.k_ref.v_ref
  87.6 88.7 %attention_forward.1 = (bf16[1024,768]{1,0:T(8,128)(2,1)S(1)}, bf16[8,768,768]{2,1,0:T(8,128)(2,1)}) custom-call(s32[1024,1]{1,0:T(8,128)S(1)} %copy.54.qids_ref, s32[1,1024]{1,0:T(1,128)S(1)} %broadcast_select_fusion.1.kcodes_ref, bf16[3,1024,768]{2,1,0:T(8,128)(2,1)S(1)} %fusion.q_ref.k_ref.v_ref, bf16[3,1024,768]{2,1,0:T(8,128)(2,1)S(1)} %fusion.q_ref.k_ref.v_ref, ...), custom_call_target="tpu_custom_call" | custom-call | tf_op jit(solution)/shard_map/attention_forward/pallas_call | solution.py:1254
  176.4 1.6 fusion.67
  178.1 0.5 multiply_reduce_fusion.6
  178.6 0.6 add_convert_fusion.2.x_ref
  179.2 21.4 %mlp_forward.1 = (bf16[1024,3072]{1,0:T(8,128)(2,1)}, f32[1024,3072]{1,0:T(8,128)}, f32[1024,768]{1,0:T(8,128)S(1)}) custom-call(bf16[1024,768]{1,0:T(8,128)(2,1)S(1)} %add_convert_fusion.2.x_ref, bf16[8,768,768]{2,1,0:T(8,128)(2,1)} %get-tuple-element.36.up_ref.down_ref, f32[1,3072]{1,0:T(1,128)S(1)} %reshape.204.bias_ref, ...), custom_call_target="tpu_custom_call" | custom-call | tf_op jit(solution)/shard_map/mlp_forward/pallas_call | solution.py:290
  200.6 0.6 fusion.53
  201.9 0.5 multiply_reduce_fusion.5
  202.4 0.9 copy-done.46
  203.3 1.7 fusion.30
  205.0 5.2 all_gather.12
  210.3 0.6 broadcast_compare_fusion
  210.9 0.9 compare_reduce_fusion
  211.8 5.8 %fusion.37 = (f32[]{:T(128)}, bf16[32,5462]{1,0:T(8,128)(2,1)S(1)}) fusion(pred[32,5462]{1,0:T(8,128)(4,1)} %compare_reduce_fusion, pred[5462]{0:T(1024)(128)(4,1)} %broadcast_compare_fusion, bf16[32,768]{1,0:T(8,128)(2,1)S(1)} %all_gather.12, bf16[768,5462]{1,0:T(8,128)(2,1)} %all-gather.4.cloned.1.call-done), kind=kOutput, calls=%fused_computation.74 | convolution fusion | flops 271614336 | bytes 8968602 | tf_op jit(solution)/shard_map/dot_general | solution.py:1403
  217.6 0.8 pad_maximum_fusion
  218.5 0.7 all-gather.8.cloned.1.call-update
  219.2 1.6 copy.57
  221.5 2.0 broadcast_select_fusion.kcodes_ref
  223.5 6.5 %fusion.68.in_ref = f32[32,768]{1,0:T(8,128)} fusion(bf16[32,5462]{1,0:T(8,128)(2,1)S(1)} %get-tuple-element.95, bf16[768,5462]{1,0:T(8,128)(2,1)} %all-gather.4.cloned.1.call-done), kind=kOutput, calls=%fused_computation.144 | convolution fusion | flops 268468224 | bytes 8837504 | tf_op jit(solution)/shard_map/gc,dc->gd/dot_general | solution.py:1415
  229.9 5.4 %class_sum.1 = f32[8,768]{1,0:T(8,128)} custom-call(f32[32,768]{1,0:T(8,128)} %fusion.68.in_ref), custom_call_target="tpu_custom_call" | custom-call | tf_op jit(solution)/shard_map/class_sum/pallas_call | solution.py:1003
  235.4 4.7 multiply_reduce_fusion
  240.1 1.5 fusion.64
  242.0 1.3 copy-done.14
  243.3 33.4 %mlp_backward.1 = (f32[4,768,768]{2,1,0:T(8,128)}, f32[4,768,768]{2,1,0:T(8,128)}, f32[1,3072]{1,0:T(1,128)S(1)}, f32[1024,768]{1,0:T(8,128)}) custom-call(bf16[1024,768]{1,0:T(8,128)(2,1)S(1)} %add_convert_fusion.2.x_ref, bf16[1024,768]{1,0:T(8,128)(2,1)S(1)} %get-tuple-element.81.dm_ref, bf16[8,768,768]{2,1,0:T(8,128)(2,1)} %get-tuple-element.36.up_ref.down_ref, ...), custom_call_target="tpu_custom_call" | custom-call | tf_op jit(solution)/shard_map/mlp_backward/pallas_call | solution.py:310
  276.7 3.1 multiply_reduce_fusion.1
  279.9 1.4 fusion.63
  281.4 0.6 convert_reduce_fusion.1
  281.9 1.7 copy-done.16
  283.6 1.5 slice-done.7
  285.1 1.4 convolution_convert_fusion.do_ref
  286.6 40.1 %attention_backward.1 = bf16[3,1024,768]{2,1,0:T(8,128)(2,1)S(1)} custom-call(s32[1,1024]{1,0:T(1,128)S(1)} %copy-done.5, s32[1024,1]{1,0:T(8,128)S(1)} %copy-done.4, bf16[3,1024,768]{2,1,0:T(8,128)(2,1)S(1)} %bitcast.84, bf16[3,1024,768]{2,1,0:T(8,128)(2,1)S(1)} %bitcast.84, bf16[3,1024,768]{2,1,0:T(8,128)(2,1)S(1)} %bitcast.84, ...), custom_call_target="tpu_custom_call" | custom-call | tf_op jit(solution)/shard_map/attention_backward/pallas_call | solution.py:205
  326.8 4.5 fusion.1
  331.3 1.7 fusion.62
  334.2 0.5 broadcast.290
  334.7 0.7 reduce.53
  335.6 0.6 pad.13.refs_5_
  336.9 2.9 convolution_bitcast_fusion.2.refs_0_
  339.8 4.9 convolution_bitcast_fusion.1.refs_2_
  344.7 6.2 %convolution_bitcast_fusion.refs_1_ = f32[3,768,768]{2,1,0:T(8,128)} fusion(bf16[3,1024,768]{2,1,0:T(8,128)(2,1)S(1)} %bitcast.86, f32[768,1024]{0,1:T(8,128)S(1)} %copy-done.20, f32[768]{0:T(1024)S(1)} %copy-done.60, f32[768]{0:T(1024)S(1)} %copy-done.53, f32[1024]{0:T(1024)S(1)} %copy-done.55, f32[1024]{0:T(1024)S(1)} %copy-done.41, f32[768]{0:T(1024)S(1)} %copy-done.39), kind=kOutput, calls=%fused_computation.43 | convolution fusion | flops 3628597248 | bytes 14959616 | tf_op jit(solution)/shard_map/td,kte->kde/dot_general | solution.py:385
  350.8 1.0 slice.142
  351.9 4.5 multiply_reduce_fusion.8
  356.3 0.7 maximum_bitcast_fusion
  357.1 0.6 pad.14.refs_6_
  357.7 7.4 %all-gather.8.cloned.1.call-done.refs_8_ = f32[13,384,768]{2,1,0:T(8,128)} async-done(((f32[13,24,768]{2,1,0:T(8,128)}), f32[13,384,768]{2,1,0:T(8,128)}) %all-gather.8.cloned.1.call-update) | async-done | bytes 15335440 | tf_op jit(solution)/shard_map/all_gather | solution.py:1398
  365.2 128.4 %reduce_gradients.1 = (f32[13,96,768]{2,1,0:T(8,128)}, f32[13,96,768]{2,1,0:T(8,128)}, f32[13,96,768]{2,1,0:T(8,128)}, f32[13,96,768]{2,1,0:T(8,128)}, f32[32,12...) custom-call(f32[1,768,768]{2,1,0:T(8,128)} %convolution_bitcast_fusion.2.refs_0_, ...), custom_call_target="tpu_custom_call" | custom-call | tf_op jit(solution)/shard_map/reduce_gradients/pallas_call | solution.py:855
  493.6 1.2 slice.122
  494.8 1.3 slice_reduce_fusion.12
  496.1 1.4 fusion.66
  498.8 0.8 slice_reduce_fusion
  500.0 8.7 %multiply_subtract_fusion = (f32[13,96,768]{2,1,0:T(8,128)}, f32[13,96,768]{2,1,0:T(8,128)}) fusion(f32[13,96,768]{2,1,0:T(8,128)} %param.22, f32[13,96,768]{2,1,0:T(8,128)} %get-tuple-element.47, f32[13,768]{1,0:T(8,128)S(1)} %bitcast.95, f32[13,96,768]{2,1,0:T(8,128)} %get-tuple-element.49, f32[]{:T(128)S(6)} %div.138), kind=kLoop, calls=%fused_computation.7 | loop fusion | flops 2875392 | bytes 19209220 | tf_op jit(solution)/shard_map/sub | solution.py:1487
  508.8 0.7 multiply_subtract_fusion.2
  509.5 3.8 multiply_subtract_fusion.1
  513.3 1.6 copy-done.25
  515.0 7.6 %multiply_add_fusion = (f32[13,96,768]{2,1,0:T(8,128)}, f32[13,96,768]{2,1,0:T(8,128)}) fusion(f32[13,96,768]{2,1,0:T(8,128)} %get-tuple-element.51, f32[13,96,768]{2,1,0:T(8,128)S(1)} %copy-done.24, f32[]{:T(128)S(6)} %mul.400, f32[13,96,768]{2,1,0:T(8,128)} %get-tuple-element.50, f32[13,96,768]{2,1,0:T(8,128)S(1)} %copy-done.25), kind=kLoop, calls=%fused_computation.5 | loop fusion | flops 5750784 | bytes 23003140 | tf_op jit(solution)/shard_map/add | solution.py:1490
  (207 shorter events, 4.6 us)
Async XLA Ops:
  7.2 72.0 %copy-start = (bf16[1024,768]{1,0:T(8,128)(2,1)S(1)}, bf16[1024,768]{1,0:T(8,128)(2,1)}, u32[]{:S(2)}) copy-start(bf16[1024,768]{1,0:T(8,128)(2,1)} %param.17) | copy-start | bytes 4718596
  7.2 204.6 %all-gather.4.cloned.1.call-start = ((), (), s32[]{:S(2)}) async-start(), calls=%async_computation | async-start | bytes 9510912 | tf_op jit(solution)/shard_map/all_gather | solution.py:1386
  10.1 340.8 %all-gather.6.cloned.1.call-start = ((), (), s32[]{:S(2)}) async-start(), calls=%async_computation.1 | async-start | bytes 3612672 | tf_op jit(solution)/shard_map/all_gather | solution.py:1420
  12.4 65.6 %copy-start.5 = (s32[1,1024]{1,0:T(1,128)S(1)}, s32[1,1024]{1,0:T(1,128)}, u32[]{:S(2)}) copy-start(s32[1,1024]{1,0:T(1,128)} %qids_ref.1) | copy-start | bytes 12292
  72.0 2.8 copy-start.7
  78.3 9.3 %copy-start.3 = (s32[1024,1]{1,0:T(8,128)}, s32[1024,1]{1,0:T(8,128)S(1)}, u32[]{:S(2)}) copy-start(s32[1024,1]{1,0:T(8,128)S(1)} %copy.54.qids_ref) | copy-start | bytes 12292
  78.5 97.9 %copy-start.38 = (f32[768]{0:T(1024)}, f32[768]{0:T(1024)S(1)}, u32[]{:S(2)}) copy-start(f32[768]{0:T(1024)S(1)} %add.197) | copy-start | bytes 9220
  78.6 4.4 copy-start.59
  78.7 4.3 copy-start.52
  78.8 99.8 %copy-start.30 = (f32[768]{0:T(1024)}, f32[768]{0:T(1024)S(1)}, u32[]{:S(2)}) copy-start(f32[768]{0:T(1024)S(1)} %mul.351) | copy-start | bytes 9220
  79.1 124.3 %copy-start.32 = (f32[768]{0:T(1024)}, f32[768]{0:T(1024)S(1)}, u32[]{:S(2)}) copy-start(f32[768]{0:T(1024)S(1)} %mul.357) | copy-start | bytes 9220
  79.2 3.7 slice-start.4
  79.2 3.7 slice-start.5
  82.1 94.3 %copy-start.18 = (f32[768,1024]{0,1:T(8,128)}, f32[768,1024]{0,1:T(8,128)S(1)}, u32[]{:S(2)}) copy-start(f32[768,1024]{0,1:T(8,128)S(1)} %get-tuple-element.101) | copy-start | bytes 9437188
  82.2 5.4 %copy-start.40 = (f32[1024]{0:T(1024)}, f32[1024]{0:T(1024)S(1)}, u32[]{:S(2)}) copy-start(f32[1024]{0:T(1024)S(1)} %broadcast_multiply_fusion.3) | copy-start | bytes 12292
  82.8 4.8 copy-start.42
  82.8 4.8 copy-start.54
  87.6 88.8 %copy-start.1 = (bf16[3,1024,768]{2,1,0:T(8,128)(2,1)}, bf16[3,1024,768]{2,1,0:T(8,128)(2,1)S(1)}, u32[]{:S(2)}) copy-start(bf16[3,1024,768]{2,1,0:T(8,128)(2,1)S(1)} %fusion.q_ref.k_ref.v_ref) | copy-start | bytes 14155780
  178.0 23.3 %copy-start.10 = (f32[1024,768]{1,0:T(8,128)}, f32[1024,768]{1,0:T(8,128)S(1)}, u32[]{:S(2)}) copy-start(f32[1024,768]{1,0:T(8,128)S(1)} %get-tuple-element.103) | copy-start | bytes 9437188
  178.6 22.0 %copy-start.44 = (f32[1024]{0:T(1024)}, f32[1024]{0:T(1024)S(1)}, u32[]{:S(2)}) copy-start(f32[1024]{0:T(1024)S(1)} %multiply_reduce_fusion.6) | copy-start | bytes 12292
  178.6 22.0 %copy-start.34 = (f32[1024]{0:T(1024)}, f32[1024]{0:T(1024)S(1)}, u32[]{:S(2)}) copy-start(f32[1024]{0:T(1024)S(1)} %fusion.51) | copy-start | bytes 12292
  201.8 3.2 copy-start.12
  201.8 3.2 copy-start.28
  201.9 9.0 %copy-start.63 = (s32[32,2]{0,1:T(2,128)S(1)}, s32[32,2]{0,1:T(2,128)}, u32[]{:S(2)}) copy-start(s32[32,2]{0,1:T(2,128)} %param.20) | copy-start | bytes 772
  203.3 6.9 %copy-start.36 = (f32[1024]{0:T(1024)}, f32[1024]{0:T(1024)S(1)}, u32[]{:S(2)}) copy-start(f32[1024]{0:T(1024)S(1)} %fusion.52) | copy-start | bytes 12292
  218.5 146.7 %all-gather.8.cloned.1.call-start = ((), (), s32[]{:S(2)}) async-start(), calls=%async_computation.2 | async-start | bytes 16293888 | tf_op jit(solution)/shard_map/all_gather | solution.py:1398
  223.4 11.9 %copy-start.29 = (f32[1024]{0:T(1024)S(1)}, f32[1024]{0:T(1024)}, u32[]{:S(2)}) copy-start(f32[1024]{0:T(1024)} %copy-done.28) | copy-start | bytes 12292
  223.5 11.9 %copy-start.33 = (f32[768]{0:T(1024)S(1)}, f32[768]{0:T(1024)}, u32[]{:S(2)}) copy-start(f32[768]{0:T(1024)} %copy-done.32) | copy-start | bytes 9220
  223.5 11.9 %copy-start.37 = (f32[1024]{0:T(1024)S(1)}, f32[1024]{0:T(1024)}, u32[]{:S(2)}) copy-start(f32[1024]{0:T(1024)} %copy-done.36) | copy-start | bytes 12292
  223.5 11.9 %copy-start.51 = (pred[1024]{0:T(1024)(128)(4,1)S(1)}, pred[1024]{0:T(1024)(128)(4,1)}, u32[]{:S(2)}) copy-start(pred[1024]{0:T(1024)(128)(4,1)} %copy-done.50) | copy-start | bytes 3076
  223.5 11.9 %copy-start.62 = (f32[8]{0:T(128)S(1)}, f32[8]{0:T(128)}, u32[]{:S(2)}) copy-start(f32[8]{0:T(128)} %copy-done.61) | copy-start | bytes 100
  235.4 4.7 copy-start.47
  235.4 4.7 copy-start.13
  243.3 33.4 %copy-start.11 = (f32[1024,768]{1,0:T(8,128)S(1)}, f32[1024,768]{1,0:T(8,128)}, u32[]{:S(2)}) copy-start(f32[1024,768]{1,0:T(8,128)} %copy-done.10) | copy-start | bytes 9437188
  243.3 33.4 %copy-start.31 = (f32[768]{0:T(1024)S(1)}, f32[768]{0:T(1024)}, u32[]{:S(2)}) copy-start(f32[768]{0:T(1024)} %copy-done.30) | copy-start | bytes 9220
  243.3 33.4 %copy-start.35 = (f32[1024]{0:T(1024)S(1)}, f32[1024]{0:T(1024)}, u32[]{:S(2)}) copy-start(f32[1024]{0:T(1024)} %copy-done.34) | copy-start | bytes 12292
  276.7 3.1 copy-start.45
  276.7 3.1 copy-start.21
  276.7 4.6 copy-start.15
  279.8 3.8 slice-start.6
  279.9 6.7 %slice-start = ((s8[4718592]{0:T(1024)(128)(4,1)}), s8[4194304]{0:T(1024)(128)(4,1)S(1)}, s32[]{:S(2)}) async-start(s8[4718592]{0:T(1024)(128)(4,1)} %bitcast.83), calls=%async_computation.3 | async-start | bytes 8388608
  281.3 3.8 slice-start.7
  281.3 5.2 slice-start.1
  286.5 40.2 %copy-start.19 = (f32[768,1024]{0,1:T(8,128)S(1)}, f32[768,1024]{0,1:T(8,128)}, u32[]{:S(2)}) copy-start(f32[768,1024]{0,1:T(8,128)} %copy-done.18) | copy-start | bytes 9437188
  286.6 40.2 %copy-start.39 = (f32[768]{0:T(1024)S(1)}, f32[768]{0:T(1024)}, u32[]{:S(2)}) copy-start(f32[768]{0:T(1024)} %copy-done.38) | copy-start | bytes 9220
  286.6 40.2 %copy-start.41 = (f32[1024]{0:T(1024)S(1)}, f32[1024]{0:T(1024)}, u32[]{:S(2)}) copy-start(f32[1024]{0:T(1024)} %copy-done.40) | copy-start | bytes 12292
  286.6 40.2 %copy-start.53 = (f32[768]{0:T(1024)S(1)}, f32[768]{0:T(1024)}, u32[]{:S(2)}) copy-start(f32[768]{0:T(1024)} %copy-done.52) | copy-start | bytes 9220
  286.6 40.2 %copy-start.55 = (f32[1024]{0:T(1024)S(1)}, f32[1024]{0:T(1024)}, u32[]{:S(2)}) copy-start(f32[1024]{0:T(1024)} %copy-done.54) | copy-start | bytes 12292
  326.8 6.9 %copy-start.2 = (bf16[3,1024,768]{2,1,0:T(8,128)(2,1)}, bf16[3,1024,768]{2,1,0:T(8,128)(2,1)S(1)}, u32[]{:S(2)}) copy-start(bf16[3,1024,768]{2,1,0:T(8,128)(2,1)S(1)} %attention_backward.1) | copy-start | bytes 14155780
  326.8 4.5 copy-start.43
  336.8 2.9 copy-start.9
  336.9 7.8 %slice-start.2 = ((s8[4718592]{0:T(1024)(128)(4,1)}), s8[4194304]{0:T(1024)(128)(4,1)S(1)}, s32[]{:S(2)}) async-start(s8[4718592]{0:T(1024)(128)(4,1)} %bitcast.85), calls=%async_computation.5 | async-start | bytes 8388608
  339.7 4.9 slice-start.3
  339.7 4.9 copy-start.20
  339.7 4.9 copy-start.60
  500.0 8.8 %copy-start.49 = (f32[15,96]{1,0:T(8,128)S(1)}, f32[15,96]{1,0:T(8,128)}, u32[]{:S(2)}) copy-start(f32[15,96]{1,0:T(8,128)} %param.30) | copy-start | bytes 17284
  500.0 8.8 %copy-start.57 = (f32[15,96]{1,0:T(8,128)S(1)}, f32[15,96]{1,0:T(8,128)}, u32[]{:S(2)}) copy-start(f32[15,96]{1,0:T(8,128)} %param.32) | copy-start | bytes 17284
  500.0 8.8 %copy-start.58 = (f32[15,96]{1,0:T(8,128)S(1)}, f32[15,96]{1,0:T(8,128)}, u32[]{:S(2)}) copy-start(f32[15,96]{1,0:T(8,128)} %param.31) | copy-start | bytes 17284
  500.0 9.5 %copy-start.22 = (f32[96,5462]{1,0:T(8,128)S(1)}, f32[96,5462]{1,0:T(8,128)}, u32[]{:S(2)}) copy-start(f32[96,5462]{1,0:T(8,128)} %param.27) | copy-start | bytes 6292228
  500.0 9.5 %copy-start.23 = (f32[96,5462]{1,0:T(8,128)S(1)}, f32[96,5462]{1,0:T(8,128)}, u32[]{:S(2)}) copy-start(f32[96,5462]{1,0:T(8,128)} %get-tuple-element.107) | copy-start | bytes 6292228
  500.0 9.5 %copy-start.26 = (f32[96,5462]{1,0:T(8,128)S(1)}, f32[96,5462]{1,0:T(8,128)}, u32[]{:S(2)}) copy-start(f32[96,5462]{1,0:T(8,128)} %param.29) | copy-start | bytes 6292228
  500.0 9.4 %copy-start.27 = (f32[96,5462]{1,0:T(8,128)S(1)}, f32[96,5462]{1,0:T(8,128)}, u32[]{:S(2)}) copy-start(f32[96,5462]{1,0:T(8,128)} %param.28) | copy-start | bytes 6292228
  509.5 3.8 copy-start.24
  509.5 5.5 %copy-start.25 = (f32[13,96,768]{2,1,0:T(8,128)S(1)}, f32[13,96,768]{2,1,0:T(8,128)}, u32[]{:S(2)}) copy-start(f32[13,96,768]{2,1,0:T(8,128)} %param.23) | copy-start | bytes 11501572
  (11 other events, 15.4 us)
Sparse Core Ops, SparseCore 0:
  10.8 150.9 all-gather.3
  218.6 63.5 all-gather.5
  284.3 80.8 all-gather.7

commit v7 on v6

--- a/solution.py
+++ b/solution.py
@@ -19,9 +19,10 @@
 CODE_TOP = 32766.0
 CODE_FLOOR = 1e-33
 PIECE = 48
+FEATURE_TILE = 128
 SPAN = 48
 SHARES = 8
-GATHER_DEPTH = 7
+GATHER_DEPTH = 4
 IMG_PACK = 8
 
 
@@ -375,24 +376,18 @@
     grad_hidden_norm, grad_gain_two, grad_shift_two = norm_two_back(grad_normed_two)
     grad_hidden = grad_output + grad_hidden_norm
     grad_attn_out = grad_hidden.astype(jnp.bfloat16)
-    grad_out_proj = jnp.einsum(
-        "te,td->ed", attended, grad_attn_out, preferred_element_type=jnp.float32
-    )
     grad_attended = jnp.einsum(
         "td,ed->te", grad_attn_out, blocks[4], preferred_element_type=jnp.float32
     ).astype(jnp.bfloat16)
     grad_qkv = attention_backward(qkv_rows, pack_ids, key_codes, grad_attended)
-    grad_qkv_proj = jnp.einsum(
-        "td,kte->kde", normed_one, grad_qkv, preferred_element_type=jnp.float32
-    )
     grad_normed_one = jnp.einsum(
         "kte,kde->td", grad_qkv, blocks[1:4], preferred_element_type=jnp.float32
     )
     norm_one_back = jax.vjp(norm_rows, embedded, vec_all[1], vec_all[2])[1]
     grad_embed_norm, grad_gain_one, grad_shift_one = norm_one_back(grad_normed_one)
     grad_embedded = (grad_hidden + grad_embed_norm).astype(jnp.bfloat16)
-    grad_patch = jnp.einsum("tp,td->pd", patch, grad_embedded, preferred_element_type=jnp.float32)
-    grad_arrays = (grad_patch[None], grad_qkv_proj, grad_out_proj[None], grad_up, grad_down)
+    lefts = (patch, normed_one, attended)
+    rights = (grad_embedded, grad_qkv, grad_attn_out)
     bias_sums = jnp.stack(
         [
             jnp.sum(grad_embedded.astype(jnp.float32), 0),
@@ -407,7 +402,7 @@
     )
     up_sums = up_sums.reshape(up_count, feature_dim)
     tail_sums = jnp.stack([jnp.sum(grad_branch.astype(jnp.float32), 0), grad_gain, grad_shift])
-    return (grad_arrays, jnp.concatenate([bias_sums, up_sums, tail_sums], 0))
+    return (lefts, rights, (grad_up, grad_down), jnp.concatenate([bias_sums, up_sums, tail_sums], 0))
 
 
 def torus_place():
@@ -437,15 +432,19 @@
 
 def reduce_kernel(counts, *refs):
     sources, refs = refs[: len(counts)], refs[len(counts) :]
-    (vec_ref, tail_ref, left_hbm, right_hbm,
-     own_hbm, left_out_hbm, right_out_hbm, step_hbm, sums_ref, tail_out_ref, vec_out_ref,
-     left_buf, right_buf, outs_buf, squares, high_buf, low_buf, sum_slots, tail_slots,
+    (patch_hbm, first_hbm, mid_hbm, dpatch_hbm, dfirst_hbm, dmid_hbm,
+     vec_ref, tail_ref, left_hbm, right_hbm,
+     own_hbm, left_out_hbm, right_out_hbm, step_hbm, wide_ref, facts_ref, vec_out_ref,
+     left_buf, right_buf, right_full, outs_buf, squares, high_buf, low_buf, sum_slots, tail_slots,
+     lhs_buf, rhs_buf, pair_sem,
      in_sem, sum_send, sum_recv, tail_send, tail_recv,
      acc, spare, kept, sent0, got0, sent1, got1, sent2, got2, sent3, got3, sent4, got4,
      ss0, gs0, ss1, gs1, ss2, gs2, ss3, gs3, ss4, gs4, codes, scales, vec_got,
      load_sem, out_sem, send_sem, recv_sem, send_scale_sem, recv_scale_sem,
      vec_send_sem, vec_recv_sem) = refs
-    total = sum(counts)
+    stored = sum(counts)
+    paired = dfirst_hbm.shape[0] + 2
+    total = stored + paired
     half, width = codes.shape[1], codes.shape[2]
     cols = width // 2
     z, y, x, core = torus_place()
@@ -500,6 +499,32 @@
             pl.when((m >= start) & (m < start + count))(one)
             start += count
 
+    def block_of(m):
+        return lax.rem(m + paired, total)
+
+    def pair_loads(m, body):
+        index = m - stored
+        last = paired - 1
+
+        def run(left, right):
+            body(pltpu.make_async_copy(left, lhs_buf.at[m % 2], pair_sem.at[m % 2, 0]))
+            body(pltpu.make_async_copy(right, rhs_buf.at[m % 2], pair_sem.at[m % 2, 1]))
+
+        pl.when(index == 0)(lambda: run(patch_hbm, dpatch_hbm))
+        pl.when((index > 0) & (index < last))(
+            lambda: run(first_hbm, dfirst_hbm.at[jnp.clip(index - 1, 0, last - 2)])
+        )
+        pl.when(index == last)(lambda: run(mid_hbm, dmid_hbm))
+
+    def pair_product(m):
+        chunk = 2 * FEATURE_TILE
+        for r in range(0, width, chunk):
+            left = lhs_buf[m % 2, :, r : r + chunk].T
+            for target, columns in ((acc.at[m % 5], own_cols), (spare.at[m % 2], other_cols)):
+                target[r : r + chunk, :] = jnp.dot(
+                    left, rhs_buf[m % 2, :, columns], preferred_element_type=jnp.float32
+                )
+
     def message(stage, m, source, scale_source, target, scale_target, mate):
         return (
             pltpu.make_async_remote_copy(
@@ -584,11 +609,23 @@
         @pl.when(t < total)
         def _():
             m = t
-            loads(m, lambda copy: copy.wait())
-
-            @pl.when(m + 1 < total)
+
+            @pl.when(m < stored)
+            def _():
+                loads(m, lambda copy: copy.wait())
+
+            @pl.when(m + 1 < stored)
             def _():
                 loads(m + 1, lambda copy: copy.start())
+
+            @pl.when((m + 1 >= stored) & (m + 1 < total))
+            def _():
+                pair_loads(m + 1, lambda copy: copy.start())
+
+            @pl.when(m >= stored)
+            def _():
+                pair_loads(m, lambda copy: copy.wait())
+                pair_product(m)
 
             span = 2 * PIECE
             encode(
@@ -744,15 +781,19 @@
 
         def ins(m):
             return (
-                pltpu.make_async_copy(left_hbm.at[m], left_buf.at[m % 2], in_sem.at[m % 2, 0]),
-                pltpu.make_async_copy(right_hbm.at[m], right_buf.at[m % 2], in_sem.at[m % 2, 1]),
+                pltpu.make_async_copy(
+                    left_hbm.at[block_of(m)], left_buf.at[m % 2], in_sem.at[m % 2, 0]
+                ),
+                pltpu.make_async_copy(
+                    right_hbm.at[:, block_of(m)], right_buf.at[m % 2], in_sem.at[m % 2, 1]
+                ),
             )
 
         def outs(m):
             targets = (own_hbm, left_out_hbm, right_out_hbm, step_hbm)
             return [
                 pltpu.make_async_copy(
-                    outs_buf.at[m % 2, n], target.at[m], out_sem.at[m % 2, n]
+                    outs_buf.at[m % 2, n], target.at[block_of(m)], out_sem.at[m % 2, n]
                 )
                 for n, target in enumerate(targets)
             ]
@@ -775,7 +816,7 @@
                 copy.wait()
             precondition_block(
                 own, codes.at[m], scales.at[m], left_buf.at[m % 2], right_buf.at[m % 2],
-                outs_buf.at[m % 2], squares.at[m], high_buf, low_buf,
+                outs_buf.at[m % 2], squares.at[m], high_buf, low_buf, right_full,
             )
             start(outs(m))
 
@@ -786,14 +827,15 @@
     def folded(row):
         return sum(row[:, n * 128 : (n + 1) * 128] for n in range(row.shape[1] // 128))
 
-    sums_ref[...] = jnp.zeros_like(sums_ref)
     layer = jnp.zeros((1, 128), jnp.float32)
+    mine = lax.rem(dp, quarter)
+    sum_slots[mine] = jnp.zeros(sum_slots.shape[1:], jnp.float32)
     for m in range(total):
         layer = layer + folded(squares[m, 0:1, :])
         for quad in range(2):
             part = squares[m, 1:2, quad * cols : (quad + 1) * cols]
-            sums_ref[2 * m + quad : 2 * m + quad + 1, :] = folded(part)
-    sum_slots[lax.rem(dp, quarter)] = sums_ref[...]
+            row = 2 * ((m + paired) % total) + quad
+            sum_slots[mine, row : row + 1, :] = folded(part)
     once = (cls == 0).astype(jnp.float32)
     first_row = lax.broadcasted_iota(jnp.int32, tail_ref.shape, 0) == 0
     tail_slots[me] = tail_ref[...] + jnp.where(first_row, once * layer, 0.0)
@@ -825,18 +867,33 @@
     value = sum_slots[0]
     for n in range(1, quarter):
         value = value + sum_slots[n]
-    sums_ref[...] = value
-    value = tail_slots[0]
+    tail = tail_slots[0]
     for n in range(1, everyone):
-        value = value + tail_slots[n]
-    tail_out_ref[...] = value
-
-
-def reduce_gradients(arrays, vec_sums, tail, root_left, right_half, dp_count, cls_count):
+        tail = tail + tail_slots[n]
+    vec = vec_out_ref[...]
+    vec_squares = jnp.sum(jnp.sum(vec * vec, 0, keepdims=True), 1, keepdims=True)
+    norm = jnp.sqrt(jnp.sum(tail[0:1], 1, keepdims=True) + vec_squares)
+    factor = CLIP_NORM / jnp.maximum(norm, CLIP_NORM)
+    mean_squares = jnp.sum(value, 1, keepdims=True) / (half * cols) * factor * factor
+    scale = SHAMPOO_RATE * factor * lax.rsqrt(mean_squares + ROOT_EPS)
+    for b in range(total):
+        for quad in range(2):
+            row = 2 * b + quad
+            wide_ref[b, :, quad * cols : (quad + 1) * cols] = jnp.broadcast_to(
+                scale[row : row + 1], (1, cols)
+            )
+    rows = lax.broadcasted_iota(jnp.int32, facts_ref.shape, 0)
+    loss = jnp.sum(tail[1:2], 1, keepdims=True)
+    facts_ref[...] = jnp.where(rows == 0, loss, jnp.where(rows == 1, norm, factor))
+
+
+def reduce_gradients(
+    arrays, lefts, rights, vec_sums, tail, root_left, right_codes, dp_count, cls_count
+):
     counts = tuple(array.shape[0] for array in arrays)
-    total = sum(counts)
-    width = arrays[0].shape[1]
-    rows = root_left.shape[1]
+    total, rows, width = root_left.shape
+    length = lefts[0].shape[0]
+    parts, coded_rows = right_codes.shape[0], right_codes.shape[2]
     half, cols = width // 2, width // 2
     sum_rows = 2 * total + -2 * total % 8
     f32, i16 = jnp.float32, jnp.int16
@@ -856,21 +913,25 @@
         functools.partial(reduce_kernel, counts),
         out_shape=(jax.ShapeDtypeStruct((total, rows, width), f32),) * 4
         + (
-            jax.ShapeDtypeStruct((sum_rows, 128), f32),
+            jax.ShapeDtypeStruct((total, 1, width), f32),
             jax.ShapeDtypeStruct(tail.shape, f32),
             jax.ShapeDtypeStruct(vec_sums.shape, f32),
         ),
-        in_specs=[hbm] * len(arrays) + [vmem, vmem, hbm, hbm],
+        in_specs=[hbm] * (len(arrays) + 6) + [vmem, vmem, hbm, hbm],
         out_specs=(hbm,) * 4 + (vmem,) * 3,
         scratch_shapes=[
             pltpu.VMEM((2, rows, width), f32),
-            pltpu.VMEM((2, half, width), f32),
+            pltpu.VMEM((2, parts, coded_rows, width), jnp.int32),
+            pltpu.VMEM((half, width), f32),
             pltpu.VMEM((2, 4, rows, width), f32),
             pltpu.VMEM((total, 2, width), f32),
             pltpu.VMEM((half, width), jnp.bfloat16),
             pltpu.VMEM((half, width), jnp.bfloat16),
             pltpu.VMEM((dp_count // 2, sum_rows, 128), f32),
             pltpu.VMEM((dp_count * cls_count,) + tail.shape, f32),
+            pltpu.VMEM((2, length, width), jnp.bfloat16),
+            pltpu.VMEM((2, length, width), jnp.bfloat16),
+            pltpu.SemaphoreType.DMA((2, 2)),
             pltpu.SemaphoreType.DMA((2, 2)),
             pltpu.SemaphoreType.DMA((dp_count // 2,)),
             pltpu.SemaphoreType.DMA((dp_count // 2,)),
@@ -907,7 +968,7 @@
             collective_id=1, has_side_effects=True, vmem_limit_bytes=60 << 20
         ),
         name="reduce_gradients",
-    )(*arrays, vec_sums, tail, root_left, right_half)
+    )(*arrays, *lefts, *rights, vec_sums, tail, root_left, right_codes)
 
 
 def split_float(values):
@@ -923,12 +984,34 @@
     return [out[n * rows : (n + 1) * rows] for n in range(len(lefts))]
 
 
+def encode_roots(part):
+    top = jnp.max(jnp.abs(part), 1, keepdims=True)
+    level = jnp.ceil(jnp.log2(jnp.maximum(top, 1e-30)))
+    codes = jnp.round(part * jnp.exp2(15.0 - level))
+    codes = jnp.clip(codes, -32767.0, 32767.0).astype(jnp.int32)
+    levels = jnp.broadcast_to(level.astype(jnp.int32), (part.shape[0], 8, part.shape[2]))
+    upper = jnp.concatenate([codes[:, 0:8], codes[:, 16:24]], 1)
+    lower = jnp.concatenate([codes[:, 8:16], levels], 1)
+    return upper * 65536 + (lower + 32768)
+
+
 def precondition_block(
-    own, codes_ref, scales_ref, left_ref, right_ref, outs_ref, squares_ref, high_ref, low_ref
+    own, codes_ref, scales_ref, left_ref, right_codes, outs_ref, squares_ref, high_ref, low_ref,
+    right_ref
 ):
     half, width = codes_ref.shape
     rows = left_ref.shape[0]
     own_rows = pl.ds(pl.multiple_of(own, PIECE), rows)
+    parts = right_codes.shape[0]
+    size = half // parts
+    for n in range(parts):
+        packed = right_codes[n]
+        upper = lax.shift_right_arithmetic(packed, jnp.full_like(packed, 16)).astype(jnp.float32)
+        lower = ((packed & 65535) - 32768).astype(jnp.float32)
+        scale = jnp.exp2(lower[8:9] - 15.0)
+        right_ref[n * size : n * size + 8, :] = upper[0:8] * scale
+        right_ref[n * size + 8 : n * size + 16, :] = lower[0:8] * scale
+        right_ref[n * size + 16 : n * size + 24, :] = upper[8:16] * scale
     for piece in range(half // PIECE):
         part = slice(piece * PIECE, (piece + 1) * PIECE)
         high_ref[part, :], low_ref[part, :] = split_float(
@@ -1022,148 +1105,84 @@
     mate_core = torus_device(z, y, x, 1 - core)
     mate_x = torus_device(z, y, 1 - x, core)
     mate_y = torus_device(z, 1 - y, x, core)
-    mate_up = torus_device(jnp.minimum(z + 1, 3), y, x, core)
-    mate_down = torus_device(jnp.maximum(z - 1, 0), y, x, core)
-    has_up = z < 3
-    has_down = z > 0
     own_cols = pl.ds(pl.multiple_of(core * cols, 128), cols)
     other_cols = pl.ds(pl.multiple_of((1 - core) * cols, 128), cols)
-
-    def share(m, zz, yy, start, size, columns=own_cols):
+    spare = rows - SPAN
+    held = x * spare
+    lone = (x * SPAN, (1 - x) * SPAN)
+
+    def share(m, zz, yy, start, size):
         begin = (zz * 2 + yy) * rows + start
-        return out_ref.at[m, pl.ds(pl.multiple_of(begin, 16), size), columns]
-
-    def copy(stage, m, source, target, mate):
+        return out_ref.at[m, pl.ds(pl.multiple_of(begin, 16), size), own_cols]
+
+    def copy(slot, arrival, m, source, target, mate):
         return pltpu.make_async_remote_copy(
             src_ref=source, dst_ref=target,
-            send_sem=send_sem.at[stage, m % 2], recv_sem=recv_sem.at[stage, m],
+            send_sem=send_sem.at[slot, m % 2], recv_sem=recv_sem.at[arrival, m],
             device_id=mate, device_id_type=MESH,
         )
-
-    span_start = x * (rows - SPAN)
-    lack = rows - SPAN
-    lack_mine = x * SPAN
-    lack_theirs = (1 - x) * SPAN
 
     def local(m):
         return pltpu.make_async_copy(
             own_ref.at[m, :, own_cols], share(m, z, y, 0, rows), copy_sem.at[m % 2]
         )
 
-    def chain(m, turn, upward):
-        origin = z - (turn - 1) if upward else z + (turn - 1)
-        stage = (turn - 1) * 2 + (0 if upward else 1)
-        target = share(m, origin, y, span_start, SPAN)
-        if turn == 1:
-            source = own_ref.at[m, pl.ds(pl.multiple_of(span_start, 16), SPAN), own_cols]
-        else:
-            source = target
-        return copy(stage, m, source, target, mate_up if upward else mate_down)
-
-    def chain_sends(turn, upward):
-        if upward:
-            return has_up & (z - (turn - 1) >= 0)
-        return has_down & (z + (turn - 1) <= 3)
-
-    def chain_comes(turn, upward):
-        return (z - turn >= 0) if upward else (z + turn <= 3)
-
-    def arriving(m, turn, upward):
-        origin = z - turn if upward else z + turn
-        stage = (turn - 1) * 2 + (0 if upward else 1)
-        target = share(m, origin, y, span_start, SPAN)
-        return copy(stage, m, target, target, mate_up)
-
-    def patch_out(m, n):
-        zz = lax.rem(z + n, 4)
-        block = share(m, zz, y, lack_mine, lack)
-        return copy(5 + n, m, block, block, mate_x)
-
-    def patch_in(m, n):
-        zz = lax.rem(z + n, 4)
-        block = share(m, zz, y, lack_theirs, lack)
-        return copy(5 + n, m, block, block, mate_x)
-
-    def cross(m, n, yy, stage, plane, mate):
-        block = share(m, plane * 2 + n, yy, 0, rows)
-        return copy(stage + n, m, block, block, mate)
+    def along(m, n, outgoing):
+        other = lax.rem(z + n, 4)
+        origin = z if outgoing else other
+        source = own_ref.at[m, pl.ds(pl.multiple_of(held, 16), SPAN), own_cols]
+        mate = torus_device(other, y, x, core)
+        return copy(n - 1, origin, m, source, share(m, origin, y, held, SPAN), mate)
+
+    def cross(m, n, outgoing):
+        block = share(m, n, y if outgoing else 1 - y, held, SPAN)
+        return copy(3 + n, 4 + n, m, block, block, mate_y)
+
+    def patch(m, n, outgoing):
+        index = lax.rem(z * 2 + y + n, SHARES)
+        block = share(m, index // 2, lax.rem(index, 2), lone[0 if outgoing else 1], spare)
+        return copy(6 + n, 7 + n, m, block, block, mate_x)
 
     def swap(m, columns):
         block = out_ref.at[m, :, columns]
-        return copy(13, m, block, block, mate_core)
+        return copy(14, 15, m, block, block, mate_core)
+
+    def finish(copies):
+        for outgoing, incoming in copies:
+            outgoing.wait_send()
+            incoming.wait_recv()
 
     def step(t):
         @pl.when(t < count)
         def _():
             local(t).start()
-            for upward in (True, False):
-                @pl.when(chain_sends(1, upward))
-                def _(upward=upward):
-                    chain(t, 1, upward).start()
-
-        for turn in (2, 3):
-            @pl.when((t >= turn - 1) & (t < count + turn - 1))
-            def _(turn=turn):
-                m = t - (turn - 1)
-                if turn == 2:
-                    local(m).wait()
-                for upward in (True, False):
-                    @pl.when(chain_sends(turn - 1, upward))
-                    def _(upward=upward):
-                        chain(m, turn - 1, upward).wait_send()
-
-                    @pl.when(chain_comes(turn - 1, upward))
-                    def _(upward=upward):
-                        arriving(m, turn - 1, upward).wait_recv()
-
-                    @pl.when(chain_sends(turn, upward))
-                    def _(upward=upward):
-                        chain(m, turn, upward).start()
+            for n in range(1, 4):
+                along(t, n, True).start()
+
+        @pl.when((t >= 1) & (t < count + 1))
+        def _():
+            m = t - 1
+            local(m).wait()
+            finish([(along(m, n, True), along(m, n, False)) for n in range(1, 4)])
+            for n in range(4):
+                cross(m, n, True).start()
+
+        @pl.when((t >= 2) & (t < count + 2))
+        def _():
+            m = t - 2
+            finish([(cross(m, n, True), cross(m, n, False)) for n in range(4)])
+            for n in range(1, SHARES):
+                patch(m, n, True).start()
 
         @pl.when((t >= 3) & (t < count + 3))
         def _():
             m = t - 3
-            for upward in (True, False):
-                @pl.when(chain_sends(3, upward))
-                def _(upward=upward):
-                    chain(m, 3, upward).wait_send()
-
-                @pl.when(chain_comes(3, upward))
-                def _(upward=upward):
-                    arriving(m, 3, upward).wait_recv()
-            if lack:
-                for n in range(1, 4):
-                    patch_out(m, n).start()
+            finish([(patch(m, n, True), patch(m, n, False)) for n in range(1, SHARES)])
+            swap(m, own_cols).start()
 
         @pl.when((t >= 4) & (t < count + 4))
         def _():
             m = t - 4
-            if lack:
-                for n in range(1, 4):
-                    patch_out(m, n).wait_send()
-                    patch_in(m, n).wait_recv()
-            for n in range(2):
-                cross(m, n, y, 9, x, mate_y).start()
-
-        @pl.when((t >= 5) & (t < count + 5))
-        def _():
-            m = t - 5
-            for n in range(2):
-                cross(m, n, y, 9, x, mate_y).wait_send()
-                cross(m, n, 1 - y, 9, x, mate_y).wait_recv()
-                cross(m, n, 1 - y, 11, x, mate_x).start()
-
-        @pl.when((t >= 6) & (t < count + 6))
-        def _():
-            m = t - 6
-            for n in range(2):
-                cross(m, n, 1 - y, 11, x, mate_x).wait_send()
-                cross(m, n, 1 - y, 11, 1 - x, mate_x).wait_recv()
-            swap(m, own_cols).start()
-
-        @pl.when((t >= 7) & (t < count + 7))
-        def _():
-            m = t - 7
             swap(m, own_cols).wait_send()
             swap(m, other_cols).wait_recv()
 
@@ -1216,8 +1235,8 @@
 
 def gather_semaphores(count):
     return [
-        pltpu.SemaphoreType.DMA((14, 2)),
-        pltpu.SemaphoreType.DMA((14, count)),
+        pltpu.SemaphoreType.DMA((15, 2)),
+        pltpu.SemaphoreType.DMA((16, count)),
         pltpu.SemaphoreType.DMA((2,)),
     ]
 
@@ -1395,9 +1414,14 @@
         return attention_forward(qkv_rows, pack_ids, key_codes), all_blocks[5:]
 
     output, mlp_blocks, saved = layer_forward(blocks, vec_all, patches, attend)
-    right_half = lax.all_gather(
-        right_part, ("dp", "cls"), axis=1, tiled=True, axis_index_groups=half_groups
-    )
+    if on_torus:
+        right_codes = lax.all_gather(
+            encode_roots(right_part), ("dp", "cls"), axis=0, axis_index_groups=half_groups
+        )
+    else:
+        right_half = lax.all_gather(
+            right_part, ("dp", "cls"), axis=1, tiled=True, axis_index_groups=half_groups
+        )
     pooled = pool_rows(output, final_gain, final_shift, pack_ids, pack_keep)
     group = lax.all_gather(pooled.astype(jnp.bfloat16), "cls", axis=0, tiled=True)
     logits = jnp.dot(group, head_low, preferred_element_type=jnp.float32)
@@ -1431,7 +1455,7 @@
 
     pool_back = jax.vjp(pool_local, output, final_gain, final_shift)[1]
     grad_output, grad_gain, grad_shift = pool_back(grad_pooled)
-    grad_arrays, grad_vectors = layer_backward(
+    lefts, rights, mlp_grads, grad_vectors = layer_backward(
         blocks,
         mlp_blocks,
         vec_all,
@@ -1448,15 +1472,27 @@
     if on_torus:
         padded = jnp.pad(grad_vectors, ((0, -grad_vectors.shape[0] % 8), (0, 0)))
         tail = jnp.pad(jnp.stack([head_squares, loss_part])[:, None], ((0, 6), (0, 127)))
-        block_rows, left_add, right_add, direction, sums, tail, vector_sum = reduce_gradients(
-            grad_arrays, padded, tail, root_left, right_half, dp_count, cls_count
+        block_rows, left_add, right_add, direction, wide_scale, facts, vector_sum = (
+            reduce_gradients(
+                mlp_grads, lefts, rights, padded, tail, root_left, right_codes,
+                dp_count, cls_count,
+            )
         )
         vector_sum = vector_sum[: grad_vectors.shape[0]]
-        loss = tail[1, 0]
-        all_squares = jnp.sum(tail[0])
-        block_squares = jnp.sum(sums[: 2 * block_count], -1).reshape(block_count, 2)
+        loss, grad_norm, factor = facts[0, 0], facts[1, 0], facts[2, 0]
     else:
-        grad_half = reduced_half(jnp.concatenate(grad_arrays, 0), half_groups)
+        over_rows = "td,te->de"
+        first_grads = [
+            jnp.einsum(over_rows, left, right, preferred_element_type=jnp.float32)[None]
+            for left, right in (
+                (lefts[0], rights[0]),
+                (lefts[1], rights[1][0]),
+                (lefts[1], rights[1][1]),
+                (lefts[1], rights[1][2]),
+                (lefts[2], rights[2]),
+            )
+        ]
+        grad_half = reduced_half(jnp.concatenate(first_grads + list(mlp_grads), 0), half_groups)
         vector_sum = lax.psum(grad_vectors, ("dp", "cls"))
         left_add, right_add, direction, block_rows = preconditioned_rows(
             grad_half, root_left, right_half, (dp_index % half_dp) * row_count
@@ -1477,14 +1513,13 @@
         all_squares = packed[4 * block_count]
         sums = packed[: 4 * block_count].reshape(2, block_count, 2)
         block_squares = jnp.where(dp_index < half_dp, sums[0], sums[1])
+        grad_norm = jnp.sqrt(all_squares + jnp.sum(vector_sum * vector_sum))
+        factor = CLIP_NORM / jnp.maximum(grad_norm, CLIP_NORM)
+        mean_squares = block_squares / (half_size * half_size) * factor * factor
+        scale = SHAMPOO_RATE * factor * lax.rsqrt(mean_squares + ROOT_EPS)
+        wide_scale = jnp.repeat(scale, half_size, axis=1)[:, None, :]
     vector_rows = lax.dynamic_slice_in_dim(vector_sum, dp_index * row_count, row_count, 1)
-    grad_norm = jnp.sqrt(all_squares + jnp.sum(vector_sum * vector_sum))
-    factor = CLIP_NORM / jnp.maximum(grad_norm, CLIP_NORM)
-    mean_squares = block_squares / (half_size * half_size)
-    mean_squares = mean_squares * factor * factor
-    scale = factor * lax.rsqrt(mean_squares + ROOT_EPS)
-    wide_scale = jnp.repeat(SHAMPOO_RATE * scale, half_size, axis=1)
-    new_blocks = enc_weights - direction * wide_scale[:, None, :]
+    new_blocks = enc_weights - direction * wide_scale
     square_factor = 0.5 * factor * factor
     new_left = 0.5 * stats_left + square_factor * left_add
     new_right = 0.5 * stats_right + square_factor * right_add

time: 539 us -> 505 us (0.937)
  Pallas kernels: 376 us -> 365 us
  waiting for transfers between devices: 8.15 us -> 0.07 us
  matrix products: 52 us -> 44.9 us
  local copies, waits for them, and re-layouts: 21.1 us -> 14.1 us
    dot_general x3 -> x0, matrix products: 13.9 us -> none  [the longest x1 6.16 us: layer_backward(): jnp.einsum('td,kte->kde', normed_one, grad_qkv, preferred_element_type=jn...]
    all_gather x1, waiting for transfers between devices: 7.44 us -> 0.01 us  [on_device(): lax.all_gather(encode_roots(right_part), ('dp', 'cls'), axis=0, axis_inde...]
    pallas_call x1, Pallas kernels: 88.7 us -> 81.9 us  [attention_forward_gathering(): pl.pallas_call(attention_gather_kernel, grid=(width // PAIR,), out_shape=...]
    pallas_call x1, Pallas kernels: 58.2 us -> 52.7 us  [gather_weights(): pl.pallas_call(gather_kernel, out_shape=(jax.ShapeDtypeStruct((count, SHA...]
    unnamed x146 -> x59, local copies, waits for them, and re-layouts: 11.5 us -> 6.64 us
  transfers between devices with their start and end apart: 3 -> 3, of which waited for: 1 -> 0; matrix products, arithmetic and copies ran while one was open for 14% -> 14% of each run, Pallas kernels for 47% -> 47%
where the time goes in v7:
time: 505 us; the launch traced here: 496 us
  Pallas kernels  365 us (72%)
  other arithmetic  49.6 us (10%)
  matrix products  44.9 us (9%)
  between operations  17.7 us (4%)
  local copies, waits for them, and re-layouts  14.1 us (3%)
  blocking collectives  5.23 us (1%)
    pallas_call x1, Pallas kernels, reduce_gradients(): pl.pallas_call(functools.partial(reduce_kernel, counts), out_shape=(jax.S...  130 us
    pallas_call x1, Pallas kernels, attention_forward_gathering(): pl.pallas_call(attention_gather_kernel, grid=(width // PAIR,), out_shape=...  81.9 us
    pallas_call x1, Pallas kernels, gather_weights(): pl.pallas_call(gather_kernel, out_shape=(jax.ShapeDtypeStruct((count, SHA...  52.7 us
    pallas_call x1, Pallas kernels, attention_backward(): pl.pallas_call(attention_backward_kernel, grid=(width // PAIR,), out_shap...  40.1 us
    pallas_call x1, Pallas kernels, mlp_backward(): pl.pallas_call(mlp_backward_kernel, grid=(up_count * split,), out_shape=(...  33.4 us
    pallas_call x1, Pallas kernels, mlp_forward(): pl.pallas_call(mlp_forward_kernel, grid=(up_count * split,), out_shape=(j...  21.4 us
  transfers between devices with their start and end apart: 3, of which 0 were waited for; matrix products, arithmetic and copies ran while one was open for 14% of the time, Pallas kernels for 47%

profile of v7, /device:TPU:0, one launch (start us, length us, event | category | flops | bytes accessed | tf_op | source)
XLA Modules:
  0.0 496.4 jit_solution(878252144007890651)
XLA Ops:
  7.2 2.7 convert_element_type.86
  10.0 2.3 convert_element_type.79
  12.5 0.5 copy-done.20
  13.0 52.7 %gather_weights.1 = (bf16[5,768,768]{2,1,0:T(8,128)(2,1)S(1)}, f32[8,16,128]{2,1,0:T(8,128)S(1)}) custom-call(bf16[5,96,768]{2,1,0:T(8,128)(2,1)S(1)} %slice.138.own_ref, f32[16,128]{1,0:T(8,128)S(1)} %pad.12.vec_ref), custom_call_target="tpu_custom_call" | custom-call | tf_op jit(solution)/shard_map/gather_weights/pallas_call | solution.py:1296
  65.7 2.4 copy-done.4
  68.2 1.3 constant_dynamic-slice_fusion
  69.5 0.1 slice_reduce_fusion.1
  69.7 0.2 copy.58.qids_ref
  70.8 3.2 add_reduce_fusion
  74.1 0.6 multiply_reduce_fusion.7
  74.9 0.6 add_convert_fusion.3.refs_3_
  75.5 7.1 %fusion.q_ref.k_ref.v_ref = bf16[3,1024,768]{2,1,0:T(8,128)(2,1)S(1)} fusion(f32[3,768]{1,0:T(4,128)S(1)} %pad_maximum_fusion.1, bf16[5,768,768]{2,1,0:T(8,128)(2,1)} %copy-done.4, bf16[1024,768]{1,0:T(8,128)(2,1)S(1)} %add_convert_fusion.3.refs_3_), kind=kOutput, calls=%fused_computation.4 | convolution fusion | flops 3628597248 | bytes 9839616 | tf_op jit(solution)/shard_map/td,kde->kte/dot_general | solution.py:336
  82.6 81.9 %attention_forward.1 = (bf16[1024,768]{1,0:T(8,128)(2,1)S(1)}, bf16[8,768,768]{2,1,0:T(8,128)(2,1)}) custom-call(s32[1024,1]{1,0:T(8,128)S(1)} %copy.58.qids_ref, s32[1,1024]{1,0:T(1,128)S(1)} %broadcast_select_fusion.1.kcodes_ref, bf16[3,1024,768]{2,1,0:T(8,128)(2,1)S(1)} %fusion.q_ref.k_ref.v_ref, bf16[3,1024,768]{2,1,0:T(8,128)(2,1)S(1)} %fusion.q_ref.k_ref.v_ref, ...), custom_call_target="tpu_custom_call" | custom-call | tf_op jit(solution)/shard_map/attention_forward/pallas_call | solution.py:1273
  164.6 3.4 fusion.67
  168.1 0.5 multiply_reduce_fusion.6
  168.6 0.6 add_convert_fusion.2.x_ref
  169.2 21.4 %mlp_forward.1 = (bf16[1024,3072]{1,0:T(8,128)(2,1)}, f32[1024,3072]{1,0:T(8,128)}, f32[1024,768]{1,0:T(8,128)S(1)}) custom-call(bf16[1024,768]{1,0:T(8,128)(2,1)S(1)} %add_convert_fusion.2.x_ref, bf16[8,768,768]{2,1,0:T(8,128)(2,1)} %get-tuple-element.36.up_ref.down_ref, f32[1,3072]{1,0:T(1,128)S(1)} %reshape.270.bias_ref, ...), custom_call_target="tpu_custom_call" | custom-call | tf_op jit(solution)/shard_map/mlp_forward/pallas_call | solution.py:291
  190.6 0.1 convert_reduce_fusion.5
  190.7 0.4 fusion.65
  191.2 0.5 multiply_reduce_fusion.5
  191.7 1.7 fusion.30
  193.4 5.2 %all_gather.13 = bf16[32,768]{1,0:T(8,128)(2,1)S(1)} all-gather(bf16[8,768]{1,0:T(8,128)(2,1)S(1)} %fusion.30), channel_id=1, replica_groups=mesh['dp'=8,'cls'=4] {'cls'}, dimensions={0}, use_global_device_ids=true | all-gather | bytes 61440 | tf_op jit(solution)/shard_map/all_gather | solution.py:1426
  198.6 1.0 compare_reduce_fusion
  199.6 5.8 %fusion.37 = (f32[]{:T(128)}, bf16[32,5462]{1,0:T(8,128)(2,1)S(1)}) fusion(pred[32,5462]{1,0:T(8,128)(4,1)} %compare_reduce_fusion, pred[5462]{0:T(1024)(128)(4,1)S(1)} %broadcast_compare_fusion, bf16[32,768]{1,0:T(8,128)(2,1)S(1)} %all_gather.13, bf16[768,5462]{1,0:T(8,128)(2,1)} %all-gather.4.cloned.1.call-done), kind=kOutput, calls=%fused_computation.73 | convolution fusion | flops 271614336 | bytes 8968602 | tf_op jit(solution)/shard_map/dot_general | solution.py:1427
  205.4 0.8 pad_maximum_fusion
  206.2 0.1 abs_reduce_fusion
  206.4 0.1 clamp_convert_fusion
  206.6 0.9 fusion.38
  207.6 0.3 copy.61
  208.7 6.4 %fusion.68.in_ref = f32[32,768]{1,0:T(8,128)} fusion(bf16[32,5462]{1,0:T(8,128)(2,1)S(1)} %get-tuple-element.98, bf16[768,5462]{1,0:T(8,128)(2,1)} %all-gather.4.cloned.1.call-done), kind=kOutput, calls=%fused_computation.148 | convolution fusion | flops 268468224 | bytes 8837504 | tf_op jit(solution)/shard_map/gc,dc->gd/dot_general | solution.py:1439
  215.1 5.4 %class_sum.1 = f32[8,768]{1,0:T(8,128)} custom-call(f32[32,768]{1,0:T(8,128)} %fusion.68.in_ref), custom_call_target="tpu_custom_call" | custom-call | tf_op jit(solution)/shard_map/class_sum/pallas_call | solution.py:1086
  220.6 4.4 multiply_reduce_fusion
  225.0 1.5 fusion.64
  226.5 0.3 convert_reduce_fusion
  226.8 33.4 %mlp_backward.1 = (f32[4,768,768]{2,1,0:T(8,128)}, f32[4,768,768]{2,1,0:T(8,128)}, f32[1,3072]{1,0:T(1,128)S(1)}, f32[1024,768]{1,0:T(8,128)}) custom-call(bf16[1024,768]{1,0:T(8,128)(2,1)S(1)} %add_convert_fusion.2.x_ref, bf16[1024,768]{1,0:T(8,128)(2,1)S(1)} %get-tuple-element.81.dm_ref, bf16[8,768,768]{2,1,0:T(8,128)(2,1)} %get-tuple-element.36.up_ref.down_ref, ...), custom_call_target="tpu_custom_call" | custom-call | tf_op jit(solution)/shard_map/mlp_backward/pallas_call | solution.py:311
  260.2 3.1 multiply_reduce_fusion.1
  263.3 3.0 fusion.63
  266.3 0.6 convert_reduce_fusion.1
  266.9 1.0 copy-done.11
  268.0 1.4 convolution_convert_fusion.do_ref
  269.4 0.8 slice-done
  270.2 0.1 slice-done.1
  270.3 40.1 %attention_backward.1.refs_6_ = bf16[3,1024,768]{2,1,0:T(8,128)(2,1)S(1)} custom-call(s32[1,1024]{1,0:T(1,128)S(1)} %copy-done.3, s32[1024,1]{1,0:T(8,128)S(1)} %broadcast_select_fusion.kcodes_ref, bf16[3,1024,768]{2,1,0:T(8,128)(2,1)S(1)} %bitcast.77, bf16[3,1024,768]{2,1,0:T(8,128)(2,1)S(1)} %bitcast.77, bf16[3,1024,768]{2,1,0:T(8,128)(2,1)S(1)} %bitcast.77, ...), custom_call_target="tpu_custom_call" | custom-call | tf_op jit(solution)/shard_map/attention_backward/pallas_call | solution.py:206
  310.5 8.1 %fusion.1 = (f32[768]{0:T(1024)S(1)}, f32[1024]{0:T(1024)S(1)}, f32[768]{0:T(1024)S(1)}, f32[1024,768,1]{1,0,2:T(8,128)S(1)}) fusion(f32[768,1024]{0,1:T(8,128)} %copy-done.9, f32[1024]{0:T(1024)S(1)} %fusion.52, f32[1024]{0:T(1024)S(1)} %broadcast_multiply_fusion.3, f32[768]{0:T(1024)S(1)} %add.211, f32[768]{0:T(1024)S(1)} %mul.337, ...), kind=kOutput, calls=%fused_computation.12 | convolution fusion | flops 3630953984 | bytes 14575616 | tf_op jit(solution)/shard_map/kte,kde->td/dot_general | solution.py:383
  318.6 1.6 fusion.62
  320.3 0.4 copy-done.12
  320.6 2.0 convert_reduce_fusion.4
  322.7 0.5 convert_reduce_fusion.2
  323.3 0.5 broadcast.303
  323.8 0.7 reduce.52
  324.6 0.6 pad.13.refs_8_
  325.9 1.0 slice.154
  326.9 3.4 multiply_reduce_fusion.8
  330.3 0.7 maximum_bitcast_fusion
  331.0 0.1 copy.63
  331.1 0.6 pad.14.refs_9_
  331.7 129.6 %reduce_gradients.1 = (f32[13,96,768]{2,1,0:T(8,128)}, f32[13,96,768]{2,1,0:T(8,128)}, f32[13,96,768]{2,1,0:T(8,128)}, f32[13,96,768]{2,1,0:T(8,128)}, f32[13,1,...) custom-call(f32[4,768,768]{2,1,0:T(8,128)} %get-tuple-element.40.refs_0_, ...), custom_call_target="tpu_custom_call" | custom-call | tf_op jit(solution)/shard_map/reduce_gradients/pallas_call | solution.py:912
  461.4 1.3 fusion.66
  462.7 0.8 copy.70
  464.8 9.8 %multiply_subtract_fusion = (f32[13,96,768]{2,1,0:T(8,128)}, f32[13,96,768]{2,1,0:T(8,128)}) fusion(f32[13,96,768]{2,1,0:T(8,128)} %param.22, f32[13,96,768]{2,1,0:T(8,128)} %get-tuple-element.46, f32[13,768]{1,0:T(8,128)S(1)} %bitcast.84, f32[13,96,768]{2,1,0:T(8,128)} %get-tuple-element.48, f32[]{:T(128)} %bitcast.18), kind=kLoop, calls=%fused_computation.7 | loop fusion | flops 2875392 | bytes 19209220 | tf_op jit(solution)/shard_map/sub | solution.py:1522
  474.6 2.1 multiply_subtract_fusion.2
  476.7 4.6 multiply_subtract_fusion.1
  481.3 0.4 copy-done.17
  481.7 7.6 %multiply_add_fusion = (f32[13,96,768]{2,1,0:T(8,128)}, f32[13,96,768]{2,1,0:T(8,128)}) fusion(f32[13,96,768]{2,1,0:T(8,128)} %get-tuple-element.50, f32[13,96,768]{2,1,0:T(8,128)S(1)} %copy-done.16, f32[]{:T(128)S(6)} %mul.388, f32[13,96,768]{2,1,0:T(8,128)} %get-tuple-element.49, f32[13,96,768]{2,1,0:T(8,128)S(1)} %copy-done.17), kind=kLoop, calls=%fused_computation.5 | loop fusion | flops 5750784 | bytes 23003140 | tf_op jit(solution)/shard_map/add | solution.py:1525
  (116 shorter events, 2.1 us)
Async XLA Ops:
  7.2 192.4 %all-gather.4.cloned.1.call-start = ((), (), s32[]{:S(2)}) async-start(), calls=%async_computation | async-start | bytes 9510912 | tf_op jit(solution)/shard_map/all_gather | solution.py:1405
  9.9 316.0 %all-gather.6.cloned.1.call-start = ((), (), s32[]{:S(2)}) async-start(), calls=%async_computation.1 | async-start | bytes 3612672 | tf_op jit(solution)/shard_map/all_gather | solution.py:1444
  12.3 0.7 copy-start.20
  12.3 57.4 %copy-start.3 = (s32[1,1024]{1,0:T(1,128)S(1)}, s32[1,1024]{1,0:T(1,128)}, u32[]{:S(2)}) copy-start(s32[1,1024]{1,0:T(1,128)} %qids_ref.1) | copy-start | bytes 12292
  65.7 2.4 copy-start.4
  74.1 90.6 %copy-start.9 = (f32[768,1024]{0,1:T(8,128)}, f32[768,1024]{0,1:T(8,128)S(1)}, u32[]{:S(2)}) copy-start(f32[768,1024]{0,1:T(8,128)S(1)} %get-tuple-element.107) | copy-start | bytes 9437188
  74.1 0.7 copy-start.21
  75.5 7.1 %copy-start.14 = (bf16[1024,768]{1,0:T(8,128)(2,1)}, bf16[1024,768]{1,0:T(8,128)(2,1)S(1)}, u32[]{:S(2)}) copy-start(bf16[1024,768]{1,0:T(8,128)(2,1)S(1)} %add_convert_fusion.3.refs_3_) | copy-start | bytes 4718596
  82.6 82.0 %copy-start = (bf16[3,1024,768]{2,1,0:T(8,128)(2,1)}, bf16[3,1024,768]{2,1,0:T(8,128)(2,1)S(1)}, u32[]{:S(2)}) copy-start(bf16[3,1024,768]{2,1,0:T(8,128)(2,1)S(1)} %fusion.q_ref.k_ref.v_ref) | copy-start | bytes 14155780
  164.6 3.5 copy-start.2
  168.1 22.6 %copy-start.5 = (f32[1024,768]{1,0:T(8,128)}, f32[1024,768]{1,0:T(8,128)S(1)}, u32[]{:S(2)}) copy-start(f32[1024,768]{1,0:T(8,128)S(1)} %get-tuple-element.109) | copy-start | bytes 9437188
  191.1 2.2 copy-start.7
  191.2 7.5 %copy-start.24 = (s32[32,2]{0,1:T(2,128)S(1)}, s32[32,2]{0,1:T(2,128)}, u32[]{:S(2)}) copy-start(s32[32,2]{0,1:T(2,128)} %param.20) | copy-start | bytes 772
  206.2 125.6 %all-gather.8.cloned.1.call-start = ((), (), s32[]{:S(2)}) async-start(), calls=%async_computation.2 | async-start | bytes 10862592 | tf_op jit(solution)/shard_map/all_gather | solution.py:1418
  220.6 4.4 copy-start.8
  226.8 33.4 %copy-start.6 = (f32[1024,768]{1,0:T(8,128)S(1)}, f32[1024,768]{1,0:T(8,128)}, u32[]{:S(2)}) copy-start(f32[1024,768]{1,0:T(8,128)} %copy-done.5) | copy-start | bytes 9437188
  260.2 7.7 %slice-start.2 = ((s8[5898240]{0:T(1024)(128)(4,1)}), s8[4194304]{0:T(1024)(128)(4,1)S(1)}, s32[]{:S(2)}) async-start(s8[5898240]{0:T(1024)(128)(4,1)} %bitcast.82), calls=%async_computation.5 | async-start | bytes 8388608
  263.3 4.7 slice-start.3
  266.3 1.7 copy-start.11
  266.3 3.9 slice-start
  268.0 1.5 copy-start.15
  268.0 2.4 slice-start.1
  310.4 12.3 %copy-start.1 = (bf16[3,1024,768]{2,1,0:T(8,128)(2,1)}, bf16[3,1024,768]{2,1,0:T(8,128)(2,1)S(1)}, u32[]{:S(2)}) copy-start(bf16[3,1024,768]{2,1,0:T(8,128)(2,1)S(1)} %attention_backward.1.refs_6_) | copy-start | bytes 14155780
  310.4 8.2 %copy-start.10 = (f32[768,1024]{0,1:T(8,128)S(1)}, f32[768,1024]{0,1:T(8,128)}, u32[]{:S(2)}) copy-start(f32[768,1024]{0,1:T(8,128)} %copy-done.9) | copy-start | bytes 9437188
  318.6 2.0 copy-start.12
  464.8 9.9 %copy-start.22 = (f32[15,96]{1,0:T(8,128)S(1)}, f32[15,96]{1,0:T(8,128)}, u32[]{:S(2)}) copy-start(f32[15,96]{1,0:T(8,128)} %param.32) | copy-start | bytes 17284
  464.8 9.9 %copy-start.23 = (f32[15,96]{1,0:T(8,128)S(1)}, f32[15,96]{1,0:T(8,128)}, u32[]{:S(2)}) copy-start(f32[15,96]{1,0:T(8,128)} %param.31) | copy-start | bytes 17284
  464.8 11.9 %copy-start.13 = (f32[96,5462]{1,0:T(8,128)S(1)}, f32[96,5462]{1,0:T(8,128)}, u32[]{:S(2)}) copy-start(f32[96,5462]{1,0:T(8,128)} %param.27) | copy-start | bytes 6292228
  464.8 11.9 %copy-start.18 = (f32[96,5462]{1,0:T(8,128)S(1)}, f32[96,5462]{1,0:T(8,128)}, u32[]{:S(2)}) copy-start(f32[96,5462]{1,0:T(8,128)} %param.29) | copy-start | bytes 6292228
  464.8 11.9 %copy-start.19 = (f32[96,5462]{1,0:T(8,128)S(1)}, f32[96,5462]{1,0:T(8,128)}, u32[]{:S(2)}) copy-start(f32[96,5462]{1,0:T(8,128)} %param.28) | copy-start | bytes 6292228
  476.7 4.6 copy-start.16
  476.7 5.0 %copy-start.17 = (f32[13,96,768]{2,1,0:T(8,128)S(1)}, f32[13,96,768]{2,1,0:T(8,128)}, u32[]{:S(2)}) copy-start(f32[13,96,768]{2,1,0:T(8,128)} %param.23) | copy-start | bytes 11501572
Sparse Core Ops, SparseCore 0:
  10.8 162.2 all-gather.3
  206.3 63.0 all-gather.5
  271.6 56.8 all-gather.7

commit v8 on v7

--- a/solution.py
+++ b/solution.py
@@ -23,6 +23,10 @@
 SPAN = 48
 SHARES = 8
 GATHER_DEPTH = 4
+CLASS_TILE = 512
+ROW_CHUNK = 7 * 128
+EARLY_CHUNKS = 3
+LATE_CHUNKS = 4
 IMG_PACK = 8
 
 
@@ -104,12 +108,8 @@
         attention_tile(tile, q_ref, k_ref, v_ref, out_ref, bias_ref)
 
 
-def attention_backward_kernel(
-    qids_ref, kcodes_ref, q_ref, k_ref, v_ref, do_ref, out_ref, bias_ref, dk_ref, dv_ref
-):
-    length = q_ref.shape[0]
-    lane = lax.broadcasted_iota(jnp.int32, (QTILE, PAIR), 1)
-    scale = jnp.bfloat16(HEAD ** (-0.5))
+def attention_back_bias(qids_ref, kcodes_ref, bias_ref):
+    length = kcodes_ref.shape[0]
 
     @pl.when(pl.program_id(0) == 0)
     def _():
@@ -121,49 +121,81 @@
             same = kcodes_ref[low:high, :] == qids_ref[:, tile * QTILE : (tile + 1) * QTILE]
             bias_ref[tile, : high - low, :] = jnp.where(same | (rows == cols), 0.0, -1e30)
 
+
+def attention_back_tile(tile, q_ref, k_ref, v_ref, do_ref, out_ref, bias_ref, dk_ref, dv_ref):
+    length = q_ref.shape[0]
+    lane = lax.broadcasted_iota(jnp.int32, (QTILE, PAIR), 1)
+    scale = jnp.bfloat16(HEAD ** (-0.5))
+    low, high = key_window(tile, length)
+    rows = pl.ds(tile * QTILE, QTILE)
+    window = pl.ds(low, high - low)
+    queries = q_ref[rows, :] * scale
+    keys = k_ref[window, :]
+    values = v_ref[window, :]
+    grads = do_ref[rows, :]
+    halves = []
+    for head in range(2):
+        mine = (lane >= head * HEAD) & (lane < (head + 1) * HEAD)
+        picked = jnp.where(mine, queries, jnp.zeros_like(queries))
+        picked_grads = jnp.where(mine, grads, jnp.zeros_like(grads))
+        scores = lax.dot_general(
+            keys, picked, (((1,), (1,)), ((), ())), preferred_element_type=jnp.float32
+        )
+        scores = scores + bias_ref[tile, : high - low, :]
+        top = jnp.max(scores, 0, keepdims=True)
+        weights = jnp.exp(scores - top)
+        probs = weights * (1.0 / jnp.sum(weights, 0, keepdims=True))
+        grad_probs = lax.dot_general(
+            values, picked_grads, (((1,), (1,)), ((), ())), preferred_element_type=jnp.float32
+        )
+        inner = jnp.sum(probs * grad_probs, 0, keepdims=True)
+        grad_scores = (probs * (grad_probs - inner)).astype(jnp.bfloat16)
+        dv_ref[window, :] += jnp.dot(
+            probs.astype(jnp.bfloat16), picked_grads, preferred_element_type=jnp.float32
+        )
+        dk_ref[window, :] += jnp.dot(
+            grad_scores, picked, preferred_element_type=jnp.float32
+        )
+        halves.append(
+            lax.dot_general(
+                grad_scores,
+                keys,
+                (((0,), (0,)), ((), ())),
+                preferred_element_type=jnp.float32,
+            )
+        )
+    grad_queries = jnp.where(lane < HEAD, halves[0], halves[1]) * HEAD ** (-0.5)
+    out_ref[0, rows, :] = grad_queries.astype(jnp.bfloat16)
+
+
+def attention_backward_kernel(
+    qids_ref, kcodes_ref, q_ref, k_ref, v_ref, do_ref, *refs
+):
+    gathering = len(refs) > 4
+    if gathering:
+        own_ref, out_ref, rows_ref, bias_ref, dk_ref, dv_ref, send_sem, recv_sem, copy_sem = refs
+        pair, tiles = pl.program_id(0), q_ref.shape[0] // QTILE
+        slots = pl.num_programs(0) * tiles
+
+        pl.when(pair == 0)(column_barrier)
+        row_step, turns = row_steps(
+            EARLY_CHUNKS, own_ref, rows_ref, send_sem, recv_sem, copy_sem
+        )
+    else:
+        out_ref, bias_ref, dk_ref, dv_ref = refs
+    attention_back_bias(qids_ref, kcodes_ref, bias_ref)
     dk_ref[...] = jnp.zeros_like(dk_ref)
     dv_ref[...] = jnp.zeros_like(dv_ref)
-    for tile in range(length // QTILE):
-        low, high = key_window(tile, length)
-        rows = pl.ds(tile * QTILE, QTILE)
-        window = pl.ds(low, high - low)
-        queries = q_ref[rows, :] * scale
-        keys = k_ref[window, :]
-        values = v_ref[window, :]
-        grads = do_ref[rows, :]
-        halves = []
-        for head in range(2):
-            mine = (lane >= head * HEAD) & (lane < (head + 1) * HEAD)
-            picked = jnp.where(mine, queries, jnp.zeros_like(queries))
-            picked_grads = jnp.where(mine, grads, jnp.zeros_like(grads))
-            scores = lax.dot_general(
-                keys, picked, (((1,), (1,)), ((), ())), preferred_element_type=jnp.float32
-            )
-            scores = scores + bias_ref[tile, : high - low, :]
-            top = jnp.max(scores, 0, keepdims=True)
-            weights = jnp.exp(scores - top)
-            probs = weights * (1.0 / jnp.sum(weights, 0, keepdims=True))
-            grad_probs = lax.dot_general(
-                values, picked_grads, (((1,), (1,)), ((), ())), preferred_element_type=jnp.float32
-            )
-            inner = jnp.sum(probs * grad_probs, 0, keepdims=True)
-            grad_scores = (probs * (grad_probs - inner)).astype(jnp.bfloat16)
-            dv_ref[window, :] += jnp.dot(
-                probs.astype(jnp.bfloat16), picked_grads, preferred_element_type=jnp.float32
-            )
-            dk_ref[window, :] += jnp.dot(
-                grad_scores, picked, preferred_element_type=jnp.float32
-            )
-            halves.append(
-                lax.dot_general(
-                    grad_scores,
-                    keys,
-                    (((0,), (0,)), ((), ())),
-                    preferred_element_type=jnp.float32,
-                )
-            )
-        grad_queries = jnp.where(lane < HEAD, halves[0], halves[1]) * HEAD ** (-0.5)
-        out_ref[0, rows, :] = grad_queries.astype(jnp.bfloat16)
+    for tile in range(q_ref.shape[0] // QTILE):
+        if gathering:
+            slot = pair * tiles + tile
+            begin, end = slot * turns // slots, (slot + 1) * turns // slots
+
+            @pl.when(begin < end)
+            def _(begin=begin):
+                row_step(begin)
+
+        attention_back_tile(tile, q_ref, k_ref, v_ref, do_ref, out_ref, bias_ref, dk_ref, dv_ref)
     out_ref[1] = dk_ref[...].astype(jnp.bfloat16)
     out_ref[2] = dv_ref[...].astype(jnp.bfloat16)
 
@@ -199,26 +231,36 @@
     )(pack_ids[:, None], key_codes[None, :], qkv_rows, qkv_rows, qkv_rows)
 
 
-def attention_backward(qkv_rows, pack_ids, key_codes, grad_attended):
+def attention_backward(qkv_rows, pack_ids, key_codes, grad_attended, own_rows=None):
     _, length, width = qkv_rows.shape
-    tiles = length // QTILE
-    window = max(high - low for low, high in (key_window(t, length) for t in range(tiles)))
+    tiles, _, window = bias_shape(length)
+    out_shape = [jax.ShapeDtypeStruct((3, length, width), jnp.bfloat16)]
+    out_specs = [pl.BlockSpec((3, length, PAIR), lambda pair: (0, 0, pair))]
+    extra_in, extra_spec, extra_scratch, collective = [], [], [], {}
+    if own_rows is not None:
+        rows_shape, extra_scratch = row_operands(own_rows, LATE_CHUNKS)
+        out_shape.append(rows_shape)
+        out_specs.append(pl.BlockSpec(memory_space=pl.ANY))
+        extra_in, extra_spec = [own_rows], [whole_spec(own_rows.shape)]
+        collective = dict(collective_id=5, has_side_effects=True)
     return pl.pallas_call(
         attention_backward_kernel,
         grid=(width // PAIR,),
-        out_shape=jax.ShapeDtypeStruct((3, length, width), jnp.bfloat16),
+        out_shape=out_shape,
         in_specs=[whole_spec((1, length)), whole_spec((length, 1))]
         + [pair_spec(length, part) for part in range(3)]
-        + [pair_spec(length)],
-        out_specs=pl.BlockSpec((3, length, PAIR), lambda pair: (0, 0, pair)),
+        + [pair_spec(length)]
+        + extra_spec,
+        out_specs=out_specs,
         scratch_shapes=[
             pltpu.VMEM((tiles, window, QTILE), jnp.float32),
             pltpu.VMEM((length, PAIR), jnp.float32),
             pltpu.VMEM((length, PAIR), jnp.float32),
-        ],
-        compiler_params=pltpu.CompilerParams(vmem_limit_bytes=40 << 20),
+        ]
+        + extra_scratch,
+        compiler_params=pltpu.CompilerParams(vmem_limit_bytes=40 << 20, **collective),
         name="attention_backward",
-    )(pack_ids[None, :], key_codes[:, None], qkv_rows, qkv_rows, qkv_rows, grad_attended)
+    )(pack_ids[None, :], key_codes[:, None], qkv_rows, qkv_rows, qkv_rows, grad_attended, *extra_in)
 
 
 def mlp_forward_kernel(x_ref, up_ref, bias_ref, down_ref, units_ref, slope_ref, out_ref):
@@ -240,10 +282,16 @@
         out_ref[rows, :] += jnp.dot(units, down_ref[...], preferred_element_type=jnp.float32)
 
 
-def mlp_backward_kernel(
-    x_ref, dm_ref, up_ref, down_ref, units_ref, slope_ref,
-    grad_up_ref, grad_down_ref, bias_ref, dx_ref, dpre_ref
-):
+def mlp_backward_kernel(x_ref, dm_ref, up_ref, down_ref, units_ref, slope_ref, *refs):
+    if len(refs) > 5:
+        own_ref, grad_up_ref, grad_down_ref, bias_ref, dx_ref, rows_ref, dpre_ref, *sems = refs
+        turn = pl.program_id(0)
+        pl.when(turn == 0)(column_barrier)
+        row_step, turns = row_steps(0, own_ref, rows_ref, *sems)
+        pl.when(turn < turns)(lambda: row_step(turn))
+    else:
+        grad_up_ref, grad_down_ref, bias_ref, dx_ref, dpre_ref = refs
+
     @pl.when(pl.program_id(0) == 0)
     def _():
         dx_ref[...] = jnp.zeros_like(dx_ref)
@@ -303,31 +351,41 @@
     )(rows, blocks, up_bias.reshape(1, hidden_size), blocks)
 
 
-def mlp_backward(rows, grad_branch, blocks, units, slopes):
+def mlp_backward(rows, grad_branch, blocks, units, slopes, own_rows=None):
     length, width = rows.shape
     up_count = blocks.shape[0] // 2
     split, resident, up, down, hidden, bias = mlp_specs(length, width, up_count)
     hidden_size = up_count * width
+    out_shape = [
+        jax.ShapeDtypeStruct((up_count, width, width), jnp.float32),
+        jax.ShapeDtypeStruct((up_count, width, width), jnp.float32),
+        jax.ShapeDtypeStruct((1, hidden_size), jnp.float32),
+        jax.ShapeDtypeStruct((length, width), jnp.float32),
+    ]
+    out_specs = [
+        pl.BlockSpec((None, width, HIDDEN_TILE), lambda t: (t // split, 0, t % split)),
+        pl.BlockSpec((None, HIDDEN_TILE, width), lambda t: (t // split, t % split, 0)),
+        bias,
+        resident,
+    ]
+    extra_in, extra_spec, extra_scratch, collective = [], [], [], {}
+    if own_rows is not None:
+        assert EARLY_CHUNKS + 2 <= up_count * split
+        rows_shape, extra_scratch = row_operands(own_rows, EARLY_CHUNKS)
+        out_shape.append(rows_shape)
+        out_specs.append(pl.BlockSpec(memory_space=pl.ANY))
+        extra_in, extra_spec = [own_rows], [whole_spec(own_rows.shape)]
+        collective = dict(collective_id=6, has_side_effects=True)
     return pl.pallas_call(
         mlp_backward_kernel,
         grid=(up_count * split,),
-        out_shape=(
-            jax.ShapeDtypeStruct((up_count, width, width), jnp.float32),
-            jax.ShapeDtypeStruct((up_count, width, width), jnp.float32),
-            jax.ShapeDtypeStruct((1, hidden_size), jnp.float32),
-            jax.ShapeDtypeStruct((length, width), jnp.float32),
-        ),
-        in_specs=[resident, resident, up, down, hidden, hidden],
-        out_specs=(
-            pl.BlockSpec((None, width, HIDDEN_TILE), lambda t: (t // split, 0, t % split)),
-            pl.BlockSpec((None, HIDDEN_TILE, width), lambda t: (t // split, t % split, 0)),
-            bias,
-            resident,
-        ),
-        scratch_shapes=[pltpu.VMEM((length, HIDDEN_TILE), jnp.bfloat16)],
-        compiler_params=pltpu.CompilerParams(vmem_limit_bytes=48 << 20),
+        out_shape=out_shape,
+        in_specs=[resident, resident, up, down, hidden, hidden] + extra_spec,
+        out_specs=out_specs,
+        scratch_shapes=[pltpu.VMEM((length, HIDDEN_TILE), jnp.bfloat16)] + extra_scratch,
+        compiler_params=pltpu.CompilerParams(vmem_limit_bytes=48 << 20, **collective),
         name="mlp_backward",
-    )(rows, grad_branch, blocks, blocks, units, slopes)
+    )(rows, grad_branch, blocks, blocks, units, slopes, *extra_in)
 
 
 def layer_forward(blocks, vec_all, patch, attend):
@@ -364,13 +422,14 @@
     grad_output,
     grad_gain,
     grad_shift,
+    own_rows=None,
 ):
     embedded, normed_one, qkv_rows, attended, hidden, normed_two, slopes, units = saved
     feature_dim = patch.shape[1]
     up_count = mlp_blocks.shape[0] // 2
     grad_branch = grad_output.astype(jnp.bfloat16)
-    grad_up, grad_down, up_sums, grad_normed_two = mlp_backward(
-        normed_two, grad_branch, mlp_blocks, units, slopes
+    grad_up, grad_down, up_sums, grad_normed_two, *early = mlp_backward(
+        normed_two, grad_branch, mlp_blocks, units, slopes, own_rows
     )
     norm_two_back = jax.vjp(norm_rows, hidden, vec_all[6], vec_all[7])[1]
     grad_hidden_norm, grad_gain_two, grad_shift_two = norm_two_back(grad_normed_two)
@@ -379,7 +438,9 @@
     grad_attended = jnp.einsum(
         "td,ed->te", grad_attn_out, blocks[4], preferred_element_type=jnp.float32
     ).astype(jnp.bfloat16)
-    grad_qkv = attention_backward(qkv_rows, pack_ids, key_codes, grad_attended)
+    grad_qkv, *late = attention_backward(
+        qkv_rows, pack_ids, key_codes, grad_attended, own_rows
+    )
     grad_normed_one = jnp.einsum(
         "kte,kde->td", grad_qkv, blocks[1:4], preferred_element_type=jnp.float32
     )
@@ -402,7 +463,8 @@
     )
     up_sums = up_sums.reshape(up_count, feature_dim)
     tail_sums = jnp.stack([jnp.sum(grad_branch.astype(jnp.float32), 0), grad_gain, grad_shift])
-    return (lefts, rights, (grad_up, grad_down), jnp.concatenate([bias_sums, up_sums, tail_sums], 0))
+    grad_vectors = jnp.concatenate([bias_sums, up_sums, tail_sums], 0)
+    return (lefts, rights, (grad_up, grad_down), grad_vectors, early + late)
 
 
 def torus_place():
@@ -1047,55 +1109,199 @@
         squares_ref[1:2, cols] = jnp.sum(direction * direction, 0, keepdims=True)
 
 
-def class_sum_kernel(in_ref, out_ref, slots, send_sem, recv_sem):
+def head_kernel(
+    image_total, pooled_ref, labels_ref, head_hbm,
+    grad_ref, rows_ref, loss_ref,
+    head_buf, group_buf, total_buf, slots, load_sem, send_sem, recv_sem, sum_send, sum_recv
+):
     dp, cls = lax.axis_index("dp"), lax.axis_index("cls")
-    total, rows = slots.shape[0], slots.shape[1]
+    count, rows, width = slots.shape
+    images = count * rows
+    classes = head_buf.shape[1]
+    load = pltpu.make_async_copy(head_hbm, head_buf, load_sem)
+    load.start()
     barrier = pltpu.get_barrier_semaphore()
-    for n in range(1, total):
+    for n in range(1, count):
         pl.semaphore_signal(
-            barrier, inc=1, device_id=(dp, lax.rem(cls + n, total)), device_id_type=MESH
-        )
-    pl.semaphore_wait(barrier, total - 1)
-
-    def part(index):
-        return in_ref.at[pl.ds(pl.multiple_of(index * rows, 8), rows)]
-
-    def copy(n, slot):
-        mate = lax.rem(cls + n, total)
+            barrier, inc=1, device_id=(dp, lax.rem(cls + n, count)), device_id_type=MESH
+        )
+    pl.semaphore_wait(barrier, count - 1)
+
+    def part(ref, index):
+        return ref.at[pl.ds(pl.multiple_of(index * rows, 8), rows)]
+
+    def share(n, slot):
         return pltpu.make_async_remote_copy(
-            src_ref=part(mate), dst_ref=slots.at[slot],
+            src_ref=pooled_ref, dst_ref=part(group_buf, slot),
             send_sem=send_sem.at[n], recv_sem=recv_sem.at[slot],
+            device_id=(dp, lax.rem(cls + n, count)), device_id_type=MESH,
+        )
+
+    for n in range(1, count):
+        share(n, cls).start()
+    part(group_buf, cls)[...] = pooled_ref[...]
+    rows_ref[:, width + classes :] = jnp.zeros(
+        (images, rows_ref.shape[1] - width - classes), rows_ref.dtype
+    )
+    for n in range(1, count):
+        share(n, cls).wait_send()
+        share(n, lax.rem(cls + n, count)).wait_recv()
+    load.wait()
+    group = group_buf[...].astype(jnp.bfloat16)
+    rows_ref[:, :width] = group
+    loss = jnp.zeros((1, 1), jnp.float32)
+    total = jnp.zeros((images, width), jnp.float32)
+    for start in range(0, classes, CLASS_TILE):
+        stop = min(classes, start + CLASS_TILE)
+        weights = head_buf[:, start:stop]
+        logits = jnp.dot(group, weights, preferred_element_type=jnp.float32)
+        ids = lax.broadcasted_iota(jnp.int32, logits.shape, 1) + (cls * classes + start)
+        target = ids == labels_ref[:, 0:1]
+        for n in range(1, labels_ref.shape[1]):
+            target = target | (ids == labels_ref[:, n : n + 1])
+        target = target.astype(jnp.float32)
+        valid = ids < LABELS_REAL
+        shrunk = jnp.exp(-jnp.abs(logits))
+        terms = jnp.maximum(logits, 0.0) + jnp.log1p(shrunk) - target * logits
+        terms = jnp.where(valid, terms, 0.0)
+        loss = loss + jnp.sum(jnp.sum(terms, 0, keepdims=True), 1, keepdims=True)
+        chance = jnp.where(logits >= 0.0, 1.0, shrunk) / (1.0 + shrunk)
+        grads = jnp.where(valid, chance - target, 0.0) / image_total
+        grads = grads.astype(jnp.bfloat16)
+        rows_ref[:, width + start : width + stop] = grads
+        total = total + lax.dot_general(
+            grads, weights, (((1,), (1,)), ((), ())), preferred_element_type=jnp.float32
+        )
+    loss_ref[...] = jnp.broadcast_to(loss / image_total, loss_ref.shape)
+    total_buf[...] = total
+
+    def back(n, slot):
+        mate = lax.rem(cls + n, count)
+        return pltpu.make_async_remote_copy(
+            src_ref=part(total_buf, mate), dst_ref=slots.at[slot],
+            send_sem=sum_send.at[n], recv_sem=sum_recv.at[slot],
             device_id=(dp, mate), device_id_type=MESH,
         )
 
-    for n in range(1, total):
-        copy(n, cls).start()
-    slots[cls] = part(cls)[...]
-    for n in range(1, total):
-        copy(n, cls).wait_send()
-        copy(n, lax.rem(cls + n, total)).wait_recv()
+    for n in range(1, count):
+        back(n, cls).start()
+    slots[cls] = part(total_buf, cls)[...]
+    for n in range(1, count):
+        back(n, cls).wait_send()
+        back(n, lax.rem(cls + n, count)).wait_recv()
     value = slots[0]
-    for n in range(1, total):
+    for n in range(1, count):
         value = value + slots[n]
-    out_ref[...] = value
-
-
-def class_sum(values, cls_count):
-    rows = values.shape[0] // cls_count
+    grad_ref[...] = value
+
+
+def classify(pooled, labels, head_low, cls_count, image_total):
+    rows, width = pooled.shape
+    images, classes = rows * cls_count, head_low.shape[1]
+    wide = ROW_CHUNK * (EARLY_CHUNKS + LATE_CHUNKS)
+    assert wide >= width + classes
+    f32 = jnp.float32
     vmem = pl.BlockSpec(memory_space=pltpu.VMEM)
     return pl.pallas_call(
-        class_sum_kernel,
-        out_shape=jax.ShapeDtypeStruct((rows, values.shape[1]), jnp.float32),
-        in_specs=[vmem],
-        out_specs=vmem,
+        functools.partial(head_kernel, image_total),
+        out_shape=(
+            jax.ShapeDtypeStruct((rows, width), f32),
+            jax.ShapeDtypeStruct((images, wide), jnp.bfloat16),
+            jax.ShapeDtypeStruct((8, 128), f32),
+        ),
+        in_specs=[vmem, vmem, pl.BlockSpec(memory_space=pltpu.HBM)],
+        out_specs=(vmem, vmem, vmem),
         scratch_shapes=[
-            pltpu.VMEM((cls_count, rows, values.shape[1]), jnp.float32),
-            pltpu.SemaphoreType.DMA((cls_count,)),
-            pltpu.SemaphoreType.DMA((cls_count,)),
-        ],
-        compiler_params=pltpu.CompilerParams(collective_id=2, has_side_effects=True),
-        name="class_sum",
-    )(values)
+            pltpu.VMEM((width, classes), jnp.bfloat16),
+            pltpu.VMEM((images, width), f32),
+            pltpu.VMEM((images, width), f32),
+            pltpu.VMEM((cls_count, rows, width), f32),
+            pltpu.SemaphoreType.DMA,
+        ]
+        + [pltpu.SemaphoreType.DMA((cls_count,)) for _ in range(4)],
+        compiler_params=pltpu.CompilerParams(
+            collective_id=2, has_side_effects=True, vmem_limit_bytes=32 << 20
+        ),
+        name="classify",
+    )(pooled, labels, head_low)
+
+
+def column_barrier():
+    barrier = pltpu.get_barrier_semaphore()
+    for n in range(1, SHARES):
+        pl.semaphore_signal(barrier, inc=1, device_id=column_mate(n), device_id_type=MESH)
+    pl.semaphore_wait(barrier, SHARES - 1)
+
+
+def row_operands(own_rows, chunks):
+    shape = (SHARES, own_rows.shape[0], chunks * ROW_CHUNK)
+    scratch = [
+        pltpu.SemaphoreType.DMA((7, 2)),
+        pltpu.SemaphoreType.DMA((8, chunks)),
+        pltpu.SemaphoreType.DMA((2,)),
+    ]
+    return jax.ShapeDtypeStruct(shape, own_rows.dtype), scratch
+
+
+def row_steps(first, own_ref, out_ref, send_sem, recv_sem, copy_sem):
+    z, y, x, core = torus_place()
+    mate_y = torus_device(z, 1 - y, x, core)
+    count = recv_sem.shape[1]
+
+    def columns(m):
+        return pl.ds(pl.multiple_of(m * ROW_CHUNK, 128), ROW_CHUNK)
+
+    def own_columns(m):
+        return own_ref.at[:, pl.ds(pl.multiple_of((m + first) * ROW_CHUNK, 128), ROW_CHUNK)]
+
+    def copy(slot, arrival, m, source, target, mate):
+        return pltpu.make_async_remote_copy(
+            src_ref=source, dst_ref=target,
+            send_sem=send_sem.at[slot, m % 2], recv_sem=recv_sem.at[arrival, m],
+            device_id=mate, device_id_type=MESH,
+        )
+
+    def local(m):
+        return pltpu.make_async_copy(
+            own_columns(m), out_ref.at[z * 2 + y, :, columns(m)], copy_sem.at[m % 2]
+        )
+
+    def along(m, n, outgoing):
+        other = lax.rem(z + n, 4)
+        origin = z if outgoing else other
+        target = out_ref.at[origin * 2 + y, :, columns(m)]
+        mate = torus_device(other, y, x, core)
+        return copy(n - 1, origin, m, own_columns(m), target, mate)
+
+    def cross(m, n, outgoing):
+        block = out_ref.at[n * 2 + (y if outgoing else 1 - y), :, columns(m)]
+        return copy(3 + n, 4 + n, m, block, block, mate_y)
+
+    def step(t):
+        @pl.when(t < count)
+        def _():
+            local(t).start()
+            for n in range(1, 4):
+                along(t, n, True).start()
+
+        @pl.when((t >= 1) & (t < count + 1))
+        def _():
+            m = t - 1
+            local(m).wait()
+            for n in range(1, 4):
+                along(m, n, True).wait_send()
+                along(m, n, False).wait_recv()
+            for n in range(4):
+                cross(m, n, True).start()
+
+        @pl.when((t >= 2) & (t < count + 2))
+        def _():
+            m = t - 2
+            for n in range(4):
+                cross(m, n, True).wait_send()
+                cross(m, n, False).wait_recv()
+
+    return step, count + 2
 
 
 def gather_steps(own_ref, out_ref, send_sem, recv_sem, copy_sem):
@@ -1423,39 +1629,35 @@
             right_part, ("dp", "cls"), axis=1, tiled=True, axis_index_groups=half_groups
         )
     pooled = pool_rows(output, final_gain, final_shift, pack_ids, pack_keep)
-    group = lax.all_gather(pooled.astype(jnp.bfloat16), "cls", axis=0, tiled=True)
-    logits = jnp.dot(group, head_low, preferred_element_type=jnp.float32)
     class_dev = head_low.shape[1]
-    class_ids = cls_index * class_dev + jnp.arange(class_dev)
-    valid = class_ids[None, :] < LABELS_REAL
-    target = jnp.any(labels[:, :, None] == class_ids[None, None, :], 1).astype(jnp.float32)
     image_total = labels.shape[0] * dp_count
-    loss_part = (
-        jnp.sum(jnp.where(valid, jax.nn.softplus(logits) - target * logits, 0.0)) / image_total
-    )
-    grad_logits = (jnp.where(valid, jax.nn.sigmoid(logits) - target, 0.0) / image_total).astype(
-        jnp.bfloat16
-    )
-    group_grad = jnp.einsum("gc,dc->gd", grad_logits, head_low, preferred_element_type=jnp.float32)
     if on_torus:
-        grad_pooled = class_sum(group_grad, cls_count)
+        grad_pooled, own_rows, loss_rows = classify(
+            lax.reduce_precision(pooled, 8, 7), labels, head_low, cls_count, image_total
+        )
+        loss_part = loss_rows[0, 0]
     else:
+        group = lax.all_gather(pooled.astype(jnp.bfloat16), "cls", axis=0, tiled=True)
+        logits = jnp.dot(group, head_low, preferred_element_type=jnp.float32)
+        class_ids = cls_index * class_dev + jnp.arange(class_dev)
+        valid = class_ids[None, :] < LABELS_REAL
+        target = jnp.any(labels[:, :, None] == class_ids[None, None, :], 1).astype(jnp.float32)
+        terms = jax.nn.softplus(logits) - target * logits
+        loss_part = jnp.sum(jnp.where(valid, terms, 0.0)) / image_total
+        grad_logits = jnp.where(valid, jax.nn.sigmoid(logits) - target, 0.0) / image_total
+        grad_logits = grad_logits.astype(jnp.bfloat16)
+        group_grad = jnp.einsum(
+            "gc,dc->gd", grad_logits, head_low, preferred_element_type=jnp.float32
+        )
         grad_pooled = lax.psum_scatter(group_grad, "cls", scatter_dimension=0, tiled=True)
-    head_rows = lax.all_gather(
-        jnp.concatenate([group, grad_logits], 1), "dp", axis=0, tiled=True
-    )
-    pooled_all, grad_logits_all = head_rows[:, :feature_dim], head_rows[:, feature_dim:]
-    pooled_mine = lax.dynamic_slice_in_dim(pooled_all, dp_index * row_count, row_count, 1)
-    head_grad = jnp.einsum(
-        "gr,gc->rc", pooled_mine, grad_logits_all, preferred_element_type=jnp.float32
-    )
+        own_rows = jnp.concatenate([group, grad_logits], 1)
 
     def pool_local(rows_in, gain, shift):
         return pool_rows(rows_in, gain, shift, pack_ids, pack_keep)
 
     pool_back = jax.vjp(pool_local, output, final_gain, final_shift)[1]
     grad_output, grad_gain, grad_shift = pool_back(grad_pooled)
-    lefts, rights, mlp_grads, grad_vectors = layer_backward(
+    lefts, rights, mlp_grads, grad_vectors, gathered = layer_backward(
         blocks,
         mlp_blocks,
         vec_all,
@@ -1466,6 +1668,17 @@
         grad_output,
         grad_gain,
         grad_shift,
+        own_rows if on_torus else None,
+    )
+    if on_torus:
+        head_rows = jnp.concatenate(gathered, 2).reshape(image_total, -1)
+    else:
+        head_rows = lax.all_gather(own_rows, "dp", axis=0, tiled=True)
+    pooled_all = head_rows[:, :feature_dim]
+    grad_logits_all = head_rows[:, feature_dim : feature_dim + class_dev]
+    pooled_mine = lax.dynamic_slice_in_dim(pooled_all, dp_index * row_count, row_count, 1)
+    head_grad = jnp.einsum(
+        "gr,gc->rc", pooled_mine, grad_logits_all, preferred_element_type=jnp.float32
     )
 
     head_squares = jnp.sum(head_grad * head_grad)

time: 505 us -> 523 us (1.036)
  Pallas kernels: 365 us -> 397 us
  matrix products: 44.9 us -> 29.2 us
  local copies, waits for them, and re-layouts: 14.1 us -> 21.1 us
  blocking collectives: 5.23 us -> 0 us
    pallas_call x2, Pallas kernels: 38.8 us -> 62.6 us  [the longest x1 49.5 us: mlp_backward(): pl.pallas_call(mlp_backward_kernel, grid=(up_count * split,), out_shape=o...]
    dot_general x2 -> x0, matrix products: 12.2 us -> none  [the longest x1 6.43 us: on_device(): jnp.einsum('gc,dc->gd', grad_logits, head_low, preferred_element_type=jnp...]
    pallas_call x1, Pallas kernels: 40.1 us -> 52 us  [attention_backward(): pl.pallas_call(attention_backward_kernel, grid=(width // PAIR,), out_shap...]
    unnamed x59 -> x70, local copies, waits for them, and re-layouts: 6.64 us -> 12.2 us
  transfers between devices with their start and end apart: 3 -> 2, of which waited for: 0 -> 0; matrix products, arithmetic and copies ran while one was open for 14% -> 11% of each run, Pallas kernels for 47% -> 53%
where the time goes in v8:
time: 523 us; the launch traced here: 514 us
  Pallas kernels  397 us (76%)
  other arithmetic  48.6 us (9%)
  matrix products  29.2 us (6%)
  local copies, waits for them, and re-layouts  21.1 us (4%)
  between operations  17.3 us (3%)
    pallas_call x1, Pallas kernels, reduce_gradients(): pl.pallas_call(functools.partial(reduce_kernel, counts), out_shape=(jax.S...  128 us
    pallas_call x1, Pallas kernels, attention_forward_gathering(): pl.pallas_call(attention_gather_kernel, grid=(width // PAIR,), out_shape=...  79.9 us
    pallas_call x1, Pallas kernels, gather_weights(): pl.pallas_call(gather_kernel, out_shape=(jax.ShapeDtypeStruct((count, SHA...  54.6 us
    pallas_call x1, Pallas kernels, attention_backward(): pl.pallas_call(attention_backward_kernel, grid=(width // PAIR,), out_shap...  52 us
    pallas_call x1, Pallas kernels, mlp_backward(): pl.pallas_call(mlp_backward_kernel, grid=(up_count * split,), out_shape=o...  49.5 us
    pallas_call x1, Pallas kernels, mlp_forward(): pl.pallas_call(mlp_forward_kernel, grid=(up_count * split,), out_shape=(j...  20.8 us
    pallas_call x1, Pallas kernels, classify(): pl.pallas_call(functools.partial(head_kernel, image_total), out_shape=(ja...  13.2 us
    unnamed x70, local copies, waits for them, and re-layouts  12.2 us
  transfers between devices with their start and end apart: 2, of which 0 were waited for; matrix products, arithmetic and copies ran while one was open for 11% of the time, Pallas kernels for 53%

profile of v8, /device:TPU:0, one launch (start us, length us, event | category | flops | bytes accessed | tf_op | source)
XLA Modules:
  0.0 513.8 jit_solution(10371843539639603427)
XLA Ops:
  7.2 2.7 convert_element_type.76
  10.0 2.3 convert_element_type.70
  12.3 1.2 copy-done.19
  13.6 54.6 %gather_weights.1 = (bf16[5,768,768]{2,1,0:T(8,128)(2,1)S(1)}, f32[8,16,128]{2,1,0:T(8,128)S(1)}) custom-call(bf16[5,96,768]{2,1,0:T(8,128)(2,1)S(1)} %slice.142.own_ref, f32[16,128]{1,0:T(8,128)S(1)} %pad.12.vec_ref), custom_call_target="tpu_custom_call" | custom-call | tf_op jit(solution)/shard_map/gather_weights/pallas_call | solution.py:1502
  68.2 2.0 constant_dynamic-slice_fusion
  70.2 0.1 abs_reduce_fusion
  70.4 0.1 clamp_convert_fusion
  70.7 0.9 fusion.35
  71.7 1.4 slice.148.own_ref
  73.1 0.1 slice_reduce_fusion.1
  73.6 0.2 copy.58.qids_ref
  74.1 0.1 reshape.262.bias_ref
  74.4 0.1 copy.61.labels_ref
  74.5 0.3 copy.62
  75.6 2.7 add_reduce_fusion
  78.4 0.6 multiply_reduce_fusion.7
  79.0 0.6 add_convert_fusion.3.refs_3_
  79.7 1.1 copy-done.20
  80.8 6.1 %fusion.q_ref.k_ref.v_ref = bf16[3,1024,768]{2,1,0:T(8,128)(2,1)S(1)} fusion(f32[3,768]{1,0:T(4,128)S(1)} %pad_maximum_fusion.1, bf16[5,768,768]{2,1,0:T(8,128)(2,1)} %copy-done.5, bf16[1024,768]{1,0:T(8,128)(2,1)S(1)} %add_convert_fusion.3.refs_3_), kind=kOutput, calls=%fused_computation.4 | convolution fusion | flops 3628597248 | bytes 9839616 | tf_op jit(solution)/shard_map/td,kde->kte/dot_general | solution.py:394
  86.9 79.9 %attention_forward.1 = (bf16[1024,768]{1,0:T(8,128)(2,1)S(1)}, bf16[8,768,768]{2,1,0:T(8,128)(2,1)}) custom-call(s32[1024,1]{1,0:T(8,128)S(1)} %copy.58.qids_ref, s32[1,1024]{1,0:T(1,128)S(1)} %broadcast_select_fusion.1.kcodes_ref, bf16[3,1024,768]{2,1,0:T(8,128)(2,1)S(1)} %fusion.q_ref.k_ref.v_ref, bf16[3,1024,768]{2,1,0:T(8,128)(2,1)S(1)} %fusion.q_ref.k_ref.v_ref, ...), custom_call_target="tpu_custom_call" | custom-call | tf_op jit(solution)/shard_map/attention_forward/pallas_call | solution.py:1479
  166.8 3.4 fusion.64
  170.2 0.5 multiply_reduce_fusion.6
  170.7 0.6 add_convert_fusion.2.x_ref
  171.3 20.8 %mlp_forward.1 = (bf16[1024,3072]{1,0:T(8,128)(2,1)}, f32[1024,3072]{1,0:T(8,128)}, f32[1024,768]{1,0:T(8,128)S(1)}) custom-call(bf16[1024,768]{1,0:T(8,128)(2,1)S(1)} %add_convert_fusion.2.x_ref, bf16[8,768,768]{2,1,0:T(8,128)(2,1)} %get-tuple-element.42.up_ref.down_ref, f32[1,3072]{1,0:T(1,128)S(1)} %reshape.262.bias_ref, ...), custom_call_target="tpu_custom_call" | custom-call | tf_op jit(solution)/shard_map/mlp_forward/pallas_call | solution.py:339
  192.1 0.1 convert_reduce_fusion.5
  192.3 0.4 fusion.62
  192.7 0.5 multiply_reduce_fusion.5
  193.3 1.1 copy-done.8
  194.4 1.7 fusion.30.pooled_ref
  196.1 3.5 copy-done.2
  199.6 13.2 %classify.1 = (f32[8,768]{1,0:T(8,128)S(1)}, bf16[32,6272]{1,0:T(8,128)(2,1)S(1)}, f32[8,128]{1,0:T(8,128)S(1)}) custom-call(f32[8,768]{1,0:T(8,128)S(1)} %fusion.30.pooled_ref, s32[32,2]{1,0:T(8,128)S(1)} %copy.61.labels_ref, bf16[768,5462]{1,0:T(8,128)(2,1)S(1)} %copy-done.2), custom_call_target="tpu_custom_call" | custom-call | tf_op jit(solution)/shard_map/classify/pallas_call | solution.py:1205
  212.8 2.2 multiply_reduce_fusion
  215.0 1.4 fusion.61
  216.4 0.3 convert_reduce_fusion
  216.8 49.5 %mlp_backward.1 = (f32[4,768,768]{2,1,0:T(8,128)}, f32[4,768,768]{2,1,0:T(8,128)}, f32[1,3072]{1,0:T(1,128)S(1)}, f32[1024,768]{1,0:T(8,128)}, bf16[8,32,2688]{2,1,0:T(8,128)(2,1)S(1)}) custom-call(bf16[1024,768]{1,0:T(8,128)(2,1)S(1)} %add_convert_fusion.2.x_ref, bf16[1024,768]{1,0:T(8,128)(2,1)S(1)} %get-tuple-element.93.dm_ref, ...), custom_call_target="tpu_custom_call" | custom-call | tf_op jit(solution)/shard_map/mlp_backward/pallas_call | solution.py:379
  266.3 3.0 multiply_reduce_fusion.1
  269.3 1.6 fusion.60
  271.0 0.6 convert_reduce_fusion.1
  271.5 1.1 copy-done.14
  272.6 1.1 copy-done.21
  273.7 2.9 convolution_convert_fusion.do_ref
  276.7 52.0 %attention_backward.1 = (bf16[3,1024,768]{2,1,0:T(8,128)(2,1)S(1)}, bf16[8,32,3584]{2,1,0:T(8,128)(2,1)S(1)}) custom-call(s32[1,1024]{1,0:T(1,128)S(1)} %copy-done.4, s32[1024,1]{1,0:T(8,128)S(1)} %broadcast_select_fusion.kcodes_ref, bf16[3,1024,768]{2,1,0:T(8,128)(2,1)S(1)} %bitcast.74, bf16[3,1024,768]{2,1,0:T(8,128)(2,1)S(1)} %bitcast.74, ...), custom_call_target="tpu_custom_call" | custom-call | tf_op jit(solution)/shard_map/attention_backward/pallas_call | solution.py:246
  328.7 0.3 pad_maximum_fusion
  328.9 1.9 copy-done.1
  330.8 0.5 slice.134
  331.3 2.6 multiply_reduce_fusion.8
  334.0 1.4 maximum_bitcast_fusion
  335.3 0.1 copy.64
  335.4 0.6 pad.14.refs_9_
  336.0 7.6 %fusion.1 = (f32[768]{0:T(1024)S(1)}, f32[1024]{0:T(1024)S(1)}, f32[768]{0:T(1024)S(1)}, f32[1024,768,1]{1,0,2:T(8,128)S(1)}) fusion(f32[768,1024]{0,1:T(8,128)S(1)} %copy-done.13, f32[1024]{0:T(1024)S(1)} %fusion.49, f32[1024]{0:T(1024)S(1)} %broadcast_multiply_fusion.3, f32[768]{0:T(1024)S(1)} %add.190, f32[768]{0:T(1024)S(1)} %mul.331, ...), kind=kOutput, calls=%fused_computation.13 | convolution fusion | flops 3630953984 | bytes 14573568 | tf_op jit(solution)/shard_map/kte,kde->td/dot_general | solution.py:444
  343.7 1.8 fusion.59
  345.6 1.8 convert_reduce_fusion.4
  347.4 0.5 convert_reduce_fusion.2
  348.0 0.5 broadcast.282
  348.5 0.7 reduce.52
  349.2 0.1 concatenate.32
  349.3 0.6 pad.13.refs_8_
  349.9 127.5 %reduce_gradients.1 = (f32[13,96,768]{2,1,0:T(8,128)}, f32[13,96,768]{2,1,0:T(8,128)}, f32[13,96,768]{2,1,0:T(8,128)}, f32[13,96,768]{2,1,0:T(8,128)}, f32[13,1,...) custom-call(f32[4,768,768]{2,1,0:T(8,128)} %get-tuple-element.48.refs_0_, ...), custom_call_target="tpu_custom_call" | custom-call | tf_op jit(solution)/shard_map/reduce_gradients/pallas_call | solution.py:974
  477.5 1.3 fusion.63
  480.1 0.8 copy.71
  480.9 7.6 %multiply_subtract_fusion.1 = (f32[96,5462]{1,0:T(8,128)}, f32[96,5462]{1,0:T(8,128)}, f32[96,5462]{1,0:T(8,128)}) fusion(f32[96,5462]{1,0:T(8,128)S(1)} %copy-done.18, f32[]{:T(128)S(6)} %sub.74, f32[]{:T(128)S(6)} %sub.73, f32[96,5462]{1,0:T(8,128)} %get-tuple-element.123, f32[]{:T(128)} %bitcast.19, f32[96,5462]{1,0:T(8,128)} %param.29, f32[96,5462]{1,0:T(8,128)} %param.28), kind=kLoop, calls=%fused_computation.49 | loop fusion | flops 8389632 | bytes 14681868 | tf_op jit(solution)/shard_map/sub | solution.py:1525
  488.4 2.1 multiply_subtract_fusion.2
  490.5 8.5 %multiply_subtract_fusion = (f32[13,96,768]{2,1,0:T(8,128)}, f32[13,96,768]{2,1,0:T(8,128)}) fusion(f32[13,96,768]{2,1,0:T(8,128)S(1)} %copy-done.16, f32[13,96,768]{2,1,0:T(8,128)} %get-tuple-element.58, f32[13,768]{1,0:T(8,128)S(1)} %bitcast.83, f32[13,96,768]{2,1,0:T(8,128)} %get-tuple-element.60, f32[]{:T(128)} %bitcast.19), kind=kLoop, calls=%fused_computation.7 | loop fusion | flops 2875392 | bytes 19209220 | tf_op jit(solution)/shard_map/sub | solution.py:1735
  499.0 7.5 %multiply_add_fusion = (f32[13,96,768]{2,1,0:T(8,128)}, f32[13,96,768]{2,1,0:T(8,128)}) fusion(f32[13,96,768]{2,1,0:T(8,128)} %get-tuple-element.62, f32[13,96,768]{2,1,0:T(8,128)S(1)} %copy-done.22, f32[]{:T(128)S(6)} %mul.380, f32[13,96,768]{2,1,0:T(8,128)} %get-tuple-element.61, f32[13,96,768]{2,1,0:T(8,128)S(1)} %copy-done.23), kind=kLoop, calls=%fused_computation.5 | loop fusion | flops 5750784 | bytes 23003140 | tf_op jit(solution)/shard_map/add | solution.py:1738
  (119 shorter events, 1.8 us)
Async XLA Ops:
  7.2 188.9 %all-gather.3.cloned.1.call-start = ((), (), s32[]{:S(2)}) async-start(), calls=%async_computation | async-start | bytes 9510912 | tf_op jit(solution)/shard_map/all_gather | solution.py:1611
  9.9 340.0 %all-gather.5.cloned.1.call-start = ((), (), s32[]{:S(2)}) async-start(), calls=%async_computation.1 | async-start | bytes 10862592 | tf_op jit(solution)/shard_map/all_gather | solution.py:1624
  10.0 3.6 copy-start.25
  12.3 1.3 copy-start.19
  68.2 2.4 copy-start.5
  70.7 2.9 copy-start.4
  70.7 3.7 copy-start.29
  70.7 3.8 copy-start.26
  70.7 4.9 copy-start.24
  78.3 88.4 %copy-start.12 = (f32[768,1024]{0,1:T(8,128)}, f32[768,1024]{0,1:T(8,128)S(1)}, u32[]{:S(2)}) copy-start(f32[768,1024]{0,1:T(8,128)S(1)} %get-tuple-element.117) | copy-start | bytes 9437188
  79.7 1.1 copy-start.20
  86.9 79.9 %copy-start = (bf16[3,1024,768]{2,1,0:T(8,128)(2,1)}, bf16[3,1024,768]{2,1,0:T(8,128)(2,1)S(1)}, u32[]{:S(2)}) copy-start(bf16[3,1024,768]{2,1,0:T(8,128)(2,1)S(1)} %fusion.q_ref.k_ref.v_ref) | copy-start | bytes 14155780
  166.8 3.5 copy-start.3
  170.2 22.1 %copy-start.6 = (f32[1024,768]{1,0:T(8,128)}, f32[1024,768]{1,0:T(8,128)S(1)}, u32[]{:S(2)}) copy-start(f32[1024,768]{1,0:T(8,128)S(1)} %get-tuple-element.119) | copy-start | bytes 9437188
  192.7 1.7 copy-start.8
  196.1 3.5 copy-start.2
  199.6 13.2 %copy-start.9 = (f32[1024,768]{1,0:T(8,128)S(1)}, f32[1024,768]{1,0:T(8,128)}, u32[]{:S(2)}) copy-start(f32[1024,768]{1,0:T(8,128)} %copy-done.8) | copy-start | bytes 9437188
  216.4 54.5 %copy-start.10 = (f32[1024,768]{1,0:T(8,128)}, f32[1024,768]{1,0:T(8,128)S(1)}, u32[]{:S(2)}) copy-start(f32[1024,768]{1,0:T(8,128)S(1)} %get-tuple-element.103) | copy-start | bytes 9437188
  216.8 49.5 %copy-start.7 = (f32[1024,768]{1,0:T(8,128)S(1)}, f32[1024,768]{1,0:T(8,128)}, u32[]{:S(2)}) copy-start(f32[1024,768]{1,0:T(8,128)} %copy-done.6) | copy-start | bytes 9437188
  266.3 3.0 copy-start.17
  270.9 1.7 copy-start.14
  271.0 5.7 %slice-start = ((s8[4718592]{0:T(1024)(128)(4,1)}), s8[4194304]{0:T(1024)(128)(4,1)S(1)}, s32[]{:S(2)}) async-start(s8[4718592]{0:T(1024)(128)(4,1)} %bitcast.73), calls=%async_computation.2 | async-start | bytes 8388608
  272.6 1.1 copy-start.21
  273.7 2.9 slice-start.1
  328.6 2.1 copy-start.1
  330.8 5.3 %copy-start.13 = (f32[768,1024]{0,1:T(8,128)S(1)}, f32[768,1024]{0,1:T(8,128)}, u32[]{:S(2)}) copy-start(f32[768,1024]{0,1:T(8,128)} %copy-done.12) | copy-start | bytes 9437188
  336.0 9.5 %copy-start.15 = (f32[1024,768]{1,0:T(8,128)S(1)}, f32[1024,768]{1,0:T(8,128)}, u32[]{:S(2)}) copy-start(f32[1024,768]{1,0:T(8,128)} %copy-done.14) | copy-start | bytes 9437188
  343.7 1.9 copy-start.11
  343.7 3.7 slice-start.2
  345.6 1.9 slice-start.3
  349.9 130.9 %copy-start.18 = (f32[96,5462]{1,0:T(8,128)S(1)}, f32[96,5462]{1,0:T(8,128)}, u32[]{:S(2)}) copy-start(f32[96,5462]{1,0:T(8,128)} %param.27) | copy-start | bytes 6292228
  480.9 7.6 %copy-start.27 = (f32[15,96]{1,0:T(8,128)S(1)}, f32[15,96]{1,0:T(8,128)}, u32[]{:S(2)}) copy-start(f32[15,96]{1,0:T(8,128)} %param.32) | copy-start | bytes 17284
  480.9 7.6 %copy-start.28 = (f32[15,96]{1,0:T(8,128)S(1)}, f32[15,96]{1,0:T(8,128)}, u32[]{:S(2)}) copy-start(f32[15,96]{1,0:T(8,128)} %param.31) | copy-start | bytes 17284
  480.9 9.6 %copy-start.16 = (f32[13,96,768]{2,1,0:T(8,128)S(1)}, f32[13,96,768]{2,1,0:T(8,128)}, u32[]{:S(2)}) copy-start(f32[13,96,768]{2,1,0:T(8,128)} %param.22) | copy-start | bytes 11501572
  490.5 8.5 %copy-start.22 = (f32[13,96,768]{2,1,0:T(8,128)S(1)}, f32[13,96,768]{2,1,0:T(8,128)}, u32[]{:S(2)}) copy-start(f32[13,96,768]{2,1,0:T(8,128)} %param.24) | copy-start | bytes 11501572
  490.5 8.5 %copy-start.23 = (f32[13,96,768]{2,1,0:T(8,128)S(1)}, f32[13,96,768]{2,1,0:T(8,128)}, u32[]{:S(2)}) copy-start(f32[13,96,768]{2,1,0:T(8,128)} %param.23) | copy-start | bytes 11501572
Sparse Core Ops, SparseCore 0:
  10.8 162.9 all-gather.2
  175.4 64.6 all-gather.4

commit v9 on v8

--- a/solution.py
+++ b/solution.py
@@ -24,9 +24,6 @@
 SHARES = 8
 GATHER_DEPTH = 4
 CLASS_TILE = 512
-ROW_CHUNK = 7 * 128
-EARLY_CHUNKS = 3
-LATE_CHUNKS = 4
 IMG_PACK = 8
 
 
@@ -169,32 +166,12 @@
 
 
 def attention_backward_kernel(
-    qids_ref, kcodes_ref, q_ref, k_ref, v_ref, do_ref, *refs
+    qids_ref, kcodes_ref, q_ref, k_ref, v_ref, do_ref, out_ref, bias_ref, dk_ref, dv_ref
 ):
-    gathering = len(refs) > 4
-    if gathering:
-        own_ref, out_ref, rows_ref, bias_ref, dk_ref, dv_ref, send_sem, recv_sem, copy_sem = refs
-        pair, tiles = pl.program_id(0), q_ref.shape[0] // QTILE
-        slots = pl.num_programs(0) * tiles
-
-        pl.when(pair == 0)(column_barrier)
-        row_step, turns = row_steps(
-            EARLY_CHUNKS, own_ref, rows_ref, send_sem, recv_sem, copy_sem
-        )
-    else:
-        out_ref, bias_ref, dk_ref, dv_ref = refs
     attention_back_bias(qids_ref, kcodes_ref, bias_ref)
     dk_ref[...] = jnp.zeros_like(dk_ref)
     dv_ref[...] = jnp.zeros_like(dv_ref)
     for tile in range(q_ref.shape[0] // QTILE):
-        if gathering:
-            slot = pair * tiles + tile
-            begin, end = slot * turns // slots, (slot + 1) * turns // slots
-
-            @pl.when(begin < end)
-            def _(begin=begin):
-                row_step(begin)
-
         attention_back_tile(tile, q_ref, k_ref, v_ref, do_ref, out_ref, bias_ref, dk_ref, dv_ref)
     out_ref[1] = dk_ref[...].astype(jnp.bfloat16)
     out_ref[2] = dv_ref[...].astype(jnp.bfloat16)
@@ -231,36 +208,26 @@
     )(pack_ids[:, None], key_codes[None, :], qkv_rows, qkv_rows, qkv_rows)
 
 
-def attention_backward(qkv_rows, pack_ids, key_codes, grad_attended, own_rows=None):
+def attention_backward(qkv_rows, pack_ids, key_codes, grad_attended):
     _, length, width = qkv_rows.shape
-    tiles, _, window = bias_shape(length)
-    out_shape = [jax.ShapeDtypeStruct((3, length, width), jnp.bfloat16)]
-    out_specs = [pl.BlockSpec((3, length, PAIR), lambda pair: (0, 0, pair))]
-    extra_in, extra_spec, extra_scratch, collective = [], [], [], {}
-    if own_rows is not None:
-        rows_shape, extra_scratch = row_operands(own_rows, LATE_CHUNKS)
-        out_shape.append(rows_shape)
-        out_specs.append(pl.BlockSpec(memory_space=pl.ANY))
-        extra_in, extra_spec = [own_rows], [whole_spec(own_rows.shape)]
-        collective = dict(collective_id=5, has_side_effects=True)
+    tiles = length // QTILE
+    window = max(high - low for low, high in (key_window(t, length) for t in range(tiles)))
     return pl.pallas_call(
         attention_backward_kernel,
         grid=(width // PAIR,),
-        out_shape=out_shape,
+        out_shape=jax.ShapeDtypeStruct((3, length, width), jnp.bfloat16),
         in_specs=[whole_spec((1, length)), whole_spec((length, 1))]
         + [pair_spec(length, part) for part in range(3)]
-        + [pair_spec(length)]
-        + extra_spec,
-        out_specs=out_specs,
+        + [pair_spec(length)],
+        out_specs=pl.BlockSpec((3, length, PAIR), lambda pair: (0, 0, pair)),
         scratch_shapes=[
             pltpu.VMEM((tiles, window, QTILE), jnp.float32),
             pltpu.VMEM((length, PAIR), jnp.float32),
             pltpu.VMEM((length, PAIR), jnp.float32),
-        ]
-        + extra_scratch,
-        compiler_params=pltpu.CompilerParams(vmem_limit_bytes=40 << 20, **collective),
+        ],
+        compiler_params=pltpu.CompilerParams(vmem_limit_bytes=40 << 20),
         name="attention_backward",
-    )(pack_ids[None, :], key_codes[:, None], qkv_rows, qkv_rows, qkv_rows, grad_attended, *extra_in)
+    )(pack_ids[None, :], key_codes[:, None], qkv_rows, qkv_rows, qkv_rows, grad_attended)
 
 
 def mlp_forward_kernel(x_ref, up_ref, bias_ref, down_ref, units_ref, slope_ref, out_ref):
@@ -282,16 +249,10 @@
         out_ref[rows, :] += jnp.dot(units, down_ref[...], preferred_element_type=jnp.float32)
 
 
-def mlp_backward_kernel(x_ref, dm_ref, up_ref, down_ref, units_ref, slope_ref, *refs):
-    if len(refs) > 5:
-        own_ref, grad_up_ref, grad_down_ref, bias_ref, dx_ref, rows_ref, dpre_ref, *sems = refs
-        turn = pl.program_id(0)
-        pl.when(turn == 0)(column_barrier)
-        row_step, turns = row_steps(0, own_ref, rows_ref, *sems)
-        pl.when(turn < turns)(lambda: row_step(turn))
-    else:
-        grad_up_ref, grad_down_ref, bias_ref, dx_ref, dpre_ref = refs
-
+def mlp_backward_kernel(
+    x_ref, dm_ref, up_ref, down_ref, units_ref, slope_ref,
+    grad_up_ref, grad_down_ref, bias_ref, dx_ref, dpre_ref
+):
     @pl.when(pl.program_id(0) == 0)
     def _():
         dx_ref[...] = jnp.zeros_like(dx_ref)
@@ -351,41 +312,31 @@
     )(rows, blocks, up_bias.reshape(1, hidden_size), blocks)
 
 
-def mlp_backward(rows, grad_branch, blocks, units, slopes, own_rows=None):
+def mlp_backward(rows, grad_branch, blocks, units, slopes):
     length, width = rows.shape
     up_count = blocks.shape[0] // 2
     split, resident, up, down, hidden, bias = mlp_specs(length, width, up_count)
     hidden_size = up_count * width
-    out_shape = [
-        jax.ShapeDtypeStruct((up_count, width, width), jnp.float32),
-        jax.ShapeDtypeStruct((up_count, width, width), jnp.float32),
-        jax.ShapeDtypeStruct((1, hidden_size), jnp.float32),
-        jax.ShapeDtypeStruct((length, width), jnp.float32),
-    ]
-    out_specs = [
-        pl.BlockSpec((None, width, HIDDEN_TILE), lambda t: (t // split, 0, t % split)),
-        pl.BlockSpec((None, HIDDEN_TILE, width), lambda t: (t // split, t % split, 0)),
-        bias,
-        resident,
-    ]
-    extra_in, extra_spec, extra_scratch, collective = [], [], [], {}
-    if own_rows is not None:
-        assert EARLY_CHUNKS + 2 <= up_count * split
-        rows_shape, extra_scratch = row_operands(own_rows, EARLY_CHUNKS)
-        out_shape.append(rows_shape)
-        out_specs.append(pl.BlockSpec(memory_space=pl.ANY))
-        extra_in, extra_spec = [own_rows], [whole_spec(own_rows.shape)]
-        collective = dict(collective_id=6, has_side_effects=True)
     return pl.pallas_call(
         mlp_backward_kernel,
         grid=(up_count * split,),
-        out_shape=out_shape,
-        in_specs=[resident, resident, up, down, hidden, hidden] + extra_spec,
-        out_specs=out_specs,
-        scratch_shapes=[pltpu.VMEM((length, HIDDEN_TILE), jnp.bfloat16)] + extra_scratch,
-        compiler_params=pltpu.CompilerParams(vmem_limit_bytes=48 << 20, **collective),
+        out_shape=(
+            jax.ShapeDtypeStruct((up_count, width, width), jnp.float32),
+            jax.ShapeDtypeStruct((up_count, width, width), jnp.float32),
+            jax.ShapeDtypeStruct((1, hidden_size), jnp.float32),
+            jax.ShapeDtypeStruct((length, width), jnp.float32),
+        ),
+        in_specs=[resident, resident, up, down, hidden, hidden],
+        out_specs=(
+            pl.BlockSpec((None, width, HIDDEN_TILE), lambda t: (t // split, 0, t % split)),
+            pl.BlockSpec((None, HIDDEN_TILE, width), lambda t: (t // split, t % split, 0)),
+            bias,
+            resident,
+        ),
+        scratch_shapes=[pltpu.VMEM((length, HIDDEN_TILE), jnp.bfloat16)],
+        compiler_params=pltpu.CompilerParams(vmem_limit_bytes=48 << 20),
         name="mlp_backward",
-    )(rows, grad_branch, blocks, blocks, units, slopes, *extra_in)
+    )(rows, grad_branch, blocks, blocks, units, slopes)
 
 
 def layer_forward(blocks, vec_all, patch, attend):
@@ -422,15 +373,16 @@
     grad_output,
     grad_gain,
     grad_shift,
-    own_rows=None,
+    released,
 ):
     embedded, normed_one, qkv_rows, attended, hidden, normed_two, slopes, units = saved
     feature_dim = patch.shape[1]
     up_count = mlp_blocks.shape[0] // 2
     grad_branch = grad_output.astype(jnp.bfloat16)
-    grad_up, grad_down, up_sums, grad_normed_two, *early = mlp_backward(
-        normed_two, grad_branch, mlp_blocks, units, slopes, own_rows
+    grad_up, grad_down, up_sums, grad_normed_two = mlp_backward(
+        normed_two, grad_branch, mlp_blocks, units, slopes
     )
+    up_sums, released = lax.optimization_barrier((up_sums, released))
     norm_two_back = jax.vjp(norm_rows, hidden, vec_all[6], vec_all[7])[1]
     grad_hidden_norm, grad_gain_two, grad_shift_two = norm_two_back(grad_normed_two)
     grad_hidden = grad_output + grad_hidden_norm
@@ -438,9 +390,7 @@
     grad_attended = jnp.einsum(
         "td,ed->te", grad_attn_out, blocks[4], preferred_element_type=jnp.float32
     ).astype(jnp.bfloat16)
-    grad_qkv, *late = attention_backward(
-        qkv_rows, pack_ids, key_codes, grad_attended, own_rows
-    )
+    grad_qkv = attention_backward(qkv_rows, pack_ids, key_codes, grad_attended)
     grad_normed_one = jnp.einsum(
         "kte,kde->td", grad_qkv, blocks[1:4], preferred_element_type=jnp.float32
     )
@@ -464,7 +414,7 @@
     up_sums = up_sums.reshape(up_count, feature_dim)
     tail_sums = jnp.stack([jnp.sum(grad_branch.astype(jnp.float32), 0), grad_gain, grad_shift])
     grad_vectors = jnp.concatenate([bias_sums, up_sums, tail_sums], 0)
-    return (lefts, rights, (grad_up, grad_down), grad_vectors, early + late)
+    return (lefts, rights, (grad_up, grad_down), grad_vectors, released)
 
 
 def torus_place():
@@ -1198,8 +1148,8 @@
 def classify(pooled, labels, head_low, cls_count, image_total):
     rows, width = pooled.shape
     images, classes = rows * cls_count, head_low.shape[1]
-    wide = ROW_CHUNK * (EARLY_CHUNKS + LATE_CHUNKS)
-    assert wide >= width + classes
+    wide = width + classes
+    wide = wide + -wide % 128
     f32 = jnp.float32
     vmem = pl.BlockSpec(memory_space=pltpu.VMEM)
     return pl.pallas_call(
@@ -1220,88 +1170,10 @@
         ]
         + [pltpu.SemaphoreType.DMA((cls_count,)) for _ in range(4)],
         compiler_params=pltpu.CompilerParams(
-            collective_id=2, has_side_effects=True, vmem_limit_bytes=32 << 20
+            collective_id=2, has_side_effects=True, vmem_limit_bytes=60 << 20
         ),
         name="classify",
     )(pooled, labels, head_low)
-
-
-def column_barrier():
-    barrier = pltpu.get_barrier_semaphore()
-    for n in range(1, SHARES):
-        pl.semaphore_signal(barrier, inc=1, device_id=column_mate(n), device_id_type=MESH)
-    pl.semaphore_wait(barrier, SHARES - 1)
-
-
-def row_operands(own_rows, chunks):
-    shape = (SHARES, own_rows.shape[0], chunks * ROW_CHUNK)
-    scratch = [
-        pltpu.SemaphoreType.DMA((7, 2)),
-        pltpu.SemaphoreType.DMA((8, chunks)),
-        pltpu.SemaphoreType.DMA((2,)),
-    ]
-    return jax.ShapeDtypeStruct(shape, own_rows.dtype), scratch
-
-
-def row_steps(first, own_ref, out_ref, send_sem, recv_sem, copy_sem):
-    z, y, x, core = torus_place()
-    mate_y = torus_device(z, 1 - y, x, core)
-    count = recv_sem.shape[1]
-
-    def columns(m):
-        return pl.ds(pl.multiple_of(m * ROW_CHUNK, 128), ROW_CHUNK)
-
-    def own_columns(m):
-        return own_ref.at[:, pl.ds(pl.multiple_of((m + first) * ROW_CHUNK, 128), ROW_CHUNK)]
-
-    def copy(slot, arrival, m, source, target, mate):
-        return pltpu.make_async_remote_copy(
-            src_ref=source, dst_ref=target,
-            send_sem=send_sem.at[slot, m % 2], recv_sem=recv_sem.at[arrival, m],
-            device_id=mate, device_id_type=MESH,
-        )
-
-    def local(m):
-        return pltpu.make_async_copy(
-            own_columns(m), out_ref.at[z * 2 + y, :, columns(m)], copy_sem.at[m % 2]
-        )
-
-    def along(m, n, outgoing):
-        other = lax.rem(z + n, 4)
-        origin = z if outgoing else other
-        target = out_ref.at[origin * 2 + y, :, columns(m)]
-        mate = torus_device(other, y, x, core)
-        return copy(n - 1, origin, m, own_columns(m), target, mate)
-
-    def cross(m, n, outgoing):
-        block = out_ref.at[n * 2 + (y if outgoing else 1 - y), :, columns(m)]
-        return copy(3 + n, 4 + n, m, block, block, mate_y)
-
-    def step(t):
-        @pl.when(t < count)
-        def _():
-            local(t).start()
-            for n in range(1, 4):
-                along(t, n, True).start()
-
-        @pl.when((t >= 1) & (t < count + 1))
-        def _():
-            m = t - 1
-            local(m).wait()
-            for n in range(1, 4):
-                along(m, n, True).wait_send()
-                along(m, n, False).wait_recv()
-            for n in range(4):
-                cross(m, n, True).start()
-
-        @pl.when((t >= 2) & (t < count + 2))
-        def _():
-            m = t - 2
-            for n in range(4):
-                cross(m, n, True).wait_send()
-                cross(m, n, False).wait_recv()
-
-    return step, count + 2
 
 
 def gather_steps(own_ref, out_ref, send_sem, recv_sem, copy_sem):
@@ -1657,7 +1529,7 @@
 
     pool_back = jax.vjp(pool_local, output, final_gain, final_shift)[1]
     grad_output, grad_gain, grad_shift = pool_back(grad_pooled)
-    lefts, rights, mlp_grads, grad_vectors, gathered = layer_backward(
+    lefts, rights, mlp_grads, grad_vectors, (own_rows, roots) = layer_backward(
         blocks,
         mlp_blocks,
         vec_all,
@@ -1668,12 +1540,9 @@
         grad_output,
         grad_gain,
         grad_shift,
-        own_rows if on_torus else None,
+        (own_rows, right_codes if on_torus else right_half),
     )
-    if on_torus:
-        head_rows = jnp.concatenate(gathered, 2).reshape(image_total, -1)
-    else:
-        head_rows = lax.all_gather(own_rows, "dp", axis=0, tiled=True)
+    head_rows = lax.all_gather(own_rows, "dp", axis=0, tiled=True)
     pooled_all = head_rows[:, :feature_dim]
     grad_logits_all = head_rows[:, feature_dim : feature_dim + class_dev]
     pooled_mine = lax.dynamic_slice_in_dim(pooled_all, dp_index * row_count, row_count, 1)
@@ -1687,7 +1556,7 @@
         tail = jnp.pad(jnp.stack([head_squares, loss_part])[:, None], ((0, 6), (0, 127)))
         block_rows, left_add, right_add, direction, wide_scale, facts, vector_sum = (
             reduce_gradients(
-                mlp_grads, lefts, rights, padded, tail, root_left, right_codes,
+                mlp_grads, lefts, rights, padded, tail, root_left, roots,
                 dp_count, cls_count,
             )
         )
@@ -1708,7 +1577,7 @@
         grad_half = reduced_half(jnp.concatenate(first_grads + list(mlp_grads), 0), half_groups)
         vector_sum = lax.psum(grad_vectors, ("dp", "cls"))
         left_add, right_add, direction, block_rows = preconditioned_rows(
-            grad_half, root_left, right_half, (dp_index % half_dp) * row_count
+            grad_half, root_left, roots, (dp_index % half_dp) * row_count
         )
         squares = jnp.sum(split_halves(direction * direction, half_size), (1, 3))
         in_top = (dp_index < half_dp).astype(jnp.float32)

time: 523 us -> 498 us (0.952)
  Pallas kernels: 397 us -> 374 us
    pallas_call x1, Pallas kernels: 49.5 us -> 33.2 us  [mlp_backward(): pl.pallas_call(mlp_backward_kernel, grid=(up_count * split,), out_shape=(...]
    pallas_call x1, Pallas kernels: 52 us -> 40.4 us  [attention_backward(): pl.pallas_call(attention_backward_kernel, grid=(width // PAIR,), out_shap...]
    unnamed x70 -> x66, local copies, waits for them, and re-layouts: 12.2 us -> 7.92 us
  transfers between devices with their start and end apart: 2 -> 3, of which waited for: 0 -> 0; matrix products, arithmetic and copies ran while one was open for 11% -> 12% of each run, Pallas kernels for 53% -> 49%
where the time goes in v9:
time: 498 us; the launch traced here: 493 us
  Pallas kernels  374 us (75%)
  other arithmetic  49.8 us (10%)
  matrix products  33.7 us (7%)
  local copies, waits for them, and re-layouts  18.7 us (4%)
  between operations  16.7 us (3%)
    pallas_call x1, Pallas kernels, reduce_gradients(): pl.pallas_call(functools.partial(reduce_kernel, counts), out_shape=(jax.S...  130 us
    pallas_call x1, Pallas kernels, attention_forward_gathering(): pl.pallas_call(attention_gather_kernel, grid=(width // PAIR,), out_shape=...  79.8 us
    pallas_call x1, Pallas kernels, gather_weights(): pl.pallas_call(gather_kernel, out_shape=(jax.ShapeDtypeStruct((count, SHA...  54.6 us
    pallas_call x1, Pallas kernels, attention_backward(): pl.pallas_call(attention_backward_kernel, grid=(width // PAIR,), out_shap...  40.4 us
    pallas_call x1, Pallas kernels, mlp_backward(): pl.pallas_call(mlp_backward_kernel, grid=(up_count * split,), out_shape=(...  33.2 us
    pallas_call x1, Pallas kernels, mlp_forward(): pl.pallas_call(mlp_forward_kernel, grid=(up_count * split,), out_shape=(j...  21.4 us
    pallas_call x1, Pallas kernels, classify(): pl.pallas_call(functools.partial(head_kernel, image_total), out_shape=(ja...  14.5 us
  transfers between devices with their start and end apart: 3, of which 0 were waited for; matrix products, arithmetic and copies ran while one was open for 12% of the time, Pallas kernels for 49%

profile of v9, /device:TPU:0, one launch (start us, length us, event | category | flops | bytes accessed | tf_op | source)
XLA Modules:
  0.0 493.1 jit_solution(17082908536804956656)
XLA Ops:
  7.2 2.7 convert_element_type.76
  10.0 2.3 convert_element_type.70
  12.3 1.2 copy-done.18
  13.6 54.6 %gather_weights.1 = (bf16[5,768,768]{2,1,0:T(8,128)(2,1)S(1)}, f32[8,16,128]{2,1,0:T(8,128)S(1)}) custom-call(bf16[5,96,768]{2,1,0:T(8,128)(2,1)S(1)} %slice.142.own_ref, f32[16,128]{1,0:T(8,128)S(1)} %pad.12.vec_ref), custom_call_target="tpu_custom_call" | custom-call | tf_op jit(solution)/shard_map/gather_weights/pallas_call | solution.py:1374
  68.2 2.0 constant_dynamic-slice_fusion
  70.2 0.1 abs_reduce_fusion
  70.4 0.1 clamp_convert_fusion
  70.7 0.9 fusion.35
  71.7 1.4 slice.148.own_ref
  73.1 0.1 slice_reduce_fusion.1
  73.6 0.2 copy.58.qids_ref
  74.1 0.1 reshape.259.bias_ref
  74.4 0.7 copy.61.labels_ref
  75.2 3.2 add_reduce_fusion
  78.4 0.6 multiply_reduce_fusion.7
  79.2 0.6 add_convert_fusion.3.refs_3_
  79.8 6.6 %fusion.q_ref.k_ref.v_ref = bf16[3,1024,768]{2,1,0:T(8,128)(2,1)S(1)} fusion(f32[3,768]{1,0:T(4,128)S(1)} %pad_maximum_fusion, bf16[5,768,768]{2,1,0:T(8,128)(2,1)} %copy-done.4, bf16[1024,768]{1,0:T(8,128)(2,1)S(1)} %add_convert_fusion.3.refs_3_), kind=kOutput, calls=%fused_computation.4 | convolution fusion | flops 3628597248 | bytes 9839616 | tf_op jit(solution)/shard_map/td,kde->kte/dot_general | solution.py:345
  86.5 79.8 %attention_forward.1 = (bf16[1024,768]{1,0:T(8,128)(2,1)S(1)}, bf16[8,768,768]{2,1,0:T(8,128)(2,1)}) custom-call(s32[1024,1]{1,0:T(8,128)S(1)} %copy.58.qids_ref, s32[1,1024]{1,0:T(1,128)S(1)} %broadcast_select_fusion.1.kcodes_ref, bf16[3,1024,768]{2,1,0:T(8,128)(2,1)S(1)} %fusion.q_ref.k_ref.v_ref, bf16[3,1024,768]{2,1,0:T(8,128)(2,1)S(1)} %fusion.q_ref.k_ref.v_ref, ...), custom_call_target="tpu_custom_call" | custom-call | tf_op jit(solution)/shard_map/attention_forward/pallas_call | solution.py:1351
  166.4 3.4 fusion.64
  169.8 0.5 multiply_reduce_fusion.6
  170.4 0.6 add_convert_fusion.2.x_ref
  170.9 21.4 %mlp_forward.1 = (bf16[1024,3072]{1,0:T(8,128)(2,1)}, f32[1024,3072]{1,0:T(8,128)}, f32[1024,768]{1,0:T(8,128)S(1)}) custom-call(bf16[1024,768]{1,0:T(8,128)(2,1)S(1)} %add_convert_fusion.2.x_ref, bf16[8,768,768]{2,1,0:T(8,128)(2,1)} %get-tuple-element.42.up_ref.down_ref, f32[1,3072]{1,0:T(1,128)S(1)} %reshape.259.bias_ref, ...), custom_call_target="tpu_custom_call" | custom-call | tf_op jit(solution)/shard_map/mlp_forward/pallas_call | solution.py:300
  192.4 0.1 convert_reduce_fusion.5
  192.5 0.4 fusion.62
  193.0 0.5 multiply_reduce_fusion.5
  193.5 1.1 copy-done.7
  194.6 2.3 fusion.30.pooled_ref
  196.9 14.5 %classify.1 = (f32[8,768]{1,0:T(8,128)}, bf16[32,6272]{1,0:T(8,128)(2,1)}, f32[8,128]{1,0:T(8,128)}) custom-call(f32[8,768]{1,0:T(8,128)} %fusion.30.pooled_ref, s32[32,2]{1,0:T(8,128)} %copy.61.labels_ref, bf16[768,5462]{1,0:T(8,128)(2,1)} %all-gather.4.cloned.1.call-done.head_hbm), custom_call_target="tpu_custom_call" | custom-call | tf_op jit(solution)/shard_map/classify/pallas_call | solution.py:1155
  211.4 4.2 multiply_reduce_fusion
  215.6 1.5 fusion.61
  217.2 0.3 convert_reduce_fusion
  217.5 1.3 copy-done.9
  218.8 33.2 %mlp_backward.1 = (f32[4,768,768]{2,1,0:T(8,128)}, f32[4,768,768]{2,1,0:T(8,128)}, f32[1,3072]{1,0:T(1,128)S(1)}, f32[1024,768]{1,0:T(8,128)}) custom-call(bf16[1024,768]{1,0:T(8,128)(2,1)S(1)} %add_convert_fusion.2.x_ref, bf16[1024,768]{1,0:T(8,128)(2,1)S(1)} %get-tuple-element.93.dm_ref, bf16[8,768,768]{2,1,0:T(8,128)(2,1)} %get-tuple-element.42.up_ref.down_ref, ...), custom_call_target="tpu_custom_call" | custom-call | tf_op jit(solution)/shard_map/mlp_backward/pallas_call | solution.py:320
  252.0 0.3 copy.62
  253.1 1.3 slice.137
  254.5 4.2 multiply_reduce_fusion.1
  258.7 1.5 fusion.60
  260.3 0.3 copy-done.10
  260.6 0.5 convert_reduce_fusion.1
  261.2 0.8 copy-done.13
  261.9 1.1 copy-done.20
  263.1 1.4 convolution_convert_fusion.do_ref
  264.5 40.4 %attention_backward.1.refs_6_ = bf16[3,1024,768]{2,1,0:T(8,128)(2,1)S(1)} custom-call(s32[1,1024]{1,0:T(1,128)S(1)} %copy-done.3, s32[1024,1]{1,0:T(8,128)S(1)} %broadcast_select_fusion.kcodes_ref, bf16[3,1024,768]{2,1,0:T(8,128)(2,1)S(1)} %bitcast.73, bf16[3,1024,768]{2,1,0:T(8,128)(2,1)S(1)} %bitcast.73, bf16[3,1024,768]{2,1,0:T(8,128)(2,1)S(1)} %bitcast.73, ...), custom_call_target="tpu_custom_call" | custom-call | tf_op jit(solution)/shard_map/attention_backward/pallas_call | solution.py:215
  304.9 8.1 %fusion.1 = (f32[768]{0:T(1024)S(1)}, f32[1024]{0:T(1024)S(1)}, f32[768]{0:T(1024)S(1)}, f32[1024,768,1]{1,0,2:T(8,128)S(1)}) fusion(f32[768,1024]{0,1:T(8,128)} %copy-done.11, f32[1024]{0:T(1024)S(1)} %fusion.49, f32[1024]{0:T(1024)S(1)} %broadcast_multiply_fusion.3, f32[768]{0:T(1024)S(1)} %add.190, f32[768]{0:T(1024)S(1)} %mul.331, ...), kind=kOutput, calls=%fused_computation.12 | convolution fusion | flops 3630953984 | bytes 14575616 | tf_op jit(solution)/shard_map/kte,kde->td/dot_general | solution.py:394
  313.1 1.6 fusion.59
  314.7 0.3 copy-done.14
  314.9 1.8 convert_reduce_fusion.4
  316.8 0.5 convert_reduce_fusion.2
  317.4 0.5 broadcast.282
  317.9 0.7 reduce.52
  318.6 0.1 concatenate.34
  318.7 0.6 pad.13.refs_8_
  319.3 1.0 slice.161
  320.3 4.4 multiply_reduce_fusion.8
  324.8 1.4 maximum_bitcast_fusion
  326.1 0.1 copy.64
  326.2 0.6 pad.14.refs_9_
  326.8 130.2 %reduce_gradients.1 = (f32[13,96,768]{2,1,0:T(8,128)}, f32[13,96,768]{2,1,0:T(8,128)}, f32[13,96,768]{2,1,0:T(8,128)}, f32[13,96,768]{2,1,0:T(8,128)}, f32[13,1,...) custom-call(f32[4,768,768]{2,1,0:T(8,128)} %get-tuple-element.47.refs_0_, ...), custom_call_target="tpu_custom_call" | custom-call | tf_op jit(solution)/shard_map/reduce_gradients/pallas_call | solution.py:924
  457.0 1.3 fusion.63
  459.6 0.8 copy.71
  460.4 7.6 %multiply_subtract_fusion.1 = (f32[96,5462]{1,0:T(8,128)}, f32[96,5462]{1,0:T(8,128)}, f32[96,5462]{1,0:T(8,128)}) fusion(f32[96,5462]{1,0:T(8,128)S(1)} %copy-done.17, f32[]{:T(128)S(6)} %sub.74, f32[]{:T(128)S(6)} %sub.73, f32[96,5462]{1,0:T(8,128)} %get-tuple-element.123, f32[]{:T(128)} %bitcast.18, f32[96,5462]{1,0:T(8,128)} %param.29, f32[96,5462]{1,0:T(8,128)} %param.28), kind=kLoop, calls=%fused_computation.48 | loop fusion | flops 8389632 | bytes 14681868 | tf_op jit(solution)/shard_map/sub | solution.py:1397
  468.0 2.1 multiply_subtract_fusion.2
  470.1 8.7 %multiply_subtract_fusion = (f32[13,96,768]{2,1,0:T(8,128)}, f32[13,96,768]{2,1,0:T(8,128)}) fusion(f32[13,96,768]{2,1,0:T(8,128)S(1)} %copy-done.15, f32[13,96,768]{2,1,0:T(8,128)} %get-tuple-element.58, f32[13,768]{1,0:T(8,128)S(1)} %bitcast.80, f32[13,96,768]{2,1,0:T(8,128)} %get-tuple-element.60, f32[]{:T(128)} %bitcast.18), kind=kLoop, calls=%fused_computation.7 | loop fusion | flops 2875392 | bytes 19209220 | tf_op jit(solution)/shard_map/sub | solution.py:1604
  478.8 7.6 %multiply_add_fusion = (f32[13,96,768]{2,1,0:T(8,128)}, f32[13,96,768]{2,1,0:T(8,128)}) fusion(f32[13,96,768]{2,1,0:T(8,128)} %get-tuple-element.62, f32[13,96,768]{2,1,0:T(8,128)S(1)} %copy-done.21, f32[]{:T(128)S(6)} %mul.380, f32[13,96,768]{2,1,0:T(8,128)} %get-tuple-element.61, f32[13,96,768]{2,1,0:T(8,128)S(1)} %copy-done.22), kind=kLoop, calls=%fused_computation.5 | loop fusion | flops 5750784 | bytes 23003140 | tf_op jit(solution)/shard_map/add | solution.py:1607
  (117 shorter events, 1.9 us)
Async XLA Ops:
  7.2 189.7 %all-gather.4.cloned.1.call-start = ((), (), s32[]{:S(2)}) async-start(), calls=%async_computation | async-start | bytes 9510912 | tf_op jit(solution)/shard_map/all_gather | solution.py:1483
  9.9 242.0 %all-gather.6.cloned.1.call-start = ((), (), s32[]{:S(2)}) async-start(), calls=%async_computation.1 | async-start | bytes 10862592 | tf_op jit(solution)/shard_map/all_gather | solution.py:1496
  10.0 3.6 copy-start.23
  12.3 1.3 copy-start.18
  68.2 2.4 copy-start.4
  70.7 3.0 copy-start.3
  70.7 3.7 copy-start.27
  71.7 247.6 %all-gather.8.cloned.1.call-start = ((), (), s32[]{:S(2)}) async-start(), calls=%async_computation.2 | async-start | bytes 3612672 | tf_op jit(solution)/shard_map/all_gather | solution.py:1545
  78.4 88.0 %copy-start.11 = (f32[768,1024]{0,1:T(8,128)}, f32[768,1024]{0,1:T(8,128)S(1)}, u32[]{:S(2)}) copy-start(f32[768,1024]{0,1:T(8,128)S(1)} %get-tuple-element.117) | copy-start | bytes 9437188
  78.4 0.7 copy-start.24
  79.8 6.6 %copy-start.19 = (bf16[1024,768]{1,0:T(8,128)(2,1)}, bf16[1024,768]{1,0:T(8,128)(2,1)S(1)}, u32[]{:S(2)}) copy-start(bf16[1024,768]{1,0:T(8,128)(2,1)S(1)} %add_convert_fusion.3.refs_3_) | copy-start | bytes 4718596
  86.5 79.9 %copy-start = (bf16[3,1024,768]{2,1,0:T(8,128)(2,1)}, bf16[3,1024,768]{2,1,0:T(8,128)(2,1)S(1)}, u32[]{:S(2)}) copy-start(bf16[3,1024,768]{2,1,0:T(8,128)(2,1)S(1)} %fusion.q_ref.k_ref.v_ref) | copy-start | bytes 14155780
  166.4 3.5 copy-start.2
  169.8 22.7 %copy-start.5 = (f32[1024,768]{1,0:T(8,128)}, f32[1024,768]{1,0:T(8,128)S(1)}, u32[]{:S(2)}) copy-start(f32[1024,768]{1,0:T(8,128)S(1)} %get-tuple-element.119) | copy-start | bytes 9437188
  192.9 1.7 copy-start.7
  211.4 4.3 copy-start.8
  217.1 1.7 copy-start.9
  253.0 5.6 %copy-start.6 = (f32[1024,768]{1,0:T(8,128)S(1)}, f32[1024,768]{1,0:T(8,128)}, u32[]{:S(2)}) copy-start(f32[1024,768]{1,0:T(8,128)} %copy-done.5) | copy-start | bytes 9437188
  253.1 5.6 %copy-start.16 = (f32[1024,768]{1,0:T(8,128)S(1)}, f32[1024,768]{1,0:T(8,128)}, u32[]{:S(2)}) copy-start(f32[1024,768]{1,0:T(8,128)} %get-tuple-element.49) | copy-start | bytes 9437188
  254.5 8.6 %slice-start.2 = ((s8[5898240]{0:T(1024)(128)(4,1)}), s8[4194304]{0:T(1024)(128)(4,1)S(1)}, s32[]{:S(2)}) async-start(s8[5898240]{0:T(1024)(128)(4,1)} %bitcast.78), calls=%async_computation.5 | async-start | bytes 8388608
  258.7 1.9 copy-start.10
  258.7 4.4 slice-start.3
  260.3 1.7 copy-start.13
  260.6 3.9 slice-start
  261.9 1.1 copy-start.20
  263.1 1.5 slice-start.1
  304.9 11.9 %copy-start.1 = (bf16[3,1024,768]{2,1,0:T(8,128)(2,1)}, bf16[3,1024,768]{2,1,0:T(8,128)(2,1)S(1)}, u32[]{:S(2)}) copy-start(bf16[3,1024,768]{2,1,0:T(8,128)(2,1)S(1)} %attention_backward.1.refs_6_) | copy-start | bytes 14155780
  304.9 8.1 %copy-start.12 = (f32[768,1024]{0,1:T(8,128)S(1)}, f32[768,1024]{0,1:T(8,128)}, u32[]{:S(2)}) copy-start(f32[768,1024]{0,1:T(8,128)} %copy-done.11) | copy-start | bytes 9437188
  313.1 1.9 copy-start.14
  326.8 133.6 %copy-start.17 = (f32[96,5462]{1,0:T(8,128)S(1)}, f32[96,5462]{1,0:T(8,128)}, u32[]{:S(2)}) copy-start(f32[96,5462]{1,0:T(8,128)} %param.27) | copy-start | bytes 6292228
  460.4 7.6 %copy-start.25 = (f32[15,96]{1,0:T(8,128)S(1)}, f32[15,96]{1,0:T(8,128)}, u32[]{:S(2)}) copy-start(f32[15,96]{1,0:T(8,128)} %param.32) | copy-start | bytes 17284
  460.4 7.6 %copy-start.26 = (f32[15,96]{1,0:T(8,128)S(1)}, f32[15,96]{1,0:T(8,128)}, u32[]{:S(2)}) copy-start(f32[15,96]{1,0:T(8,128)} %param.31) | copy-start | bytes 17284
  460.4 9.7 %copy-start.15 = (f32[13,96,768]{2,1,0:T(8,128)S(1)}, f32[13,96,768]{2,1,0:T(8,128)}, u32[]{:S(2)}) copy-start(f32[13,96,768]{2,1,0:T(8,128)} %param.22) | copy-start | bytes 11501572
  470.1 8.7 %copy-start.21 = (f32[13,96,768]{2,1,0:T(8,128)S(1)}, f32[13,96,768]{2,1,0:T(8,128)}, u32[]{:S(2)}) copy-start(f32[13,96,768]{2,1,0:T(8,128)} %param.24) | copy-start | bytes 11501572
  470.1 8.7 %copy-start.22 = (f32[13,96,768]{2,1,0:T(8,128)S(1)}, f32[13,96,768]{2,1,0:T(8,128)}, u32[]{:S(2)}) copy-start(f32[13,96,768]{2,1,0:T(8,128)} %param.23) | copy-start | bytes 11501572
Sparse Core Ops, SparseCore 0:
  10.8 163.0 all-gather.3
  175.4 59.1 all-gather.5
  252.1 62.9 all-gather.7

commit v10 on v9

--- a/solution.py
+++ b/solution.py
@@ -283,9 +283,9 @@
 def mlp_specs(length, width, up_count):
     split = width // HIDDEN_TILE
     resident = pl.BlockSpec((length, width), lambda t: (0, 0))
-    up = pl.BlockSpec((None, width, HIDDEN_TILE), lambda t: (t // split, 0, t % split))
+    up = pl.BlockSpec((None, width, HIDDEN_TILE), lambda t: (5 + t // split, 0, t % split))
     down = pl.BlockSpec(
-        (None, HIDDEN_TILE, width), lambda t: (up_count + t // split, t % split, 0)
+        (None, HIDDEN_TILE, width), lambda t: (5 + up_count + t // split, t % split, 0)
     )
     hidden = pl.BlockSpec((length, HIDDEN_TILE), lambda t: (0, t))
     bias = pl.BlockSpec((1, HIDDEN_TILE), lambda t: (0, t))
@@ -294,7 +294,7 @@
 
 def mlp_forward(rows, blocks, up_bias):
     length, width = rows.shape
-    up_count = blocks.shape[0] // 2
+    up_count = (blocks.shape[0] - 5) // 2
     split, resident, up, down, hidden, bias = mlp_specs(length, width, up_count)
     hidden_size = up_count * width
     return pl.pallas_call(
@@ -314,7 +314,7 @@
 
 def mlp_backward(rows, grad_branch, blocks, units, slopes):
     length, width = rows.shape
-    up_count = blocks.shape[0] // 2
+    up_count = (blocks.shape[0] - 5) // 2
     split, resident, up, down, hidden, bias = mlp_specs(length, width, up_count)
     hidden_size = up_count * width
     return pl.pallas_call(
@@ -339,7 +339,8 @@
     )(rows, grad_branch, blocks, blocks, units, slopes)
 
 
-def layer_forward(blocks, vec_all, patch, attend):
+def layer_forward(blocks, vec_all, patch, pack_ids, key_codes):
+    up_count = (blocks.shape[0] - 5) // 2
     embedded = jnp.dot(patch, blocks[0], preferred_element_type=jnp.float32) + vec_all[0]
     normed_one = norm_rows(embedded, vec_all[1], vec_all[2]).astype(jnp.bfloat16)
     qkv_rows = jnp.einsum(
@@ -347,24 +348,21 @@
     )
     qkv_bias = jnp.stack([vec_all[3], jnp.zeros_like(vec_all[3]), vec_all[4]])
     qkv_rows = (qkv_rows + qkv_bias[:, None, :]).astype(jnp.bfloat16)
-    attended, mlp_blocks = attend(qkv_rows)
-    up_count = mlp_blocks.shape[0] // 2
+    attended = attention_forward(qkv_rows, pack_ids, key_codes)
     hidden = (
         embedded + jnp.dot(attended, blocks[4], preferred_element_type=jnp.float32) + vec_all[5]
     )
     normed_two = norm_rows(hidden, vec_all[6], vec_all[7]).astype(jnp.bfloat16)
-    units, slopes, branch = mlp_forward(normed_two, mlp_blocks, vec_all[8 : 8 + up_count])
+    units, slopes, branch = mlp_forward(normed_two, blocks, vec_all[8 : 8 + up_count])
     output = hidden + branch + vec_all[8 + up_count]
     return (
         output,
-        mlp_blocks,
         (embedded, normed_one, qkv_rows, attended, hidden, normed_two, slopes, units),
     )
 
 
 def layer_backward(
     blocks,
-    mlp_blocks,
     vec_all,
     patch,
     saved,
@@ -377,10 +375,10 @@
 ):
     embedded, normed_one, qkv_rows, attended, hidden, normed_two, slopes, units = saved
     feature_dim = patch.shape[1]
-    up_count = mlp_blocks.shape[0] // 2
+    up_count = (blocks.shape[0] - 5) // 2
     grad_branch = grad_output.astype(jnp.bfloat16)
     grad_up, grad_down, up_sums, grad_normed_two = mlp_backward(
-        normed_two, grad_branch, mlp_blocks, units, slopes
+        normed_two, grad_branch, blocks, units, slopes
     )
     up_sums, released = lax.optimization_barrier((up_sums, released))
     norm_two_back = jax.vjp(norm_rows, hidden, vec_all[6], vec_all[7])[1]
@@ -1319,54 +1317,6 @@
     ]
 
 
-def attention_gather_kernel(
-    qids_ref, kcodes_ref, q_ref, k_ref, v_ref, own_ref, out_ref, blocks_ref,
-    bias_ref, send_sem, recv_sem, copy_sem
-):
-    pair, tiles = pl.program_id(0), q_ref.shape[0] // QTILE
-    slots = pl.num_programs(0) * tiles
-
-    @pl.when(pair == 0)
-    def _():
-        gather_barrier()
-
-    gather_step, turns = gather_steps(own_ref, blocks_ref, send_sem, recv_sem, copy_sem)
-    attention_bias(qids_ref, kcodes_ref, bias_ref)
-    for tile in range(tiles):
-        slot = pair * tiles + tile
-        begin, end = slot * turns // slots, (slot + 1) * turns // slots
-
-        @pl.when(begin < end)
-        def _(begin=begin):
-            gather_step(begin)
-
-        attention_tile(tile, q_ref, k_ref, v_ref, out_ref, bias_ref)
-
-
-def attention_forward_gathering(qkv_rows, pack_ids, key_codes, own):
-    _, length, width = qkv_rows.shape
-    count, rows, _ = own.shape
-    tiles = length // QTILE
-    assert count + GATHER_DEPTH <= tiles * (width // PAIR)
-    return pl.pallas_call(
-        attention_gather_kernel,
-        grid=(width // PAIR,),
-        out_shape=(
-            jax.ShapeDtypeStruct((length, width), jnp.bfloat16),
-            jax.ShapeDtypeStruct((count, SHARES * rows, width), own.dtype),
-        ),
-        in_specs=[whole_spec((length, 1)), whole_spec((1, length))]
-        + [pair_spec(length, part) for part in range(3)]
-        + [whole_spec(own.shape)],
-        out_specs=(pair_spec(length), pl.BlockSpec(memory_space=pl.ANY)),
-        scratch_shapes=[pltpu.VMEM(bias_shape(length), jnp.float32)] + gather_semaphores(count),
-        compiler_params=pltpu.CompilerParams(
-            collective_id=4, has_side_effects=True, vmem_limit_bytes=40 << 20
-        ),
-        name="attention_forward",
-    )(pack_ids[:, None], key_codes[None, :], qkv_rows, qkv_rows, qkv_rows, own)
-
-
 def gather_weights(own, vec):
     count, rows, width = own.shape
     hbm = pl.BlockSpec(memory_space=pl.ANY)
@@ -1382,7 +1332,7 @@
         scratch_shapes=gather_semaphores(count)
         + [pltpu.SemaphoreType.DMA((SHARES,)), pltpu.SemaphoreType.DMA((SHARES,))],
         compiler_params=pltpu.CompilerParams(
-            collective_id=3, has_side_effects=True, vmem_limit_bytes=32 << 20
+            collective_id=3, has_side_effects=True, vmem_limit_bytes=60 << 20
         ),
         name="gather_weights",
     )(own, vec)
@@ -1400,6 +1350,66 @@
 def split_halves(values, half_size):
     block_count, row_count, feature_dim = values.shape
     return values.reshape(block_count, row_count, 2, half_size)
+
+
+def finish_kernel(
+    facts_ref, wide_ref, own_ref, left_add_ref, right_add_ref, step_ref, enc_ref, left_ref, right_ref,
+    new_ref, grad_ref, new_left_ref, new_right_ref
+):
+    factor = facts_ref[2:3, 0:1]
+    share = 0.5 * factor * factor
+    new_ref[...] = enc_ref[...] - step_ref[...] * wide_ref[...]
+    grad_ref[...] = own_ref[...] * factor
+    new_left_ref[...] = 0.5 * left_ref[...] + share * left_add_ref[...]
+    new_right_ref[...] = 0.5 * right_ref[...] + share * right_add_ref[...]
+
+
+def finish_blocks(facts, wide_scale, *arrays):
+    count, rows, width = arrays[0].shape
+    block = pl.BlockSpec((None, rows, width), lambda b: (b, 0, 0))
+    return pl.pallas_call(
+        finish_kernel,
+        grid=(count,),
+        out_shape=(jax.ShapeDtypeStruct((count, rows, width), jnp.float32),) * 4,
+        in_specs=[
+            pl.BlockSpec(facts.shape, lambda b: (0, 0)),
+            pl.BlockSpec((None, 1, width), lambda b: (b, 0, 0)),
+        ]
+        + [block] * len(arrays),
+        out_specs=(block,) * 4,
+        compiler_params=pltpu.CompilerParams(vmem_limit_bytes=32 << 20),
+        name="finish_blocks",
+    )(facts, wide_scale, *arrays)
+
+
+def adam_kernel(
+    facts_ref, fixes_ref, weight_ref, grad_ref, first_ref, second_ref,
+    new_ref, new_first_ref, new_second_ref
+):
+    grad = grad_ref[...] * facts_ref[2:3, 0:1]
+    weight = weight_ref[...]
+    first = BETA_FIRST * first_ref[...] + (1.0 - BETA_FIRST) * grad
+    second = BETA_SECOND * second_ref[...] + (1.0 - BETA_SECOND) * grad * grad
+    root = jnp.sqrt(second / fixes_ref[1:2, 0:1]) + ADAM_EPS
+    update = first / fixes_ref[0:1, 0:1] / root + WEIGHT_DECAY * weight
+    new_ref[...] = weight - ADAM_RATE * update
+    new_first_ref[...] = first
+    new_second_ref[...] = second
+
+
+def adam_rows(facts, fixes, *arrays):
+    rows, width = arrays[0].shape
+    block = pl.BlockSpec((8, width), lambda r: (r, 0))
+    small = pl.BlockSpec(facts.shape, lambda r: (0, 0))
+    return pl.pallas_call(
+        adam_kernel,
+        grid=(rows // 8,),
+        out_shape=(jax.ShapeDtypeStruct((rows, width), jnp.float32),) * 3,
+        in_specs=[small, small] + [block] * 4,
+        out_specs=(block,) * 3,
+        compiler_params=pltpu.CompilerParams(vmem_limit_bytes=32 << 20),
+        name="adam_rows",
+    )(facts, fixes, *arrays)
 
 
 def reduced_half(values, half_groups):
@@ -1468,16 +1478,15 @@
     if on_torus:
         vec_block = jnp.pad(vectors, ((0, -vectors.shape[0] % 8), (0, -row_count % 128)))
         own_low = enc_weights.astype(jnp.bfloat16)
-        blocks, vec_blocks = gather_weights(own_low[:5], vec_block)
+        blocks, vec_blocks = gather_weights(own_low, vec_block)
         right_part, vec_blocks = lax.optimization_barrier((my_part(root_right), vec_blocks))
         vec_low = jnp.transpose(vec_blocks[:, : vectors.shape[0], :row_count], (1, 0, 2))
         vec_all = lax.reduce_precision(vec_low.reshape(vectors.shape[0], feature_dim), 8, 7)
     else:
         right_part = my_part(root_right)
-        all_blocks = lax.all_gather(
+        blocks = lax.all_gather(
             my_part(enc_weights.astype(jnp.bfloat16)), ("dp", "cls"), axis=1, tiled=True
         )
-        blocks = all_blocks[:5]
         vec_low = lax.all_gather(vectors.astype(jnp.bfloat16), "dp", axis=1, tiled=True)
         vec_all = vec_low.astype(jnp.float32)
     head_low = lax.all_gather(head_weights.astype(jnp.bfloat16), "dp", axis=0, tiled=True)
@@ -1486,12 +1495,7 @@
     pack_ids, pack_keep = image_ids[0], keep[0]
     key_codes = jnp.where(pack_keep == 1, pack_ids, -1)
 
-    def attend(qkv_rows):
-        if on_torus:
-            return attention_forward_gathering(qkv_rows, pack_ids, key_codes, own_low[5:])
-        return attention_forward(qkv_rows, pack_ids, key_codes), all_blocks[5:]
-
-    output, mlp_blocks, saved = layer_forward(blocks, vec_all, patches, attend)
+    output, saved = layer_forward(blocks, vec_all, patches, pack_ids, key_codes)
     if on_torus:
         right_codes = lax.all_gather(
             encode_roots(right_part), ("dp", "cls"), axis=0, axis_index_groups=half_groups
@@ -1531,7 +1535,6 @@
     grad_output, grad_gain, grad_shift = pool_back(grad_pooled)
     lefts, rights, mlp_grads, grad_vectors, (own_rows, roots) = layer_backward(
         blocks,
-        mlp_blocks,
         vec_all,
         patches,
         saved,
@@ -1601,20 +1604,32 @@
         scale = SHAMPOO_RATE * factor * lax.rsqrt(mean_squares + ROOT_EPS)
         wide_scale = jnp.repeat(scale, half_size, axis=1)[:, None, :]
     vector_rows = lax.dynamic_slice_in_dim(vector_sum, dp_index * row_count, row_count, 1)
-    new_blocks = enc_weights - direction * wide_scale
-    square_factor = 0.5 * factor * factor
-    new_left = 0.5 * stats_left + square_factor * left_add
-    new_right = 0.5 * stats_right + square_factor * right_add
     count = step.astype(jnp.float32)
     new_vec, new_vec_m, new_vec_v = adam_step(vectors, vector_rows * factor, vec_m, vec_v, count)
-    new_head, new_head_m, new_head_v = adam_step(
-        head_weights, head_grad * factor, head_m, head_v, count
-    )
+    if on_torus:
+        new_blocks, block_clip, new_left, new_right = finish_blocks(
+            facts, wide_scale, block_rows, left_add, right_add, direction,
+            enc_weights, stats_left, stats_right,
+        )
+        fixes = jnp.stack([1.0 - jnp.power(BETA_FIRST, count), 1.0 - jnp.power(BETA_SECOND, count)])
+        fixes = jnp.broadcast_to(jnp.pad(fixes, (0, 6))[:, None], facts.shape)
+        new_head, new_head_m, new_head_v = adam_rows(
+            facts, fixes, head_weights, head_grad, head_m, head_v
+        )
+    else:
+        block_clip = block_rows * factor
+        new_blocks = enc_weights - direction * wide_scale
+        square_factor = 0.5 * factor * factor
+        new_left = 0.5 * stats_left + square_factor * left_add
+        new_right = 0.5 * stats_right + square_factor * right_add
+        new_head, new_head_m, new_head_v = adam_step(
+            head_weights, head_grad * factor, head_m, head_v, count
+        )
     return (
         loss,
         grad_norm,
         new_blocks,
-        block_rows * factor,
+        block_clip,
         new_left,
         new_right,
         new_vec,

time: 498 us -> 505 us (1.014)
  other arithmetic: 49.8 us -> 27.1 us
  Pallas kernels: 374 us -> 395 us
  local copies, waits for them, and re-layouts: 18.7 us -> 26.4 us
    pallas_call x1, Pallas kernels: 54.6 us -> 112 us  [gather_weights(): pl.pallas_call(gather_kernel, out_shape=(jax.ShapeDtypeStruct((count, SHA...]
    pallas_call x1 -> x3, Pallas kernels: 79.8 us -> 44 us  [the longest x1 25.6 us: attention_forward(): pl.pallas_call(attention_forward_kernel, grid=(width // PAIR,), out_shape...]
    unnamed x66 -> x75, local copies, waits for them, and re-layouts: 7.92 us -> 17.3 us
    sub x1 -> x0, other arithmetic: 8.67 us -> none  [on_device(): new_blocks = enc_weights - direction * wide_scale]
    add x1 -> x0, other arithmetic: 7.62 us -> none  [on_device(): new_right = 0.5 * stats_right + square_factor * right_add]
    sub x2 -> x1, other arithmetic: 9.66 us -> 2.07 us  [adam_step(): return (weight - ADAM_RATE * update, first, second)]
  transfers between devices with their start and end apart: 3 -> 3, of which waited for: 0 -> 0; matrix products, arithmetic and copies ran while one was open for 12% -> 12% of each run, Pallas kernels for 49% -> 50%
where the time goes in v10:
time: 505 us; the launch traced here: 499 us
  Pallas kernels  395 us (78%)
  matrix products  35.2 us (7%)
  other arithmetic  27.1 us (5%)
  local copies, waits for them, and re-layouts  26.4 us (5%)
  between operations  15.4 us (3%)
    pallas_call x1, Pallas kernels, reduce_gradients(): pl.pallas_call(functools.partial(reduce_kernel, counts), out_shape=(jax.S...  129 us
    pallas_call x1, Pallas kernels, gather_weights(): pl.pallas_call(gather_kernel, out_shape=(jax.ShapeDtypeStruct((count, SHA...  112 us
    pallas_call x1, Pallas kernels, attention_backward(): pl.pallas_call(attention_backward_kernel, grid=(width // PAIR,), out_shap...  40.1 us
    pallas_call x1, Pallas kernels, mlp_backward(): pl.pallas_call(mlp_backward_kernel, grid=(up_count * split,), out_shape=(...  33.4 us
    pallas_call x1, Pallas kernels, attention_forward(): pl.pallas_call(attention_forward_kernel, grid=(width // PAIR,), out_shape...  25.6 us
    pallas_call x1, Pallas kernels, mlp_forward(): pl.pallas_call(mlp_forward_kernel, grid=(up_count * split,), out_shape=(j...  21.5 us
    unnamed x75, local copies, waits for them, and re-layouts  17.3 us
    pallas_call x1, Pallas kernels, classify(): pl.pallas_call(functools.partial(head_kernel, image_total), out_shape=(ja...  14.8 us
  transfers between devices with their start and end apart: 3, of which 0 were waited for; matrix products, arithmetic and copies ran while one was open for 12% of the time, Pallas kernels for 50%

profile of v10, /device:TPU:0, one launch (start us, length us, event | category | flops | bytes accessed | tf_op | source)
XLA Modules:
  0.0 499.5 jit_solution(7537454521013654594)
XLA Ops:
  7.2 2.7 convert_element_type.78
  10.0 3.6 convert_element_type.72.own_ref
  13.6 0.6 pad.16.vec_ref
  14.2 112.4 %gather_weights.1 = (bf16[13,768,768]{2,1,0:T(8,128)(2,1)}, f32[8,16,128]{2,1,0:T(8,128)}) custom-call(bf16[13,96,768]{2,1,0:T(8,128)(2,1)} %convert_element_type.72.own_ref, f32[16,128]{1,0:T(8,128)} %pad.16.vec_ref), custom_call_target="tpu_custom_call" | custom-call | tf_op jit(solution)/shard_map/gather_weights/pallas_call | solution.py:1324
  126.6 1.3 constant_dynamic-slice_fusion
  127.9 0.1 abs_reduce_fusion
  128.1 0.1 clamp_convert_fusion
  128.3 0.9 fusion.34
  129.3 0.1 slice_reduce_fusion.1
  129.9 0.2 copy.58.qids_ref
  130.6 0.7 copy.61.labels_ref
  131.4 2.7 add_reduce_fusion
  134.2 0.6 multiply_reduce_fusion.7
  135.0 0.6 add_convert_fusion.3.refs_3_
  135.6 1.1 copy-done.26
  136.7 6.3 %fusion.q_ref.k_ref.v_ref = bf16[3,1024,768]{2,1,0:T(8,128)(2,1)S(1)} fusion(f32[3,768]{1,0:T(4,128)S(1)} %pad_maximum_fusion, bf16[13,768,768]{2,1,0:T(8,128)(2,1)} %get-tuple-element.43.up_ref.down_ref, bf16[1024,768]{1,0:T(8,128)(2,1)S(1)} %add_convert_fusion.3.refs_3_), kind=kOutput, calls=%fused_computation.4 | convolution fusion | flops 3628597248 | bytes 9839616 | tf_op jit(solution)/shard_map/td,kde->kte/dot_general | solution.py:346
  143.0 25.6 %attention_forward.1.refs_4_ = bf16[1024,768]{1,0:T(8,128)(2,1)S(1)} custom-call(s32[1024,1]{1,0:T(8,128)S(1)} %copy.58.qids_ref, s32[1,1024]{1,0:T(1,128)S(1)} %broadcast_select_fusion.1.kcodes_ref, bf16[3,1024,768]{2,1,0:T(8,128)(2,1)S(1)} %fusion.q_ref.k_ref.v_ref, bf16[3,1024,768]{2,1,0:T(8,128)(2,1)S(1)} %fusion.q_ref.k_ref.v_ref, ...), custom_call_target="tpu_custom_call" | custom-call | tf_op jit(solution)/shard_map/attention_forward/pallas_call | solution.py:198
  168.7 3.5 fusion.63
  172.2 0.5 multiply_reduce_fusion.6
  172.7 0.6 add_convert_fusion.2.x_ref
  173.3 21.5 %mlp_forward.1 = (bf16[1024,3072]{1,0:T(8,128)(2,1)}, f32[1024,3072]{1,0:T(8,128)}, f32[1024,768]{1,0:T(8,128)S(1)}) custom-call(bf16[1024,768]{1,0:T(8,128)(2,1)S(1)} %add_convert_fusion.2.x_ref, bf16[13,768,768]{2,1,0:T(8,128)(2,1)} %get-tuple-element.43.up_ref.down_ref, f32[1,3072]{1,0:T(1,128)S(1)} %reshape.260.bias_ref, ...), custom_call_target="tpu_custom_call" | custom-call | tf_op jit(solution)/shard_map/mlp_forward/pallas_call | solution.py:300
  194.8 0.1 convert_reduce_fusion.5
  195.0 0.4 fusion.61
  195.4 0.5 multiply_reduce_fusion.5
  196.0 1.1 copy-done.19
  197.1 2.3 fusion.29.pooled_ref
  199.4 14.8 %classify.1 = (f32[8,768]{1,0:T(8,128)}, bf16[32,6272]{1,0:T(8,128)(2,1)}, f32[8,128]{1,0:T(8,128)}) custom-call(f32[8,768]{1,0:T(8,128)} %fusion.29.pooled_ref, s32[32,2]{1,0:T(8,128)} %copy.61.labels_ref, bf16[768,5462]{1,0:T(8,128)(2,1)} %all-gather.4.cloned.1.call-done.head_hbm), custom_call_target="tpu_custom_call" | custom-call | tf_op jit(solution)/shard_map/classify/pallas_call | solution.py:1153
  214.1 4.2 multiply_reduce_fusion
  218.4 1.5 fusion.60
  219.9 0.3 convert_reduce_fusion
  220.2 1.3 copy-done.21
  221.5 33.4 %mlp_backward.1 = (f32[4,768,768]{2,1,0:T(8,128)}, f32[4,768,768]{2,1,0:T(8,128)}, f32[1,3072]{1,0:T(1,128)S(1)}, f32[1024,768]{1,0:T(8,128)}) custom-call(bf16[1024,768]{1,0:T(8,128)(2,1)S(1)} %add_convert_fusion.2.x_ref, bf16[1024,768]{1,0:T(8,128)(2,1)S(1)} %get-tuple-element.100.dm_ref, bf16[13,768,768]{2,1,0:T(8,128)(2,1)} %get-tuple-element.43.up_ref.down_ref, ...), custom_call_target="tpu_custom_call" | custom-call | tf_op jit(solution)/shard_map/mlp_backward/pallas_call | solution.py:320
  255.0 0.3 copy.62
  256.1 1.2 slice.129
  257.3 4.2 multiply_reduce_fusion.1
  261.6 0.5 copy-done.25
  262.1 1.4 fusion.59
  263.5 0.6 copy-done.22
  264.1 0.5 convert_reduce_fusion.1
  264.7 3.6 convolution_convert_fusion.do_ref
  268.4 40.1 %attention_backward.1.refs_6_ = bf16[3,1024,768]{2,1,0:T(8,128)(2,1)S(1)} custom-call(s32[1,1024]{1,0:T(1,128)S(1)} %copy-done.14, s32[1024,1]{1,0:T(8,128)S(1)} %broadcast_select_fusion.kcodes_ref, bf16[3,1024,768]{2,1,0:T(8,128)(2,1)S(1)} %bitcast.72, bf16[3,1024,768]{2,1,0:T(8,128)(2,1)S(1)} %bitcast.72, bf16[3,1024,768]{2,1,0:T(8,128)(2,1)S(1)} %bitcast.72, ...), custom_call_target="tpu_custom_call" | custom-call | tf_op jit(solution)/shard_map/attention_backward/pallas_call | solution.py:215
  308.6 8.2 %fusion.1 = (f32[768]{0:T(1024)S(1)}, f32[1024]{0:T(1024)S(1)}, f32[768]{0:T(1024)S(1)}, f32[1024,768,1]{1,0,2:T(8,128)S(1)}) fusion(f32[768,1024]{0,1:T(8,128)S(1)} %copy-done.24, f32[1024]{0:T(1024)S(1)} %fusion.48, f32[1024]{0:T(1024)S(1)} %broadcast_multiply_fusion.2, f32[768]{0:T(1024)S(1)} %add.171, f32[768]{0:T(1024)S(1)} %mul.254, ...), kind=kOutput, calls=%fused_computation.8 | convolution fusion | flops 3630953984 | bytes 14573568 | tf_op jit(solution)/shard_map/kte,kde->td/dot_general | solution.py:392
  316.8 1.5 fusion.58
  318.3 1.8 convert_reduce_fusion.4
  320.2 0.5 convert_reduce_fusion.2
  320.7 0.5 broadcast.279
  321.2 0.7 reduce.52
  322.0 0.6 pad.17.refs_8_
  322.7 1.0 slice.151
  323.7 4.4 multiply_reduce_fusion.8
  328.1 1.4 maximum_bitcast_fusion
  329.6 0.6 pad.18.refs_9_
  330.2 129.0 %reduce_gradients.1 = (f32[13,96,768]{2,1,0:T(8,128)}, f32[13,96,768]{2,1,0:T(8,128)}, f32[13,96,768]{2,1,0:T(8,128)}, f32[13,96,768]{2,1,0:T(8,128)}, f32[13,1,...) custom-call(f32[4,768,768]{2,1,0:T(8,128)} %get-tuple-element.50.refs_0_, ...), custom_call_target="tpu_custom_call" | custom-call | tf_op jit(solution)/shard_map/reduce_gradients/pallas_call | solution.py:922
  459.2 1.3 fusion.62
  460.6 1.6 copy-done.4
  462.2 1.6 copy-done.12
  463.7 1.6 copy-done.13
  465.3 0.7 copy-done.16
  466.0 5.9 %adam_rows.1 = (f32[96,5462]{1,0:T(8,128)}, f32[96,5462]{1,0:T(8,128)}, f32[96,5462]{1,0:T(8,128)}) custom-call(f32[8,128]{1,0:T(8,128)S(1)} %copy-done.16, f32[8,128]{1,0:T(8,128)S(1)} %broadcast_in_dim.34.fixes_ref, f32[96,5462]{1,0:T(8,128)S(1)} %copy-done.3, f32[96,5462]{1,0:T(8,128)S(1)} %copy-done.4, f32[96,5462]{1,0:T(8,128)S(1)} %copy-done.12, ...), custom_call_target="tpu_custom_call" | custom-call | tf_op jit(solution)/shard_map/adam_rows/pallas_call | solution.py:1404
  471.9 2.1 multiply_subtract_fusion
  474.0 2.1 copy-done.9
  476.1 2.1 copy-done.10
  478.2 2.1 copy-done.11
  480.3 12.5 %finish_blocks.1 = (f32[13,96,768]{2,1,0:T(8,128)}, f32[13,96,768]{2,1,0:T(8,128)}, f32[13,96,768]{2,1,0:T(8,128)}, f32[13,96,768]{2,1,0:T(8,128)}) custom-call(f32[8,128]{1,0:T(8,128)S(1)} %copy-done.16, f32[13,1,768]{2,1,0:T(1,128)S(1)} %copy-done.15, f32[13,96,768]{2,1,0:T(8,128)S(1)} %copy-done.8, f32[13,96,768]{2,1,0:T(8,128)S(1)} %copy-done.9, ...), custom_call_target="tpu_custom_call" | custom-call | tf_op jit(solution)/shard_map/finish_blocks/pallas_call | solution.py:1370
  (124 shorter events, 2.1 us)
Async XLA Ops:
  7.2 192.2 %all-gather.4.cloned.1.call-start = ((), (), s32[]{:S(2)}) async-start(), calls=%async_computation | async-start | bytes 9510912 | tf_op jit(solution)/shard_map/all_gather | solution.py:1492
  9.9 3.6 copy-start.30
  9.9 245.0 %all-gather.6.cloned.1.call-start = ((), (), s32[]{:S(2)}) async-start(), calls=%async_computation.1 | async-start | bytes 10862592 | tf_op jit(solution)/shard_map/all_gather | solution.py:1500
  128.0 1.3 copy-start.29
  128.1 1.8 copy-start.14
  128.2 2.5 copy-start.34
  128.2 3.2 copy-start.28
  129.3 193.4 %all-gather.8.cloned.1.call-start = ((), (), s32[]{:S(2)}) async-start(), calls=%async_computation.2 | async-start | bytes 3612672 | tf_op jit(solution)/shard_map/all_gather | solution.py:1548
  130.1 12.9 %copy-start.6 = (s32[1024,1]{1,0:T(8,128)}, s32[1024,1]{1,0:T(8,128)S(1)}, u32[]{:S(2)}) copy-start(s32[1024,1]{1,0:T(8,128)S(1)} %copy.58.qids_ref) | copy-start | bytes 12292
  134.1 34.5 %copy-start.23 = (f32[768,1024]{0,1:T(8,128)}, f32[768,1024]{0,1:T(8,128)S(1)}, u32[]{:S(2)}) copy-start(f32[768,1024]{0,1:T(8,128)S(1)} %get-tuple-element.124) | copy-start | bytes 9437188
  134.2 0.7 copy-start.31
  135.6 1.1 copy-start.26
  143.0 25.6 %copy-start = (bf16[3,1024,768]{2,1,0:T(8,128)(2,1)}, bf16[3,1024,768]{2,1,0:T(8,128)(2,1)S(1)}, u32[]{:S(2)}) copy-start(bf16[3,1024,768]{2,1,0:T(8,128)(2,1)S(1)} %fusion.q_ref.k_ref.v_ref) | copy-start | bytes 14155780
  168.7 3.5 copy-start.5
  172.2 22.8 %copy-start.17 = (f32[1024,768]{1,0:T(8,128)}, f32[1024,768]{1,0:T(8,128)S(1)}, u32[]{:S(2)}) copy-start(f32[1024,768]{1,0:T(8,128)S(1)} %get-tuple-element.126) | copy-start | bytes 9437188
  195.4 1.7 copy-start.19
  214.1 4.2 copy-start.20
  219.9 1.7 copy-start.21
  221.5 34.5 %copy-start.7 = (s32[1024,1]{1,0:T(8,128)S(1)}, s32[1024,1]{1,0:T(8,128)}, u32[]{:S(2)}) copy-start(s32[1024,1]{1,0:T(8,128)} %copy-done.6) | copy-start | bytes 12292
  257.3 4.2 copy-start.18
  257.3 4.7 copy-start.25
  262.1 2.1 copy-start.22
  264.1 4.2 slice-start
  264.7 3.7 copy-start.27
  264.7 3.7 slice-start.1
  268.4 40.1 %copy-start.24 = (f32[768,1024]{0,1:T(8,128)S(1)}, f32[768,1024]{0,1:T(8,128)}, u32[]{:S(2)}) copy-start(f32[768,1024]{0,1:T(8,128)} %copy-done.23) | copy-start | bytes 9437188
  308.5 11.6 %copy-start.1 = (bf16[3,1024,768]{2,1,0:T(8,128)(2,1)}, bf16[3,1024,768]{2,1,0:T(8,128)(2,1)S(1)}, u32[]{:S(2)}) copy-start(bf16[3,1024,768]{2,1,0:T(8,128)(2,1)S(1)} %attention_backward.1.refs_6_) | copy-start | bytes 14155780
  330.2 130.4 %copy-start.3 = (f32[96,5462]{1,0:T(8,128)S(1)}, f32[96,5462]{1,0:T(8,128)}, u32[]{:S(2)}) copy-start(f32[96,5462]{1,0:T(8,128)} %weight_ref.1) | copy-start | bytes 6292228
  460.6 1.6 copy-start.4
  462.2 1.6 copy-start.12
  463.7 1.6 copy-start.13
  465.3 0.7 copy-start.16
  466.0 5.9 %copy-start.32 = (f32[15,96]{1,0:T(8,128)S(1)}, f32[15,96]{1,0:T(8,128)}, u32[]{:S(2)}) copy-start(f32[15,96]{1,0:T(8,128)} %param.32) | copy-start | bytes 17284
  466.0 5.9 %copy-start.33 = (f32[15,96]{1,0:T(8,128)S(1)}, f32[15,96]{1,0:T(8,128)}, u32[]{:S(2)}) copy-start(f32[15,96]{1,0:T(8,128)} %param.31) | copy-start | bytes 17284
  466.0 8.0 %copy-start.2 = (f32[13,96,768]{2,1,0:T(8,128)S(1)}, f32[13,96,768]{2,1,0:T(8,128)}, u32[]{:S(2)}) copy-start(f32[13,96,768]{2,1,0:T(8,128)} %enc_ref.1) | copy-start | bytes 11501572
  466.0 8.0 %copy-start.8 = (f32[13,96,768]{2,1,0:T(8,128)S(1)}, f32[13,96,768]{2,1,0:T(8,128)}, u32[]{:S(2)}) copy-start(f32[13,96,768]{2,1,0:T(8,128)} %get-tuple-element.62.own_ref) | copy-start | bytes 11501572
  466.0 8.0 %copy-start.15 = (f32[13,1,768]{2,1,0:T(1,128)S(1)}, f32[13,1,768]{2,1,0:T(1,128)}, u32[]{:S(2)}) copy-start(f32[13,1,768]{2,1,0:T(1,128)} %get-tuple-element.61.wide_ref) | copy-start | bytes 119812
  474.0 2.1 copy-start.9
  476.1 2.1 copy-start.10
  478.2 2.1 copy-start.11
Sparse Core Ops, SparseCore 0:
  10.8 166.8 all-gather.3
  179.9 59.8 all-gather.5
  255.1 61.7 all-gather.7

commit v11 on v10

--- a/solution.py
+++ b/solution.py
@@ -283,9 +283,9 @@
 def mlp_specs(length, width, up_count):
     split = width // HIDDEN_TILE
     resident = pl.BlockSpec((length, width), lambda t: (0, 0))
-    up = pl.BlockSpec((None, width, HIDDEN_TILE), lambda t: (5 + t // split, 0, t % split))
+    up = pl.BlockSpec((None, width, HIDDEN_TILE), lambda t: (t // split, 0, t % split))
     down = pl.BlockSpec(
-        (None, HIDDEN_TILE, width), lambda t: (5 + up_count + t // split, t % split, 0)
+        (None, HIDDEN_TILE, width), lambda t: (up_count + t // split, t % split, 0)
     )
     hidden = pl.BlockSpec((length, HIDDEN_TILE), lambda t: (0, t))
     bias = pl.BlockSpec((1, HIDDEN_TILE), lambda t: (0, t))
@@ -294,7 +294,7 @@
 
 def mlp_forward(rows, blocks, up_bias):
     length, width = rows.shape
-    up_count = (blocks.shape[0] - 5) // 2
+    up_count = blocks.shape[0] // 2
     split, resident, up, down, hidden, bias = mlp_specs(length, width, up_count)
     hidden_size = up_count * width
     return pl.pallas_call(
@@ -314,7 +314,7 @@
 
 def mlp_backward(rows, grad_branch, blocks, units, slopes):
     length, width = rows.shape
-    up_count = (blocks.shape[0] - 5) // 2
+    up_count = blocks.shape[0] // 2
     split, resident, up, down, hidden, bias = mlp_specs(length, width, up_count)
     hidden_size = up_count * width
     return pl.pallas_call(
@@ -339,8 +339,7 @@
     )(rows, grad_branch, blocks, blocks, units, slopes)
 
 
-def layer_forward(blocks, vec_all, patch, pack_ids, key_codes):
-    up_count = (blocks.shape[0] - 5) // 2
+def layer_forward(blocks, vec_all, patch, attend):
     embedded = jnp.dot(patch, blocks[0], preferred_element_type=jnp.float32) + vec_all[0]
     normed_one = norm_rows(embedded, vec_all[1], vec_all[2]).astype(jnp.bfloat16)
     qkv_rows = jnp.einsum(
@@ -348,21 +347,24 @@
     )
     qkv_bias = jnp.stack([vec_all[3], jnp.zeros_like(vec_all[3]), vec_all[4]])
     qkv_rows = (qkv_rows + qkv_bias[:, None, :]).astype(jnp.bfloat16)
-    attended = attention_forward(qkv_rows, pack_ids, key_codes)
+    attended, mlp_blocks = attend(qkv_rows)
+    up_count = mlp_blocks.shape[0] // 2
     hidden = (
         embedded + jnp.dot(attended, blocks[4], preferred_element_type=jnp.float32) + vec_all[5]
     )
     normed_two = norm_rows(hidden, vec_all[6], vec_all[7]).astype(jnp.bfloat16)
-    units, slopes, branch = mlp_forward(normed_two, blocks, vec_all[8 : 8 + up_count])
+    units, slopes, branch = mlp_forward(normed_two, mlp_blocks, vec_all[8 : 8 + up_count])
     output = hidden + branch + vec_all[8 + up_count]
     return (
         output,
+        mlp_blocks,
         (embedded, normed_one, qkv_rows, attended, hidden, normed_two, slopes, units),
     )
 
 
 def layer_backward(
     blocks,
+    mlp_blocks,
     vec_all,
     patch,
     saved,
@@ -375,10 +377,10 @@
 ):
     embedded, normed_one, qkv_rows, attended, hidden, normed_two, slopes, units = saved
     feature_dim = patch.shape[1]
-    up_count = (blocks.shape[0] - 5) // 2
+    up_count = mlp_blocks.shape[0] // 2
     grad_branch = grad_output.astype(jnp.bfloat16)
     grad_up, grad_down, up_sums, grad_normed_two = mlp_backward(
-        normed_two, grad_branch, blocks, units, slopes
+        normed_two, grad_branch, mlp_blocks, units, slopes
     )
     up_sums, released = lax.optimization_barrier((up_sums, released))
     norm_two_back = jax.vjp(norm_rows, hidden, vec_all[6], vec_all[7])[1]
@@ -1317,6 +1319,54 @@
     ]
 
 
+def attention_gather_kernel(
+    qids_ref, kcodes_ref, q_ref, k_ref, v_ref, own_ref, out_ref, blocks_ref,
+    bias_ref, send_sem, recv_sem, copy_sem
+):
+    pair, tiles = pl.program_id(0), q_ref.shape[0] // QTILE
+    slots = pl.num_programs(0) * tiles
+
+    @pl.when(pair == 0)
+    def _():
+        gather_barrier()
+
+    gather_step, turns = gather_steps(own_ref, blocks_ref, send_sem, recv_sem, copy_sem)
+    attention_bias(qids_ref, kcodes_ref, bias_ref)
+    for tile in range(tiles):
+        slot = pair * tiles + tile
+        begin, end = slot * turns // slots, (slot + 1) * turns // slots
+
+        @pl.when(begin < end)
+        def _(begin=begin):
+            gather_step(begin)
+
+        attention_tile(tile, q_ref, k_ref, v_ref, out_ref, bias_ref)
+
+
+def attention_forward_gathering(qkv_rows, pack_ids, key_codes, own):
+    _, length, width = qkv_rows.shape
+    count, rows, _ = own.shape
+    tiles = length // QTILE
+    assert count + GATHER_DEPTH <= tiles * (width // PAIR)
+    return pl.pallas_call(
+        attention_gather_kernel,
+        grid=(width // PAIR,),
+        out_shape=(
+            jax.ShapeDtypeStruct((length, width), jnp.bfloat16),
+            jax.ShapeDtypeStruct((count, SHARES * rows, width), own.dtype),
+        ),
+        in_specs=[whole_spec((length, 1)), whole_spec((1, length))]
+        + [pair_spec(length, part) for part in range(3)]
+        + [whole_spec(own.shape)],
+        out_specs=(pair_spec(length), pl.BlockSpec(memory_space=pl.ANY)),
+        scratch_shapes=[pltpu.VMEM(bias_shape(length), jnp.float32)] + gather_semaphores(count),
+        compiler_params=pltpu.CompilerParams(
+            collective_id=4, has_side_effects=True, vmem_limit_bytes=40 << 20
+        ),
+        name="attention_forward",
+    )(pack_ids[:, None], key_codes[None, :], qkv_rows, qkv_rows, qkv_rows, own)
+
+
 def gather_weights(own, vec):
     count, rows, width = own.shape
     hbm = pl.BlockSpec(memory_space=pl.ANY)
@@ -1332,7 +1382,7 @@
         scratch_shapes=gather_semaphores(count)
         + [pltpu.SemaphoreType.DMA((SHARES,)), pltpu.SemaphoreType.DMA((SHARES,))],
         compiler_params=pltpu.CompilerParams(
-            collective_id=3, has_side_effects=True, vmem_limit_bytes=60 << 20
+            collective_id=3, has_side_effects=True, vmem_limit_bytes=32 << 20
         ),
         name="gather_weights",
     )(own, vec)
@@ -1377,7 +1427,7 @@
         ]
         + [block] * len(arrays),
         out_specs=(block,) * 4,
-        compiler_params=pltpu.CompilerParams(vmem_limit_bytes=32 << 20),
+        compiler_params=pltpu.CompilerParams(vmem_limit_bytes=60 << 20),
         name="finish_blocks",
     )(facts, wide_scale, *arrays)
 
@@ -1407,7 +1457,7 @@
         out_shape=(jax.ShapeDtypeStruct((rows, width), jnp.float32),) * 3,
         in_specs=[small, small] + [block] * 4,
         out_specs=(block,) * 3,
-        compiler_params=pltpu.CompilerParams(vmem_limit_bytes=32 << 20),
+        compiler_params=pltpu.CompilerParams(vmem_limit_bytes=60 << 20),
         name="adam_rows",
     )(facts, fixes, *arrays)
 
@@ -1478,15 +1528,16 @@
     if on_torus:
         vec_block = jnp.pad(vectors, ((0, -vectors.shape[0] % 8), (0, -row_count % 128)))
         own_low = enc_weights.astype(jnp.bfloat16)
-        blocks, vec_blocks = gather_weights(own_low, vec_block)
+        blocks, vec_blocks = gather_weights(own_low[:5], vec_block)
         right_part, vec_blocks = lax.optimization_barrier((my_part(root_right), vec_blocks))
         vec_low = jnp.transpose(vec_blocks[:, : vectors.shape[0], :row_count], (1, 0, 2))
         vec_all = lax.reduce_precision(vec_low.reshape(vectors.shape[0], feature_dim), 8, 7)
     else:
         right_part = my_part(root_right)
-        blocks = lax.all_gather(
+        all_blocks = lax.all_gather(
             my_part(enc_weights.astype(jnp.bfloat16)), ("dp", "cls"), axis=1, tiled=True
         )
+        blocks = all_blocks[:5]
         vec_low = lax.all_gather(vectors.astype(jnp.bfloat16), "dp", axis=1, tiled=True)
         vec_all = vec_low.astype(jnp.float32)
     head_low = lax.all_gather(head_weights.astype(jnp.bfloat16), "dp", axis=0, tiled=True)
@@ -1495,7 +1546,12 @@
     pack_ids, pack_keep = image_ids[0], keep[0]
     key_codes = jnp.where(pack_keep == 1, pack_ids, -1)
 
-    output, saved = layer_forward(blocks, vec_all, patches, pack_ids, key_codes)
+    def attend(qkv_rows):
+        if on_torus:
+            return attention_forward_gathering(qkv_rows, pack_ids, key_codes, own_low[5:])
+        return attention_forward(qkv_rows, pack_ids, key_codes), all_blocks[5:]
+
+    output, mlp_blocks, saved = layer_forward(blocks, vec_all, patches, attend)
     if on_torus:
         right_codes = lax.all_gather(
             encode_roots(right_part), ("dp", "cls"), axis=0, axis_index_groups=half_groups
@@ -1535,6 +1591,7 @@
     grad_output, grad_gain, grad_shift = pool_back(grad_pooled)
     lefts, rights, mlp_grads, grad_vectors, (own_rows, roots) = layer_backward(
         blocks,
+        mlp_blocks,
         vec_all,
         patches,
         saved,

time: 505 us -> 501 us (level)
  local copies, waits for them, and re-layouts: 26.4 us -> 18.4 us
  Pallas kernels: 395 us -> 402 us
    pallas_call x1, Pallas kernels: 112 us -> 54.6 us  [gather_weights(): pl.pallas_call(gather_kernel, out_shape=(jax.ShapeDtypeStruct((count, SHA...]
    pallas_call x1, Pallas kernels: 25.6 us -> 80.2 us  [attention_forward_gathering(): pl.pallas_call(attention_gather_kernel, grid=(width // PAIR,), out_shape=...]
    unnamed x75 -> x57, local copies, waits for them, and re-layouts: 17.3 us -> 7.01 us
    pallas_call x1, Pallas kernels: 12.5 us -> 18 us  [finish_blocks(): pl.pallas_call(finish_kernel, grid=(count,), out_shape=(jax.ShapeDtypeStr...]
  transfers between devices with their start and end apart: 3 -> 3, of which waited for: 0 -> 0; matrix products, arithmetic and copies ran while one was open for 12% -> 12% of each run, Pallas kernels for 50% -> 49%
where the time goes in v11:
time: 501 us; the launch traced here: 496 us
  Pallas kernels  402 us (80%)
  matrix products  33.7 us (7%)
  other arithmetic  26 us (5%)
  local copies, waits for them, and re-layouts  18.4 us (4%)
  between operations  15.6 us (3%)
    pallas_call x1, Pallas kernels, reduce_gradients(): pl.pallas_call(functools.partial(reduce_kernel, counts), out_shape=(jax.S...  131 us
    pallas_call x1, Pallas kernels, attention_forward_gathering(): pl.pallas_call(attention_gather_kernel, grid=(width // PAIR,), out_shape=...  80.2 us
    pallas_call x1, Pallas kernels, gather_weights(): pl.pallas_call(gather_kernel, out_shape=(jax.ShapeDtypeStruct((count, SHA...  54.6 us
    pallas_call x1, Pallas kernels, attention_backward(): pl.pallas_call(attention_backward_kernel, grid=(width // PAIR,), out_shap...  40.2 us
    pallas_call x1, Pallas kernels, mlp_backward(): pl.pallas_call(mlp_backward_kernel, grid=(up_count * split,), out_shape=(...  33.2 us
    pallas_call x1, Pallas kernels, mlp_forward(): pl.pallas_call(mlp_forward_kernel, grid=(up_count * split,), out_shape=(j...  21.4 us
    pallas_call x1, Pallas kernels, finish_blocks(): pl.pallas_call(finish_kernel, grid=(count,), out_shape=(jax.ShapeDtypeStr...  18 us
    pallas_call x1, Pallas kernels, classify(): pl.pallas_call(functools.partial(head_kernel, image_total), out_shape=(ja...  14.1 us
  transfers between devices with their start and end apart: 3, of which 0 were waited for; matrix products, arithmetic and copies ran while one was open for 12% of the time, Pallas kernels for 49%

profile of v11, /device:TPU:0, one launch (start us, length us, event | category | flops | bytes accessed | tf_op | source)
XLA Modules:
  0.0 496.3 jit_solution(6931519361969488023)
XLA Ops:
  7.2 2.7 convert_element_type.78
  10.0 2.3 convert_element_type.72
  12.3 1.2 copy-done.16
  13.6 54.6 %gather_weights.1 = (bf16[5,768,768]{2,1,0:T(8,128)(2,1)S(1)}, f32[8,16,128]{2,1,0:T(8,128)S(1)}) custom-call(bf16[5,96,768]{2,1,0:T(8,128)(2,1)S(1)} %slice.142.own_ref, f32[16,128]{1,0:T(8,128)S(1)} %pad.16.vec_ref), custom_call_target="tpu_custom_call" | custom-call | tf_op jit(solution)/shard_map/gather_weights/pallas_call | solution.py:1374
  68.2 2.0 constant_dynamic-slice_fusion
  70.2 0.1 abs_reduce_fusion
  70.4 0.1 clamp_convert_fusion
  70.7 0.9 fusion.34
  71.7 1.4 slice.148.own_ref
  73.1 0.1 slice_reduce_fusion.1
  73.5 0.1 slice.118
  73.6 0.2 copy.58.qids_ref
  74.1 0.1 reshape.260.bias_ref
  74.4 0.7 copy.61.labels_ref
  75.2 3.2 add_reduce_fusion
  78.4 0.6 multiply_reduce_fusion.7
  79.2 0.6 add_convert_fusion.3.refs_3_
  79.8 6.6 %fusion.q_ref.k_ref.v_ref = bf16[3,1024,768]{2,1,0:T(8,128)(2,1)S(1)} fusion(f32[3,768]{1,0:T(4,128)S(1)} %pad_maximum_fusion, bf16[5,768,768]{2,1,0:T(8,128)(2,1)} %copy-done.4, bf16[1024,768]{1,0:T(8,128)(2,1)S(1)} %add_convert_fusion.3.refs_3_), kind=kOutput, calls=%fused_computation.4 | convolution fusion | flops 3628597248 | bytes 9839616 | tf_op jit(solution)/shard_map/td,kde->kte/dot_general | solution.py:345
  86.5 80.2 %attention_forward.1 = (bf16[1024,768]{1,0:T(8,128)(2,1)S(1)}, bf16[8,768,768]{2,1,0:T(8,128)(2,1)}) custom-call(s32[1024,1]{1,0:T(8,128)S(1)} %copy.58.qids_ref, s32[1,1024]{1,0:T(1,128)S(1)} %broadcast_select_fusion.1.kcodes_ref, bf16[3,1024,768]{2,1,0:T(8,128)(2,1)S(1)} %fusion.q_ref.k_ref.v_ref, bf16[3,1024,768]{2,1,0:T(8,128)(2,1)S(1)} %fusion.q_ref.k_ref.v_ref, ...), custom_call_target="tpu_custom_call" | custom-call | tf_op jit(solution)/shard_map/attention_forward/pallas_call | solution.py:1351
  166.7 3.4 fusion.63
  170.2 0.5 multiply_reduce_fusion.6
  170.7 0.6 add_convert_fusion.2.x_ref
  171.3 21.4 %mlp_forward.1 = (bf16[1024,3072]{1,0:T(8,128)(2,1)}, f32[1024,3072]{1,0:T(8,128)}, f32[1024,768]{1,0:T(8,128)S(1)}) custom-call(bf16[1024,768]{1,0:T(8,128)(2,1)S(1)} %add_convert_fusion.2.x_ref, bf16[8,768,768]{2,1,0:T(8,128)(2,1)} %get-tuple-element.49.up_ref.down_ref, f32[1,3072]{1,0:T(1,128)S(1)} %reshape.260.bias_ref, ...), custom_call_target="tpu_custom_call" | custom-call | tf_op jit(solution)/shard_map/mlp_forward/pallas_call | solution.py:300
  192.7 0.1 convert_reduce_fusion.5
  192.8 0.4 fusion.61
  193.3 0.5 multiply_reduce_fusion.5
  193.8 1.1 copy-done.7
  194.9 2.3 fusion.29.pooled_ref
  197.2 14.1 %classify.1 = (f32[8,768]{1,0:T(8,128)}, bf16[32,6272]{1,0:T(8,128)(2,1)}, f32[8,128]{1,0:T(8,128)}) custom-call(f32[8,768]{1,0:T(8,128)} %fusion.29.pooled_ref, s32[32,2]{1,0:T(8,128)} %copy.61.labels_ref, bf16[768,5462]{1,0:T(8,128)(2,1)} %all-gather.4.cloned.1.call-done.head_hbm), custom_call_target="tpu_custom_call" | custom-call | tf_op jit(solution)/shard_map/classify/pallas_call | solution.py:1155
  211.3 4.2 multiply_reduce_fusion
  215.6 1.5 fusion.60
  217.1 0.3 convert_reduce_fusion
  217.4 1.3 copy-done.9
  218.7 33.2 %mlp_backward.1 = (f32[4,768,768]{2,1,0:T(8,128)}, f32[4,768,768]{2,1,0:T(8,128)}, f32[1,3072]{1,0:T(1,128)S(1)}, f32[1024,768]{1,0:T(8,128)}) custom-call(bf16[1024,768]{1,0:T(8,128)(2,1)S(1)} %add_convert_fusion.2.x_ref, bf16[1024,768]{1,0:T(8,128)(2,1)S(1)} %get-tuple-element.104.dm_ref, bf16[8,768,768]{2,1,0:T(8,128)(2,1)} %get-tuple-element.49.up_ref.down_ref, ...), custom_call_target="tpu_custom_call" | custom-call | tf_op jit(solution)/shard_map/mlp_backward/pallas_call | solution.py:320
  251.9 0.3 copy.62
  253.1 1.3 slice.137
  254.5 4.2 multiply_reduce_fusion.1
  258.7 1.5 fusion.59
  260.3 0.3 copy-done.10
  260.6 0.5 convert_reduce_fusion.1
  261.2 0.8 copy-done.13
  261.9 1.4 convolution_convert_fusion.do_ref
  263.4 1.0 slice-done
  264.4 40.2 %attention_backward.1.refs_6_ = bf16[3,1024,768]{2,1,0:T(8,128)(2,1)S(1)} custom-call(s32[1,1024]{1,0:T(1,128)S(1)} %copy-done.3, s32[1024,1]{1,0:T(8,128)S(1)} %broadcast_select_fusion.kcodes_ref, bf16[3,1024,768]{2,1,0:T(8,128)(2,1)S(1)} %bitcast.72, bf16[3,1024,768]{2,1,0:T(8,128)(2,1)S(1)} %bitcast.72, bf16[3,1024,768]{2,1,0:T(8,128)(2,1)S(1)} %bitcast.72, ...), custom_call_target="tpu_custom_call" | custom-call | tf_op jit(solution)/shard_map/attention_backward/pallas_call | solution.py:215
  304.6 8.1 %fusion.1 = (f32[768]{0:T(1024)S(1)}, f32[1024]{0:T(1024)S(1)}, f32[768]{0:T(1024)S(1)}, f32[1024,768,1]{1,0,2:T(8,128)S(1)}) fusion(f32[768,1024]{0,1:T(8,128)} %copy-done.11, f32[1024]{0:T(1024)S(1)} %fusion.48, f32[1024]{0:T(1024)S(1)} %broadcast_multiply_fusion.2, f32[768]{0:T(1024)S(1)} %add.171, f32[768]{0:T(1024)S(1)} %mul.254, ...), kind=kOutput, calls=%fused_computation.8 | convolution fusion | flops 3630953984 | bytes 14575616 | tf_op jit(solution)/shard_map/kte,kde->td/dot_general | solution.py:394
  312.8 1.6 fusion.58
  314.4 0.3 copy-done.14
  314.7 1.8 convert_reduce_fusion.4
  316.5 0.5 convert_reduce_fusion.2
  317.1 0.5 broadcast.279
  317.6 0.7 reduce.52
  318.3 0.1 concatenate.34
  318.4 0.6 pad.17.refs_8_
  319.0 1.0 slice.161
  320.1 4.4 multiply_reduce_fusion.8
  324.5 1.4 maximum_bitcast_fusion
  325.9 0.1 copy.64
  325.9 0.6 pad.18.refs_9_
  326.6 130.5 %reduce_gradients.1 = (f32[13,96,768]{2,1,0:T(8,128)}, f32[13,96,768]{2,1,0:T(8,128)}, f32[13,96,768]{2,1,0:T(8,128)}, f32[13,96,768]{2,1,0:T(8,128)}, f32[13,1,...) custom-call(f32[4,768,768]{2,1,0:T(8,128)} %get-tuple-element.54.refs_0_, ...), custom_call_target="tpu_custom_call" | custom-call | tf_op jit(solution)/shard_map/reduce_gradients/pallas_call | solution.py:924
  457.1 1.3 fusion.62
  458.4 0.7 broadcast_in_dim.34.fixes_ref
  459.0 10.1 %adam_rows.1 = (f32[96,5462]{1,0:T(8,128)}, f32[96,5462]{1,0:T(8,128)}, f32[96,5462]{1,0:T(8,128)}) custom-call(f32[8,128]{1,0:T(8,128)} %get-tuple-element.64.facts_ref, f32[8,128]{1,0:T(8,128)} %broadcast_in_dim.34.fixes_ref, f32[96,5462]{1,0:T(8,128)} %weight_ref.1, f32[96,5462]{1,0:T(8,128)} %get-tuple-element.134.grad_ref, f32[96,5462]{1,0:T(8,128)} %first_ref.1, ...), custom_call_target="tpu_custom_call" | custom-call | tf_op jit(solution)/shard_map/adam_rows/pallas_call | solution.py:1454
  469.2 2.1 multiply_subtract_fusion
  471.3 18.0 %finish_blocks.1 = (f32[13,96,768]{2,1,0:T(8,128)}, f32[13,96,768]{2,1,0:T(8,128)}, f32[13,96,768]{2,1,0:T(8,128)}, f32[13,96,768]{2,1,0:T(8,128)}) custom-call(f32[8,128]{1,0:T(8,128)} %get-tuple-element.64.facts_ref, f32[13,1,768]{2,1,0:T(1,128)} %get-tuple-element.65.wide_ref, f32[13,96,768]{2,1,0:T(8,128)} %get-tuple-element.66.own_ref, ...), custom_call_target="tpu_custom_call" | custom-call | tf_op jit(solution)/shard_map/finish_blocks/pallas_call | solution.py:1420
  (109 shorter events, 1.8 us)
Async XLA Ops:
  7.2 190.0 %all-gather.4.cloned.1.call-start = ((), (), s32[]{:S(2)}) async-start(), calls=%async_computation | async-start | bytes 9510912 | tf_op jit(solution)/shard_map/all_gather | solution.py:1543
  9.9 242.0 %all-gather.6.cloned.1.call-start = ((), (), s32[]{:S(2)}) async-start(), calls=%async_computation.1 | async-start | bytes 10862592 | tf_op jit(solution)/shard_map/all_gather | solution.py:1556
  10.0 3.6 copy-start.19
  12.3 1.3 copy-start.16
  68.2 2.4 copy-start.4
  70.7 3.0 copy-start.3
  70.7 3.7 copy-start.23
  71.7 247.4 %all-gather.8.cloned.1.call-start = ((), (), s32[]{:S(2)}) async-start(), calls=%async_computation.2 | async-start | bytes 3612672 | tf_op jit(solution)/shard_map/all_gather | solution.py:1605
  78.4 88.3 %copy-start.11 = (f32[768,1024]{0,1:T(8,128)}, f32[768,1024]{0,1:T(8,128)S(1)}, u32[]{:S(2)}) copy-start(f32[768,1024]{0,1:T(8,128)S(1)} %get-tuple-element.128) | copy-start | bytes 9437188
  78.4 0.7 copy-start.20
  79.8 6.6 %copy-start.17 = (bf16[1024,768]{1,0:T(8,128)(2,1)}, bf16[1024,768]{1,0:T(8,128)(2,1)S(1)}, u32[]{:S(2)}) copy-start(bf16[1024,768]{1,0:T(8,128)(2,1)S(1)} %add_convert_fusion.3.refs_3_) | copy-start | bytes 4718596
  86.4 80.2 %copy-start = (bf16[3,1024,768]{2,1,0:T(8,128)(2,1)}, bf16[3,1024,768]{2,1,0:T(8,128)(2,1)S(1)}, u32[]{:S(2)}) copy-start(bf16[3,1024,768]{2,1,0:T(8,128)(2,1)S(1)} %fusion.q_ref.k_ref.v_ref) | copy-start | bytes 14155780
  166.7 3.5 copy-start.2
  170.1 22.7 %copy-start.5 = (f32[1024,768]{1,0:T(8,128)}, f32[1024,768]{1,0:T(8,128)S(1)}, u32[]{:S(2)}) copy-start(f32[1024,768]{1,0:T(8,128)S(1)} %get-tuple-element.130) | copy-start | bytes 9437188
  193.3 1.7 copy-start.7
  211.3 4.3 copy-start.8
  217.1 1.7 copy-start.9
  253.0 5.6 %copy-start.6 = (f32[1024,768]{1,0:T(8,128)S(1)}, f32[1024,768]{1,0:T(8,128)}, u32[]{:S(2)}) copy-start(f32[1024,768]{1,0:T(8,128)} %copy-done.5) | copy-start | bytes 9437188
  253.0 5.6 %copy-start.15 = (f32[1024,768]{1,0:T(8,128)S(1)}, f32[1024,768]{1,0:T(8,128)}, u32[]{:S(2)}) copy-start(f32[1024,768]{1,0:T(8,128)} %get-tuple-element.56) | copy-start | bytes 9437188
  254.5 7.5 %slice-start.2 = ((s8[5898240]{0:T(1024)(128)(4,1)}), s8[4194304]{0:T(1024)(128)(4,1)S(1)}, s32[]{:S(2)}) async-start(s8[5898240]{0:T(1024)(128)(4,1)} %bitcast.77), calls=%async_computation.5 | async-start | bytes 8388608
  258.7 1.9 copy-start.10
  258.7 3.2 slice-start.3
  260.3 1.7 copy-start.13
  260.6 3.8 slice-start
  261.9 1.5 copy-start.18
  261.9 2.5 slice-start.1
  304.6 11.9 %copy-start.1 = (bf16[3,1024,768]{2,1,0:T(8,128)(2,1)}, bf16[3,1024,768]{2,1,0:T(8,128)(2,1)S(1)}, u32[]{:S(2)}) copy-start(bf16[3,1024,768]{2,1,0:T(8,128)(2,1)S(1)} %attention_backward.1.refs_6_) | copy-start | bytes 14155780
  304.6 8.1 %copy-start.12 = (f32[768,1024]{0,1:T(8,128)S(1)}, f32[768,1024]{0,1:T(8,128)}, u32[]{:S(2)}) copy-start(f32[768,1024]{0,1:T(8,128)} %copy-done.11) | copy-start | bytes 9437188
  312.8 1.9 copy-start.14
  459.0 10.1 %copy-start.21 = (f32[15,96]{1,0:T(8,128)S(1)}, f32[15,96]{1,0:T(8,128)}, u32[]{:S(2)}) copy-start(f32[15,96]{1,0:T(8,128)} %param.32) | copy-start | bytes 17284
  459.0 10.1 %copy-start.22 = (f32[15,96]{1,0:T(8,128)S(1)}, f32[15,96]{1,0:T(8,128)}, u32[]{:S(2)}) copy-start(f32[15,96]{1,0:T(8,128)} %param.31) | copy-start | bytes 17284
Sparse Core Ops, SparseCore 0:
  10.8 162.9 all-gather.3
  175.4 59.2 all-gather.5
  252.1 63.1 all-gather.7

commit v12 on v9

--- a/solution.py
+++ b/solution.py
@@ -339,7 +339,7 @@
     )(rows, grad_branch, blocks, blocks, units, slopes)
 
 
-def layer_forward(blocks, vec_all, patch, attend):
+def attend_rows(blocks, vec_all, patch, pack_ids, key_codes):
     embedded = jnp.dot(patch, blocks[0], preferred_element_type=jnp.float32) + vec_all[0]
     normed_one = norm_rows(embedded, vec_all[1], vec_all[2]).astype(jnp.bfloat16)
     qkv_rows = jnp.einsum(
@@ -347,7 +347,12 @@
     )
     qkv_bias = jnp.stack([vec_all[3], jnp.zeros_like(vec_all[3]), vec_all[4]])
     qkv_rows = (qkv_rows + qkv_bias[:, None, :]).astype(jnp.bfloat16)
-    attended, mlp_blocks = attend(qkv_rows)
+    attended = attention_forward(qkv_rows, pack_ids, key_codes)
+    return attended, embedded, normed_one, qkv_rows
+
+
+def layer_forward(blocks, vec_all, attend):
+    attended, mlp_blocks, embedded, normed_one, qkv_rows = attend()
     up_count = mlp_blocks.shape[0] // 2
     hidden = (
         embedded + jnp.dot(attended, blocks[4], preferred_element_type=jnp.float32) + vec_all[5]
@@ -1320,51 +1325,88 @@
 
 
 def attention_gather_kernel(
-    qids_ref, kcodes_ref, q_ref, k_ref, v_ref, own_ref, out_ref, blocks_ref,
+    qids_ref, kcodes_ref, patch_ref, first_ref, vec_ref, own_ref,
+    out_ref, blocks_ref, embedded_ref, normed_ref, qkv_ref,
     bias_ref, send_sem, recv_sem, copy_sem
 ):
-    pair, tiles = pl.program_id(0), q_ref.shape[0] // QTILE
+    turn, tiles = pl.program_id(0), patch_ref.shape[0] // QTILE
     slots = pl.num_programs(0) * tiles
-
-    @pl.when(pair == 0)
-    def _():
-        gather_barrier()
-
+    pair = jnp.maximum(turn - 1, 0)
+    columns = pl.ds(pl.multiple_of(pair * PAIR, PAIR), PAIR)
+    pl.when(turn == 0)(gather_barrier)
     gather_step, turns = gather_steps(own_ref, blocks_ref, send_sem, recv_sem, copy_sem)
     attention_bias(qids_ref, kcodes_ref, bias_ref)
+
+    def project(index):
+        rows = pl.ds(index * QTILE, QTILE)
+        embedded = jnp.dot(patch_ref[rows, :], first_ref[0], preferred_element_type=jnp.float32)
+        embedded = embedded + vec_ref[0:1, :]
+        embedded_ref[rows, :] = embedded
+        normed = norm_rows(embedded, vec_ref[1:2, :], vec_ref[2:3, :]).astype(jnp.bfloat16)
+        normed_ref[rows, :] = normed
+        for part, shift in enumerate((vec_ref[3:4, :], None, vec_ref[4:5, :])):
+            value = jnp.dot(normed, first_ref[1 + part], preferred_element_type=jnp.float32)
+            value = value if shift is None else value + shift
+            qkv_ref[part, rows, :] = value.astype(jnp.bfloat16)
+
     for tile in range(tiles):
-        slot = pair * tiles + tile
+        slot = turn * tiles + tile
         begin, end = slot * turns // slots, (slot + 1) * turns // slots
 
         @pl.when(begin < end)
         def _(begin=begin):
             gather_step(begin)
 
-        attention_tile(tile, q_ref, k_ref, v_ref, out_ref, bias_ref)
-
-
-def attention_forward_gathering(qkv_rows, pack_ids, key_codes, own):
-    _, length, width = qkv_rows.shape
+        @pl.when(turn == 0)
+        def _(tile=tile):
+            project(tile)
+
+        @pl.when(turn > 0)
+        def _(tile=tile):
+            views = [qkv_ref.at[part, :, columns] for part in range(3)]
+            attention_tile(tile, *views, out_ref, bias_ref)
+
+
+def attention_forward_gathering(patch, first_blocks, vec_all, pack_ids, key_codes, own):
+    length, width = patch.shape
     count, rows, _ = own.shape
     tiles = length // QTILE
-    assert count + GATHER_DEPTH <= tiles * (width // PAIR)
+    steps = 1 + width // PAIR
+    assert count + GATHER_DEPTH <= tiles * steps
+    bf16 = jnp.bfloat16
     return pl.pallas_call(
         attention_gather_kernel,
-        grid=(width // PAIR,),
+        grid=(steps,),
         out_shape=(
-            jax.ShapeDtypeStruct((length, width), jnp.bfloat16),
+            jax.ShapeDtypeStruct((length, width), bf16),
             jax.ShapeDtypeStruct((count, SHARES * rows, width), own.dtype),
+            jax.ShapeDtypeStruct((length, width), jnp.float32),
+            jax.ShapeDtypeStruct((length, width), bf16),
+            jax.ShapeDtypeStruct((3, length, width), bf16),
         ),
-        in_specs=[whole_spec((length, 1)), whole_spec((1, length))]
-        + [pair_spec(length, part) for part in range(3)]
-        + [whole_spec(own.shape)],
-        out_specs=(pair_spec(length), pl.BlockSpec(memory_space=pl.ANY)),
+        in_specs=[
+            whole_spec((length, 1)),
+            whole_spec((1, length)),
+            whole_spec((length, width)),
+            pl.BlockSpec(
+                first_blocks.shape, lambda turn: (0, 0, 0), pipeline_mode=pl.Buffered(1)
+            ),
+            whole_spec(vec_all.shape),
+            whole_spec(own.shape),
+        ],
+        out_specs=(
+            pl.BlockSpec((length, PAIR), lambda turn: (0, jnp.maximum(turn - 1, 0))),
+            pl.BlockSpec(memory_space=pl.ANY),
+            whole_spec((length, width)),
+            whole_spec((length, width)),
+            whole_spec((3, length, width)),
+        ),
         scratch_shapes=[pltpu.VMEM(bias_shape(length), jnp.float32)] + gather_semaphores(count),
         compiler_params=pltpu.CompilerParams(
-            collective_id=4, has_side_effects=True, vmem_limit_bytes=40 << 20
+            collective_id=4, has_side_effects=True, vmem_limit_bytes=56 << 20
         ),
         name="attention_forward",
-    )(pack_ids[:, None], key_codes[None, :], qkv_rows, qkv_rows, qkv_rows, own)
+    )(pack_ids[:, None], key_codes[None, :], patch, first_blocks, vec_all, own)
 
 
 def gather_weights(own, vec):
@@ -1486,12 +1528,15 @@
     pack_ids, pack_keep = image_ids[0], keep[0]
     key_codes = jnp.where(pack_keep == 1, pack_ids, -1)
 
-    def attend(qkv_rows):
+    def attend():
         if on_torus:
-            return attention_forward_gathering(qkv_rows, pack_ids, key_codes, own_low[5:])
-        return attention_forward(qkv_rows, pack_ids, key_codes), all_blocks[5:]
-
-    output, mlp_blocks, saved = layer_forward(blocks, vec_all, patches, attend)
+            return attention_forward_gathering(
+                patches, blocks, vec_all, pack_ids, key_codes, own_low[5:]
+            )
+        attended, *rest = attend_rows(blocks, vec_all, patches, pack_ids, key_codes)
+        return (attended, all_blocks[5:], *rest)
+
+    output, mlp_blocks, saved = layer_forward(blocks, vec_all, attend)
     if on_torus:
         right_codes = lax.all_gather(
             encode_roots(right_part), ("dp", "cls"), axis=0, axis_index_groups=half_groups

time: 498 us -> 502 us (level)
  matrix products: 33.7 us -> 20 us
  Pallas kernels: 374 us -> 385 us
    pallas_call x1, Pallas kernels: 79.8 us -> 92.3 us  [attention_forward_gathering(): pl.pallas_call(attention_gather_kernel, grid=(steps,), out_shape=(jax.Sha...]
    dot_general x2 -> x0, matrix products: 9.83 us -> none  [the longest x1 6.61 us: layer_forward(): jnp.einsum('td,kde->kte', normed_one, blocks[1:4], preferred_element_type...]
  transfers between devices with their start and end apart: 3 -> 3, of which waited for: 0 -> 0; matrix products, arithmetic and copies ran while one was open for 12% -> 10% of each run, Pallas kernels for 49% -> 52%
where the time goes in v12:
time: 502 us; the launch traced here: 493 us
  Pallas kernels  385 us (77%)
  other arithmetic  53.3 us (11%)
  matrix products  20 us (4%)
  local copies, waits for them, and re-layouts  18.1 us (4%)
  between operations  16.7 us (3%)
    pallas_call x1, Pallas kernels, reduce_gradients(): pl.pallas_call(functools.partial(reduce_kernel, counts), out_shape=(jax.S...  131 us
    pallas_call x1, Pallas kernels, attention_forward_gathering(): pl.pallas_call(attention_gather_kernel, grid=(steps,), out_shape=(jax.Sha...  92.3 us
    pallas_call x1, Pallas kernels, gather_weights(): pl.pallas_call(gather_kernel, out_shape=(jax.ShapeDtypeStruct((count, SHA...  53.4 us
    pallas_call x1, Pallas kernels, attention_backward(): pl.pallas_call(attention_backward_kernel, grid=(width // PAIR,), out_shap...  40.3 us
    pallas_call x1, Pallas kernels, mlp_backward(): pl.pallas_call(mlp_backward_kernel, grid=(up_count * split,), out_shape=(...  32.8 us
    pallas_call x1, Pallas kernels, mlp_forward(): pl.pallas_call(mlp_forward_kernel, grid=(up_count * split,), out_shape=(j...  20.8 us
    pallas_call x1, Pallas kernels, classify(): pl.pallas_call(functools.partial(head_kernel, image_total), out_shape=(ja...  14.2 us
  transfers between devices with their start and end apart: 3, of which 0 were waited for; matrix products, arithmetic and copies ran while one was open for 10% of the time, Pallas kernels for 52%

profile of v12, /device:TPU:0, one launch (start us, length us, event | category | flops | bytes accessed | tf_op | source)
XLA Modules:
  0.0 492.9 jit_solution(4712313135695244536)
XLA Ops:
  7.2 2.7 convert_element_type.65
  10.0 2.3 convert_element_type.62
  12.4 53.4 %gather_weights.1 = (bf16[5,768,768]{2,1,0:T(8,128)(2,1)S(1)}, f32[8,16,128]{2,1,0:T(8,128)S(1)}) custom-call(bf16[5,96,768]{2,1,0:T(8,128)(2,1)S(1)} %slice.110.own_ref, f32[16,128]{1,0:T(8,128)S(1)} %pad.12.vec_ref), custom_call_target="tpu_custom_call" | custom-call | tf_op jit(solution)/shard_map/gather_weights/pallas_call | solution.py:1416
  65.8 2.0 constant_dynamic-slice_fusion
  67.8 0.1 abs_reduce_fusion
  68.0 0.1 clamp_convert_fusion
  68.3 0.9 fusion.25
  69.3 1.1 slice.111.own_ref
  70.4 0.7 reduce_precision.12.vec_ref
  71.1 1.0 copy.50.qids_ref
  72.2 0.1 slice_reduce_fusion
  72.5 0.1 reshape.252.bias_ref
  72.8 0.7 copy.53.labels_ref
  73.5 0.3 copy.54
  73.8 0.6 broadcast_select_fusion.1.kcodes_ref
  74.4 92.3 %attention_forward.1 = (bf16[1024,768]{1,0:T(8,128)(2,1)}, bf16[8,768,768]{2,1,0:T(8,128)(2,1)}, f32[1024,768]{1,0:T(8,128)}, bf16[1024,768]{1,0:T(8,128)(2,1)}, bf16[3,1024,768]{2,1,0:T(8,128)(2,1)}) custom-call(s32[1024,1]{1,0:T(8,128)} %copy.50.qids_ref, s32[1,1024]{1,0:T(1,128)} %broadcast_select_fusion.1.kcodes_ref, bf16[1024,768]{1,0:T(8,128)(2,1)} %refs_2_.1, ...), custom_call_target="tpu_custom_call" | custom-call | tf_op jit(solution)/shard_map/attention_forward/pallas_call | solution.py:1377
  166.7 2.3 reduce_sum.233
  169.8 3.2 fusion.54
  173.1 0.5 multiply_reduce_fusion.7
  173.6 0.6 add_convert_fusion.1.x_ref
  174.1 20.8 %mlp_forward.1 = (bf16[1024,3072]{1,0:T(8,128)(2,1)}, f32[1024,3072]{1,0:T(8,128)}, f32[1024,768]{1,0:T(8,128)S(1)}) custom-call(bf16[1024,768]{1,0:T(8,128)(2,1)S(1)} %add_convert_fusion.1.x_ref, bf16[8,768,768]{2,1,0:T(8,128)(2,1)} %get-tuple-element.46.up_ref.down_ref, f32[1,3072]{1,0:T(1,128)S(1)} %reshape.252.bias_ref, ...), custom_call_target="tpu_custom_call" | custom-call | tf_op jit(solution)/shard_map/mlp_forward/pallas_call | solution.py:300
  195.0 0.1 convert_reduce_fusion.5
  195.1 0.4 fusion.52
  195.5 0.5 multiply_reduce_fusion.6
  196.1 1.1 copy-done.5
  197.2 2.3 fusion.20.pooled_ref
  199.5 14.2 %classify.1 = (f32[8,768]{1,0:T(8,128)}, bf16[32,6272]{1,0:T(8,128)(2,1)}, f32[8,128]{1,0:T(8,128)}) custom-call(f32[8,768]{1,0:T(8,128)} %fusion.20.pooled_ref, s32[32,2]{1,0:T(8,128)} %copy.53.labels_ref, bf16[768,5462]{1,0:T(8,128)(2,1)} %all-gather.4.cloned.1.call-done.head_hbm), custom_call_target="tpu_custom_call" | custom-call | tf_op jit(solution)/shard_map/classify/pallas_call | solution.py:1160
  213.7 4.2 multiply_reduce_fusion
  218.0 1.6 fusion.51
  219.6 0.3 convert_reduce_fusion
  219.9 1.3 copy-done.7
  221.2 32.8 %mlp_backward.1 = (f32[4,768,768]{2,1,0:T(8,128)}, f32[4,768,768]{2,1,0:T(8,128)}, f32[1,3072]{1,0:T(1,128)S(1)}, f32[1024,768]{1,0:T(8,128)}) custom-call(bf16[1024,768]{1,0:T(8,128)(2,1)S(1)} %add_convert_fusion.1.x_ref, bf16[1024,768]{1,0:T(8,128)(2,1)S(1)} %get-tuple-element.95.dm_ref, bf16[8,768,768]{2,1,0:T(8,128)(2,1)} %get-tuple-element.46.up_ref.down_ref, ...), custom_call_target="tpu_custom_call" | custom-call | tf_op jit(solution)/shard_map/mlp_backward/pallas_call | solution.py:320
  254.1 2.5 multiply_reduce_fusion.3
  256.6 1.2 broadcast_select_fusion.kcodes_ref
  257.9 1.2 slice.105
  259.1 3.0 multiply_reduce_fusion.1
  262.1 1.4 fusion.50
  263.5 0.5 copy-done.8
  264.0 0.5 convert_reduce_fusion.1
  264.6 0.5 copy-done.11
  265.1 1.4 convolution_convert_fusion.do_ref
  266.6 1.1 slice-done
  267.7 40.3 %attention_backward.1.refs_6_ = bf16[3,1024,768]{2,1,0:T(8,128)(2,1)S(1)} custom-call(s32[1,1024]{1,0:T(1,128)S(1)} %copy-done.2, s32[1024,1]{1,0:T(8,128)S(1)} %broadcast_select_fusion.kcodes_ref, bf16[3,1024,768]{2,1,0:T(8,128)(2,1)S(1)} %bitcast.45, bf16[3,1024,768]{2,1,0:T(8,128)(2,1)S(1)} %bitcast.45, bf16[3,1024,768]{2,1,0:T(8,128)(2,1)S(1)} %bitcast.45, ...), custom_call_target="tpu_custom_call" | custom-call | tf_op jit(solution)/shard_map/attention_backward/pallas_call | solution.py:215
  308.0 4.4 fusion.2
  312.4 1.5 fusion.49
  313.9 0.4 copy-done.12
  314.3 1.9 convert_reduce_fusion.4
  316.3 0.5 convert_reduce_fusion.2
  316.9 0.5 broadcast.265
  317.4 0.7 reduce.35
  318.1 0.1 concatenate.34
  318.2 0.6 pad.13.refs_8_
  318.8 1.0 slice.125
  319.9 4.4 multiply_reduce_fusion.8
  324.3 1.4 maximum_bitcast_fusion
  325.6 0.1 copy.56
  325.7 0.6 pad.14.refs_9_
  326.3 130.7 %reduce_gradients.1 = (f32[13,96,768]{2,1,0:T(8,128)}, f32[13,96,768]{2,1,0:T(8,128)}, f32[13,96,768]{2,1,0:T(8,128)}, f32[13,96,768]{2,1,0:T(8,128)}, f32[13,1,...) custom-call(f32[4,768,768]{2,1,0:T(8,128)} %get-tuple-element.51.refs_0_, ...), custom_call_target="tpu_custom_call" | custom-call | tf_op jit(solution)/shard_map/reduce_gradients/pallas_call | solution.py:929
  457.1 1.3 fusion.53
  459.7 0.8 copy.60
  460.5 7.6 %multiply_subtract_fusion.1 = (f32[96,5462]{1,0:T(8,128)}, f32[96,5462]{1,0:T(8,128)}, f32[96,5462]{1,0:T(8,128)}) fusion(f32[96,5462]{1,0:T(8,128)S(1)} %copy-done.15, f32[]{:T(128)S(6)} %sub.70, f32[]{:T(128)S(6)} %sub.69, f32[96,5462]{1,0:T(8,128)} %get-tuple-element.123, f32[]{:T(128)} %bitcast.14, f32[96,5462]{1,0:T(8,128)} %param.29, f32[96,5462]{1,0:T(8,128)} %param.28), kind=kLoop, calls=%fused_computation.40 | loop fusion | flops 8389632 | bytes 14681868 | tf_op jit(solution)/shard_map/sub | solution.py:1439
  468.0 2.1 multiply_subtract_fusion.2
  470.1 8.5 %multiply_subtract_fusion = (f32[13,96,768]{2,1,0:T(8,128)}, f32[13,96,768]{2,1,0:T(8,128)}) fusion(f32[13,96,768]{2,1,0:T(8,128)S(1)} %copy-done.13, f32[13,96,768]{2,1,0:T(8,128)} %get-tuple-element.64, f32[13,768]{1,0:T(8,128)S(1)} %bitcast.52, f32[13,96,768]{2,1,0:T(8,128)} %get-tuple-element.66, f32[]{:T(128)} %bitcast.14), kind=kLoop, calls=%fused_computation.5 | loop fusion | flops 2875392 | bytes 19209220 | tf_op jit(solution)/shard_map/sub | solution.py:1649
  478.6 7.5 %multiply_add_fusion = (f32[13,96,768]{2,1,0:T(8,128)}, f32[13,96,768]{2,1,0:T(8,128)}) fusion(f32[13,96,768]{2,1,0:T(8,128)} %get-tuple-element.68, f32[13,96,768]{2,1,0:T(8,128)S(1)} %copy-done.17, f32[]{:T(128)S(6)} %mul.368, f32[13,96,768]{2,1,0:T(8,128)} %get-tuple-element.67, f32[13,96,768]{2,1,0:T(8,128)S(1)} %copy-done.18), kind=kLoop, calls=%fused_computation.3 | loop fusion | flops 5750784 | bytes 23003140 | tf_op jit(solution)/shard_map/add | solution.py:1652
  (103 shorter events, 1.3 us)
Async XLA Ops:
  7.2 192.3 %all-gather.4.cloned.1.call-start = ((), (), s32[]{:S(2)}) async-start(), calls=%async_computation | async-start | bytes 9510912 | tf_op jit(solution)/shard_map/all_gather | solution.py:1525
  9.9 244.1 %all-gather.6.cloned.1.call-start = ((), (), s32[]{:S(2)}) async-start(), calls=%async_computation.1 | async-start | bytes 10862592 | tf_op jit(solution)/shard_map/all_gather | solution.py:1541
  10.0 2.4 copy-start.19
  65.8 2.4 copy-start.1
  68.3 2.9 copy-start.2
  68.3 4.5 copy-start.23
  68.3 5.2 %copy-start.20 = (s32[1,1024]{1,0:T(1,128)S(1)}, s32[1,1024]{1,0:T(1,128)}, u32[]{:S(2)}) copy-start(s32[1,1024]{1,0:T(1,128)} %param.19) | copy-start | bytes 12292
  69.2 249.6 %all-gather.8.cloned.1.call-start = ((), (), s32[]{:S(2)}) async-start(), calls=%async_computation.2 | async-start | bytes 3612672 | tf_op jit(solution)/shard_map/all_gather | solution.py:1590
  166.7 3.1 copy-start.9
  173.0 22.0 %copy-start.3 = (f32[1024,768]{1,0:T(8,128)}, f32[1024,768]{1,0:T(8,128)S(1)}, u32[]{:S(2)}) copy-start(f32[1024,768]{1,0:T(8,128)S(1)} %get-tuple-element.119) | copy-start | bytes 9437188
  195.5 1.7 copy-start.5
  213.7 4.2 copy-start.6
  219.6 1.7 copy-start.7
  254.0 5.0 %copy-start.4 = (f32[1024,768]{1,0:T(8,128)S(1)}, f32[1024,768]{1,0:T(8,128)}, u32[]{:S(2)}) copy-start(f32[1024,768]{1,0:T(8,128)} %copy-done.3) | copy-start | bytes 9437188
  256.6 5.4 %copy-start.14 = (f32[1024,768]{1,0:T(8,128)S(1)}, f32[1024,768]{1,0:T(8,128)}, u32[]{:S(2)}) copy-start(f32[1024,768]{1,0:T(8,128)} %get-tuple-element.54) | copy-start | bytes 9437188
  259.1 6.1 %slice-start.2 = ((s8[5898240]{0:T(1024)(128)(4,1)}), s8[4194304]{0:T(1024)(128)(4,1)S(1)}, s32[]{:S(2)}) async-start(s8[5898240]{0:T(1024)(128)(4,1)} %bitcast.46), calls=%async_computation.5 | async-start | bytes 8388608
  262.1 1.9 copy-start.8
  262.1 3.1 slice-start.3
  263.4 1.7 copy-start.11
  264.0 3.7 slice-start
  265.1 1.4 copy-start.16
  265.1 2.6 slice-start.1
  267.7 40.3 %copy-start.10 = (f32[1024,768]{1,0:T(8,128)S(1)}, f32[1024,768]{1,0:T(8,128)}, u32[]{:S(2)}) copy-start(f32[1024,768]{1,0:T(8,128)} %get-tuple-element.44) | copy-start | bytes 9437188
  308.0 8.3 %copy-start = (bf16[3,1024,768]{2,1,0:T(8,128)(2,1)}, bf16[3,1024,768]{2,1,0:T(8,128)(2,1)S(1)}, u32[]{:S(2)}) copy-start(bf16[3,1024,768]{2,1,0:T(8,128)(2,1)S(1)} %attention_backward.1.refs_6_) | copy-start | bytes 14155780
  312.4 1.9 copy-start.12
  326.3 134.1 %copy-start.15 = (f32[96,5462]{1,0:T(8,128)S(1)}, f32[96,5462]{1,0:T(8,128)}, u32[]{:S(2)}) copy-start(f32[96,5462]{1,0:T(8,128)} %param.27) | copy-start | bytes 6292228
  460.5 7.6 %copy-start.21 = (f32[15,96]{1,0:T(8,128)S(1)}, f32[15,96]{1,0:T(8,128)}, u32[]{:S(2)}) copy-start(f32[15,96]{1,0:T(8,128)} %param.32) | copy-start | bytes 17284
  460.5 7.6 %copy-start.22 = (f32[15,96]{1,0:T(8,128)S(1)}, f32[15,96]{1,0:T(8,128)}, u32[]{:S(2)}) copy-start(f32[15,96]{1,0:T(8,128)} %param.31) | copy-start | bytes 17284
  460.5 9.6 %copy-start.13 = (f32[13,96,768]{2,1,0:T(8,128)S(1)}, f32[13,96,768]{2,1,0:T(8,128)}, u32[]{:S(2)}) copy-start(f32[13,96,768]{2,1,0:T(8,128)} %param.22) | copy-start | bytes 11501572
  470.1 8.5 %copy-start.17 = (f32[13,96,768]{2,1,0:T(8,128)S(1)}, f32[13,96,768]{2,1,0:T(8,128)}, u32[]{:S(2)}) copy-start(f32[13,96,768]{2,1,0:T(8,128)} %param.24) | copy-start | bytes 11501572
  470.1 8.5 %copy-start.18 = (f32[13,96,768]{2,1,0:T(8,128)S(1)}, f32[13,96,768]{2,1,0:T(8,128)}, u32[]{:S(2)}) copy-start(f32[13,96,768]{2,1,0:T(8,128)} %param.23) | copy-start | bytes 11501572
Sparse Core Ops, SparseCore 0:
  10.8 161.7 all-gather.3
  174.8 59.0 all-gather.5
  254.2 63.6 all-gather.7

commit v13 on v9

--- a/solution.py
+++ b/solution.py
@@ -14,7 +14,7 @@
 QTILE = 256
 PAIR = 2 * HEAD
 ROWS = 256
-HIDDEN_TILE = 384
+HIDDEN_TILE = 768
 MESH = pl.DeviceIdType.MESH
 CODE_TOP = 32766.0
 CODE_FLOOR = 1e-33

time: 498 us -> 486 us (0.976)
  Pallas kernels: 374 us -> 362 us
    pallas_call x1, Pallas kernels: 33.2 us -> 26.5 us  [mlp_backward(): pl.pallas_call(mlp_backward_kernel, grid=(up_count * split,), out_shape=(...]
  transfers between devices with their start and end apart: 3 -> 3, of which waited for: 0 -> 0; matrix products, arithmetic and copies ran while one was open for 12% -> 12% of each run, Pallas kernels for 49% -> 48%
where the time goes in v13:
time: 486 us; the launch traced here: 482 us
  Pallas kernels  362 us (74%)
  other arithmetic  49.7 us (10%)
  matrix products  33.7 us (7%)
  local copies, waits for them, and re-layouts  18.7 us (4%)
  between operations  16.8 us (3%)
    pallas_call x1, Pallas kernels, reduce_gradients(): pl.pallas_call(functools.partial(reduce_kernel, counts), out_shape=(jax.S...  130 us
    pallas_call x1, Pallas kernels, attention_forward_gathering(): pl.pallas_call(attention_gather_kernel, grid=(width // PAIR,), out_shape=...  79.8 us
    pallas_call x1, Pallas kernels, gather_weights(): pl.pallas_call(gather_kernel, out_shape=(jax.ShapeDtypeStruct((count, SHA...  54.6 us
    pallas_call x1, Pallas kernels, attention_backward(): pl.pallas_call(attention_backward_kernel, grid=(width // PAIR,), out_shap...  40.1 us
    pallas_call x1, Pallas kernels, mlp_backward(): pl.pallas_call(mlp_backward_kernel, grid=(up_count * split,), out_shape=(...  26.5 us
    pallas_call x1, Pallas kernels, mlp_forward(): pl.pallas_call(mlp_forward_kernel, grid=(up_count * split,), out_shape=(j...  17 us
    pallas_call x1, Pallas kernels, classify(): pl.pallas_call(functools.partial(head_kernel, image_total), out_shape=(ja...  14.5 us
  transfers between devices with their start and end apart: 3, of which 0 were waited for; matrix products, arithmetic and copies ran while one was open for 12% of the time, Pallas kernels for 48%

profile of v13, /device:TPU:0, one launch (start us, length us, event | category | flops | bytes accessed | tf_op | source)
XLA Modules:
  0.0 481.5 jit_solution(5400039101024876139)
XLA Ops:
  7.2 2.7 convert_element_type.76
  10.0 2.3 convert_element_type.70
  12.3 1.2 copy-done.18
  13.6 54.6 %gather_weights.1 = (bf16[5,768,768]{2,1,0:T(8,128)(2,1)S(1)}, f32[8,16,128]{2,1,0:T(8,128)S(1)}) custom-call(bf16[5,96,768]{2,1,0:T(8,128)(2,1)S(1)} %slice.142.own_ref, f32[16,128]{1,0:T(8,128)S(1)} %pad.12.vec_ref), custom_call_target="tpu_custom_call" | custom-call | tf_op jit(solution)/shard_map/gather_weights/pallas_call | solution.py:1374
  68.2 2.0 constant_dynamic-slice_fusion
  70.2 0.1 abs_reduce_fusion
  70.4 0.1 clamp_convert_fusion
  70.7 0.9 fusion.35
  71.7 1.4 slice.148.own_ref
  73.1 0.1 slice_reduce_fusion.1
  73.6 0.2 copy.58.qids_ref
  74.1 0.1 reshape.259.bias_ref
  74.4 0.7 copy.61.labels_ref
  75.2 3.2 add_reduce_fusion
  78.4 0.6 multiply_reduce_fusion.7
  79.2 0.6 add_convert_fusion.3.refs_3_
  79.8 6.6 %fusion.q_ref.k_ref.v_ref = bf16[3,1024,768]{2,1,0:T(8,128)(2,1)S(1)} fusion(f32[3,768]{1,0:T(4,128)S(1)} %pad_maximum_fusion, bf16[5,768,768]{2,1,0:T(8,128)(2,1)} %copy-done.4, bf16[1024,768]{1,0:T(8,128)(2,1)S(1)} %add_convert_fusion.3.refs_3_), kind=kOutput, calls=%fused_computation.4 | convolution fusion | flops 3628597248 | bytes 9839616 | tf_op jit(solution)/shard_map/td,kde->kte/dot_general | solution.py:345
  86.5 79.8 %attention_forward.1 = (bf16[1024,768]{1,0:T(8,128)(2,1)S(1)}, bf16[8,768,768]{2,1,0:T(8,128)(2,1)}) custom-call(s32[1024,1]{1,0:T(8,128)S(1)} %copy.58.qids_ref, s32[1,1024]{1,0:T(1,128)S(1)} %broadcast_select_fusion.1.kcodes_ref, bf16[3,1024,768]{2,1,0:T(8,128)(2,1)S(1)} %fusion.q_ref.k_ref.v_ref, bf16[3,1024,768]{2,1,0:T(8,128)(2,1)S(1)} %fusion.q_ref.k_ref.v_ref, ...), custom_call_target="tpu_custom_call" | custom-call | tf_op jit(solution)/shard_map/attention_forward/pallas_call | solution.py:1351
  166.4 3.4 fusion.64
  169.8 0.5 multiply_reduce_fusion.6
  170.4 0.6 add_convert_fusion.2.x_ref
  170.9 17.0 %mlp_forward.1 = (bf16[1024,3072]{1,0:T(8,128)(2,1)}, f32[1024,3072]{1,0:T(8,128)}, f32[1024,768]{1,0:T(8,128)S(1)}) custom-call(bf16[1024,768]{1,0:T(8,128)(2,1)S(1)} %add_convert_fusion.2.x_ref, bf16[8,768,768]{2,1,0:T(8,128)(2,1)} %get-tuple-element.42.up_ref.down_ref, f32[1,3072]{1,0:T(1,128)S(1)} %reshape.259.bias_ref, ...), custom_call_target="tpu_custom_call" | custom-call | tf_op jit(solution)/shard_map/mlp_forward/pallas_call | solution.py:300
  187.9 0.1 convert_reduce_fusion.5
  188.1 0.4 fusion.62
  188.5 0.5 multiply_reduce_fusion.5
  189.0 1.1 copy-done.7
  190.2 2.3 fusion.30.pooled_ref
  192.5 14.5 %classify.1 = (f32[8,768]{1,0:T(8,128)}, bf16[32,6272]{1,0:T(8,128)(2,1)}, f32[8,128]{1,0:T(8,128)}) custom-call(f32[8,768]{1,0:T(8,128)} %fusion.30.pooled_ref, s32[32,2]{1,0:T(8,128)} %copy.61.labels_ref, bf16[768,5462]{1,0:T(8,128)(2,1)} %all-gather.4.cloned.1.call-done.head_hbm), custom_call_target="tpu_custom_call" | custom-call | tf_op jit(solution)/shard_map/classify/pallas_call | solution.py:1155
  207.0 4.2 multiply_reduce_fusion
  211.2 1.5 fusion.61
  212.7 0.3 convert_reduce_fusion
  213.1 1.3 copy-done.9
  214.4 26.5 %mlp_backward.1 = (f32[4,768,768]{2,1,0:T(8,128)}, f32[4,768,768]{2,1,0:T(8,128)}, f32[1,3072]{1,0:T(1,128)S(1)}, f32[1024,768]{1,0:T(8,128)}) custom-call(bf16[1024,768]{1,0:T(8,128)(2,1)S(1)} %add_convert_fusion.2.x_ref, bf16[1024,768]{1,0:T(8,128)(2,1)S(1)} %get-tuple-element.93.dm_ref, bf16[8,768,768]{2,1,0:T(8,128)(2,1)} %get-tuple-element.42.up_ref.down_ref, ...), custom_call_target="tpu_custom_call" | custom-call | tf_op jit(solution)/shard_map/mlp_backward/pallas_call | solution.py:320
  240.9 0.3 copy.62
  242.0 1.3 slice.137
  243.4 3.9 multiply_reduce_fusion.1
  247.3 1.5 fusion.60
  248.9 0.3 copy-done.10
  249.2 0.5 convert_reduce_fusion.1
  249.8 0.8 copy-done.13
  250.5 1.1 copy-done.20
  251.7 1.4 convolution_convert_fusion.do_ref
  253.2 40.1 %attention_backward.1.refs_6_ = bf16[3,1024,768]{2,1,0:T(8,128)(2,1)S(1)} custom-call(s32[1,1024]{1,0:T(1,128)S(1)} %copy-done.3, s32[1024,1]{1,0:T(8,128)S(1)} %broadcast_select_fusion.kcodes_ref, bf16[3,1024,768]{2,1,0:T(8,128)(2,1)S(1)} %bitcast.73, bf16[3,1024,768]{2,1,0:T(8,128)(2,1)S(1)} %bitcast.73, bf16[3,1024,768]{2,1,0:T(8,128)(2,1)S(1)} %bitcast.73, ...), custom_call_target="tpu_custom_call" | custom-call | tf_op jit(solution)/shard_map/attention_backward/pallas_call | solution.py:215
  293.3 8.1 %fusion.1 = (f32[768]{0:T(1024)S(1)}, f32[1024]{0:T(1024)S(1)}, f32[768]{0:T(1024)S(1)}, f32[1024,768,1]{1,0,2:T(8,128)S(1)}) fusion(f32[768,1024]{0,1:T(8,128)} %copy-done.11, f32[1024]{0:T(1024)S(1)} %fusion.49, f32[1024]{0:T(1024)S(1)} %broadcast_multiply_fusion.3, f32[768]{0:T(1024)S(1)} %add.190, f32[768]{0:T(1024)S(1)} %mul.331, ...), kind=kOutput, calls=%fused_computation.12 | convolution fusion | flops 3630953984 | bytes 14575616 | tf_op jit(solution)/shard_map/kte,kde->td/dot_general | solution.py:394
  301.4 1.6 fusion.59
  303.1 0.3 copy-done.14
  303.3 2.0 convert_reduce_fusion.4
  305.4 0.5 convert_reduce_fusion.2
  306.0 0.5 broadcast.282
  306.5 0.7 reduce.52
  307.2 0.1 concatenate.34
  307.3 0.6 pad.13.refs_8_
  307.9 1.0 slice.161
  308.9 4.4 multiply_reduce_fusion.8
  313.4 1.4 maximum_bitcast_fusion
  314.7 0.1 copy.64
  314.8 0.6 pad.14.refs_9_
  315.4 129.9 %reduce_gradients.1 = (f32[13,96,768]{2,1,0:T(8,128)}, f32[13,96,768]{2,1,0:T(8,128)}, f32[13,96,768]{2,1,0:T(8,128)}, f32[13,96,768]{2,1,0:T(8,128)}, f32[13,1,...) custom-call(f32[4,768,768]{2,1,0:T(8,128)} %get-tuple-element.47.refs_0_, ...), custom_call_target="tpu_custom_call" | custom-call | tf_op jit(solution)/shard_map/reduce_gradients/pallas_call | solution.py:924
  445.4 1.3 fusion.63
  448.0 0.8 copy.71
  448.8 7.6 %multiply_subtract_fusion.1 = (f32[96,5462]{1,0:T(8,128)}, f32[96,5462]{1,0:T(8,128)}, f32[96,5462]{1,0:T(8,128)}) fusion(f32[96,5462]{1,0:T(8,128)S(1)} %copy-done.17, f32[]{:T(128)S(6)} %sub.74, f32[]{:T(128)S(6)} %sub.73, f32[96,5462]{1,0:T(8,128)} %get-tuple-element.123, f32[]{:T(128)} %bitcast.18, f32[96,5462]{1,0:T(8,128)} %param.29, f32[96,5462]{1,0:T(8,128)} %param.28), kind=kLoop, calls=%fused_computation.48 | loop fusion | flops 8389632 | bytes 14681868 | tf_op jit(solution)/shard_map/sub | solution.py:1397
  456.4 2.1 multiply_subtract_fusion.2
  458.5 8.7 %multiply_subtract_fusion = (f32[13,96,768]{2,1,0:T(8,128)}, f32[13,96,768]{2,1,0:T(8,128)}) fusion(f32[13,96,768]{2,1,0:T(8,128)S(1)} %copy-done.15, f32[13,96,768]{2,1,0:T(8,128)} %get-tuple-element.58, f32[13,768]{1,0:T(8,128)S(1)} %bitcast.80, f32[13,96,768]{2,1,0:T(8,128)} %get-tuple-element.60, f32[]{:T(128)} %bitcast.18), kind=kLoop, calls=%fused_computation.7 | loop fusion | flops 2875392 | bytes 19209220 | tf_op jit(solution)/shard_map/sub | solution.py:1604
  467.1 7.6 %multiply_add_fusion = (f32[13,96,768]{2,1,0:T(8,128)}, f32[13,96,768]{2,1,0:T(8,128)}) fusion(f32[13,96,768]{2,1,0:T(8,128)} %get-tuple-element.62, f32[13,96,768]{2,1,0:T(8,128)S(1)} %copy-done.21, f32[]{:T(128)S(6)} %mul.380, f32[13,96,768]{2,1,0:T(8,128)} %get-tuple-element.61, f32[13,96,768]{2,1,0:T(8,128)S(1)} %copy-done.22), kind=kLoop, calls=%fused_computation.5 | loop fusion | flops 5750784 | bytes 23003140 | tf_op jit(solution)/shard_map/add | solution.py:1607
  (117 shorter events, 1.9 us)
Async XLA Ops:
  7.2 185.3 %all-gather.4.cloned.1.call-start = ((), (), s32[]{:S(2)}) async-start(), calls=%async_computation | async-start | bytes 9510912 | tf_op jit(solution)/shard_map/all_gather | solution.py:1483
  9.9 230.9 %all-gather.6.cloned.1.call-start = ((), (), s32[]{:S(2)}) async-start(), calls=%async_computation.1 | async-start | bytes 10862592 | tf_op jit(solution)/shard_map/all_gather | solution.py:1496
  10.0 3.6 copy-start.23
  12.3 1.3 copy-start.18
  68.2 2.4 copy-start.4
  70.7 3.0 copy-start.3
  70.7 3.7 copy-start.27
  71.7 236.2 %all-gather.8.cloned.1.call-start = ((), (), s32[]{:S(2)}) async-start(), calls=%async_computation.2 | async-start | bytes 3612672 | tf_op jit(solution)/shard_map/all_gather | solution.py:1545
  78.4 88.0 %copy-start.11 = (f32[768,1024]{0,1:T(8,128)}, f32[768,1024]{0,1:T(8,128)S(1)}, u32[]{:S(2)}) copy-start(f32[768,1024]{0,1:T(8,128)S(1)} %get-tuple-element.117) | copy-start | bytes 9437188
  78.4 0.7 copy-start.24
  79.8 6.7 %copy-start.19 = (bf16[1024,768]{1,0:T(8,128)(2,1)}, bf16[1024,768]{1,0:T(8,128)(2,1)S(1)}, u32[]{:S(2)}) copy-start(bf16[1024,768]{1,0:T(8,128)(2,1)S(1)} %add_convert_fusion.3.refs_3_) | copy-start | bytes 4718596
  86.5 79.8 %copy-start = (bf16[3,1024,768]{2,1,0:T(8,128)(2,1)}, bf16[3,1024,768]{2,1,0:T(8,128)(2,1)S(1)}, u32[]{:S(2)}) copy-start(bf16[3,1024,768]{2,1,0:T(8,128)(2,1)S(1)} %fusion.q_ref.k_ref.v_ref) | copy-start | bytes 14155780
  166.3 3.5 copy-start.2
  169.8 18.2 %copy-start.5 = (f32[1024,768]{1,0:T(8,128)}, f32[1024,768]{1,0:T(8,128)S(1)}, u32[]{:S(2)}) copy-start(f32[1024,768]{1,0:T(8,128)S(1)} %get-tuple-element.119) | copy-start | bytes 9437188
  188.5 1.7 copy-start.7
  206.9 4.2 copy-start.8
  212.7 1.7 copy-start.9
  241.9 5.4 %copy-start.6 = (f32[1024,768]{1,0:T(8,128)S(1)}, f32[1024,768]{1,0:T(8,128)}, u32[]{:S(2)}) copy-start(f32[1024,768]{1,0:T(8,128)} %copy-done.5) | copy-start | bytes 9437188
  241.9 5.4 %copy-start.16 = (f32[1024,768]{1,0:T(8,128)S(1)}, f32[1024,768]{1,0:T(8,128)}, u32[]{:S(2)}) copy-start(f32[1024,768]{1,0:T(8,128)} %get-tuple-element.49) | copy-start | bytes 9437188
  243.3 8.3 %slice-start.2 = ((s8[5898240]{0:T(1024)(128)(4,1)}), s8[4194304]{0:T(1024)(128)(4,1)S(1)}, s32[]{:S(2)}) async-start(s8[5898240]{0:T(1024)(128)(4,1)} %bitcast.78), calls=%async_computation.5 | async-start | bytes 8388608
  247.3 1.9 copy-start.10
  247.3 4.4 slice-start.3
  248.9 1.7 copy-start.13
  249.2 3.9 slice-start
  250.5 1.1 copy-start.20
  251.7 1.5 slice-start.1
  293.3 12.1 %copy-start.1 = (bf16[3,1024,768]{2,1,0:T(8,128)(2,1)}, bf16[3,1024,768]{2,1,0:T(8,128)(2,1)S(1)}, u32[]{:S(2)}) copy-start(bf16[3,1024,768]{2,1,0:T(8,128)(2,1)S(1)} %attention_backward.1.refs_6_) | copy-start | bytes 14155780
  293.3 8.1 %copy-start.12 = (f32[768,1024]{0,1:T(8,128)S(1)}, f32[768,1024]{0,1:T(8,128)}, u32[]{:S(2)}) copy-start(f32[768,1024]{0,1:T(8,128)} %copy-done.11) | copy-start | bytes 9437188
  301.4 1.9 copy-start.14
  315.4 133.3 %copy-start.17 = (f32[96,5462]{1,0:T(8,128)S(1)}, f32[96,5462]{1,0:T(8,128)}, u32[]{:S(2)}) copy-start(f32[96,5462]{1,0:T(8,128)} %param.27) | copy-start | bytes 6292228
  448.8 7.6 %copy-start.25 = (f32[15,96]{1,0:T(8,128)S(1)}, f32[15,96]{1,0:T(8,128)}, u32[]{:S(2)}) copy-start(f32[15,96]{1,0:T(8,128)} %param.32) | copy-start | bytes 17284
  448.8 7.6 %copy-start.26 = (f32[15,96]{1,0:T(8,128)S(1)}, f32[15,96]{1,0:T(8,128)}, u32[]{:S(2)}) copy-start(f32[15,96]{1,0:T(8,128)} %param.31) | copy-start | bytes 17284
  448.8 9.7 %copy-start.15 = (f32[13,96,768]{2,1,0:T(8,128)S(1)}, f32[13,96,768]{2,1,0:T(8,128)}, u32[]{:S(2)}) copy-start(f32[13,96,768]{2,1,0:T(8,128)} %param.22) | copy-start | bytes 11501572
  458.5 8.7 %copy-start.21 = (f32[13,96,768]{2,1,0:T(8,128)S(1)}, f32[13,96,768]{2,1,0:T(8,128)}, u32[]{:S(2)}) copy-start(f32[13,96,768]{2,1,0:T(8,128)} %param.24) | copy-start | bytes 11501572
  458.5 8.7 %copy-start.22 = (f32[13,96,768]{2,1,0:T(8,128)S(1)}, f32[13,96,768]{2,1,0:T(8,128)}, u32[]{:S(2)}) copy-start(f32[13,96,768]{2,1,0:T(8,128)} %param.23) | copy-start | bytes 11501572
Sparse Core Ops, SparseCore 0:
  10.8 162.9 all-gather.3
  175.4 59.1 all-gather.5
  241.0 63.0 all-gather.7

commit v14 on v13

--- a/solution.py
+++ b/solution.py
@@ -11,7 +11,7 @@
 HEAD = 64
 LABELS_REAL = 21843
 IMAGE_MAX = 196
-QTILE = 256
+QTILE = 512
 PAIR = 2 * HEAD
 ROWS = 256
 HIDDEN_TILE = 768

time: 486 us -> 485 us (level)
  no operation moved by 1% of the time
where the time goes in v14:
time: 485 us; the launch traced here: 480 us
  Pallas kernels  361 us (74%)
  other arithmetic  49.7 us (10%)
  matrix products  33.8 us (7%)
  local copies, waits for them, and re-layouts  18.7 us (4%)
  between operations  16.8 us (3%)
    pallas_call x1, Pallas kernels, reduce_gradients(): pl.pallas_call(functools.partial(reduce_kernel, counts), out_shape=(jax.S...  130 us
    pallas_call x1, Pallas kernels, attention_forward_gathering(): pl.pallas_call(attention_gather_kernel, grid=(width // PAIR,), out_shape=...  80.1 us
    pallas_call x1, Pallas kernels, gather_weights(): pl.pallas_call(gather_kernel, out_shape=(jax.ShapeDtypeStruct((count, SHA...  54.6 us
    pallas_call x1, Pallas kernels, attention_backward(): pl.pallas_call(attention_backward_kernel, grid=(width // PAIR,), out_shap...  37.5 us
    pallas_call x1, Pallas kernels, mlp_backward(): pl.pallas_call(mlp_backward_kernel, grid=(up_count * split,), out_shape=(...  26.5 us
    pallas_call x1, Pallas kernels, mlp_forward(): pl.pallas_call(mlp_forward_kernel, grid=(up_count * split,), out_shape=(j...  17 us
    pallas_call x1, Pallas kernels, classify(): pl.pallas_call(functools.partial(head_kernel, image_total), out_shape=(ja...  14.8 us
  transfers between devices with their start and end apart: 3, of which 0 were waited for; matrix products, arithmetic and copies ran while one was open for 12% of the time, Pallas kernels for 48%

profile of v14, /device:TPU:0, one launch (start us, length us, event | category | flops | bytes accessed | tf_op | source)
XLA Modules:
  0.0 479.8 jit_solution(18157078226836721154)
XLA Ops:
  7.2 2.7 convert_element_type.76
  10.0 2.3 convert_element_type.70
  12.3 1.2 copy-done.18
  13.6 54.6 %gather_weights.1 = (bf16[5,768,768]{2,1,0:T(8,128)(2,1)S(1)}, f32[8,16,128]{2,1,0:T(8,128)S(1)}) custom-call(bf16[5,96,768]{2,1,0:T(8,128)(2,1)S(1)} %slice.142.own_ref, f32[16,128]{1,0:T(8,128)S(1)} %pad.12.vec_ref), custom_call_target="tpu_custom_call" | custom-call | tf_op jit(solution)/shard_map/gather_weights/pallas_call | solution.py:1374
  68.2 2.0 constant_dynamic-slice_fusion
  70.2 0.1 abs_reduce_fusion
  70.4 0.1 clamp_convert_fusion
  70.7 0.9 fusion.35
  71.7 1.4 slice.148.own_ref
  73.1 0.1 slice_reduce_fusion.1
  73.6 0.2 copy.58.qids_ref
  74.1 0.1 reshape.259.bias_ref
  74.4 0.7 copy.61.labels_ref
  75.2 3.2 add_reduce_fusion
  78.4 0.6 multiply_reduce_fusion.7
  79.2 0.6 add_convert_fusion.3.refs_3_
  79.8 6.6 %fusion.q_ref.k_ref.v_ref = bf16[3,1024,768]{2,1,0:T(8,128)(2,1)S(1)} fusion(f32[3,768]{1,0:T(4,128)S(1)} %pad_maximum_fusion, bf16[5,768,768]{2,1,0:T(8,128)(2,1)} %copy-done.4, bf16[1024,768]{1,0:T(8,128)(2,1)S(1)} %add_convert_fusion.3.refs_3_), kind=kOutput, calls=%fused_computation.4 | convolution fusion | flops 3628597248 | bytes 9839616 | tf_op jit(solution)/shard_map/td,kde->kte/dot_general | solution.py:345
  86.5 80.1 %attention_forward.1 = (bf16[1024,768]{1,0:T(8,128)(2,1)S(1)}, bf16[8,768,768]{2,1,0:T(8,128)(2,1)}) custom-call(s32[1024,1]{1,0:T(8,128)S(1)} %copy.58.qids_ref, s32[1,1024]{1,0:T(1,128)S(1)} %broadcast_select_fusion.1.kcodes_ref, bf16[3,1024,768]{2,1,0:T(8,128)(2,1)S(1)} %fusion.q_ref.k_ref.v_ref, bf16[3,1024,768]{2,1,0:T(8,128)(2,1)S(1)} %fusion.q_ref.k_ref.v_ref, ...), custom_call_target="tpu_custom_call" | custom-call | tf_op jit(solution)/shard_map/attention_forward/pallas_call | solution.py:1351
  166.6 3.4 fusion.64
  170.1 0.5 multiply_reduce_fusion.6
  170.6 0.6 add_convert_fusion.2.x_ref
  171.2 17.0 %mlp_forward.1 = (bf16[1024,3072]{1,0:T(8,128)(2,1)}, f32[1024,3072]{1,0:T(8,128)}, f32[1024,768]{1,0:T(8,128)S(1)}) custom-call(bf16[1024,768]{1,0:T(8,128)(2,1)S(1)} %add_convert_fusion.2.x_ref, bf16[8,768,768]{2,1,0:T(8,128)(2,1)} %get-tuple-element.42.up_ref.down_ref, f32[1,3072]{1,0:T(1,128)S(1)} %reshape.259.bias_ref, ...), custom_call_target="tpu_custom_call" | custom-call | tf_op jit(solution)/shard_map/mlp_forward/pallas_call | solution.py:300
  188.2 0.1 convert_reduce_fusion.5
  188.3 0.4 fusion.62
  188.8 0.5 multiply_reduce_fusion.5
  189.3 1.1 copy-done.7
  190.4 2.3 fusion.30.pooled_ref
  192.7 14.8 %classify.1 = (f32[8,768]{1,0:T(8,128)}, bf16[32,6272]{1,0:T(8,128)(2,1)}, f32[8,128]{1,0:T(8,128)}) custom-call(f32[8,768]{1,0:T(8,128)} %fusion.30.pooled_ref, s32[32,2]{1,0:T(8,128)} %copy.61.labels_ref, bf16[768,5462]{1,0:T(8,128)(2,1)} %all-gather.4.cloned.1.call-done.head_hbm), custom_call_target="tpu_custom_call" | custom-call | tf_op jit(solution)/shard_map/classify/pallas_call | solution.py:1155
  207.5 4.2 multiply_reduce_fusion
  211.7 1.5 fusion.61
  213.3 0.3 convert_reduce_fusion
  213.6 1.3 copy-done.9
  214.9 26.5 %mlp_backward.1 = (f32[4,768,768]{2,1,0:T(8,128)}, f32[4,768,768]{2,1,0:T(8,128)}, f32[1,3072]{1,0:T(1,128)S(1)}, f32[1024,768]{1,0:T(8,128)}) custom-call(bf16[1024,768]{1,0:T(8,128)(2,1)S(1)} %add_convert_fusion.2.x_ref, bf16[1024,768]{1,0:T(8,128)(2,1)S(1)} %get-tuple-element.93.dm_ref, bf16[8,768,768]{2,1,0:T(8,128)(2,1)} %get-tuple-element.42.up_ref.down_ref, ...), custom_call_target="tpu_custom_call" | custom-call | tf_op jit(solution)/shard_map/mlp_backward/pallas_call | solution.py:320
  241.4 0.3 copy.62
  242.5 1.3 slice.137
  243.9 3.9 multiply_reduce_fusion.1
  247.8 1.5 fusion.60
  249.4 0.3 copy-done.10
  249.7 0.5 convert_reduce_fusion.1
  250.3 0.8 copy-done.13
  251.0 1.1 copy-done.20
  252.2 1.4 convolution_convert_fusion.do_ref
  253.7 37.5 %attention_backward.1.refs_6_ = bf16[3,1024,768]{2,1,0:T(8,128)(2,1)S(1)} custom-call(s32[1,1024]{1,0:T(1,128)S(1)} %copy-done.3, s32[1024,1]{1,0:T(8,128)S(1)} %broadcast_select_fusion.kcodes_ref, bf16[3,1024,768]{2,1,0:T(8,128)(2,1)S(1)} %bitcast.73, bf16[3,1024,768]{2,1,0:T(8,128)(2,1)S(1)} %bitcast.73, bf16[3,1024,768]{2,1,0:T(8,128)(2,1)S(1)} %bitcast.73, ...), custom_call_target="tpu_custom_call" | custom-call | tf_op jit(solution)/shard_map/attention_backward/pallas_call | solution.py:215
  291.1 8.1 %fusion.1 = (f32[768]{0:T(1024)S(1)}, f32[1024]{0:T(1024)S(1)}, f32[768]{0:T(1024)S(1)}, f32[1024,768,1]{1,0,2:T(8,128)S(1)}) fusion(f32[768,1024]{0,1:T(8,128)} %copy-done.11, f32[1024]{0:T(1024)S(1)} %fusion.49, f32[1024]{0:T(1024)S(1)} %broadcast_multiply_fusion.3, f32[768]{0:T(1024)S(1)} %add.190, f32[768]{0:T(1024)S(1)} %mul.331, ...), kind=kOutput, calls=%fused_computation.12 | convolution fusion | flops 3630953984 | bytes 14575616 | tf_op jit(solution)/shard_map/kte,kde->td/dot_general | solution.py:394
  299.3 1.6 fusion.59
  300.9 0.3 copy-done.14
  301.2 2.0 convert_reduce_fusion.4
  303.3 0.5 convert_reduce_fusion.2
  303.8 0.5 broadcast.282
  304.3 0.7 reduce.52
  305.0 0.1 concatenate.34
  305.1 0.6 pad.13.refs_8_
  305.8 1.0 slice.161
  306.8 4.4 multiply_reduce_fusion.8
  311.2 1.4 maximum_bitcast_fusion
  312.6 0.1 copy.64
  312.7 0.6 pad.14.refs_9_
  313.3 130.4 %reduce_gradients.1 = (f32[13,96,768]{2,1,0:T(8,128)}, f32[13,96,768]{2,1,0:T(8,128)}, f32[13,96,768]{2,1,0:T(8,128)}, f32[13,96,768]{2,1,0:T(8,128)}, f32[13,1,...) custom-call(f32[4,768,768]{2,1,0:T(8,128)} %get-tuple-element.47.refs_0_, ...), custom_call_target="tpu_custom_call" | custom-call | tf_op jit(solution)/shard_map/reduce_gradients/pallas_call | solution.py:924
  443.7 1.3 fusion.63
  446.3 0.8 copy.71
  447.1 7.6 %multiply_subtract_fusion.1 = (f32[96,5462]{1,0:T(8,128)}, f32[96,5462]{1,0:T(8,128)}, f32[96,5462]{1,0:T(8,128)}) fusion(f32[96,5462]{1,0:T(8,128)S(1)} %copy-done.17, f32[]{:T(128)S(6)} %sub.74, f32[]{:T(128)S(6)} %sub.73, f32[96,5462]{1,0:T(8,128)} %get-tuple-element.123, f32[]{:T(128)} %bitcast.18, f32[96,5462]{1,0:T(8,128)} %param.29, f32[96,5462]{1,0:T(8,128)} %param.28), kind=kLoop, calls=%fused_computation.48 | loop fusion | flops 8389632 | bytes 14681868 | tf_op jit(solution)/shard_map/sub | solution.py:1397
  454.7 2.1 multiply_subtract_fusion.2
  456.8 8.7 %multiply_subtract_fusion = (f32[13,96,768]{2,1,0:T(8,128)}, f32[13,96,768]{2,1,0:T(8,128)}) fusion(f32[13,96,768]{2,1,0:T(8,128)S(1)} %copy-done.15, f32[13,96,768]{2,1,0:T(8,128)} %get-tuple-element.58, f32[13,768]{1,0:T(8,128)S(1)} %bitcast.80, f32[13,96,768]{2,1,0:T(8,128)} %get-tuple-element.60, f32[]{:T(128)} %bitcast.18), kind=kLoop, calls=%fused_computation.7 | loop fusion | flops 2875392 | bytes 19209220 | tf_op jit(solution)/shard_map/sub | solution.py:1604
  465.5 7.6 %multiply_add_fusion = (f32[13,96,768]{2,1,0:T(8,128)}, f32[13,96,768]{2,1,0:T(8,128)}) fusion(f32[13,96,768]{2,1,0:T(8,128)} %get-tuple-element.62, f32[13,96,768]{2,1,0:T(8,128)S(1)} %copy-done.21, f32[]{:T(128)S(6)} %mul.380, f32[13,96,768]{2,1,0:T(8,128)} %get-tuple-element.61, f32[13,96,768]{2,1,0:T(8,128)S(1)} %copy-done.22), kind=kLoop, calls=%fused_computation.5 | loop fusion | flops 5750784 | bytes 23003140 | tf_op jit(solution)/shard_map/add | solution.py:1607
  (117 shorter events, 1.9 us)
Async XLA Ops:
  7.2 185.5 %all-gather.4.cloned.1.call-start = ((), (), s32[]{:S(2)}) async-start(), calls=%async_computation | async-start | bytes 9510912 | tf_op jit(solution)/shard_map/all_gather | solution.py:1483
  9.9 231.4 %all-gather.6.cloned.1.call-start = ((), (), s32[]{:S(2)}) async-start(), calls=%async_computation.1 | async-start | bytes 10862592 | tf_op jit(solution)/shard_map/all_gather | solution.py:1496
  10.0 3.6 copy-start.23
  12.3 1.3 copy-start.18
  68.2 2.4 copy-start.4
  70.7 3.0 copy-start.3
  70.7 3.7 copy-start.27
  71.7 234.1 %all-gather.8.cloned.1.call-start = ((), (), s32[]{:S(2)}) async-start(), calls=%async_computation.2 | async-start | bytes 3612672 | tf_op jit(solution)/shard_map/all_gather | solution.py:1545
  78.4 88.2 %copy-start.11 = (f32[768,1024]{0,1:T(8,128)}, f32[768,1024]{0,1:T(8,128)S(1)}, u32[]{:S(2)}) copy-start(f32[768,1024]{0,1:T(8,128)S(1)} %get-tuple-element.117) | copy-start | bytes 9437188
  78.4 0.7 copy-start.24
  79.8 6.7 %copy-start.19 = (bf16[1024,768]{1,0:T(8,128)(2,1)}, bf16[1024,768]{1,0:T(8,128)(2,1)S(1)}, u32[]{:S(2)}) copy-start(bf16[1024,768]{1,0:T(8,128)(2,1)S(1)} %add_convert_fusion.3.refs_3_) | copy-start | bytes 4718596
  86.5 80.1 %copy-start = (bf16[3,1024,768]{2,1,0:T(8,128)(2,1)}, bf16[3,1024,768]{2,1,0:T(8,128)(2,1)S(1)}, u32[]{:S(2)}) copy-start(bf16[3,1024,768]{2,1,0:T(8,128)(2,1)S(1)} %fusion.q_ref.k_ref.v_ref) | copy-start | bytes 14155780
  166.6 3.5 copy-start.2
  170.1 18.2 %copy-start.5 = (f32[1024,768]{1,0:T(8,128)}, f32[1024,768]{1,0:T(8,128)S(1)}, u32[]{:S(2)}) copy-start(f32[1024,768]{1,0:T(8,128)S(1)} %get-tuple-element.119) | copy-start | bytes 9437188
  188.8 1.7 copy-start.7
  207.5 4.2 copy-start.8
  213.2 1.7 copy-start.9
  242.4 5.4 %copy-start.6 = (f32[1024,768]{1,0:T(8,128)S(1)}, f32[1024,768]{1,0:T(8,128)}, u32[]{:S(2)}) copy-start(f32[1024,768]{1,0:T(8,128)} %copy-done.5) | copy-start | bytes 9437188
  242.4 5.4 %copy-start.16 = (f32[1024,768]{1,0:T(8,128)S(1)}, f32[1024,768]{1,0:T(8,128)}, u32[]{:S(2)}) copy-start(f32[1024,768]{1,0:T(8,128)} %get-tuple-element.49) | copy-start | bytes 9437188
  243.9 8.3 %slice-start.2 = ((s8[5898240]{0:T(1024)(128)(4,1)}), s8[4194304]{0:T(1024)(128)(4,1)S(1)}, s32[]{:S(2)}) async-start(s8[5898240]{0:T(1024)(128)(4,1)} %bitcast.78), calls=%async_computation.5 | async-start | bytes 8388608
  247.8 1.9 copy-start.10
  247.8 4.4 slice-start.3
  249.4 1.7 copy-start.13
  249.7 3.9 slice-start
  251.0 1.1 copy-start.20
  252.2 1.5 slice-start.1
  291.1 12.1 %copy-start.1 = (bf16[3,1024,768]{2,1,0:T(8,128)(2,1)}, bf16[3,1024,768]{2,1,0:T(8,128)(2,1)S(1)}, u32[]{:S(2)}) copy-start(bf16[3,1024,768]{2,1,0:T(8,128)(2,1)S(1)} %attention_backward.1.refs_6_) | copy-start | bytes 14155780
  291.1 8.2 %copy-start.12 = (f32[768,1024]{0,1:T(8,128)S(1)}, f32[768,1024]{0,1:T(8,128)}, u32[]{:S(2)}) copy-start(f32[768,1024]{0,1:T(8,128)} %copy-done.11) | copy-start | bytes 9437188
  299.3 1.9 copy-start.14
  313.3 133.8 %copy-start.17 = (f32[96,5462]{1,0:T(8,128)S(1)}, f32[96,5462]{1,0:T(8,128)}, u32[]{:S(2)}) copy-start(f32[96,5462]{1,0:T(8,128)} %param.27) | copy-start | bytes 6292228
  447.1 7.6 %copy-start.25 = (f32[15,96]{1,0:T(8,128)S(1)}, f32[15,96]{1,0:T(8,128)}, u32[]{:S(2)}) copy-start(f32[15,96]{1,0:T(8,128)} %param.32) | copy-start | bytes 17284
  447.1 7.6 %copy-start.26 = (f32[15,96]{1,0:T(8,128)S(1)}, f32[15,96]{1,0:T(8,128)}, u32[]{:S(2)}) copy-start(f32[15,96]{1,0:T(8,128)} %param.31) | copy-start | bytes 17284
  447.1 9.7 %copy-start.15 = (f32[13,96,768]{2,1,0:T(8,128)S(1)}, f32[13,96,768]{2,1,0:T(8,128)}, u32[]{:S(2)}) copy-start(f32[13,96,768]{2,1,0:T(8,128)} %param.22) | copy-start | bytes 11501572
  456.8 8.7 %copy-start.21 = (f32[13,96,768]{2,1,0:T(8,128)S(1)}, f32[13,96,768]{2,1,0:T(8,128)}, u32[]{:S(2)}) copy-start(f32[13,96,768]{2,1,0:T(8,128)} %param.24) | copy-start | bytes 11501572
  456.8 8.7 %copy-start.22 = (f32[13,96,768]{2,1,0:T(8,128)S(1)}, f32[13,96,768]{2,1,0:T(8,128)}, u32[]{:S(2)}) copy-start(f32[13,96,768]{2,1,0:T(8,128)} %param.23) | copy-start | bytes 11501572
Sparse Core Ops, SparseCore 0:
  10.8 162.9 all-gather.3
  175.4 59.3 all-gather.5
  241.5 62.4 all-gather.7
